TPU v7x, 32 devices: a whole 2x2x4 slice. The times are simulated.
32 devices in a mesh: batch: 8 (over z, y), grp: 4 (over x, core).
Axes of the slice: x: 2, y: 2, z: 4, core: 2. Of those that a mesh axis runs over, the one named last changes fastest.
Arguments:
- tokens: bfloat16 [8192, 768], P(('batch', 'grp')), may hold values from -6 to 6
- dest: int32 [8192, 1], P(('batch', 'grp')), may hold values from 0 to 7; in each aligned block of 256 rows (0 to 255, 256 to 511, ...) at most 64 rows name the same one
- seg_ids: int32 [32, 512], P(('batch', 'grp')), may hold values from 0 to 7, never falling along the last dimension, each value on 1 to 128 neighbouring positions
- cot_out: bfloat16 [8192, 768], P(('batch', 'grp')), may hold values from -6 to 6
- cot_align: bfloat16 [8192, 1024], P(('batch', 'grp')), may hold values from -6 to 6
- ln1_gain: bfloat16 [768], replicated, may hold values from 0.5 to 1.5
- ln1_bias: bfloat16 [768], replicated, may hold values from -1 to 1
- w_qkv: bfloat16 [768, 2304], replicated, may hold values from -0.21875 to 0.21875
- q_bias: bfloat16 [768], replicated, may hold values from -1 to 1
- v_bias: bfloat16 [768], replicated, may hold values from -1 to 1
- w_out: bfloat16 [768, 768], replicated, may hold values from -1.75 to 1.75
- out_bias: bfloat16 [768], replicated, may hold values from -1 to 1
- ln2_gain: bfloat16 [768], replicated, may hold values from 0.5 to 1.5
- ln2_bias: bfloat16 [768], replicated, may hold values from -1 to 1
- w_up: bfloat16 [768, 3072], replicated, may hold values from -0.21875 to 0.21875
- up_bias: bfloat16 [3072], replicated, may hold values from -1 to 1
- w_down: bfloat16 [3072, 768], replicated, may hold values from -0.109375 to 0.109375
- down_bias: bfloat16 [768], replicated, may hold values from -1 to 1
- ln3_gain: bfloat16 [768], replicated, may hold values from 0.5 to 1.5
- ln3_bias: bfloat16 [768], replicated, may hold values from -1 to 1
- w_align: bfloat16 [768, 1024], replicated, may hold values from -0.21875 to 0.21875
- align_bias: bfloat16 [1024], replicated, may hold values from -1 to 1
Outputs:
- out_tokens: bfloat16 [8192, 768], P(('batch', 'grp'))
- aligned_tokens: bfloat16 [8192, 1024], P(('batch', 'grp'))
- grad_tokens: bfloat16 [8192, 768], P(('batch', 'grp'))
- grad_ln1_gain: float32 [768], replicated
- grad_ln1_bias: float32 [768], replicated
- grad_w_qkv: float32 [768, 2304], P('batch', 'grp')
- grad_q_bias: float32 [768], replicated
- grad_v_bias: float32 [768], replicated
- grad_w_out: float32 [768, 768], P('batch', 'grp')
- grad_out_bias: float32 [768], replicated
- grad_ln2_gain: float32 [768], replicated
- grad_ln2_bias: float32 [768], replicated
- grad_w_up: float32 [768, 3072], P('batch', 'grp')
- grad_up_bias: float32 [3072], replicated
- grad_w_down: float32 [3072, 768], P('batch', 'grp')
- grad_down_bias: float32 [768], replicated
- grad_ln3_gain: float32 [768], replicated
- grad_ln3_bias: float32 [768], replicated
- grad_w_align: float32 [768, 1024], P('batch', 'grp')
- grad_align_bias: float32 [1024], replicated
Inputs may be any that keep to these rules, and one draw needn't show every extreme that they name: `dest`: within the 256 rows of one device no destination is named by more than 64 rows, a bound that some block reaches. `seg_ids`: along each device's 512 slots the clip numbers never fall; each clip takes 1 to 128 slots and some clip exactly 128.
All inputs are finite; a program needn't handle non-finite values.
Results may differ from a plain program's by a relative error of at most 0.012.
Values may be sent and summed in bfloat16 or wider, within the bound.
No kernel may reach another device: no remote copies, remote signals or barrier semaphores. Data moves between devices by JAX's collectives and lax.ppermute only.
A program may use at most 192 MiB of HBM per device.

v0:
```python
import jax
import jax.numpy as jnp
from jax import lax
from jax.sharding import PartitionSpec as P

H = 12


layer_eps = 1e-06
masked_value = -1e30


def normalize(values, gain_row, shift_row):
    average = jnp.mean(values, axis=-1, keepdims=True)
    centered = values - average
    variance = jnp.mean(centered * centered, axis=-1, keepdims=True)
    return centered * lax.rsqrt(variance + layer_eps) * gain_row + shift_row


def exact_gelu(values):
    return jax.nn.gelu(values, approximate=False)


def row_matmul(left_side, right_side):
    return jnp.dot(left_side, right_side, preferred_element_type=jnp.float32)


def left_transposed(left_side, right_side):
    return lax.dot_general(
        left_side, right_side, (((0,), (0,)), ((), ())), preferred_element_type=jnp.float32
    )


def right_transposed(left_side, right_side):
    return lax.dot_general(
        left_side, right_side, (((1,), (1,)), ((), ())), preferred_element_type=jnp.float32
    )


def column_sum(values):
    return jnp.sum(values.astype(jnp.float32), axis=0)


def tiled_blocks(matrix, row_parts, column_parts):
    rows_total, columns_total = matrix.shape
    shaped = matrix.reshape(
        row_parts, rows_total // row_parts, column_parts, columns_total // column_parts
    )
    shaped = jnp.transpose(shaped, (0, 2, 1, 3))
    return shaped.reshape(
        row_parts * column_parts, rows_total // row_parts, columns_total // column_parts
    )


def per_device(
    tokens,
    dest,
    seg_ids,
    cot_out,
    cot_align,
    ln1_gain,
    ln1_bias,
    w_qkv,
    q_bias,
    v_bias,
    w_out,
    out_bias,
    ln2_gain,
    ln2_bias,
    w_up,
    up_bias,
    w_down,
    down_bias,
    ln3_gain,
    ln3_bias,
    w_align,
    align_bias,
):
    model_width = tokens.shape[1]
    align_width = cot_align.shape[1]
    seq_rows = seg_ids.shape[1]
    peer_count = lax.axis_size("batch")
    group_count = lax.axis_size("grp")
    capacity = seq_rows // peer_count
    head_count = H
    head_size = model_width // head_count
    score_scale = head_size ** (-0.5)
    targets = dest[:, 0]
    onehot = (targets[:, None] == jnp.arange(peer_count, dtype=jnp.int32)[None, :]).astype(
        jnp.int32
    )
    earlier = jnp.cumsum(onehot, axis=0) - onehot
    offset = jnp.sum(earlier * onehot, axis=1)
    slot_index = targets * capacity + offset

    def pack_rows(rows):
        empty = jnp.zeros((seq_rows,) + rows.shape[1:], rows.dtype)
        return empty.at[slot_index].set(rows).reshape((peer_count, capacity) + rows.shape[1:])

    flag_rows = jnp.ones((tokens.shape[0],), jnp.bfloat16)
    recv_rows, recv_grad, recv_align, recv_flag = (
        lax.all_to_all(pack_rows(tokens), "batch", split_axis=0, concat_axis=0, tiled=True),
        lax.all_to_all(pack_rows(cot_out), "batch", split_axis=0, concat_axis=0, tiled=True),
        lax.all_to_all(pack_rows(cot_align), "batch", split_axis=0, concat_axis=0, tiled=True),
        lax.all_to_all(pack_rows(flag_rows), "batch", split_axis=0, concat_axis=0, tiled=True),
    )
    inputs = recv_rows.reshape(seq_rows, model_width).astype(jnp.float32)
    is_live = recv_flag.reshape(seq_rows) > 0.5
    segments = seg_ids[0]
    key_index = jnp.arange(seq_rows, dtype=jnp.int32)
    block_rows = min(512, seq_rows)
    gain_one = ln1_gain.astype(jnp.float32)
    normed_one, norm_one_back = jax.vjp(normalize, inputs, gain_one, ln1_bias.astype(jnp.float32))
    act_one = normed_one.astype(jnp.bfloat16)
    joined = row_matmul(act_one, w_qkv)
    queries = (
        (joined[:, :model_width] + q_bias.astype(jnp.float32))
        .astype(jnp.bfloat16)
        .reshape(seq_rows, head_count, head_size)
    )
    key_rows = (
        joined[:, model_width : 2 * model_width]
        .astype(jnp.bfloat16)
        .reshape(seq_rows, head_count, head_size)
    )
    value_rows = (
        (joined[:, 2 * model_width :] + v_bias.astype(jnp.float32))
        .astype(jnp.bfloat16)
        .reshape(seq_rows, head_count, head_size)
    )

    def block_scores(block_start):
        query_index = block_start + jnp.arange(block_rows, dtype=jnp.int32)
        same_clip = segments[:, None] == segments[None, :]
        usable = is_live[None, :] | (query_index[:, None] == key_index[None, :])
        raw_scores = (
            jnp.einsum("qhd,khd->hqk", queries, key_rows, preferred_element_type=jnp.float32)
            * score_scale
        )
        return jnp.where((same_clip & usable)[None], raw_scores, masked_value)

    block_start = 0
    scores = block_scores(block_start)
    row_max = jnp.max(scores, axis=-1, keepdims=True)
    powered = jnp.exp(scores - row_max)
    denominator = jnp.sum(powered, axis=-1, keepdims=True)
    probs_low = (powered / denominator).astype(jnp.bfloat16)
    context_parts = jnp.einsum(
        "hqk,khd->qhd", probs_low, value_rows, preferred_element_type=jnp.float32
    )
    lse_parts = [row_max + jnp.log(denominator)]
    context = context_parts.reshape(seq_rows, model_width).astype(jnp.bfloat16)
    middle = inputs + row_matmul(context, w_out) + out_bias.astype(jnp.float32)
    normed_two, norm_two_back = jax.vjp(
        normalize, middle, ln2_gain.astype(jnp.float32), ln2_bias.astype(jnp.float32)
    )
    act_two = normed_two.astype(jnp.bfloat16)
    hidden_pre = row_matmul(act_two, w_up) + up_bias.astype(jnp.float32)
    hidden_act, gelu_back = jax.vjp(exact_gelu, hidden_pre)
    hidden_low = hidden_act.astype(jnp.bfloat16)
    result = middle + row_matmul(hidden_low, w_down) + down_bias.astype(jnp.float32)
    normed_three, norm_three_back = jax.vjp(
        normalize, result, ln3_gain.astype(jnp.float32), ln3_bias.astype(jnp.float32)
    )
    act_three = normed_three.astype(jnp.bfloat16)
    aligned = row_matmul(act_three, w_align) + align_bias.astype(jnp.float32)
    grad_aligned = recv_align.reshape(seq_rows, align_width)
    grad_w_align = left_transposed(act_three, grad_aligned)
    grad_align_bias = column_sum(grad_aligned)
    grad_result_part, grad_ln3_gain, grad_ln3_bias = norm_three_back(
        right_transposed(grad_aligned, w_align)
    )
    grad_result = recv_grad.reshape(seq_rows, model_width).astype(jnp.float32) + grad_result_part
    grad_mlp = grad_result.astype(jnp.bfloat16)
    grad_w_down = left_transposed(hidden_low, grad_mlp)
    grad_down_bias = column_sum(grad_mlp)
    (grad_pre,) = gelu_back(right_transposed(grad_mlp, w_down))
    grad_pre_low = grad_pre.astype(jnp.bfloat16)
    grad_w_up = left_transposed(act_two, grad_pre_low)
    grad_up_bias = column_sum(grad_pre_low)
    grad_middle_part, grad_ln2_gain, grad_ln2_bias = norm_two_back(
        right_transposed(grad_pre_low, w_up)
    )
    grad_middle = grad_result + grad_middle_part
    grad_branch = grad_middle.astype(jnp.bfloat16)
    grad_w_out = left_transposed(context, grad_branch)
    grad_out_bias = column_sum(grad_branch)
    grad_context = (
        right_transposed(grad_branch, w_out)
        .astype(jnp.bfloat16)
        .reshape(seq_rows, head_count, head_size)
    )
    grad_keys = jnp.zeros((seq_rows, head_count, head_size), jnp.float32)
    grad_values = jnp.zeros((seq_rows, head_count, head_size), jnp.float32)
    query_parts = []
    for block_number, block_start in enumerate(range(0, seq_rows, block_rows)):
        scores = block_scores(block_start)
        probs = jnp.exp(scores - lse_parts[block_number])
        probs_low = probs.astype(jnp.bfloat16)
        grad_values = jnp.einsum(
            "hqk,qhd->khd", probs_low, grad_context, preferred_element_type=jnp.float32
        )
        grad_probs = jnp.einsum(
            "qhd,khd->hqk", grad_context, value_rows, preferred_element_type=jnp.float32
        )
        inner_sum = jnp.sum(grad_probs * probs, axis=-1, keepdims=True)
        grad_scores = (probs * (grad_probs - inner_sum)).astype(jnp.bfloat16)
        query_parts.append(
            jnp.einsum("hqk,khd->qhd", grad_scores, key_rows, preferred_element_type=jnp.float32)
            * score_scale
        )
        grad_keys = (
            jnp.einsum("hqk,qhd->khd", grad_scores, queries, preferred_element_type=jnp.float32)
            * score_scale
        )
    grad_queries = query_parts[0]
    grad_joined = jnp.concatenate(
        [
            grad_queries.reshape(seq_rows, model_width),
            grad_keys.reshape(seq_rows, model_width),
            grad_values.reshape(seq_rows, model_width),
        ],
        axis=1,
    ).astype(jnp.bfloat16)
    grad_w_qkv = left_transposed(act_one, grad_joined)
    grad_q_bias = column_sum(grad_joined[:, :model_width])
    grad_v_bias = column_sum(grad_joined[:, 2 * model_width :])
    grad_input_part, grad_ln1_gain, grad_ln1_bias = norm_one_back(
        right_transposed(grad_joined, w_qkv)
    )
    grad_input = grad_middle + grad_input_part

    def block_view(rows):
        return rows.reshape((peer_count, capacity) + rows.shape[1:])

    back_result, back_aligned, back_grad = (
        lax.all_to_all(
            block_view(result.astype(jnp.bfloat16)),
            "batch",
            split_axis=0,
            concat_axis=0,
            tiled=True,
        ),
        lax.all_to_all(
            block_view(aligned.astype(jnp.bfloat16)),
            "batch",
            split_axis=0,
            concat_axis=0,
            tiled=True,
        ),
        lax.all_to_all(
            block_view(grad_input.astype(jnp.bfloat16)),
            "batch",
            split_axis=0,
            concat_axis=0,
            tiled=True,
        ),
    )
    out_tokens = back_result.reshape(seq_rows, model_width)[slot_index]
    aligned_tokens = back_aligned.reshape(seq_rows, align_width)[slot_index]
    grad_tokens = back_grad.reshape(seq_rows, model_width)[slot_index]
    (
        sum_ln1_gain,
        sum_ln1_bias,
        sum_q_bias,
        sum_v_bias,
        sum_out_bias,
        sum_ln2_gain,
        sum_ln2_bias,
        sum_up_bias,
        sum_down_bias,
        sum_ln3_gain,
        sum_ln3_bias,
        sum_align_bias,
    ) = lax.psum(
        (
            grad_ln1_gain,
            grad_ln1_bias,
            grad_q_bias,
            grad_v_bias,
            grad_out_bias,
            grad_ln2_gain,
            grad_ln2_bias,
            grad_up_bias,
            grad_down_bias,
            grad_ln3_gain,
            grad_ln3_bias,
            grad_align_bias,
        ),
        ("batch", "grp"),
    )
    block_sums = (
        lax.psum_scatter(
            tiled_blocks(grad_w_qkv, peer_count, group_count),
            ("batch", "grp"),
            scatter_dimension=0,
            tiled=True,
        ),
        lax.psum_scatter(
            tiled_blocks(grad_w_out, peer_count, group_count),
            ("batch", "grp"),
            scatter_dimension=0,
            tiled=True,
        ),
        lax.psum_scatter(
            tiled_blocks(grad_w_up, peer_count, group_count),
            ("batch", "grp"),
            scatter_dimension=0,
            tiled=True,
        ),
        lax.psum_scatter(
            tiled_blocks(grad_w_down, peer_count, group_count),
            ("batch", "grp"),
            scatter_dimension=0,
            tiled=True,
        ),
        lax.psum_scatter(
            tiled_blocks(grad_w_align, peer_count, group_count),
            ("batch", "grp"),
            scatter_dimension=0,
            tiled=True,
        ),
    )
    sum_w_qkv = block_sums[0][0]
    sum_w_out = block_sums[1][0]
    sum_w_up = block_sums[2][0]
    sum_w_down = block_sums[3][0]
    sum_w_align = block_sums[4][0]
    return (
        out_tokens,
        aligned_tokens,
        grad_tokens,
        sum_ln1_gain,
        sum_ln1_bias,
        sum_w_qkv,
        sum_q_bias,
        sum_v_bias,
        sum_w_out,
        sum_out_bias,
        sum_ln2_gain,
        sum_ln2_bias,
        sum_w_up,
        sum_up_bias,
        sum_w_down,
        sum_down_bias,
        sum_ln3_gain,
        sum_ln3_bias,
        sum_w_align,
        sum_align_bias,
    )


def solution(mesh):
    return jax.shard_map(
        per_device,
        mesh=mesh,
        in_specs=(
            P(("batch", "grp"), None),
            P(("batch", "grp"), None),
            P(("batch", "grp"), None),
            P(("batch", "grp"), None),
            P(("batch", "grp"), None),
            P(),
            P(),
            P(),
            P(),
            P(),
            P(),
            P(),
            P(),
            P(),
            P(),
            P(),
            P(),
            P(),
            P(),
            P(),
            P(),
            P(),
        ),
        out_specs=(
            P(("batch", "grp"), None),
            P(("batch", "grp"), None),
            P(("batch", "grp"), None),
            P(),
            P(),
            P("batch", "grp"),
            P(),
            P(),
            P("batch", "grp"),
            P(),
            P(),
            P(),
            P("batch", "grp"),
            P(),
            P("batch", "grp"),
            P(),
            P(),
            P(),
            P("batch", "grp"),
            P(),
        ),
        check_vma=False,
    )
```

profile of v0, /device:TPU:0, one launch (start us, length us, event | category | flops | bytes accessed | tf_op | source)
XLA Modules:
  0.0 800.7 jit_solution(46928050250351384)
XLA Ops:
  11.6 2.2 scatter_custom_fusion.1
  14.4 7.3 all-to-all-start.1
  21.7 3.0 scatter_custom_fusion
  24.7 3.3 all-to-all-done.1
  28.1 4.2 all-to-all-start
  45.7 3.0 scatter_custom_fusion.2
  48.8 3.1 scatter_custom_fusion.3
  54.3 6.3 all-to-all-start.5
  61.9 1.5 fusion.25
  63.5 1.5 fusion.21
  65.1 2.0 fusion.64
  69.5 2.3 copy.90
  71.8 2.3 copy.91
  74.1 2.3 copy.88
  76.5 3.5 fusion.12
  80.0 3.7 fusion
  84.7 4.9 fusion.30
  89.7 2.4 fusion.62
  92.4 20.0 %multiply_convert_fusion.1 = (bf16[512,3072]{1,0:T(8,128)(2,1)S(1)}, f32[512,3072]{1,0:T(8,128)}, f32[512,3072]{1,0:T(8,128)}) fusion(f32[3072]{0:T(1024)S(1)} %copy-done.41, bf16[768,3072]{1,0:T(8,128)(2,1)} %param.36, f32[512,768]{1,0:T(8,128)S(1)} %get-tuple-element.63, f32[768]{0:T(1024)S(1)} %copy-done.50, f32[768]{0:T(1024)S(1)} %copy-done.37, ...), kind=kOutput, calls=%fused_computation.21 | convolution fusion | flops 2521694208 | bytes 22042624 | tf_op jit(solution)/shard_map/dot_general | solution.py:25
  112.5 2.7 fusion.63
  116.6 6.0 all-to-all-start.4
  122.7 4.2 multiply_reduce_fusion.1
  127.0 2.4 fusion.60
  129.4 11.3 %all-to-all-done.4 = bf16[8,64,768]{2,1,0:T(8,128)(2,1)} async-done(((bf16[8,64,768]{2,1,0:T(8,128)(2,1)}), bf16[8,64,768]{2,1,0:T(8,128)(2,1)}, u32[]{:S(2)}, u32[]{:S(2)}) %all-to-all-start.4) | async-done | bytes 786464 | tf_op jit(solution)/shard_map/all_to_all | solution.py:103
  140.7 2.5 convert_reduce_fusion.3
  143.2 9.8 %convert_reduce_fusion = (f32[3072]{0:T(1024)}, bf16[512,3072]{1,0:T(8,128)(2,1)S(1)}) fusion(f32[512,3072]{1,0:T(8,128)} %get-tuple-element.53, f32[512,3072]{1,0:T(8,128)} %get-tuple-element.64, f32[3072]{0:T(1024)S(1)} %copy-done.42, bf16[512,768]{1,0:T(8,128)(2,1)S(1)} %get-tuple-element.45, bf16[3072,768]{1,0:T(8,128)(2,1)} %param.38), kind=kOutput, calls=%fused_computation.18 | convolution fusion | flops 2442654720 | bytes 21258240 | tf_op jit(solution)/shard_map/dot_general | solution.py:35
  153.0 7.0 multiply_reduce_fusion.2
  161.5 3.0 convert_bitcast_fusion
  164.5 2.3 copy.98
  166.8 4.0 fusion.66
  170.9 2.3 copy.97
  174.6 2.4 copy.103
  177.0 2.3 copy.102
  179.3 3.5 convolution_convert_fusion
  182.8 2.3 copy.93
  185.1 4.1 fusion.68
  189.6 13.7 %multiply_reduce_fusion = (f32[12,512]{1,0:T(8,128)S(1)}, f32[12,512,512]{1,2,0:T(8,128)}) fusion(f32[12,512]{1,0:T(8,128)} %log_add_fusion, f32[12,512,512]{1,2,0:T(8,128)} %copy-done.1, pred[512,512]{0,1:T(8,128)(4,1)} %fusion.32, bf16[512,12,64]{0,2,1:T(8,128)(2,1)} %bitcast.196, bf16[512,12,64]{0,2,1:T(8,128)(2,1)} %bitcast.195), kind=kOutput, calls=%fused_computation.8 | convolution fusion | flops 418375680 | bytes 27049984 | tf_op jit(solution)/shard_map/qhd,khd->hqk/dot_general | solution.py:203
  203.4 7.2 multiply_convert_fusion
  211.8 2.9 multiply_convert_fusion.2
  214.7 3.1 fusion.27
  219.3 4.4 fusion.65
  224.4 8.9 %fusion.53 = f32[768,3072]{1,0:T(8,128)} fusion(bf16[512,3072]{1,0:T(8,128)(2,1)} %copy-done.55, f32[512,768]{1,0:T(8,128)} %copy-done.9, f32[768]{0:T(1024)} %convert_element_type.155, f32[768]{0:T(1024)S(1)} %copy-done.39, f32[512]{0:T(512)S(1)} %copy-done.48, f32[512]{0:T(512)S(1)} %broadcast_multiply_fusion.2), kind=kOutput, calls=%fused_computation.129 | convolution fusion | flops 2417885184 | bytes 14166016 | tf_op jit(solution)/shard_map/dot_general | solution.py:29
  233.2 12.5 %reshape.372 = f32[8,96,4,768]{3,2,1,0:T(4,128)} reshape(f32[768,3072]{1,0:T(8,128)} %fusion.53) | data formatting | bytes 18874368 | tf_op jit(solution)/shard_map/reshape | solution.py:46
  245.8 9.0 %copy.99 = f32[8,4,96,768]{3,2,1,0:T(8,128)} copy(f32[8,4,96,768]{3,1,2,0:T(4,128)} %bitcast.179) | data formatting | bytes 18874368 | tf_op jit(solution)/shard_map/transpose | solution.py:49
  255.3 8.4 %fusion.67 = f32[3072,768]{0,1:T(8,128)} fusion(bf16[512,3072]{1,0:T(8,128)(2,1)} %copy-done.54, bf16[512,768]{1,0:T(8,128)(2,1)} %copy-done.18), kind=kOutput, calls=%fused_computation.141 | convolution fusion | flops 2415919104 | bytes 13369344 | tf_op jit(solution)/shard_map/dot_general | solution.py:29
  263.7 5.9 copy.112
  269.6 5.4 copy.101
  275.7 3.0 add_convert_fusion.1
  278.7 28.1 %all_to_all.40 = bf16[8,64,1024]{2,1,0:T(8,128)(2,1)} all-to-all(bf16[8,64,1024]{2,1,0:T(8,128)(2,1)S(1)} %bitcast.210), channel_id=1, replica_groups=mesh['batch'=8,'grp'=4] {'batch'}, dimensions={0} | all-to-all | bytes 2097152 | tf_op jit(solution)/shard_map/all_to_all | solution.py:244
  306.8 4.2 all-to-all-start.2
  311.1 4.8 fusion.57
  315.9 2.1 fusion.22
  318.0 2.6 convert_reduce_fusion.4
  320.5 12.9 %all-to-all-done.2 = bf16[8,64,768]{2,1,0:T(8,128)(2,1)} async-done(((bf16[8,64,768]{2,1,0:T(8,128)(2,1)}), bf16[8,64,768]{2,1,0:T(8,128)(2,1)}, u32[]{:S(2)}, u32[]{:S(2)}) %all-to-all-start.2) | async-done | bytes 786464 | tf_op jit(solution)/shard_map/all_to_all | solution.py:237
  333.4 4.4 all-to-all-start.6
  339.1 1.4 convert_reduce_fusion.1
  340.5 2.3 convert_reduce_fusion.5
  342.7 43.1 %all-reduce = (f32[768]{0:T(1024)}, f32[768]{0:T(1024)}, f32[768]{0:T(1024)}, f32[768]{0:T(1024)}, f32[768]{0:T(1024)}, /*index=5*/f32[768]{0:T(1024)}, f32[768]...) all-reduce(f32[768]{0:T(1024)S(1)} %get-tuple-element.24, ...), channel_id=1, replica_groups=mesh['batch'=8,'grp'=4] {'batch','grp'}, use_global_device_ids=true, to_apply=%region_23.24 | all-reduce | flops 11776 | bytes 94208 | tf_op jit(solution)/shard_map/psum | solution.py:275
  385.8 3.9 gather_fusion.1
  389.7 3.4 gather_fusion
  393.1 3.4 gather_fusion.2
  396.5 114.2 %reduce-scatter.6.cloned.1.call-done = f32[1,96,576]{2,1,0:T(8,128)} async-done(((f32[32,96,576]{2,1,0:T(8,128)}), f32[1,96,576]{2,1,0:T(8,128)}) %reduce-scatter.6.cloned.1.call-update) | async-done | bytes 221200 | tf_op jit(solution)/shard_map/reduce_scatter | solution.py:293
  510.7 142.3 %reduce-scatter.10.cloned.1.call-done = f32[1,96,768]{2,1,0:T(8,128)} async-done(((f32[32,96,768]{2,1,0:T(8,128)}), f32[1,96,768]{2,1,0:T(8,128)}) %reduce-scatter.10.cloned.1.call-update) | async-done | bytes 294928 | tf_op jit(solution)/shard_map/reduce_scatter | solution.py:305
  653.0 141.0 %reduce-scatter.12.cloned.1.call-done = f32[1,384,192]{1,2,0:T(8,128)} async-done(((f32[32,384,192]{1,2,0:T(8,128)}), f32[1,384,192]{1,2,0:T(8,128)}) %reduce-scatter.12.cloned.1.call-update) | async-done | bytes 294928 | tf_op jit(solution)/shard_map/reduce_scatter | solution.py:311
  (188 shorter events, 36.5 us)
Async XLA Ops:
  7.2 57.8 %copy-start = (bf16[768,2304]{1,0:T(8,128)(2,1)S(1)}, bf16[768,2304]{1,0:T(8,128)(2,1)}, u32[]{:S(2)}) copy-start(bf16[768,2304]{1,0:T(8,128)(2,1)} %param.29) | copy-start | bytes 10616836
  8.6 44.7 %copy-start.43 = (s32[1,512]{1,0:T(1,128)S(1)}, s32[1,512]{1,0:T(1,128)}, u32[]{:S(2)}) copy-start(s32[1,512]{1,0:T(1,128)} %param.24) | copy-start | bytes 6148
  11.6 42.7 %copy-start.49 = (s32[256,1]{0,1:T(1,128)}, s32[256,1]{0,1:T(1,128)S(1)}, u32[]{:S(2)}) copy-start(s32[256,1]{0,1:T(1,128)S(1)} %compare_select_fusion) | copy-start | bytes 3076
  14.4 13.7 %all-to-all-start.1 = ((bf16[8,1,64]{2,1,0:T(2,128)(2,1)}), bf16[8,1,64]{2,1,0:T(2,128)(2,1)S(1)}, u32[]{:S(2)}, u32[]{:S(2)}) async-start(bf16[8,1,64]{2,1,0:T(2,128)(2,1)} %all_to_all.32), calls=%async_computation.1 | async-start | bytes 8192 | tf_op jit(solution)/shard_map/all_to_all | solution.py:105
  28.1 26.2 %all-to-all-start = ((bf16[8,64,768]{2,1,0:T(8,128)(2,1)}), bf16[8,64,768]{2,1,0:T(8,128)(2,1)}, u32[]{:S(2)}, u32[]{:S(2)}) async-start(bf16[8,64,768]{2,1,0:T(8,128)(2,1)} %bitcast.206), calls=%async_computation | async-start | bytes 1572864 | tf_op jit(solution)/shard_map/all_to_all | solution.py:102
  33.0 32.0 %copy-start.22 = (f32[768]{0:T(1024)}, f32[768]{0:T(1024)S(1)}, u32[]{:S(2)}) copy-start(f32[768]{0:T(1024)S(1)} %convert_element_type.142) | copy-start | bytes 9220
  54.3 62.3 %all-to-all-start.5 = ((bf16[8,64,1024]{2,1,0:T(8,128)(2,1)}), bf16[8,64,1024]{2,1,0:T(8,128)(2,1)}, u32[]{:S(2)}, u32[]{:S(2)}) async-start(bf16[8,64,1024]{2,1,0:T(8,128)(2,1)} %bitcast.193), calls=%async_computation.5 | async-start | bytes 2097152 | tf_op jit(solution)/shard_map/all_to_all | solution.py:104
  61.9 5.2 copy-start.24
  63.5 3.6 copy-start.28
  63.5 3.6 copy-start.26
  65.0 2.1 copy-start.14
  65.0 3.1 copy-start.35
  65.0 3.0 copy-start.36
  80.0 4.6 copy-start.1
  80.0 4.7 copy-start.19
  83.7 5.9 copy-start.21
  84.7 4.9 copy-start.52
  84.7 4.9 copy-start.53
  89.6 2.8 copy-start.16
  89.6 2.7 copy-start.37
  89.6 2.7 copy-start.41
  89.7 2.7 copy-start.50
  89.7 22.7 %slice-start.3 = ((s8[4718592]{0:T(1024)(128)(4,1)}), s8[4194304]{0:T(1024)(128)(4,1)S(1)}, s32[]{:S(2)}) async-start(s8[4718592]{0:T(1024)(128)(4,1)} %bitcast.223), calls=%async_computation.20 | async-start | bytes 8388608
  92.0 20.4 %copy-start.9 = (f32[512,768]{1,0:T(8,128)}, f32[512,768]{1,0:T(8,128)S(1)}, u32[]{:S(2)}) copy-start(f32[512,768]{1,0:T(8,128)S(1)} %get-tuple-element.63) | copy-start | bytes 4718596
  92.4 20.0 %copy-start.46 = (f32[512]{0:T(512)}, f32[512]{0:T(512)S(1)}, u32[]{:S(2)}) copy-start(f32[512]{0:T(512)S(1)} %fusion.43) | copy-start | bytes 6148
  92.4 20.0 %copy-start.51 = (f32[768]{0:T(1024)S(1)}, f32[768]{0:T(1024)}, u32[]{:S(2)}) copy-start(f32[768]{0:T(1024)} %convert_element_type.159) | copy-start | bytes 9220
  92.4 20.0 %slice-start.4 = ((s8[4718592]{0:T(1024)(128)(4,1)}), s8[524288]{0:T(1024)(128)(4,1)S(1)}, s32[]{:S(2)}) async-start(s8[4718592]{0:T(1024)(128)(4,1)} %bitcast.223), calls=%async_computation.21 | async-start | bytes 1048576
  112.4 2.7 copy-start.54
  116.6 24.1 %all-to-all-start.4 = ((bf16[8,64,768]{2,1,0:T(8,128)(2,1)}), bf16[8,64,768]{2,1,0:T(8,128)(2,1)}, u32[]{:S(2)}, u32[]{:S(2)}) async-start(bf16[8,64,768]{2,1,0:T(8,128)(2,1)} %bitcast.205), calls=%async_computation.4 | async-start | bytes 1572864 | tf_op jit(solution)/shard_map/all_to_all | solution.py:103
  122.6 273.9 %reduce-scatter.8.cloned.1.call-start = ((), (), s32[]{:S(2)}) async-start(), calls=%async_computation.13 | async-start | bytes 3244032 | tf_op jit(solution)/shard_map/reduce_scatter | solution.py:299
  122.7 4.3 copy-start.44
  122.7 4.3 copy-start.8
  122.7 4.3 copy-start.31
  122.7 4.3 copy-start.33
  140.7 2.5 copy-start.42
  143.2 9.8 %copy-start.18 = (bf16[512,768]{1,0:T(8,128)(2,1)}, bf16[512,768]{1,0:T(8,128)(2,1)S(1)}, u32[]{:S(2)}) copy-start(bf16[512,768]{1,0:T(8,128)(2,1)S(1)} %get-tuple-element.45) | copy-start | bytes 2359300
  143.2 9.8 %copy-start.10 = (f32[512,768]{1,0:T(8,128)S(1)}, f32[512,768]{1,0:T(8,128)}, u32[]{:S(2)}) copy-start(f32[512,768]{1,0:T(8,128)} %copy-done.9) | copy-start | bytes 4718596
  143.2 9.8 %copy-start.38 = (f32[768]{0:T(1024)S(1)}, f32[768]{0:T(1024)}, u32[]{:S(2)}) copy-start(f32[768]{0:T(1024)} %convert_element_type.154) | copy-start | bytes 9220
  143.2 9.8 %copy-start.47 = (f32[512]{0:T(512)S(1)}, f32[512]{0:T(512)}, u32[]{:S(2)}) copy-start(f32[512]{0:T(512)} %copy-done.46) | copy-start | bytes 6148
  153.0 7.1 copy-start.55
  170.8 225.7 %reduce-scatter.14.cloned.1.call-start = ((), (), s32[]{:S(2)}) async-start(), calls=%async_computation.16 | async-start | bytes 3244032 | tf_op jit(solution)/shard_map/reduce_scatter | solution.py:317
  189.3 321.5 %reduce-scatter.6.cloned.1.call-start = ((), (), s32[]{:S(2)}) async-start(), calls=%async_computation.12 | async-start | bytes 8110080 | tf_op jit(solution)/shard_map/reduce_scatter | solution.py:293
  189.5 13.8 %slice-start = ((s8[12582912]{0:T(1024)(128)(4,1)}), s8[4194304]{0:T(1024)(128)(4,1)S(1)}, s32[]{:S(2)}) async-start(s8[12582912]{0:T(1024)(128)(4,1)} %bitcast.175), calls=%async_computation.17 | async-start | bytes 8388608
  189.5 13.8 %slice-start.1 = ((s8[12582912]{0:T(1024)(128)(4,1)}), s8[4194304]{0:T(1024)(128)(4,1)S(1)}, s32[]{:S(2)}) async-start(s8[12582912]{0:T(1024)(128)(4,1)} %bitcast.175), calls=%async_computation.18 | async-start | bytes 8388608
  189.5 13.8 %slice-start.2 = ((s8[12582912]{0:T(1024)(128)(4,1)}), s8[4194304]{0:T(1024)(128)(4,1)S(1)}, s32[]{:S(2)}) async-start(s8[12582912]{0:T(1024)(128)(4,1)} %bitcast.175), calls=%async_computation.19 | async-start | bytes 8388608
  189.5 13.8 %copy-start.6 = (pred[512,512]{0,1:T(8,128)(4,1)S(1)}, pred[512,512]{0,1:T(8,128)(4,1)}, u32[]{:S(2)}) copy-start(pred[512,512]{0,1:T(8,128)(4,1)} %fusion.32) | copy-start | bytes 786436
  189.6 13.8 %copy-start.20 = (f32[12,512]{1,0:T(8,128)S(1)}, f32[12,512]{1,0:T(8,128)}, u32[]{:S(2)}) copy-start(f32[12,512]{1,0:T(8,128)} %log_add_fusion) | copy-start | bytes 73732
  203.4 7.2 copy-start.3
  211.7 6.1 copy-start.4
  211.7 2.9 copy-start.12
  214.7 3.2 copy-start.15
  217.8 5.9 copy-start.13
  217.8 1.5 copy-start.17
  223.7 429.3 %reduce-scatter.10.cloned.1.call-start = ((), (), s32[]{:S(2)}) async-start(), calls=%async_computation.14 | async-start | bytes 9732096 | tf_op jit(solution)/shard_map/reduce_scatter | solution.py:305
  254.8 539.1 %reduce-scatter.12.cloned.1.call-start = ((), (), s32[]{:S(2)}) async-start(), calls=%async_computation.15 | async-start | bytes 9732096 | tf_op jit(solution)/shard_map/reduce_scatter | solution.py:311
  278.6 32.4 %copy-start.23 = (f32[768]{0:T(1024)S(1)}, f32[768]{0:T(1024)}, u32[]{:S(2)}) copy-start(f32[768]{0:T(1024)} %copy-done.22) | copy-start | bytes 9220
  278.6 32.4 %copy-start.25 = (f32[512]{0:T(512)S(1)}, f32[512]{0:T(512)}, u32[]{:S(2)}) copy-start(f32[512]{0:T(512)} %copy-done.24) | copy-start | bytes 6148
  306.8 26.6 %all-to-all-start.2 = ((bf16[8,64,768]{2,1,0:T(8,128)(2,1)}), bf16[8,64,768]{2,1,0:T(8,128)(2,1)}, u32[]{:S(2)}, u32[]{:S(2)}) async-start(bf16[8,64,768]{2,1,0:T(8,128)(2,1)} %bitcast.198), calls=%async_computation.2 | async-start | bytes 1572864 | tf_op jit(solution)/shard_map/all_to_all | solution.py:237
  311.0 4.8 copy-start.29
  311.0 4.8 copy-start.27
  315.9 2.1 copy-start.11
  320.5 22.2 %copy-start.30 = (f32[768]{0:T(1024)S(1)}, f32[768]{0:T(1024)}, u32[]{:S(2)}) copy-start(f32[768]{0:T(1024)} %get-tuple-element.44) | copy-start | bytes 9220
  333.4 59.7 %all-to-all-start.6 = ((bf16[8,64,768]{2,1,0:T(8,128)(2,1)}), bf16[8,64,768]{2,1,0:T(8,128)(2,1)}, u32[]{:S(2)}, u32[]{:S(2)}) async-start(bf16[8,64,768]{2,1,0:T(8,128)(2,1)} %bitcast.201), calls=%async_computation.6 | async-start | bytes 1572864 | tf_op jit(solution)/shard_map/all_to_all | solution.py:251
  385.8 3.9 copy-start.40
  (8 other events, 7.3 us)
Sparse Core Ops, SparseCore 0:
  171.0 100.4 reduce-scatter.7
  277.5 105.4 reduce-scatter.13
  389.2 121.4 reduce-scatter.5
  518.0 134.8 reduce-scatter.9
  659.3 134.6 reduce-scatter.11
where the time goes:
time: 809 us; the launch traced here: 801 us
  waiting for transfers between devices  425 us (53%)
  matrix products  118 us (15%)
  local copies, waits for them, and re-layouts  81.8 us (10%)
  blocking collectives  71.2 us (9%)
  other arithmetic  56.2 us (7%)
  starting transfers between devices  33.2 us (4%)
  between operations  14.8 us (2%)
    reduce_scatter x1, waiting for transfers between devices, per_device(): lax.psum_scatter(tiled_blocks(grad_w_up, peer_count, group_count), ('batc...  142 us
    reduce_scatter x1, waiting for transfers between devices, per_device(): lax.psum_scatter(tiled_blocks(grad_w_down, peer_count, group_count), ('ba...  141 us
    reduce_scatter x1, waiting for transfers between devices, per_device(): lax.psum_scatter(tiled_blocks(grad_w_qkv, peer_count, group_count), ('bat...  114 us
    psum x1, blocking collectives, per_device(): lax.psum((grad_ln1_gain, grad_ln1_bias, grad_q_bias, grad_v_bias, grad_ou...  43.1 us
    dot_general x5, matrix products, row_matmul(): return jnp.dot(left_side, right_side, preferred_element_type=jnp.float32)  30 us
    dot_general x5, matrix products, left_transposed(): lax.dot_general(left_side, right_side, (((0,), (0,)), ((), ())), preferre...  29.8 us
    dot_general x5, matrix products, right_transposed(): lax.dot_general(left_side, right_side, (((1,), (1,)), ((), ())), preferre...  29.4 us
    all_to_all x1, blocking collectives, per_device(): lax.all_to_all(block_view(aligned.astype(jnp.bfloat16)), 'batch', split_a...  28.1 us
  transfers between devices with their start and end apart: 11, of which 6 were waited for; matrix products, arithmetic and copies ran while one was open for 27% of the time, Pallas kernels for 0%

commit v1 on v0

v1 whole, which is shorter than its diff:
```python
import functools

import jax
import jax.numpy as jnp
from jax import lax
from jax.experimental import pallas as pl
from jax.experimental.pallas import tpu as pltpu
from jax.sharding import PartitionSpec as P

H = 12
CLIPMAX = 128
EPS = 1e-06
MASKED = -1e30
DEAD = 16.0
AXES = ("batch", "grp")
F32 = jnp.float32
BF16 = jnp.bfloat16
VMEM_BIG = 64_000_000


def dot(a, b):
    return jnp.dot(a, b, preferred_element_type=F32)


def dot_nt(a, b):
    return lax.dot_general(a, b, (((1,), (1,)), ((), ())), preferred_element_type=F32)


def dot_tn(a, b):
    return lax.dot_general(a, b, (((0,), (0,)), ((), ())), preferred_element_type=F32)


def iota(shape, axis):
    return lax.broadcasted_iota(jnp.int32, shape, axis)


def row_loop(total, step, body):
    def one(i, carry):
        body(pl.ds(pl.multiple_of(i * step, step), step))
        return carry

    lax.fori_loop(0, total // step, one, 0)


def norm_parts(v):
    centered = v - jnp.mean(v, axis=-1, keepdims=True)
    rstd = lax.rsqrt(jnp.mean(centered * centered, axis=-1, keepdims=True) + EPS)
    return centered * rstd, rstd


def norm_back(g_out, gain, hat, rstd):
    t = g_out * gain
    return rstd * (
        t - jnp.mean(t, axis=-1, keepdims=True) - hat * jnp.mean(t * hat, axis=-1, keepdims=True)
    )


def slot_column(dest_col, peers, capacity):
    rows = dest_col.shape[0]
    onehot = (dest_col == iota((rows, peers), 1)).astype(F32)
    before = (iota((rows, rows), 0) > iota((rows, rows), 1)).astype(BF16)
    earlier = dot(before, onehot.astype(BF16))
    offset = jnp.sum(earlier * onehot, axis=1, keepdims=True).astype(jnp.int32)
    return dest_col * capacity + offset


def slot_row(dest_row, peers, capacity):
    rows = dest_row.shape[1]
    onehot = (dest_row == iota((peers, rows), 0)).astype(F32)
    before = (iota((rows, rows), 0) < iota((rows, rows), 1)).astype(BF16)
    earlier = dot(onehot.astype(BF16), before)
    offset = jnp.sum(earlier * onehot, axis=0, keepdims=True).astype(jnp.int32)
    return dest_row * capacity + offset


def placing(dest_row, peers, capacity):
    rows = dest_row.shape[1]
    slots = peers * capacity
    return iota((slots, rows), 0) == slot_row(dest_row, peers, capacity)


def fetching(dest_col, peers, capacity):
    rows = dest_col.shape[0]
    slots = peers * capacity
    return (iota((rows, slots), 1) == slot_column(dest_col, peers, capacity)).astype(BF16)


def pack_kernel(peers, capacity, dest_row, tokens, out):
    place = placing(dest_row[...], peers, capacity)
    held = jnp.sum(place.astype(F32), axis=1, keepdims=True)
    rows = dot(place.astype(BF16), tokens[...])
    out[...] = jnp.where(held > 0.5, rows, DEAD).astype(BF16)


def windows(slots):
    block = CLIPMAX
    return [
        (n * block, max(0, (n - 1) * block), min(slots, (n + 2) * block))
        for n in range(slots // block)
    ]


def live_lanes(packed_ref):
    turned = jnp.transpose(packed_ref[:, 0:128].astype(F32))
    return turned[0:1, :] < DEAD * 0.5


def attention_kernel(
    packed, seg_row, seg_col, gain, shift, w_qkv, q_bias, v_bias, ctx, qkv, a1, lse, bias
):
    slots, width = packed.shape
    block = CLIPMAX
    live = live_lanes(packed)
    for n, (start, low, high) in enumerate(windows(slots)):
        rows, keys = (block, high - low), slice(low, high)
        same = seg_col[start : start + block, :] == seg_row[:, keys]
        own = (start + iota(rows, 0)) == (low + iota(rows, 1))
        usable = live[:, keys] | own
        bias[n, :, 0 : high - low] = jnp.where(same & usable, 0.0, MASKED)

    gain_f, shift_f = gain[...].astype(F32), shift[...].astype(F32)

    def norm_rows(r):
        x = packed[r, :].astype(F32)
        x = jnp.where(x[:, 0:1] < DEAD * 0.5, x, 0.0)
        hat, _ = norm_parts(x)
        a1[r, :] = (hat * gain_f + shift_f).astype(BF16)

    row_loop(slots, 32, norm_rows)

    piece = 256
    for part, part_bias in ((0, q_bias), (1, None), (2, v_bias)):
        for c in range(width // piece):
            cols = slice(part * width + c * piece, part * width + (c + 1) * piece)
            made = dot(a1[...], w_qkv[:, cols])
            if part_bias is not None:
                made = made + part_bias[:, c * piece : (c + 1) * piece].astype(F32)
            qkv[:, cols] = made.astype(BF16)

    lse[...] = jnp.zeros_like(lse)
    scale = jnp.asarray(64**-0.5, BF16)

    def pair(hp, carry):
        def lanes(part):
            return pl.ds(pl.multiple_of(part * width + hp * 128, 128), 128)

        first = iota((block, 128), 1) < 64
        for n, (start, low, high) in enumerate(windows(slots)):
            q = qkv[start : start + block, lanes(0)] * scale
            k = qkv[low:high, lanes(1)]
            v = qkv[low:high, lanes(2)]
            mask = bias[n, :, 0 : high - low]
            found = []
            logs = lse[start : start + block, :]
            for side in range(2):
                mine = first if side == 0 else ~first
                s = dot_nt(jnp.where(mine, q, jnp.zeros_like(q)), k) + mask
                top = jnp.max(s, axis=-1, keepdims=True)
                e = jnp.exp(s - top)
                total = jnp.sum(e, axis=-1, keepdims=True)
                p = (e / total).astype(BF16)
                found.append(dot(p, v))
                logs = jnp.where(
                    iota((block, 128), 1) == 2 * hp + side, top + jnp.log(total), logs
                )
            lse[start : start + block, :] = logs
            ctx[start : start + block, lanes(0)] = jnp.where(first, found[0], found[1]).astype(BF16)
        return carry

    lax.fori_loop(0, width // 128, pair, 0)


def attention_back_kernel(
    packed, g_ctx, qkv, a1, lse, seg_row, seg_col, gain, w_qkv,
    g_joined, g_rows, small, bias, lse_t, live_col, gk, gv, acc,
):
    slots, width = packed.shape
    block = CLIPMAX
    live = packed[:, 0:1].astype(F32) < DEAD * 0.5
    for n, (start, low, high) in enumerate(windows(slots)):
        shape, keys = (high - low, block), slice(low, high)
        same = seg_col[keys, :] == seg_row[:, start : start + block]
        own = (low + iota(shape, 0)) == (start + iota(shape, 1))
        usable = live[keys, :] | own
        bias[n, 0 : high - low, :] = jnp.where(same & usable, 0.0, MASKED)
    lse_t[...] = jnp.transpose(lse[...])
    scale = jnp.asarray(64**-0.5, BF16)

    def pair(hp, carry):
        def lanes(part):
            return pl.ds(pl.multiple_of(part * width + hp * 128, 128), 128)

        gk[...] = jnp.zeros_like(gk)
        gv[...] = jnp.zeros_like(gv)
        first = iota((block, 128), 1) < 64
        for n, (start, low, high) in enumerate(windows(slots)):
            here = slice(start, start + block)
            q = qkv[here, lanes(0)] * scale
            g = g_ctx[here, lanes(0)]
            k = qkv[low:high, lanes(1)]
            v = qkv[low:high, lanes(2)]
            mask = bias[n, 0 : high - low, :]
            zero = jnp.zeros_like(q)
            gq, sum_k, sum_v = None, None, None
            for side in range(2):
                mine = first if side == 0 else ~first
                q_own, g_own = jnp.where(mine, q, zero), jnp.where(mine, g, zero)
                s = dot_nt(k, q_own) + mask
                logs = jnp.where(iota((16, block), 0) == 2 * hp + side, lse_t[0:16, here], 0.0)
                p = jnp.exp(s - jnp.sum(logs, axis=0, keepdims=True))
                gp = dot_nt(v, g_own)
                inner = jnp.sum(gp * p, axis=0, keepdims=True)
                gs = (p * (gp - inner)).astype(BF16)
                part_v = dot(p.astype(BF16), g_own)
                part_k = dot(gs, q_own)
                part_q = dot_tn(gs, k)
                if side == 0:
                    gq, sum_k, sum_v = part_q, part_k, part_v
                else:
                    gq, sum_k, sum_v = jnp.where(first, gq, part_q), sum_k + part_k, sum_v + part_v
            gk[low:high, :] += sum_k
            gv[low:high, :] += sum_v
            g_joined[here, lanes(0)] = (gq * (64**-0.5)).astype(BF16)
        g_joined[:, lanes(1)] = gk[...].astype(BF16)
        g_joined[:, lanes(2)] = gv[...].astype(BF16)
        return carry

    lax.fori_loop(0, width // 128, pair, 0)

    acc[...] = dot_nt(g_joined[...], w_qkv[...])
    small[...] = jnp.zeros_like(small)
    gain_f = gain[...].astype(F32)

    def back_rows(r):
        x = packed[r, :].astype(F32)
        x = jnp.where(x[:, 0:1] < DEAD * 0.5, x, 0.0)
        hat, rstd = norm_parts(x)
        g_out = acc[r, :]
        small[0:1, :] += jnp.sum(g_out * hat, axis=0, keepdims=True)
        small[1:2, :] += jnp.sum(g_out, axis=0, keepdims=True)
        small[2:3, :] += jnp.sum(g_joined[r, 0:width].astype(F32), axis=0, keepdims=True)
        small[3:4, :] += jnp.sum(g_joined[r, 2 * width :].astype(F32), axis=0, keepdims=True)
        g_rows[r, :] = norm_back(g_out, gain_f, hat, rstd).astype(BF16)

    row_loop(slots, 32, back_rows)


def erfc_of(z):
    t = 1.0 / (1.0 + 0.5 * z)
    poly = 0.17087277
    for c in (
        -0.82215223, 1.48851587, -1.13520398, 0.27886807, -0.18628806,
        0.09678418, 0.37409196, 1.00002368, -1.26551223,
    ):
        poly = poly * t + c
    return t * jnp.exp(poly - z * z)


def rows_kernel(
    peers, capacity,
    arrived, tokens, dest_col, dest_row, cot_out, cot_align,
    w_out, out_bias, gain2, shift2, w_up, up_bias, w_down, down_bias, gain3, shift3, w_align, align_bias,
    y_out, al_out, g_packed, g_mid, a2, a3, ctx, hidden, gub, gyb, gmb, small,
    slope, mid, hat2, rstd2, acc,
):
    rows, width = tokens.shape
    wide = w_up.shape[1]
    piece = 256
    small[...] = jnp.zeros_like(small)

    ctx[...] = dot(fetching(dest_col[...], peers, capacity), arrived[...]).astype(BF16)
    acc[...] = dot(ctx[...], w_out[...])

    def to_mid(r):
        m = tokens[r, :].astype(F32) + acc[r, :] + out_bias[...].astype(F32)
        mid[r, :] = m
        hat, rstd = norm_parts(m)
        hat2[r, :] = hat
        rstd2[r, :] = jnp.broadcast_to(rstd, (rstd.shape[0], 128))
        a2[r, :] = (hat * gain2[...].astype(F32) + shift2[...].astype(F32)).astype(BF16)

    row_loop(rows, 32, to_mid)

    acc[...] = mid[...] + down_bias[...].astype(F32)

    def up(c, carry):
        cols = pl.ds(pl.multiple_of(c * piece, piece), piece)
        u = dot(a2[...], w_up[:, cols]) + up_bias[:, cols].astype(F32)
        tail = 0.5 * erfc_of(jnp.abs(u) * (0.5**0.5))
        below = jnp.where(u < 0.0, tail, 1.0 - tail)
        bell = jnp.exp(-0.5 * u * u) * 0.3989422804014327
        slope[:, cols] = below + u * bell
        made = (u * below).astype(BF16)
        hidden[:, cols] = made
        acc[...] += dot(made, w_down[cols, :])
        return carry

    lax.fori_loop(0, wide // piece, up, 0)

    def to_a3(r):
        y = acc[r, :]
        y_out[r, :] = y.astype(BF16)
        hat, rstd = norm_parts(y)
        a3[r, :] = (hat * gain3[...].astype(F32) + shift3[...].astype(F32)).astype(BF16)

    row_loop(rows, 32, to_a3)
    al_out[...] = (dot(a3[...], w_align[...]) + align_bias[...].astype(F32)).astype(BF16)
    mid[...] = dot_nt(cot_align[...], w_align[...])

    def back3(r):
        hat, rstd = norm_parts(acc[r, :])
        g_out = mid[r, :]
        gy = cot_out[r, :].astype(F32) + norm_back(g_out, gain3[...].astype(F32), hat, rstd)
        low = gy.astype(BF16)
        g_mid[r, :] = gy
        gyb[r, :] = low
        small[0:1, :] += jnp.sum(g_out * hat, axis=0, keepdims=True)
        small[1:2, :] += jnp.sum(g_out, axis=0, keepdims=True)
        small[2:3, :] += jnp.sum(low.astype(F32), axis=0, keepdims=True)
        for c in range(cot_align.shape[1] // piece):
            at = 10 * width + c * piece
            small[at // width : at // width + 1, at % width : at % width + piece] += jnp.sum(
                cot_align[r, c * piece : (c + 1) * piece].astype(F32), axis=0, keepdims=True
            )

    row_loop(rows, 32, back3)

    acc[...] = jnp.zeros_like(acc)
    for c in range(wide // piece):
        cols = slice(c * piece, (c + 1) * piece)
        low = (slope[:, cols] * dot_nt(gyb[...], w_down[cols, :])).astype(BF16)
        gub[:, cols] = low
        at = 6 * width + c * piece
        small[at // width : at // width + 1, at % width : at % width + piece] = jnp.sum(
            low.astype(F32), axis=0, keepdims=True
        )
        acc[...] += dot_nt(low, w_up[:, cols])

    def back2(r):
        hat, g_out = hat2[r, :], acc[r, :]
        gm = g_mid[r, :] + norm_back(g_out, gain2[...].astype(F32), hat, rstd2[r, 0:1])
        low = gm.astype(BF16)
        g_mid[r, :] = gm
        gmb[r, :] = low
        small[3:4, :] += jnp.sum(g_out * hat, axis=0, keepdims=True)
        small[4:5, :] += jnp.sum(g_out, axis=0, keepdims=True)
        small[5:6, :] += jnp.sum(low.astype(F32), axis=0, keepdims=True)

    row_loop(rows, 32, back2)
    g_ctx = dot_nt(gmb[...], w_out[...]).astype(BF16)
    place = placing(dest_row[...], peers, capacity).astype(BF16)
    g_packed[...] = dot(place, g_ctx).astype(BF16)


def last_kernel(peers, capacity, dest_col, g_mid, arrived, out):
    out[...] = (g_mid[...] + dot(fetching(dest_col[...], peers, capacity), arrived[...])).astype(
        BF16
    )


def turned_rows(order, lhs):
    count = order.shape[0]
    pick = (iota((count, count), 1) == order).astype(BF16)
    return dot_nt(pick, lhs).astype(BF16)


def spare_columns(ref, index, step, load):
    tile = pl.multiple_of((index * step) // 128 * 128, 128)
    part = ref[:, pl.ds(tile, load)].astype(F32)
    return jnp.where((index * step) % 128 == 64, pltpu.roll(part, load - 64, 1), part).astype(BF16)


def grad_a_kernel(ids, order, a2, a3, ctx, gub, da, gmb, keep, send, t2, t3, t1):
    step = pl.program_id(0)
    block = ids[1] ^ relative(step)

    @pl.when(step == 0)
    def _():
        t2[...] = turned_rows(order[...], a2[...])
        t3[...] = turned_rows(order[...], a3[...])
        t1[...] = turned_rows(order[...], ctx[...])

    own = spare_columns(gmb, block, gmb.shape[1] // 4, 256)

    def write(out):
        out[0, :, 0:768] = dot(t2[...], gub[...]).astype(BF16)
        out[0, :, 768:1024] = dot(t3[...], da[...]).astype(BF16)
        out[0, :, 1024:1280] = dot(t1[...], own).astype(BF16)

    pl.when(step < 2)(lambda: write(send))
    pl.when(step >= 2)(lambda: write(keep))


def relative(step):
    return jnp.where(step < 2, 1, 0) + 2 * (step % 2)


def grad_a(ids, order, a2, a3, ctx, gub, da, gmb):
    rows = a2.shape[0]
    whole = lambda shape: pl.BlockSpec(shape, lambda i, ids: (0, 0))
    column = lambda c: pl.BlockSpec((rows, c), lambda i, ids: (0, ids[1] ^ relative(i)))
    half = jax.ShapeDtypeStruct((2, 768, 1280), BF16)
    return pl.pallas_call(
        grad_a_kernel,
        name="grad_up_align_out",
        out_shape=(half, half),
        grid_spec=pltpu.PrefetchScalarGridSpec(
            num_scalar_prefetch=1,
            grid=(4,),
            in_specs=[
                whole((768, 1)),
                whole((rows, 768)),
                whole((rows, 768)),
                whole((rows, 768)),
                column(768),
                column(256),
                whole((rows, 768)),
            ],
            out_specs=(
                pl.BlockSpec((1, 768, 1280), lambda i, ids: (jnp.maximum(i - 2, 0), 0, 0)),
                pl.BlockSpec((1, 768, 1280), lambda i, ids: (jnp.minimum(i, 1), 0, 0)),
            ),
            scratch_shapes=[pltpu.VMEM((768, rows), BF16)] * 3,
        ),
        compiler_params=pltpu.CompilerParams(vmem_limit_bytes=VMEM_BIG),
        cost_estimate=pl.CostEstimate(
            flops=2 * rows * 768 * 5120, bytes_accessed=12_000_000, transcendentals=0
        ),
    )(ids, order, a2, a3, ctx, gub, da, gmb)


def grad_b_kernel(ids, order, gyb, hidden, keep, send, turned):
    @pl.when(pl.program_id(0) == 0)
    def _():
        turned[...] = turned_rows(order[...], gyb[...])

    made = dot(turned[...], hidden[...]).astype(BF16).reshape(4, 192, 384)
    keep[0, :, 0] = made[0:2]
    send[0, :, 0] = made[2:4]


def grad_b(ids, order, gyb, hidden):
    rows = gyb.shape[0]
    half = jax.ShapeDtypeStruct((2, 2, 4, 192, 384), BF16)
    index = lambda i: (i >> 2) + (((i >> 1) & 1) << 1) + ((i & 1) << 2)
    spec = pl.BlockSpec((1, 2, 1, 192, 384), lambda i, ids: (i // 4, 0, i % 4, 0, 0))
    return pl.pallas_call(
        grad_b_kernel,
        name="grad_down",
        out_shape=(half, half),
        grid_spec=pltpu.PrefetchScalarGridSpec(
            num_scalar_prefetch=1,
            grid=(8,),
            in_specs=[
                pl.BlockSpec((768, 1), lambda i, ids: (0, 0)),
                pl.BlockSpec((rows, 768), lambda i, ids: (0, 0)),
                pl.BlockSpec((rows, 384), lambda i, ids: (0, ids[0] ^ index(i))),
            ],
            out_specs=(spec, spec),
            scratch_shapes=[pltpu.VMEM((768, rows), BF16)],
        ),
        compiler_params=pltpu.CompilerParams(vmem_limit_bytes=VMEM_BIG),
        cost_estimate=pl.CostEstimate(
            flops=2 * rows * 768 * 3072, bytes_accessed=8_000_000, transcendentals=0
        ),
    )(ids, order, gyb, hidden)


def grad_c_kernel(ids, order, a1, g_joined, keep_x, send_x, keep_y, send_y, turned):
    step = pl.program_id(0)

    @pl.when(step == 0)
    def _():
        turned[...] = turned_rows(order[...], a1[...])

    own = spare_columns(g_joined, ids[1] ^ relative(step), g_joined.shape[1] // 4, 640)
    made = dot(turned[...], own).astype(BF16)

    def write(out_x, out_y):
        out_x[0] = made[0:384]
        out_y[:, 0] = made[384:768].reshape(2, 192, 640)

    pl.when(step < 2)(lambda: write(send_x, send_y))
    pl.when(step >= 2)(lambda: write(keep_x, keep_y))


def grad_c(ids, order, a1, g_joined):
    rows = a1.shape[0]
    half_x = jax.ShapeDtypeStruct((2, 384, 640), BF16)
    half_y = jax.ShapeDtypeStruct((2, 2, 192, 640), BF16)
    later = lambda i: jnp.maximum(i - 2, 0)
    sooner = lambda i: jnp.minimum(i, 1)
    return pl.pallas_call(
        grad_c_kernel,
        name="grad_qkv",
        out_shape=(half_x, half_x, half_y, half_y),
        grid_spec=pltpu.PrefetchScalarGridSpec(
            num_scalar_prefetch=1,
            grid=(4,),
            in_specs=[
                pl.BlockSpec((768, 1), lambda i, ids: (0, 0)),
                pl.BlockSpec((rows, 768), lambda i, ids: (0, 0)),
                pl.BlockSpec((rows, 2304), lambda i, ids: (0, 0)),
            ],
            out_specs=(
                pl.BlockSpec((1, 384, 640), lambda i, ids: (later(i), 0, 0)),
                pl.BlockSpec((1, 384, 640), lambda i, ids: (sooner(i), 0, 0)),
                pl.BlockSpec((2, 1, 192, 640), lambda i, ids: (0, later(i), 0, 0)),
                pl.BlockSpec((2, 1, 192, 640), lambda i, ids: (0, sooner(i), 0, 0)),
            ),
            scratch_shapes=[pltpu.VMEM((768, rows), BF16)],
        ),
        compiler_params=pltpu.CompilerParams(vmem_limit_bytes=VMEM_BIG),
        cost_estimate=pl.CostEstimate(
            flops=2 * rows * 768 * 2560, bytes_accessed=8_000_000, transcendentals=0
        ),
    )(ids, order, a1, g_joined)


def flip(value, axis, bit, peers, groups):
    pairs = []
    for b in range(peers):
        for g in range(groups):
            other = (b ^ bit, g) if axis == "batch" else (b, g ^ bit)
            pairs.append((b * groups + g, other[0] * groups + other[1]))
    return lax.ppermute(value, AXES, pairs)


STEPS_X = (("grp", 1), ("grp", 2), ("batch", 1), ("batch", 2), ("batch", 4))
STEPS_Y = (("grp", 1), ("batch", 1), ("grp", 2), ("batch", 2), ("batch", 4))


def reduce_blocks(keep, send, steps, peers, groups):
    for axis, bit in steps[:-1]:
        came = flip(send, axis, bit, peers, groups)
        half = keep.shape[0] // 2
        keep, send = keep[:half] + came[:half], keep[half:] + came[half:]
    came = flip(send, *steps[-1], peers, groups)
    return keep[0].astype(F32) + came[0].astype(F32)


def tiled_blocks(matrix, row_parts, column_parts):
    r, c = matrix.shape
    shaped = matrix.reshape(row_parts, r // row_parts, column_parts, c // column_parts)
    return jnp.transpose(shaped, (0, 2, 1, 3)).reshape(
        row_parts * column_parts, r // row_parts, c // column_parts
    )


def scattered(matrix, peers, groups):
    return lax.psum_scatter(
        tiled_blocks(matrix, peers, groups), AXES, scatter_dimension=0, tiled=True
    )[0]


def call(kernel, name, out_shape, scratch, flops, nbytes, *args):
    return pl.pallas_call(
        kernel,
        name=name,
        out_shape=out_shape,
        scratch_shapes=scratch,
        compiler_params=pltpu.CompilerParams(vmem_limit_bytes=VMEM_BIG),
        cost_estimate=pl.CostEstimate(flops=flops, bytes_accessed=nbytes, transcendentals=0),
    )(*args)


def exchange(packed, peers):
    shaped = packed.reshape(peers, packed.shape[0] // peers, packed.shape[1])
    return lax.all_to_all(shaped, "batch", split_axis=0, concat_axis=0, tiled=True).reshape(
        packed.shape
    )


def per_device(
    tokens, dest, seg_ids, cot_out, cot_align,
    ln1_gain, ln1_bias, w_qkv, q_bias, v_bias, w_out, out_bias,
    ln2_gain, ln2_bias, w_up, up_bias, w_down, down_bias,
    ln3_gain, ln3_bias, w_align, align_bias,
):
    rows, width = tokens.shape
    align = cot_align.shape[1]
    wide = w_up.shape[1]
    slots = seg_ids.shape[1]
    peers, groups = lax.axis_size("batch"), lax.axis_size("grp")
    capacity = slots // peers
    dest_row = dest.reshape(1, rows)
    seg_col = seg_ids.reshape(slots, 1)
    line = lambda v: v.reshape(1, v.shape[0])
    shape = jax.ShapeDtypeStruct
    windows_count = slots // CLIPMAX

    packed = call(
        functools.partial(pack_kernel, peers, capacity), "pack_tokens",
        shape((slots, width), BF16), [], 2 * slots * rows * width, 1_500_000,
        dest_row, tokens,
    )
    packed = exchange(packed, peers)

    ctx, qkv, a1, lse = call(
        attention_kernel, "attention",
        (shape((slots, width), BF16), shape((slots, 3 * width), BF16), shape((slots, width), BF16), shape((slots, 128), F32)),
        [pltpu.VMEM((windows_count, CLIPMAX, 3 * CLIPMAX), F32)],
        2 * slots * width * 3 * width + 4 * slots * slots * width, 9_000_000,
        packed, seg_ids, seg_col, line(ln1_gain), line(ln1_bias), w_qkv, line(q_bias), line(v_bias),
    )
    ctx = exchange(ctx, peers)

    low = lambda c: shape((rows, c), BF16)
    y, al, g_packed, g_mid, a2, a3, ctx_rows, hidden, gub, gyb, gmb, small_rows = call(
        functools.partial(rows_kernel, peers, capacity), "rows",
        (low(width), low(align), shape((slots, width), BF16), shape((rows, width), F32), low(width), low(width), low(width),
         low(wide), low(wide), low(width), low(width), shape((16, width), F32)),
        [pltpu.VMEM((rows, wide), F32), pltpu.VMEM((rows, width), F32), pltpu.VMEM((rows, width), F32),
         pltpu.VMEM((rows, 128), F32), pltpu.VMEM((rows, width), F32)],
        8 * rows * width * (width + 2 * wide + align), 22_000_000,
        ctx, tokens, dest, dest_row, cot_out, cot_align,
        w_out, line(out_bias), line(ln2_gain), line(ln2_bias), w_up, line(up_bias), w_down, line(down_bias),
        line(ln3_gain), line(ln3_bias), w_align, line(align_bias),
    )
    g_arrived = exchange(g_packed, peers)

    fast = peers == 8 and groups == 4 and (width, wide, align) == (768, 3072, 1024)
    if fast:
        b, g = lax.axis_index("batch"), lax.axis_index("grp")
        ids = jnp.stack([b, g]).astype(jnp.int32)
        place = jnp.arange(8)
        turn = (place >> 2) + (((place >> 1) & 1) << 1) + ((place & 1) << 2)
        rel_b = b ^ turn
        order_a = (rel_b[:, None] * 96 + jnp.arange(96)[None, :]).reshape(768, 1)
        order_c = (
            rel_b[None, :, None] * 96 + jnp.arange(2)[:, None, None] * 48 + jnp.arange(48)
        ).reshape(768, 1)
        rel_g = g ^ jnp.array([0, 2, 1, 3])
        order_b = (rel_g[:, None] * 192 + jnp.arange(192)[None, :]).reshape(768, 1)
        keep_a, send_a = grad_a(ids, order_a, a2, a3, ctx_rows, gub, cot_align, gmb)
        sum_a = reduce_blocks(
            keep_a.reshape(16, 96, 1280), send_a.reshape(16, 96, 1280), STEPS_X, peers, groups
        )
        keep_b, send_b = grad_b(ids, order_b, gyb, hidden)
        sum_b = reduce_blocks(
            keep_b.reshape(16, 192, 384), send_b.reshape(16, 192, 384), STEPS_Y, peers, groups
        )
        sum_up, sum_align, sum_out = sum_a[:, :768], sum_a[:, 768:1024], sum_a[:, 1024:1216]
        sum_down = sum_b.T
    else:
        left = lambda a, c: lax.dot_general(a, c, (((0,), (0,)), ((), ())), preferred_element_type=F32)
        sum_up, sum_align, sum_out, sum_down = (
            scattered(left(a2, gub), peers, groups),
            scattered(left(a3, cot_align), peers, groups),
            scattered(left(ctx_rows, gmb), peers, groups),
            scattered(left(hidden, gyb), peers, groups),
        )

    g_joined, g_rows, small_slots = call(
        attention_back_kernel, "attention_back",
        (shape((slots, 3 * width), BF16), shape((slots, width), BF16), shape((8, width), F32)),
        [pltpu.VMEM((windows_count, 3 * CLIPMAX, CLIPMAX), F32), pltpu.VMEM((128, slots), F32), pltpu.VMEM((slots, 128), F32),
         pltpu.VMEM((slots, 128), F32), pltpu.VMEM((slots, 128), F32), pltpu.VMEM((slots, width), F32)],
        2 * slots * width * 3 * width + 12 * slots * slots * width, 12_000_000,
        packed, g_arrived, qkv, a1, lse, seg_ids, seg_col, line(ln1_gain), w_qkv,
    )
    g_back = exchange(g_rows, peers)
    if fast:
        keep_x, send_x, keep_y, send_y = grad_c(ids, order_c, a1, g_joined)
        sum_x = reduce_blocks(
            keep_x.reshape(16, 48, 640), send_x.reshape(16, 48, 640), STEPS_X, peers, groups
        )
        sum_y = reduce_blocks(
            keep_y.reshape(16, 48, 640), send_y.reshape(16, 48, 640), STEPS_Y, peers, groups
        )
        sum_qkv = jnp.concatenate([sum_x, sum_y], axis=0)[:, :576]
    else:
        sum_qkv = scattered(left(a1, g_joined), peers, groups)

    grad_tokens = call(
        functools.partial(last_kernel, peers, capacity), "grad_tokens",
        low(width), [], 2 * slots * rows * width, 2_000_000,
        dest, g_mid, g_back,
    )
    total = jnp.concatenate([small_rows, small_slots], axis=0)
    if fast:
        for axis, bit in STEPS_X:
            total = total + flip(total, axis, bit, peers, groups)
    else:
        total = lax.psum(total, AXES)
    sum_up_bias = total[6:10].reshape(4 * width)[:wide]
    sum_align_bias = total[10:12].reshape(2 * width)[:align]
    return (
        y, al, grad_tokens,
        total[16], total[17], sum_qkv, total[18], total[19],
        sum_out, total[5], total[3], total[4],
        sum_up, sum_up_bias, sum_down, total[2],
        total[0], total[1], sum_align, sum_align_bias,
    )


def solution(mesh):
    row, one = P(AXES, None), P()
    matrix = P("batch", "grp")
    return jax.shard_map(
        per_device,
        mesh=mesh,
        in_specs=(row,) * 5 + (one,) * 17,
        out_specs=(
            row, row, row, one, one, matrix, one, one, matrix, one,
            one, one, matrix, one, matrix, one, one, one, matrix, one,
        ),
        check_vma=False,
    )
```

time: 809 us -> 334 us (0.41)
  waiting for transfers between devices: 425 us -> 113 us
  Pallas kernels: 0 us -> 121 us
  matrix products: 118 us -> 0 us
  blocking collectives: 71.2 us -> 0 us
  local copies, waits for them, and re-layouts: 81.8 us -> 30.9 us
  other arithmetic: 56.2 us -> 21.6 us
  between operations: 14.8 us -> 1.03 us
  starting transfers between devices: 33.2 us -> 44.9 us
    reduce_scatter x5 -> x0, waiting for transfers between devices: 397 us -> none  [the longest x1 142 us: per_device(): lax.psum_scatter(tiled_blocks(grad_w_up, peer_count, group_count), ('batc...]
    pallas_call x0 -> x8, Pallas kernels: none -> 121 us  [the longest x5 92.8 us: call(): pl.pallas_call(kernel, name=name, out_shape=out_shape, scratch_shapes=scr...]
    dot_general x21 -> x0, matrix products: 118 us -> none  [the longest x5 30 us: row_matmul(): return jnp.dot(left_side, right_side, preferred_element_type=jnp.float32)]
    ppermute x0 -> x25, waiting for transfers between devices: none -> 69 us  [flip(): return lax.ppermute(value, AXES, pairs)]
    psum x1 -> x0, blocking collectives: 43.1 us -> none  [per_device(): lax.psum((grad_ln1_gain, grad_ln1_bias, grad_q_bias, grad_v_bias, grad_ou...]
    all_to_all x1 -> x0, blocking collectives: 28.1 us -> none  [per_device(): lax.all_to_all(block_view(aligned.astype(jnp.bfloat16)), 'batch', split_a...]
    ppermute x0 -> x25, starting transfers between devices: none -> 26.3 us  [flip(): return lax.ppermute(value, AXES, pairs)]
    convert_element_type x16 -> x0, other arithmetic: 25.1 us -> none  [the longest x1 7.19 us: per_device(): grad_scores = (probs * (grad_probs - inner_sum)).astype(jnp.bfloat16)]
  transfers between devices with their start and end apart: 11 -> 29, of which waited for: 6 -> 12; matrix products, arithmetic and copies ran while one was open for 27% -> 14% of each run, Pallas kernels for 0% -> 15%
where the time goes in v1:
time: 334 us; the launch traced here: 333 us
  Pallas kernels  121 us (36%)
  waiting for transfers between devices  113 us (34%)
  starting transfers between devices  44.9 us (13%)
  local copies, waits for them, and re-layouts  30.9 us (9%)
  other arithmetic  21.6 us (6%)
    pallas_call x5, Pallas kernels, call(): pl.pallas_call(kernel, name=name, out_shape=out_shape, scratch_shapes=scr...  92.8 us
    ppermute x25, waiting for transfers between devices, flip(): return lax.ppermute(value, AXES, pairs)  69 us
    all_to_all x4, waiting for transfers between devices, exchange(): lax.all_to_all(shaped, 'batch', split_axis=0, concat_axis=0, tiled=True)  44.3 us
    ppermute x25, starting transfers between devices, flip(): return lax.ppermute(value, AXES, pairs)  26.3 us
    add x16, other arithmetic, reduce_blocks(): keep, send = (keep[:half] + came[:half], keep[half:] + came[half:])  19.1 us
    all_to_all x4, starting transfers between devices, exchange(): lax.all_to_all(shaped, 'batch', split_axis=0, concat_axis=0, tiled=True)  18.6 us
    slice x4, local copies, waits for them, and re-layouts, reduce_blocks(): keep, send = (keep[:half] + came[:half], keep[half:] + came[half:])  10.8 us
    pallas_call x1, Pallas kernels, grad_a(): pl.pallas_call(grad_a_kernel, name='grad_up_align_out', out_shape=(half,...  9.54 us
  transfers between devices with their start and end apart: 29, of which 12 were waited for; matrix products, arithmetic and copies ran while one was open for 14% of the time, Pallas kernels for 15%

profile of v1, /device:TPU:0, one launch (start us, length us, event | category | flops | bytes accessed | tf_op | source)
XLA Modules:
  0.0 332.5 jit_solution(14428096236145009842)
XLA Ops:
  0.7 2.5 pack_tokens.1
  3.2 7.3 %all-to-all-start = ((bf16[8,64,768]{2,1,0:T(8,128)(2,1)}), bf16[8,64,768]{2,1,0:T(8,128)(2,1)S(1)}, u32[]{:S(2)}, u32[]{:S(2)}) async-start(bf16[8,64,768]{2,1,0:T(8,128)(2,1)} %bitcast.39), calls=%async_computation | async-start | bytes 1572864 | tf_op jit(solution)/shard_map/all_to_all | solution.py:569
  10.5 0.9 copy.45.seg_col
  13.7 17.0 %all-to-all-done = bf16[8,64,768]{2,1,0:T(8,128)(2,1)S(1)} async-done(((bf16[8,64,768]{2,1,0:T(8,128)(2,1)}), bf16[8,64,768]{2,1,0:T(8,128)(2,1)S(1)}, u32[]{:S(2)}, u32[]{:S(2)}) %all-to-all-start) | async-done | bytes 786464 | tf_op jit(solution)/shard_map/all_to_all | solution.py:569
  30.7 0.9 copy-done.8
  31.6 26.3 %attention.1 = (bf16[512,768]{1,0:T(8,128)(2,1)}, bf16[512,2304]{1,0:T(8,128)(2,1)}, bf16[512,768]{1,0:T(8,128)(2,1)}, f32[512,128]{1,0:T(8,128)}) custom-call(bf16[512,768]{1,0:T(8,128)(2,1)} %bitcast.44, s32[1,512]{1,0:T(1,128)} %seg_row.3, s32[512,1]{1,0:T(8,128)} %copy.45.seg_col, bf16[1,768]{1,0:T(2,128)(2,1)} %reshape.293.gain, ...), custom_call_target="tpu_custom_call" | custom-call | flops 2617245696 | bytes 9000000 | tf_op jit(solution)/shard_map/attention/pallas_call | solution.py:557
  57.9 3.7 %all-to-all-start.1 = ((bf16[8,64,768]{2,1,0:T(8,128)(2,1)}), bf16[8,64,768]{2,1,0:T(8,128)(2,1)S(1)}, u32[]{:S(2)}, u32[]{:S(2)}) async-start(bf16[8,64,768]{2,1,0:T(8,128)(2,1)} %bitcast.47), calls=%async_computation.1 | async-start | bytes 1572864 | tf_op jit(solution)/shard_map/all_to_all | solution.py:569
  61.6 0.8 copy.46.dest_col
  67.2 1.0 add.307.order
  68.9 12.9 %all-to-all-done.1 = bf16[8,64,768]{2,1,0:T(8,128)(2,1)S(1)} async-done(((bf16[8,64,768]{2,1,0:T(8,128)(2,1)}), bf16[8,64,768]{2,1,0:T(8,128)(2,1)S(1)}, u32[]{:S(2)}, u32[]{:S(2)}) %all-to-all-start.1) | async-done | bytes 786464 | tf_op jit(solution)/shard_map/all_to_all | solution.py:569
  81.8 1.0 copy-done.9
  82.8 32.9 %rows.1 = (bf16[256,768]{1,0:T(8,128)(2,1)}, bf16[256,1024]{1,0:T(8,128)(2,1)}, bf16[512,768]{1,0:T(8,128)(2,1)}, f32[256,768]{1,0:T(8,128)}, bf16[256,768]{1,0:...) custom-call(bf16[512,768]{1,0:T(8,128)(2,1)} %bitcast.46, ...), custom_call_target="tpu_custom_call" | custom-call | flops 12482248704 | bytes 22000000 | tf_op jit(solution)/shard_map/rows/pallas_call | solution.py:557
  115.7 9.5 %grad_up_align_out.1 = (bf16[2,768,1280]{2,1,0:T(8,128)(2,1)}, bf16[2,768,1280]{2,1,0:T(8,128)(2,1)}) custom-call(s32[2]{0:T(128)} %pad_add_fusion.ids, s32[768,1]{1,0:T(8,128)} %add.307.order, bf16[256,768]{1,0:T(8,128)(2,1)} %get-tuple-element.63.a2, bf16[256,768]{1,0:T(8,128)(2,1)} %get-tuple-element.64.a3, bf16[256,768]{1,0:T(8,128)(2,1)} %get-tuple-element.65.ctx, ...), custom_call_target="tpu_custom_call" | custom-call | flops 2013265920 | bytes 12000000 | tf_op jit(solution)/shard_map/grad_up_align_out/pallas_call | solution.py:403
  125.4 3.8 %all-to-all-start.2 = ((bf16[8,64,768]{2,1,0:T(8,128)(2,1)}), bf16[8,64,768]{2,1,0:T(8,128)(2,1)S(1)}, u32[]{:S(2)}, u32[]{:S(2)}) async-start(bf16[8,64,768]{2,1,0:T(8,128)(2,1)} %bitcast.6), calls=%async_computation.2 | async-start | bytes 1572864 | tf_op jit(solution)/shard_map/all_to_all | solution.py:569
  129.2 0.9 add.306.order
  130.2 1.0 add.308.order
  131.2 4.3 %fusion.7 = (bf16[1,768,1280]{2,1,0:T(8,128)(2,1)}, bf16[1,768,1280]{2,1,0:T(8,128)(2,1)}) fusion(bf16[2,768,1280]{2,1,0:T(8,128)(2,1)} %get-tuple-element.68), kind=kLoop, calls=%fused_computation.66 | loop fusion | bytes 7864320 | tf_op jit(solution)/shard_map/slice | solution.py:537
  135.6 14.4 %all-to-all-done.2 = bf16[8,64,768]{2,1,0:T(8,128)(2,1)S(1)} async-done(((bf16[8,64,768]{2,1,0:T(8,128)(2,1)}), bf16[8,64,768]{2,1,0:T(8,128)(2,1)S(1)}, u32[]{:S(2)}, u32[]{:S(2)}) %all-to-all-start.2) | async-done | bytes 786464 | tf_op jit(solution)/shard_map/all_to_all | solution.py:569
  149.9 0.9 copy-done.10
  150.8 28.2 %attention_back.1 = (bf16[512,2304]{1,0:T(8,128)(2,1)}, bf16[512,768]{1,0:T(8,128)(2,1)}, f32[8,768]{1,0:T(8,128)}) custom-call(bf16[512,768]{1,0:T(8,128)(2,1)} %bitcast.45, bf16[512,768]{1,0:T(8,128)(2,1)} %bitcast.48, bf16[512,2304]{1,0:T(8,128)(2,1)} %get-tuple-element.52.qkv, bf16[512,768]{1,0:T(8,128)(2,1)} %get-tuple-element.53.a1, ...), custom_call_target="tpu_custom_call" | custom-call | flops 4227858432 | bytes 12000000 | tf_op jit(solution)/shard_map/attention_back/pallas_call | solution.py:557
  179.0 0.7 constant_dynamic-update-slice_fusion
  179.8 9.0 %grad_down.1 = (bf16[2,2,4,192,384]{4,3,2,1,0:T(8,128)(2,1)}, bf16[2,2,4,192,384]{4,3,2,1,0:T(8,128)(2,1)}) custom-call(s32[2]{0:T(128)} %pad_add_fusion.ids, s32[768,1]{1,0:T(8,128)} %add.308.order, bf16[256,768]{1,0:T(8,128)(2,1)} %get-tuple-element.70.gyb, bf16[256,3072]{1,0:T(8,128)(2,1)} %get-tuple-element.71.hidden), custom_call_target="tpu_custom_call" | custom-call | flops 1207959552 | bytes 8000000 | tf_op jit(solution)/shard_map/grad_down/pallas_call | solution.py:447
  189.3 1.6 collective-permute-start.1
  190.8 3.4 %fusion.8 = (bf16[1,2,4,192,384]{4,3,2,1,0:T(8,128)(2,1)}, bf16[1,2,4,192,384]{4,3,2,1,0:T(8,128)(2,1)}) fusion(bf16[2,2,4,192,384]{4,3,2,1,0:T(8,128)(2,1)} %get-tuple-element.72), kind=kLoop, calls=%fused_computation.67 | loop fusion | bytes 4718592 | tf_op jit(solution)/shard_map/slice | solution.py:537
  194.3 3.8 %all-to-all-start.3 = ((bf16[8,64,768]{2,1,0:T(8,128)(2,1)}), bf16[8,64,768]{2,1,0:T(8,128)(2,1)S(1)}, u32[]{:S(2)}, u32[]{:S(2)}) async-start(bf16[8,64,768]{2,1,0:T(8,128)(2,1)} %bitcast.8), calls=%async_computation.3 | async-start | bytes 1572864 | tf_op jit(solution)/shard_map/all_to_all | solution.py:569
  198.1 1.9 collective-permute-start.2
  200.0 9.5 %grad_qkv.1 = (bf16[2,384,640]{2,1,0:T(8,128)(2,1)}, bf16[2,384,640]{2,1,0:T(8,128)(2,1)}, bf16[2,2,192,640]{3,2,1,0:T(8,128)(2,1)}, bf16[2,2,192,640]{3,2,1,0:T(8,128)(2,1)}) custom-call(s32[2]{0:T(128)} %pad_add_fusion.ids, s32[768,1]{1,0:T(8,128)} %add.306.order, bf16[512,768]{1,0:T(8,128)(2,1)} %get-tuple-element.53.a1, ...), custom_call_target="tpu_custom_call" | custom-call | flops 2013265920 | bytes 8000000 | tf_op jit(solution)/shard_map/grad_qkv/pallas_call | solution.py:493
  209.5 1.5 collective-permute-start.3
  211.0 2.0 fusion.10
  214.1 5.1 %collective-permute-start.4 = (f32[24,768]{1,0:T(8,128)S(1)}, f32[24,768]{1,0:T(8,128)S(1)}, u32[]{:S(2)}, u32[]{:S(2)}) collective-permute-start(f32[24,768]{1,0:T(8,128)S(1)} %add.247), channel_id=1, source_target_pairs={{0,16},{1,17},{2,18},{3,19},{4,20},{5,21},{6,22},{7,23},{8,24},{9,... | collective-permute-start | bytes 221192 | tf_op jit(solution)/shard_map/ppermute | solution.py:526
  219.2 4.7 %slice_add_fusion.1 = (bf16[8,96,1280]{2,1,0:T(8,128)(2,1)S(1)}, bf16[8,96,1280]{2,1,0:T(8,128)(2,1)}) fusion(bf16[8,96,1280]{2,1,0:T(8,128)(2,1)S(1)} %bitcast.36, bf16[16,96,1280]{2,1,0:T(8,128)(2,1)} %collective-permute-done.15, bf16[8,96,1280]{2,1,0:T(8,128)(2,1)} %bitcast.37), kind=kLoop, calls=%fused_computation.1 | loop fusion | flops 1966080 | bytes 11796480 | tf_op jit(solution)/shard_map/add | solution.py:537
  224.4 1.1 fusion.9
  225.5 0.6 reshape.314
  226.7 0.7 slice_reduce_fusion
  227.4 2.4 slice_add_fusion.11
  229.8 2.4 slice_add_fusion.13
  232.3 1.5 collective-permute-start.6
  233.8 3.3 slice_add_fusion.3
  237.0 1.9 collective-permute-start.21
  238.9 0.9 copy-done.4
  239.8 3.0 grad_tokens.1
  242.7 1.4 slice_add_fusion.19
  244.1 2.2 collective-permute-start.12
  246.3 32.3 %collective-permute-done.6 = bf16[8,48,640]{2,1,0:T(8,128)(2,1)} collective-permute-done((bf16[8,48,640]{2,1,0:T(8,128)(2,1)}, bf16[8,48,640]{2,1,0:T(8,128)(2,1)}, u32[]{:S(2)}, u32[]{:S(2)}) %collective-permute-start.6) | collective-permute-done | bytes 491552 | tf_op jit(solution)/shard_map/ppermute | solution.py:526
  278.6 1.4 slice_add_fusion.21
  280.0 1.0 collective-permute-start.7
  281.2 0.6 collective-permute-start.13
  281.8 1.8 slice_add_fusion.5
  283.6 1.0 collective-permute-start.17
  284.7 1.4 slice_add_fusion.7
  286.7 2.2 collective-permute-done.7
  289.6 0.8 collective-permute-start.14
  290.4 3.5 %collective-permute-done.8 = bf16[2,48,640]{2,1,0:T(8,128)(2,1)S(1)} collective-permute-done((bf16[2,48,640]{2,1,0:T(8,128)(2,1)S(1)}, bf16[2,48,640]{2,1,0:T(8,128)(2,1)S(1)}, u32[]{:S(2)}, u32[]{:S(2)}) %collective-permute-start.8) | collective-permute-done | bytes 122912 | tf_op jit(solution)/shard_map/ppermute | solution.py:526
  294.5 3.5 %collective-permute-done.22 = bf16[4,192,384]{2,1,0:T(8,128)(2,1)S(1)} collective-permute-done((bf16[4,192,384]{2,1,0:T(8,128)(2,1)S(1)}, bf16[4,192,384]{2,1,0:T(8,128)(2,1)S(1)}, u32[]{:S(2)}, u32[]{:S(2)}) %collective-permute-start.22) | collective-permute-done | bytes 589856 | tf_op jit(solution)/shard_map/ppermute | solution.py:526
  298.1 1.6 collective-permute-start.23
  299.7 6.4 %collective-permute-done.17 = bf16[4,96,1280]{2,1,0:T(8,128)(2,1)S(1)} collective-permute-done((bf16[4,96,1280]{2,1,0:T(8,128)(2,1)S(1)}, bf16[4,96,1280]{2,1,0:T(8,128)(2,1)S(1)}, u32[]{:S(2)}, u32[]{:S(2)}) %collective-permute-start.17) | collective-permute-done | bytes 983072 | tf_op jit(solution)/shard_map/ppermute | solution.py:526
  306.2 1.6 collective-permute-start.18
  308.6 11.1 %collective-permute-done.18 = bf16[2,96,1280]{2,1,0:T(8,128)(2,1)S(1)} collective-permute-done((bf16[2,96,1280]{2,1,0:T(8,128)(2,1)S(1)}, bf16[2,96,1280]{2,1,0:T(8,128)(2,1)S(1)}, u32[]{:S(2)}, u32[]{:S(2)}) %collective-permute-start.18) | collective-permute-done | bytes 491552 | tf_op jit(solution)/shard_map/ppermute | solution.py:526
  319.8 0.7 pad_maximum_fusion
  320.5 0.8 add_bitcast_fusion.1
  321.3 9.1 %collective-permute-done.19 = bf16[1,96,1280]{2,1,0:T(8,128)(2,1)S(1)} collective-permute-done((bf16[1,96,1280]{2,1,0:T(8,128)(2,1)S(1)}, bf16[1,96,1280]{2,1,0:T(8,128)(2,1)S(1)}, u32[]{:S(2)}, u32[]{:S(2)}) %collective-permute-start.19) | collective-permute-done | bytes 245792 | tf_op jit(solution)/shard_map/ppermute | solution.py:526
  330.5 0.6 slice.402
  331.1 0.7 slice.406
  331.9 0.6 slice.425
  (122 shorter events, 14.0 us)
Async XLA Ops:
  0.7 9.8 %copy-start.14 = (s32[1,512]{1,0:T(1,128)S(1)}, s32[1,512]{1,0:T(1,128)}, u32[]{:S(2)}) copy-start(s32[1,512]{1,0:T(1,128)} %seg_row.3) | copy-start | bytes 6148
  0.7 10.7 %copy-start.16 = (bf16[768]{0:T(1024)(128)(2,1)S(1)}, bf16[768]{0:T(1024)(128)(2,1)}, u32[]{:S(2)}) copy-start(bf16[768]{0:T(1024)(128)(2,1)} %param.28) | copy-start | bytes 4612
  0.7 11.2 %copy-start.17 = (bf16[768]{0:T(1024)(128)(2,1)S(1)}, bf16[768]{0:T(1024)(128)(2,1)}, u32[]{:S(2)}) copy-start(bf16[768]{0:T(1024)(128)(2,1)} %param.29) | copy-start | bytes 4612
  0.7 11.8 %copy-start.18 = (bf16[768]{0:T(1024)(128)(2,1)S(1)}, bf16[768]{0:T(1024)(128)(2,1)}, u32[]{:S(2)}) copy-start(bf16[768]{0:T(1024)(128)(2,1)} %param.31) | copy-start | bytes 4612
  0.7 12.4 %copy-start.19 = (bf16[768]{0:T(1024)(128)(2,1)S(1)}, bf16[768]{0:T(1024)(128)(2,1)}, u32[]{:S(2)}) copy-start(bf16[768]{0:T(1024)(128)(2,1)} %param.32) | copy-start | bytes 4612
  3.2 27.5 %all-to-all-start = ((bf16[8,64,768]{2,1,0:T(8,128)(2,1)}), bf16[8,64,768]{2,1,0:T(8,128)(2,1)S(1)}, u32[]{:S(2)}, u32[]{:S(2)}) async-start(bf16[8,64,768]{2,1,0:T(8,128)(2,1)} %bitcast.39), calls=%async_computation | async-start | bytes 1572864 | tf_op jit(solution)/shard_map/all_to_all | solution.py:569
  30.7 0.9 copy-start.8
  31.6 30.1 %copy-start.13 = (s32[256,1]{0,1:T(1,128)S(1)}, s32[256,1]{0,1:T(1,128)}, u32[]{:S(2)}) copy-start(s32[256,1]{0,1:T(1,128)} %param.24) | copy-start | bytes 3076
  31.6 30.9 %copy-start.20 = (bf16[768]{0:T(1024)(128)(2,1)S(1)}, bf16[768]{0:T(1024)(128)(2,1)}, u32[]{:S(2)}) copy-start(bf16[768]{0:T(1024)(128)(2,1)} %param.34) | copy-start | bytes 4612
  31.6 31.5 %copy-start.21 = (bf16[768]{0:T(1024)(128)(2,1)S(1)}, bf16[768]{0:T(1024)(128)(2,1)}, u32[]{:S(2)}) copy-start(bf16[768]{0:T(1024)(128)(2,1)} %param.35) | copy-start | bytes 4612
  31.6 32.0 %copy-start.22 = (bf16[768]{0:T(1024)(128)(2,1)S(1)}, bf16[768]{0:T(1024)(128)(2,1)}, u32[]{:S(2)}) copy-start(bf16[768]{0:T(1024)(128)(2,1)} %param.36) | copy-start | bytes 4612
  31.6 32.6 %copy-start.12 = (bf16[3072]{0:T(1024)(128)(2,1)S(1)}, bf16[3072]{0:T(1024)(128)(2,1)}, u32[]{:S(2)}) copy-start(bf16[3072]{0:T(1024)(128)(2,1)} %param.38) | copy-start | bytes 18436
  31.6 33.2 %copy-start.23 = (bf16[768]{0:T(1024)(128)(2,1)S(1)}, bf16[768]{0:T(1024)(128)(2,1)}, u32[]{:S(2)}) copy-start(bf16[768]{0:T(1024)(128)(2,1)} %param.40) | copy-start | bytes 4612
  31.6 33.8 %copy-start.24 = (bf16[768]{0:T(1024)(128)(2,1)S(1)}, bf16[768]{0:T(1024)(128)(2,1)}, u32[]{:S(2)}) copy-start(bf16[768]{0:T(1024)(128)(2,1)} %param.41) | copy-start | bytes 4612
  31.6 34.4 %copy-start.25 = (bf16[768]{0:T(1024)(128)(2,1)S(1)}, bf16[768]{0:T(1024)(128)(2,1)}, u32[]{:S(2)}) copy-start(bf16[768]{0:T(1024)(128)(2,1)} %param.42) | copy-start | bytes 4612
  31.6 34.9 %copy-start.15 = (bf16[1024]{0:T(1024)(128)(2,1)S(1)}, bf16[1024]{0:T(1024)(128)(2,1)}, u32[]{:S(2)}) copy-start(bf16[1024]{0:T(1024)(128)(2,1)} %param.44) | copy-start | bytes 6148
  57.9 23.9 %all-to-all-start.1 = ((bf16[8,64,768]{2,1,0:T(8,128)(2,1)}), bf16[8,64,768]{2,1,0:T(8,128)(2,1)S(1)}, u32[]{:S(2)}, u32[]{:S(2)}) async-start(bf16[8,64,768]{2,1,0:T(8,128)(2,1)} %bitcast.47), calls=%async_computation.1 | async-start | bytes 1572864 | tf_op jit(solution)/shard_map/all_to_all | solution.py:569
  81.8 1.0 copy-start.9
  125.2 4.9 %copy-start.26 = (s32[4]{0:T(128)S(1)}, s32[4]{0:T(128)}, u32[]{:S(2)}) copy-start(s32[4]{0:T(128)} %constant.22.clone) | copy-start | bytes 52
  125.2 6.0 %copy-start.11 = (f32[16,768]{1,0:T(8,128)S(1)}, f32[16,768]{1,0:T(8,128)}, u32[]{:S(2)}) copy-start(f32[16,768]{1,0:T(8,128)} %get-tuple-element.56) | copy-start | bytes 147460
  125.2 94.0 %collective-permute-start.15 = (bf16[16,96,1280]{2,1,0:T(8,128)(2,1)}, bf16[16,96,1280]{2,1,0:T(8,128)(2,1)}, u32[]{:S(2)}, u32[]{:S(2)}) collective-permute-start(bf16[16,96,1280]{2,1,0:T(8,128)(2,1)} %bitcast.52), channel_id=1, source_target_pairs={{0,1},{1,0},{2,3},{3,2},{4,5},{5,4},{6,7},{7,6},{8,9},{9,8},{10,11... | collective-permute-start | bytes 11796488 | tf_op jit(solution)/shard_map/ppermute | solution.py:526
  125.4 24.6 %all-to-all-start.2 = ((bf16[8,64,768]{2,1,0:T(8,128)(2,1)}), bf16[8,64,768]{2,1,0:T(8,128)(2,1)S(1)}, u32[]{:S(2)}, u32[]{:S(2)}) async-start(bf16[8,64,768]{2,1,0:T(8,128)(2,1)} %bitcast.6), calls=%async_computation.2 | async-start | bytes 1572864 | tf_op jit(solution)/shard_map/all_to_all | solution.py:569
  149.9 0.9 copy-start.10
  179.8 9.5 %collective-permute-start = (f32[24,768]{1,0:T(8,128)S(1)}, f32[24,768]{1,0:T(8,128)S(1)}, u32[]{:S(2)}, u32[]{:S(2)}) collective-permute-start(f32[24,768]{1,0:T(8,128)S(1)} %constant_dynamic-update-slice_fusion), channel_id=1, source_target_pairs={{0,1},{1,0},{2,3},{3,2},{4,5},{5,4},{6,7},{7,6},{8,9},{9,8},{10,11... | collective-permute-start | bytes 221192 | tf_op jit(solution)/shard_map/ppermute | solution.py:526
  188.8 45.0 %collective-permute-start.20 = (bf16[16,192,384]{2,1,0:T(8,128)(2,1)}, bf16[16,192,384]{2,1,0:T(8,128)(2,1)}, u32[]{:S(2)}, u32[]{:S(2)}) collective-permute-start(bf16[16,192,384]{2,1,0:T(8,128)(2,1)} %bitcast.53), channel_id=1, source_target_pairs={{0,1},{1,0},{2,3},{3,2},{4,5},{5,4},{6,7},{7,6},{8,9},{9,8},{10,11... | collective-permute-start | bytes 7077896 | tf_op jit(solution)/shard_map/ppermute | solution.py:526
  189.3 8.8 %collective-permute-start.1 = (f32[24,768]{1,0:T(8,128)S(1)}, f32[24,768]{1,0:T(8,128)S(1)}, u32[]{:S(2)}, u32[]{:S(2)}) collective-permute-start(f32[24,768]{1,0:T(8,128)S(1)} %add.244), channel_id=1, source_target_pairs={{0,2},{1,3},{2,0},{3,1},{4,6},{5,7},{6,4},{7,5},{8,10},{9,11},{10,... | collective-permute-start | bytes 221192 | tf_op jit(solution)/shard_map/ppermute | solution.py:526
  194.3 44.6 %all-to-all-start.3 = ((bf16[8,64,768]{2,1,0:T(8,128)(2,1)}), bf16[8,64,768]{2,1,0:T(8,128)(2,1)S(1)}, u32[]{:S(2)}, u32[]{:S(2)}) async-start(bf16[8,64,768]{2,1,0:T(8,128)(2,1)} %bitcast.8), calls=%async_computation.3 | async-start | bytes 1572864 | tf_op jit(solution)/shard_map/all_to_all | solution.py:569
  198.1 11.4 %collective-permute-start.2 = (f32[24,768]{1,0:T(8,128)S(1)}, f32[24,768]{1,0:T(8,128)S(1)}, u32[]{:S(2)}, u32[]{:S(2)}) collective-permute-start(f32[24,768]{1,0:T(8,128)S(1)} %add.245), channel_id=1, source_target_pairs={{0,4},{1,5},{2,6},{3,7},{4,0},{5,1},{6,2},{7,3},{8,12},{9,13},{10,... | collective-permute-start | bytes 221192 | tf_op jit(solution)/shard_map/ppermute | solution.py:526
  209.5 9.8 %copy-start = (bf16[1,768,1280]{2,1,0:T(8,128)(2,1)S(1)}, bf16[1,768,1280]{2,1,0:T(8,128)(2,1)}, u32[]{:S(2)}) copy-start(bf16[1,768,1280]{2,1,0:T(8,128)(2,1)} %get-tuple-element.88) | copy-start | bytes 5898244
  209.5 4.6 %collective-permute-start.3 = (f32[24,768]{1,0:T(8,128)S(1)}, f32[24,768]{1,0:T(8,128)S(1)}, u32[]{:S(2)}, u32[]{:S(2)}) collective-permute-start(f32[24,768]{1,0:T(8,128)S(1)} %add.246), channel_id=1, source_target_pairs={{0,8},{1,9},{2,10},{3,11},{4,12},{5,13},{6,14},{7,15},{8,0},{9,1},... | collective-permute-start | bytes 221192 | tf_op jit(solution)/shard_map/ppermute | solution.py:526
  213.1 14.4 %collective-permute-start.10 = (bf16[16,48,640]{2,1,0:T(8,128)(2,1)}, bf16[16,48,640]{2,1,0:T(8,128)(2,1)}, u32[]{:S(2)}, u32[]{:S(2)}) collective-permute-start(bf16[16,48,640]{2,1,0:T(8,128)(2,1)} %bitcast.55), channel_id=1, source_target_pairs={{0,1},{1,0},{2,3},{3,2},{4,5},{5,4},{6,7},{7,6},{8,9},{9,8},{10,11... | collective-permute-start | bytes 2949128 | tf_op jit(solution)/shard_map/ppermute | solution.py:526
  213.1 16.7 %collective-permute-start.5 = (bf16[16,48,640]{2,1,0:T(8,128)(2,1)}, bf16[16,48,640]{2,1,0:T(8,128)(2,1)}, u32[]{:S(2)}, u32[]{:S(2)}) collective-permute-start(bf16[16,48,640]{2,1,0:T(8,128)(2,1)} %bitcast.54), channel_id=1, source_target_pairs={{0,1},{1,0},{2,3},{3,2},{4,5},{5,4},{6,7},{7,6},{8,9},{9,8},{10,11... | collective-permute-start | bytes 2949128 | tf_op jit(solution)/shard_map/ppermute | solution.py:526
  214.1 11.4 %collective-permute-start.4 = (f32[24,768]{1,0:T(8,128)S(1)}, f32[24,768]{1,0:T(8,128)S(1)}, u32[]{:S(2)}, u32[]{:S(2)}) collective-permute-start(f32[24,768]{1,0:T(8,128)S(1)} %add.247), channel_id=1, source_target_pairs={{0,16},{1,17},{2,18},{3,19},{4,20},{5,21},{6,22},{7,23},{8,24},{9,... | collective-permute-start | bytes 221192 | tf_op jit(solution)/shard_map/ppermute | solution.py:526
  219.2 5.2 %copy-start.7 = (bf16[2,384,640]{2,1,0:T(8,128)(2,1)S(1)}, bf16[2,384,640]{2,1,0:T(8,128)(2,1)}, u32[]{:S(2)}) copy-start(bf16[2,384,640]{2,1,0:T(8,128)(2,1)} %get-tuple-element.59) | copy-start | bytes 2949124
  223.9 57.9 %collective-permute-start.16 = (bf16[8,96,1280]{2,1,0:T(8,128)(2,1)}, bf16[8,96,1280]{2,1,0:T(8,128)(2,1)}, u32[]{:S(2)}, u32[]{:S(2)}) collective-permute-start(bf16[8,96,1280]{2,1,0:T(8,128)(2,1)} %get-tuple-element.87), channel_id=1, source_target_pairs={{0,2},{1,3},{2,0},{3,1},{4,6},{5,7},{6,4},{7,5},{8,10},{9,11},{10,... | collective-permute-start | bytes 5898248 | tf_op jit(solution)/shard_map/ppermute | solution.py:526
  226.1 3.7 %copy-start.5 = (bf16[1,384,640]{2,1,0:T(8,128)(2,1)S(1)}, bf16[1,384,640]{2,1,0:T(8,128)(2,1)}, u32[]{:S(2)}) copy-start(bf16[1,384,640]{2,1,0:T(8,128)(2,1)} %get-tuple-element.104) | copy-start | bytes 1474564
  226.1 3.7 %copy-start.6 = (bf16[1,384,640]{2,1,0:T(8,128)(2,1)S(1)}, bf16[1,384,640]{2,1,0:T(8,128)(2,1)}, u32[]{:S(2)}) copy-start(bf16[1,384,640]{2,1,0:T(8,128)(2,1)} %get-tuple-element.105) | copy-start | bytes 1474564
  229.8 4.0 %copy-start.2 = (bf16[1,2,4,192,384]{4,3,2,1,0:T(8,128)(2,1)S(1)}, bf16[1,2,4,192,384]{4,3,2,1,0:T(8,128)(2,1)}, u32[]{:S(2)}) copy-start(bf16[1,2,4,192,384]{4,3,2,1,0:T(8,128)(2,1)} %get-tuple-element.94) | copy-start | bytes 3538948
  229.8 4.0 %copy-start.3 = (bf16[1,2,4,192,384]{4,3,2,1,0:T(8,128)(2,1)S(1)}, bf16[1,2,4,192,384]{4,3,2,1,0:T(8,128)(2,1)}, u32[]{:S(2)}) copy-start(bf16[1,2,4,192,384]{4,3,2,1,0:T(8,128)(2,1)} %get-tuple-element.95) | copy-start | bytes 3538948
  229.8 13.0 %collective-permute-start.11 = (bf16[8,48,640]{2,1,0:T(8,128)(2,1)}, bf16[8,48,640]{2,1,0:T(8,128)(2,1)}, u32[]{:S(2)}, u32[]{:S(2)}) collective-permute-start(bf16[8,48,640]{2,1,0:T(8,128)(2,1)} %get-tuple-element.109), channel_id=1, source_target_pairs={{0,4},{1,5},{2,6},{3,7},{4,0},{5,1},{6,2},{7,3},{8,12},{9,13},{10,... | collective-permute-start | bytes 1474568 | tf_op jit(solution)/shard_map/ppermute | solution.py:526
  232.3 46.4 %collective-permute-start.6 = (bf16[8,48,640]{2,1,0:T(8,128)(2,1)}, bf16[8,48,640]{2,1,0:T(8,128)(2,1)}, u32[]{:S(2)}, u32[]{:S(2)}) collective-permute-start(bf16[8,48,640]{2,1,0:T(8,128)(2,1)} %get-tuple-element.103), channel_id=1, source_target_pairs={{0,2},{1,3},{2,0},{3,1},{4,6},{5,7},{6,4},{7,5},{8,10},{9,11},{10,... | collective-permute-start | bytes 1474568 | tf_op jit(solution)/shard_map/ppermute | solution.py:526
  237.0 47.6 %collective-permute-start.21 = (bf16[8,192,384]{2,1,0:T(8,128)(2,1)}, bf16[8,192,384]{2,1,0:T(8,128)(2,1)}, u32[]{:S(2)}, u32[]{:S(2)}) collective-permute-start(bf16[8,192,384]{2,1,0:T(8,128)(2,1)} %get-tuple-element.93), channel_id=1, source_target_pairs={{0,4},{1,5},{2,6},{3,7},{4,0},{5,1},{6,2},{7,3},{8,12},{9,13},{10,... | collective-permute-start | bytes 3538952 | tf_op jit(solution)/shard_map/ppermute | solution.py:526
  238.9 0.9 copy-start.4
  244.1 37.0 %collective-permute-start.12 = (bf16[4,48,640]{2,1,0:T(8,128)(2,1)S(1)}, bf16[4,48,640]{2,1,0:T(8,128)(2,1)S(1)}, u32[]{:S(2)}, u32[]{:S(2)}) collective-permute-start(bf16[4,48,640]{2,1,0:T(8,128)(2,1)S(1)} %get-tuple-element.107), channel_id=1, source_target_pairs={{0,2},{1,3},{2,0},{3,1},{4,6},{5,7},{6,4},{7,5},{8,10},{9,11},{10,... | collective-permute-start | bytes 737288 | tf_op jit(solution)/shard_map/ppermute | solution.py:526
  280.0 8.9 %collective-permute-start.7 = (bf16[4,48,640]{2,1,0:T(8,128)(2,1)S(1)}, bf16[4,48,640]{2,1,0:T(8,128)(2,1)S(1)}, u32[]{:S(2)}, u32[]{:S(2)}) collective-permute-start(bf16[4,48,640]{2,1,0:T(8,128)(2,1)S(1)} %get-tuple-element.101), channel_id=1, source_target_pairs={{0,4},{1,5},{2,6},{3,7},{4,0},{5,1},{6,2},{7,3},{8,12},{9,13},{10,... | collective-permute-start | bytes 737288 | tf_op jit(solution)/shard_map/ppermute | solution.py:526
  281.2 8.4 %collective-permute-start.13 = (bf16[2,48,640]{2,1,0:T(8,128)(2,1)S(1)}, bf16[2,48,640]{2,1,0:T(8,128)(2,1)S(1)}, u32[]{:S(2)}, u32[]{:S(2)}) collective-permute-start(bf16[2,48,640]{2,1,0:T(8,128)(2,1)S(1)} %get-tuple-element.115), channel_id=1, source_target_pairs={{0,8},{1,9},{2,10},{3,11},{4,12},{5,13},{6,14},{7,15},{8,0},{9,1},... | collective-permute-start | bytes 368648 | tf_op jit(solution)/shard_map/ppermute | solution.py:526
  281.8 2.8 copy-start.1
  283.6 22.5 %collective-permute-start.17 = (bf16[4,96,1280]{2,1,0:T(8,128)(2,1)S(1)}, bf16[4,96,1280]{2,1,0:T(8,128)(2,1)S(1)}, u32[]{:S(2)}, u32[]{:S(2)}) collective-permute-start(bf16[4,96,1280]{2,1,0:T(8,128)(2,1)S(1)} %get-tuple-element.85), channel_id=1, source_target_pairs={{0,4},{1,5},{2,6},{3,7},{4,0},{5,1},{6,2},{7,3},{8,12},{9,13},{10,... | collective-permute-start | bytes 2949128 | tf_op jit(solution)/shard_map/ppermute | solution.py:526
  286.1 11.9 %collective-permute-start.22 = (bf16[4,192,384]{2,1,0:T(8,128)(2,1)S(1)}, bf16[4,192,384]{2,1,0:T(8,128)(2,1)S(1)}, u32[]{:S(2)}, u32[]{:S(2)}) collective-permute-start(bf16[4,192,384]{2,1,0:T(8,128)(2,1)S(1)} %get-tuple-element.91), channel_id=1, source_target_pairs={{0,2},{1,3},{2,0},{3,1},{4,6},{5,7},{6,4},{7,5},{8,10},{9,11},{10,... | collective-permute-start | bytes 1769480 | tf_op jit(solution)/shard_map/ppermute | solution.py:526
  288.9 4.9 %collective-permute-start.8 = (bf16[2,48,640]{2,1,0:T(8,128)(2,1)S(1)}, bf16[2,48,640]{2,1,0:T(8,128)(2,1)S(1)}, u32[]{:S(2)}, u32[]{:S(2)}) collective-permute-start(bf16[2,48,640]{2,1,0:T(8,128)(2,1)S(1)} %get-tuple-element.113), channel_id=1, source_target_pairs={{0,8},{1,9},{2,10},{3,11},{4,12},{5,13},{6,14},{7,15},{8,0},{9,1},... | collective-permute-start | bytes 368648 | tf_op jit(solution)/shard_map/ppermute | solution.py:526
  289.6 18.3 %collective-permute-start.14 = (bf16[1,48,640]{2,1,0:T(8,128)(2,1)S(1)}, bf16[1,48,640]{2,1,0:T(8,128)(2,1)S(1)}, u32[]{:S(2)}, u32[]{:S(2)}) collective-permute-start(bf16[1,48,640]{2,1,0:T(8,128)(2,1)S(1)} %slice_add_fusion.28), channel_id=1, source_target_pairs={{0,16},{1,17},{2,18},{3,19},{4,20},{5,21},{6,22},{7,23},{8,24},{9,... | collective-permute-start | bytes 184328 | tf_op jit(solution)/shard_map/ppermute | solution.py:526
  293.9 14.0 %collective-permute-start.9 = (bf16[1,48,640]{2,1,0:T(8,128)(2,1)S(1)}, bf16[1,48,640]{2,1,0:T(8,128)(2,1)S(1)}, u32[]{:S(2)}, u32[]{:S(2)}) collective-permute-start(bf16[1,48,640]{2,1,0:T(8,128)(2,1)S(1)} %slice_add_fusion.30), channel_id=1, source_target_pairs={{0,16},{1,17},{2,18},{3,19},{4,20},{5,21},{6,22},{7,23},{8,24},{9,... | collective-permute-start | bytes 184328 | tf_op jit(solution)/shard_map/ppermute | solution.py:526
  298.1 9.9 %collective-permute-start.23 = (bf16[2,192,384]{2,1,0:T(8,128)(2,1)S(1)}, bf16[2,192,384]{2,1,0:T(8,128)(2,1)S(1)}, u32[]{:S(2)}, u32[]{:S(2)}) collective-permute-start(bf16[2,192,384]{2,1,0:T(8,128)(2,1)S(1)} %get-tuple-element.99), channel_id=1, source_target_pairs={{0,8},{1,9},{2,10},{3,11},{4,12},{5,13},{6,14},{7,15},{8,0},{9,1},... | collective-permute-start | bytes 884744 | tf_op jit(solution)/shard_map/ppermute | solution.py:526
  306.2 13.5 %collective-permute-start.18 = (bf16[2,96,1280]{2,1,0:T(8,128)(2,1)S(1)}, bf16[2,96,1280]{2,1,0:T(8,128)(2,1)S(1)}, u32[]{:S(2)}, u32[]{:S(2)}) collective-permute-start(bf16[2,96,1280]{2,1,0:T(8,128)(2,1)S(1)} %get-tuple-element.97), channel_id=1, source_target_pairs={{0,8},{1,9},{2,10},{3,11},{4,12},{5,13},{6,14},{7,15},{8,0},{9,1},... | collective-permute-start | bytes 1474568 | tf_op jit(solution)/shard_map/ppermute | solution.py:526
  308.0 12.5 %collective-permute-start.24 = (bf16[1,192,384]{2,1,0:T(8,128)(2,1)S(1)}, bf16[1,192,384]{2,1,0:T(8,128)(2,1)S(1)}, u32[]{:S(2)}, u32[]{:S(2)}) collective-permute-start(bf16[1,192,384]{2,1,0:T(8,128)(2,1)S(1)} %slice_add_fusion.22), channel_id=1, source_target_pairs={{0,16},{1,17},{2,18},{3,19},{4,20},{5,21},{6,22},{7,23},{8,24},{9,... | collective-permute-start | bytes 442376 | tf_op jit(solution)/shard_map/ppermute | solution.py:526
  319.7 10.7 %collective-permute-start.19 = (bf16[1,96,1280]{2,1,0:T(8,128)(2,1)S(1)}, bf16[1,96,1280]{2,1,0:T(8,128)(2,1)S(1)}, u32[]{:S(2)}, u32[]{:S(2)}) collective-permute-start(bf16[1,96,1280]{2,1,0:T(8,128)(2,1)S(1)} %slice_add_fusion.16), channel_id=1, source_target_pairs={{0,16},{1,17},{2,18},{3,19},{4,20},{5,21},{6,22},{7,23},{8,24},{9,... | collective-permute-start | bytes 737288 | tf_op jit(solution)/shard_map/ppermute | solution.py:526

commit v2 on v1

v2 whole, which is shorter than its diff:
```python
import functools

import jax
import jax.numpy as jnp
from jax import lax
from jax.experimental import pallas as pl
from jax.experimental.pallas import tpu as pltpu
from jax.sharding import PartitionSpec as P

H = 12
CLIPMAX = 128
EPS = 1e-06
MASKED = -1e30
DEAD = 16.0
AXES = ("batch", "grp")
SMEM = pl.BlockSpec(memory_space=pltpu.SMEM)
VMEM = pl.BlockSpec(memory_space=pltpu.VMEM)
HBM = pl.BlockSpec(memory_space=pltpu.HBM)
F32 = jnp.float32
BF16 = jnp.bfloat16


def dot(a, b):
    return jnp.dot(a, b, preferred_element_type=F32)


def dot_nt(a, b):
    return lax.dot_general(a, b, (((1,), (1,)), ((), ())), preferred_element_type=F32)


def dot_tn(a, b):
    return lax.dot_general(a, b, (((0,), (0,)), ((), ())), preferred_element_type=F32)


def iota(shape, axis):
    return lax.broadcasted_iota(jnp.int32, shape, axis)


def row_loop(total, step, body):
    def one(i, carry):
        body(pl.ds(pl.multiple_of(i * step, step), step))
        return carry

    lax.fori_loop(0, total // step, one, 0)


def norm_parts(v):
    centered = v - jnp.mean(v, axis=-1, keepdims=True)
    rstd = lax.rsqrt(jnp.mean(centered * centered, axis=-1, keepdims=True) + EPS)
    return centered * rstd, rstd


def norm_back(g_out, gain, hat, rstd):
    t = g_out * gain
    return rstd * (
        t - jnp.mean(t, axis=-1, keepdims=True) - hat * jnp.mean(t * hat, axis=-1, keepdims=True)
    )


def slot_column(dest_col, me, peers, capacity):
    rows = dest_col.shape[0]
    onehot = (dest_col == iota((rows, peers), 1)).astype(F32)
    before = (iota((rows, rows), 0) > iota((rows, rows), 1)).astype(BF16)
    earlier = dot(before, onehot.astype(BF16))
    offset = jnp.sum(earlier * onehot, axis=1, keepdims=True).astype(jnp.int32)
    return (dest_col ^ me) * capacity + offset


def slot_row(dest_row, me, peers, capacity):
    rows = dest_row.shape[1]
    onehot = (dest_row == iota((peers, rows), 0)).astype(F32)
    before = (iota((rows, rows), 0) < iota((rows, rows), 1)).astype(BF16)
    earlier = dot(onehot.astype(BF16), before)
    offset = jnp.sum(earlier * onehot, axis=0, keepdims=True).astype(jnp.int32)
    return (dest_row ^ me) * capacity + offset


def placing(dest_row, me, peers, capacity):
    shape = (peers * capacity, dest_row.shape[1])
    return iota(shape, 0) == slot_row(dest_row, me, peers, capacity)


def fetching(dest_col, me, peers, capacity):
    shape = (dest_col.shape[0], peers * capacity)
    return (iota(shape, 1) == slot_column(dest_col, me, peers, capacity)).astype(BF16)


def own_index(ids, blocks):
    return ids[0] if blocks > 1 else 0


def block_rows(ids, k, refs):
    size = refs[0].shape[0]
    if len(refs) == 1:
        return pl.ds(0, size)
    return pl.ds(pl.multiple_of((ids[0] ^ k) * size, size), size)


def pack_kernel(peers, capacity, ids, dest_row, tokens, *outs):
    place = placing(dest_row[...], own_index(ids, len(outs)), peers, capacity)
    held = jnp.sum(place.astype(F32), axis=1, keepdims=True)
    rows = jnp.where(held > 0.5, dot(place.astype(BF16), tokens[...]), DEAD).astype(BF16)
    size = outs[0].shape[0]
    for k, out in enumerate(outs):
        out[...] = rows[k * size : (k + 1) * size]


def windows(slots):
    block = CLIPMAX
    return [
        (n * block, max(0, (n - 1) * block), min(slots, (n + 2) * block))
        for n in range(slots // block)
    ]


def write_bias(packed, seg_row, seg_col, bias):
    block = CLIPMAX
    live = packed[:, 0:1].astype(F32) < DEAD * 0.5
    for n, (start, low, high) in enumerate(windows(packed.shape[0])):
        shape, keys = (high - low, block), slice(low, high)
        same = seg_col[keys, :] == seg_row[:, start : start + block]
        own = (low + iota(shape, 0)) == (start + iota(shape, 1))
        made = jnp.where(same & (live[keys, :] | own), 0.0, MASKED)
        bias[n, 0 : high - low, 0:block] = made
        bias[n, 0 : high - low, block:] = made


def stacked(rows):
    first = iota(rows.shape, 1) < 64
    zero = jnp.zeros_like(rows)
    return jnp.concatenate([jnp.where(first, rows, zero), jnp.where(first, zero, rows)], axis=0)


def unstacked(turned):
    half = turned.shape[1] // 2
    upper = iota((128, half), 0) < 64
    return jnp.transpose(jnp.where(upper, turned[:, :half], turned[:, half:]))


def attention_kernel(blocks, ids, *refs):
    arrived, refs = refs[:blocks], refs[blocks:]
    (seg_row, seg_col, gain, shift, w_hbm, q_bias, v_bias,
     ctx, qkv_out, natural_out, a1, lse,
     bias, turned_v, w_qkv, qkv, packed, in_sems, w_sem, out_sems) = refs
    slots, width = packed.shape
    block = CLIPMAX
    fetches = []
    for k, ref in enumerate(arrived):
        to = packed.at[block_rows(ids, k, arrived), :]
        fetches.append(pltpu.make_async_copy(ref, to, in_sems.at[k]))
        fetches[-1].start()
    weights = pltpu.make_async_copy(w_hbm, w_qkv, w_sem)
    weights.start()
    for fetch in fetches:
        fetch.wait()
    keep = pltpu.make_async_copy(packed, natural_out, out_sems.at[0])
    keep.start()
    write_bias(packed, seg_row, seg_col, bias)
    gain_f, shift_f = gain[...].astype(F32), shift[...].astype(F32)

    def norm_rows(r):
        x = packed[r, :].astype(F32)
        x = jnp.where(x[:, 0:1] < DEAD * 0.5, x, 0.0)
        hat, _ = norm_parts(x)
        a1[r, :] = (hat * gain_f + shift_f).astype(BF16)

    row_loop(slots, 32, norm_rows)
    weights.wait()

    piece = 256
    for part, part_bias in ((0, q_bias), (1, None), (2, v_bias)):
        for c in range(width // piece):
            cols = slice(part * width + c * piece, part * width + (c + 1) * piece)
            made = dot(a1[...], w_qkv[:, cols])
            if part_bias is not None:
                made = made + part_bias[:, c * piece : (c + 1) * piece].astype(F32)
            qkv[:, cols] = made.astype(BF16)
    keep_qkv = pltpu.make_async_copy(qkv, qkv_out, out_sems.at[1])
    keep_qkv.start()

    scale = jnp.asarray(64**-0.5, BF16)

    def pair(hp, carry):
        def lanes(part):
            return pl.ds(pl.multiple_of(part * width + hp * 128, 128), 128)

        turned_v[...] = jnp.transpose(qkv[:, lanes(2)].astype(F32)).astype(BF16)
        scores = []
        for n, (start, low, high) in enumerate(windows(slots)):
            q = stacked(qkv[start : start + block, lanes(0)] * scale)
            scores.append(dot_nt(qkv[low:high, lanes(1)], q) + bias[n, 0 : high - low, :])
        for n, (start, low, high) in enumerate(windows(slots)):
            s = scores[n]
            top = jnp.max(s, axis=0, keepdims=True)
            e = jnp.exp(s - top)
            total = jnp.sum(e, axis=0, keepdims=True)
            lse[hp, n : n + 1, :] = top + jnp.log(total)
            found = dot(turned_v[:, low:high], e.astype(BF16)) * (1.0 / total)
            ctx[start : start + block, lanes(0)] = unstacked(found).astype(BF16)
        return carry

    lax.fori_loop(0, width // 128, pair, 0)
    keep.wait()
    keep_qkv.wait()


def attention_back_kernel(shared, traffic, ids, *refs):
    (g_ctx, packed, qkv, lse, a1, seg_row, seg_col, gain, w_hbm), refs = refs[:9], refs[9:]
    (g_rows, g_joined, small), refs = refs[:3], refs[3:]
    if shared:
        (send, turned), refs = refs[:2], refs[2:]
    bias, turned_k, gk, gv, acc, sums, w_qkv, w_sem = refs[:8]
    slots, width = packed.shape
    block = CLIPMAX
    weights = pltpu.make_async_copy(w_hbm, w_qkv, w_sem)
    weights.start()
    traffic.need(1, 6)
    write_bias(packed, seg_row, seg_col, bias)
    traffic.need(2, 3, 4)
    scale = jnp.asarray(64**-0.5, BF16)

    def pair(hp, carry):
        def lanes(part):
            return pl.ds(pl.multiple_of(part * width + hp * 128, 128), 128)

        if shared:
            a1_turned = refs[8]
            a1_turned[lanes(0), :] = jnp.transpose(a1[:, lanes(0)].astype(F32)).astype(BF16)
        turned_k[...] = jnp.transpose(qkv[:, lanes(1)].astype(F32)).astype(BF16)
        gk[...] = jnp.zeros_like(gk)
        gv[...] = jnp.zeros_like(gv)
        first = []
        for n, (start, low, high) in enumerate(windows(slots)):
            here = slice(start, start + block)
            q = stacked(qkv[here, lanes(0)] * scale)
            g = stacked(g_ctx[here, lanes(0)])
            s = dot_nt(qkv[low:high, lanes(1)], q) + bias[n, 0 : high - low, :]
            first.append((q, g, s, dot_nt(qkv[low:high, lanes(2)], g)))
        for n, (start, low, high) in enumerate(windows(slots)):
            here = slice(start, start + block)
            q, g, s, gp = first[n]
            p = jnp.exp(s - lse[hp, n : n + 1, :])
            inner = jnp.sum(gp * p, axis=0, keepdims=True)
            gs = (p * (gp - inner)).astype(BF16)
            gv[low:high, :] += dot(p.astype(BF16), g)
            gk[low:high, :] += dot(gs, q)
            gq = dot(turned_k[:, low:high], gs) * (64**-0.5)
            g_joined[here, lanes(0)] = unstacked(gq).astype(BF16)
        g_joined[:, lanes(1)] = gk[...].astype(BF16)
        g_joined[:, lanes(2)] = gv[...].astype(BF16)
        return carry

    lax.fori_loop(0, width // 128, pair, 0)

    weights.wait()
    acc[...] = dot_nt(g_joined[...], w_qkv[...])
    ones = jnp.ones((8, slots), BF16)
    small[2:3, :] = dot(ones, g_joined[:, 0:width])[0:1]
    small[3:4, :] = dot(ones, g_joined[:, 2 * width :])[0:1]
    small[4:8, :] = jnp.zeros_like(small[4:8, :])
    sums[...] = jnp.zeros_like(sums)
    gain_f = gain[...].astype(F32)

    def back_rows(r):
        x = packed[r, :].astype(F32)
        x = jnp.where(x[:, 0:1] < DEAD * 0.5, x, 0.0)
        hat, rstd = norm_parts(x)
        g_out = acc[r, :]
        sums[0] += folded(g_out * hat)
        sums[1] += folded(g_out)
        g_rows[r, :] = norm_back(g_out, gain_f, hat, rstd).astype(BF16)

    row_loop(slots, 32, back_rows)
    small[0:1, :] = jnp.sum(sums[0], axis=0, keepdims=True)
    small[1:2, :] = jnp.sum(sums[1], axis=0, keepdims=True)
    if shared:
        set_blocks(refs[8], turned, ids, 2, 8, 2)
        joined_products(sender(send, joined_place, JOINED_BASE, (JOINED_ROWS,) * 2), 1, ids, turned, g_joined)
        write_small(small, send, 32 * JOINED_ROWS)


def folded(rows):
    total = rows[0:8]
    for i in range(8, rows.shape[0], 8):
        total = total + rows[i : i + 8]
    return total


def gelu_parts(u):
    bell = jnp.exp(-0.5 * u * u)
    t = 1.0 / (1.0 + 0.305 * jnp.abs(u))
    poly = 0.03669796139001846
    for c in (
        -0.15298233926296234, 0.18570539355278015, -0.03796539083123207, 0.12101536989212036,
        0.10342279821634293, 0.12246651202440262, 0.12163975089788437,
    ):
        poly = poly * t + c
    tail = bell * (poly * t)
    below = jnp.where(u < 0.0, tail, 1.0 - tail)
    return below, below + u * (bell * 0.3989422804014327)


def rows_kernel(peers, capacity, shared, traffic, ids, *refs):
    (whole, tokens, dest_col, dest_row, cot_out, cot_align, out_hbm, out_bias, gain2, shift2, up_hbm, up_bias, down_hbm, down_bias,
     gain3, shift3, align_hbm, align_bias), refs = refs[:18], refs[18:]
    (y_out, al_out, g_packed, g_mid, hidden, gub, a2, a3, ctx, gyb, gmb, small), refs = refs[:12], refs[12:]
    if shared:
        (send_1, send_2, turned_d, turned_3, turned_2, turned_1, small_e), refs = refs[:7], refs[7:]
    (mid, acc, hat2, rstd2, slope, u_a, u_b, h_a, h_b, sums, w_out, w_up, w_down, w_align, sems), refs = refs[:15], refs[15:]
    rows, width = tokens.shape
    wide = hidden.shape[1]
    piece = u_a.shape[1]
    loads = [
        pltpu.make_async_copy(source, to, sems.at[k])
        for k, (source, to) in enumerate(
            ((out_hbm, w_out), (up_hbm, w_up), (down_hbm, w_down), (align_hbm, w_align))
        )
    ]
    for load in loads:
        load.start()

    fetch = fetching(dest_col[...], 0, peers, capacity)
    ctx[...] = dot(fetch, whole[...]).astype(BF16)
    loads[0].wait()
    acc[...] = dot(ctx[...], w_out[...])

    def to_mid(r):
        m = tokens[r, :].astype(F32) + acc[r, :] + out_bias[...].astype(F32)
        hat, rstd = norm_parts(m)
        hat2[r, :] = hat
        rstd2[r, :] = jnp.broadcast_to(rstd, (rstd.shape[0], 128))
        a2[r, :] = (hat * gain2[...].astype(F32) + shift2[...].astype(F32)).astype(BF16)
        acc[r, :] = m + down_bias[...].astype(F32)

    row_loop(rows, 32, to_mid)

    def columns(i):
        return pl.ds(pl.multiple_of(i * piece, piece), piece)

    def up(i):
        return dot(a2[...], w_up[:, columns(i)]) + up_bias[:, columns(i)].astype(F32)

    def bend(i, u_ref, h_ref):
        u = u_ref[...]
        below, bent = gelu_parts(u)
        slope[:, columns(i)] = bent
        made = (u * below).astype(BF16)
        hidden[:, columns(i)] = made
        h_ref[...] = made

    last = wide // piece - 1
    h_b[...] = jnp.zeros_like(h_b)
    loads[1].wait()
    u_a[...] = up(0)
    loads[2].wait()

    def two(j, carry):
        u_b[...] = up(2 * j + 1)
        acc[...] += dot(h_b[...], w_down[columns(jnp.maximum(2 * j - 1, 0)), :])
        bend(2 * j, u_a, h_a)
        u_a[...] = up(jnp.minimum(2 * j + 2, last))
        acc[...] += dot(h_a[...], w_down[columns(2 * j), :])
        bend(2 * j + 1, u_b, h_b)
        return carry

    lax.fori_loop(0, (last + 1) // 2, two, 0)
    acc[...] += dot(h_b[...], w_down[columns(last), :])
    traffic.ready(4)

    def to_a3(r):
        y = acc[r, :]
        y_out[r, :] = y.astype(BF16)
        hat, _ = norm_parts(y)
        a3[r, :] = (hat * gain3[...].astype(F32) + shift3[...].astype(F32)).astype(BF16)

    row_loop(rows, 32, to_a3)
    loads[3].wait()
    al_out[...] = (dot(a3[...], w_align[...]) + align_bias[...].astype(F32)).astype(BF16)
    traffic.ready(0, 1)
    mid[...] = dot_nt(cot_align[...], w_align[...])
    sums[...] = jnp.zeros_like(sums)

    def back3(r):
        hat, rstd = norm_parts(acc[r, :])
        g_out = mid[r, :]
        gy = cot_out[r, :].astype(F32) + norm_back(g_out, gain3[...].astype(F32), hat, rstd)
        g_mid[r, :] = gy
        gyb[r, :] = gy.astype(BF16)
        sums[0] += folded(g_out * hat)
        sums[1] += folded(g_out)

    row_loop(rows, 32, back3)
    small[...] = jnp.zeros_like(small)
    small[0:1, :] = jnp.sum(sums[0], axis=0, keepdims=True)
    small[1:2, :] = jnp.sum(sums[1], axis=0, keepdims=True)
    ones = jnp.ones((8, rows), BF16)
    small[2:3, :] = dot(ones, gyb[...])[0:1]
    align = dot(ones, cot_align[...])[0:1]
    small[3:4, :] = align[:, :width]
    small[4:5, 0 : align.shape[1] - width] = align[:, width:]

    acc[...] = jnp.zeros_like(acc)
    for c in range(wide // 512):
        cols = slice(c * 512, (c + 1) * 512)
        low = (slope[:, cols] * dot_nt(gyb[...], w_down[cols, :])).astype(BF16)
        gub[:, cols] = low
        acc[...] += dot_nt(low, w_up[:, cols])
    traffic.ready(5)
    sums[...] = jnp.zeros_like(sums)

    def back2(r):
        hat, g_out = hat2[r, :], acc[r, :]
        gm = g_mid[r, :] + norm_back(g_out, gain2[...].astype(F32), hat, rstd2[r, 0:1])
        g_mid[r, :] = gm
        gmb[r, :] = gm.astype(BF16)
        sums[0] += folded(g_out * hat)
        sums[1] += folded(g_out)

    row_loop(rows, 32, back2)
    traffic.ready(3, 10)
    g_ctx = dot_nt(gmb[...], w_out[...]).astype(BF16)
    place = placing(dest_row[...], 0, peers, capacity).astype(BF16)
    g_packed[...] = dot(place, g_ctx).astype(BF16)
    traffic.ready(2)
    small[8:9, :] = jnp.sum(sums[0], axis=0, keepdims=True)
    small[9:10, :] = jnp.sum(sums[1], axis=0, keepdims=True)
    small[10:11, :] = dot(ones, gmb[...])[0:1]
    g_up = dot(ones, gub[...])[0:1]
    for c in range(wide // width):
        small[11 + c : 12 + c, :] = g_up[:, c * width : (c + 1) * width]
    if shared:
        (natural,) = refs
        turn(gyb, natural, turned_d, ids, 10, 4)
        traffic.ready(14)
        put = sender(send_1, early_place, (0,), EARLY_PARTS)
        first_products(put, 1, ids, turned_d, hidden)
        small_e[...] = rows_of_small(small[...])
        write_small(small, send_1, SENT_1)
        traffic.ready(12, 18)
        turn(a2, natural, turned_2, ids, 2, 8)
        turn(ctx, natural, turned_1, ids, 2, 8)
        turn(a3, natural, turned_3, ids, 2, 8)
        traffic.ready(15, 16, 17)
        put = sender(send_2, early_place, (None, 0, SENT_BASE), EARLY_PARTS)
        second_products(put, 1, ids, turned_3, turned_2, turned_1, cot_align, gub, gmb)


def last_kernel(peers, capacity, ids, arrived, dest_col, g_mid, out):
    fetch = fetching(dest_col[...], 0, peers, capacity)
    out[...] = (g_mid[...] + dot(fetch, arrived[...])).astype(BF16)


EARLY_PARTS, JOINED_ROWS = (576, 480, 480), 240
SENT_1, SENT_2, SENT_BASE, JOINED_BASE = 16 * 576, 16 * 960, 16 * 480, (0, 16 * 240)


def set_blocks(natural, out, ids, first, count, parts):
    size = natural.shape[0] // count // parts
    for j in range(count):
        for part in range(parts):
            to = part * count * size + ids[first + j] * size
            at = (j * parts + part) * size
            out[pl.ds(pl.multiple_of(to, size), size), :] = natural[at : at + size, :]


def turn(source, natural, out, ids, first, count):
    for c in range(source.shape[1] // 128):
        at = slice(c * 128, (c + 1) * 128)
        natural[at, :] = jnp.transpose(source[:, at].astype(F32)).astype(BF16)
    set_blocks(natural, out, ids, first, count, 1)


def spare_columns(ref, index, step, load):
    tile = pl.multiple_of((index * step) // 128 * 128, 128)
    part = ref[:, pl.ds(tile, load)].astype(F32)
    return jnp.where((index * step) % 128 == 64, pltpu.roll(part, load - 64, 1), part).astype(BF16)


def batch_relative(i):
    return (i >> 2) + (((i >> 1) & 1) << 1) + ((i & 1) << 2)


def joined_place(part, x, i):
    return (x * 8 + i) if part == 0 else (i >> 2) * 8 + x * 4 + (i & 3)


def early_place(part, x, i):
    y, low, high = i >> 2, (i >> 1) & 1, i & 1
    return (x * 8 + low * 4 + y * 2 + high, y * 8 + x * 4 + low * 2 + high, low * 8 + y * 4 + x * 2 + high)[part]


def sender(send, place, bases, sizes):
    def put(part, x, i, at, value):
        at = bases[part] + place(part, x, i) * sizes[part] + at
        send[at : at + value.shape[0], :] = value.astype(BF16)

    return put


def keeper(came, place, bases, sizes, outs):
    def put(part, x, i, at, value):
        where, count = place(part, x, i), value.shape[0]
        start = bases[part] + where * sizes[part] + at
        there = came[start : start + count, :].astype(F32)
        start = (where & 7) * sizes[part] + at
        outs[part][where >> 3][start : start + count, :] = (value + there).astype(BF16)

    return put


def split_small(value):
    high = value.astype(BF16)
    return high, (value - high.astype(F32)).astype(BF16)


def write_small(small, out, base):
    count = small.shape[0]
    for c in range(6):
        high, rest = split_small(small[:, c * 128 : (c + 1) * 128])
        out[base + c * count : base + (c + 1) * count, :] = high
        out[base + (6 + c) * count : base + (7 + c) * count, :] = rest


def both_small(small, came):
    high, rest = split_small(small)
    count = small.shape[0]
    there = came[:count].astype(F32) + came[count:].astype(F32)
    return (high.astype(F32) + rest.astype(F32)) + there


def rows_of_small(small):
    return jnp.concatenate([small[:, c * 128 : (c + 1) * 128] for c in range(6)], axis=0)


def own_columns(ids, core, x, step):
    return pl.ds(pl.multiple_of((ids[1] ^ (core + 2 * x)) * step, 128), step)


def first_products(put, core, ids, turned_d, hidden):
    for i in range(8):
        at = pl.ds(pl.multiple_of((ids[0] ^ batch_relative(i)) * 384, 128), 384)
        made = dot(turned_d[core * 384 : core * 384 + 384, :], hidden[:, at])
        for x in range(2):
            for c in range(3):
                put(0, x, i, c * 192, made[x * 192 : x * 192 + 192, c * 128 : c * 128 + 128])


def second_products(put, core, ids, turned_3, turned_2, turned_1, da, gub, gmb):
    for x in range(2):
        for c in range(3):
            at = pl.ds(pl.multiple_of((ids[1] ^ (core + 2 * x)) * 768 + c * 256, 128), 256)
            made = dot(turned_2[...], gub[:, at])
            for i in range(8):
                for half in range(2):
                    rows = made[i * 96 : i * 96 + 96, half * 128 : half * 128 + 128]
                    slab = 2 * c + half
                    put(1 + slab // 5, x, i, slab % 5 * 96, rows)
        align = dot(turned_3[...], da[:, own_columns(ids, core, x, 256)])
        out = dot(turned_1[...], spare_columns(gmb, ids[1] ^ (core + 2 * x), 192, 256))
        for i in range(8):
            for half in range(2):
                part = slice(half * 128, half * 128 + 128)
                put(2, x, i, 96 + half * 96, align[i * 96 : i * 96 + 96, part])
                put(2, x, i, 288 + half * 96, out[i * 96 : i * 96 + 96, part])


def joined_products(put, core, ids, turned, g_joined):
    for x in range(2):
        own = spare_columns(g_joined, ids[1] ^ (core + 2 * x), 576, 640)
        for c, slabs in ((0, 2), (2, 2), (4, 1)):
            made = dot(turned[...], own[:, c * 128 : (c + slabs) * 128])
            for part in range(2):
                for i in range(8):
                    at = part * 384 + i * 48
                    for k in range(slabs):
                        put(part, x, i, (c + k) * 48, made[at : at + 48, k * 128 : k * 128 + 128])


def first_keep(ids, turned_d, hidden, came, small, keep, send, total):
    put = keeper(came, early_place, (0,), EARLY_PARTS, ((keep, send),))
    first_products(put, 0, ids, turned_d, hidden)
    pass_small(small, came, SENT_1, total, send, 8 * EARLY_PARTS[0])


def second_keep(ids, turned_3, turned_2, turned_1, da, gub, gmb, came, keep_1, send_1, keep_2, send_2):
    outs = (None, (keep_1, send_1), (keep_2, send_2))
    put = keeper(came, early_place, (None, 0, SENT_BASE), EARLY_PARTS, outs)
    second_products(put, 0, ids, turned_3, turned_2, turned_1, da, gub, gmb)


def joined_keep(ids, turned, g_joined, came, small, keep_x, send_x, keep_y, send_y, total):
    outs = ((keep_x, send_x), (keep_y, send_y))
    put = keeper(came, joined_place, JOINED_BASE, (JOINED_ROWS,) * 2, outs)
    joined_products(put, 0, ids, turned, g_joined)
    pass_small_of(rows_of_small(small[...]), came, 32 * JOINED_ROWS, total, send_x, 8 * JOINED_ROWS)


def pass_small(small, came, from_row, total, send, to_row):
    pass_small_of(small[...], came, from_row, total, send, to_row)


def pass_small_of(small, came, from_row, total, send, to_row):
    count = small.shape[0]
    both = both_small(small, came[from_row : from_row + 2 * count, :])
    total[...] = both
    if send is not None:
        high, rest = split_small(both)
        send[to_row : to_row + count, :] = high
        send[to_row + count : to_row + 2 * count, :] = rest


def added(keep, came, at, count):
    rows = slice(at, at + count)
    return keep[rows, :].astype(F32) + came[rows, :].astype(F32)


def step_parts(ids, *refs):
    keeps, cames, small = refs[0:3], refs[3:6], refs[6]
    outs, sends, total = refs[7:10], refs[10:13], refs[13]
    for keep, came, out, send in zip(keeps, cames, outs, sends):
        half = keep.shape[0] // 2
        out[...] = added(keep, came, 0, half).astype(BF16)
        send[0:half, :] = added(keep, came, half, half).astype(BF16)
    half = keeps[0].shape[0] // 2
    pass_small(small, cames[0], 2 * half, total, sends[0], half)


def step_parts_last(ids, *refs):
    keeps, cames, small = refs[0:3], refs[3:6], refs[6]
    outs, send, total = refs[7:10], refs[10], refs[11]
    at = 0
    for keep, came, out in zip(keeps, cames, outs):
        half = keep.shape[0] // 2
        out[...] = added(keep, came, 0, half).astype(BF16)
        send[at : at + half, :] = added(keep, came, half, half).astype(BF16)
        at += half
    pass_small(small, cames[0], keeps[0].shape[0], total, send, at)


def step_apart(ids, keep_x, came_x, keep_y, came_y, *refs):
    small, out_x, send_x, out_y, send_y, total = refs
    half = keep_x.shape[0] // 2
    for keep, came, out, send in ((keep_x, came_x, out_x, send_x), (keep_y, came_y, out_y, send_y)):
        out[...] = added(keep, came, 0, half).astype(BF16)
        send[0:half, :] = added(keep, came, half, half).astype(BF16)
    pass_small(small, came_x, 2 * half, total, send_x, half)


def step_meet(ids, keep_x, came_x, keep_y, came_y, *refs):
    small, out, send, total = refs
    half = keep_x.shape[0] // 2
    for part, (keep, came) in enumerate(((keep_x, came_x), (keep_y, came_y))):
        at = slice(part * half, (part + 1) * half)
        out[at, :] = added(keep, came, 0, half).astype(BF16)
        send[at, :] = added(keep, came, half, half).astype(BF16)
    pass_small(small, came_x, 2 * half, total, send, 2 * half)


def step_joint(ids, keep, came, *refs):
    small, out, send, total = refs
    half = keep.shape[0] // 4
    for part in range(2):
        at = slice(part * half, (part + 1) * half)
        out[at, :] = added(keep, came, part * 2 * half, half).astype(BF16)
        send[at, :] = added(keep, came, part * 2 * half + half, half).astype(BF16)
    pass_small(small, came, 4 * half, total, send, 2 * half)


def small_columns(small, out):
    count = out.shape[0]
    for c in range(6):
        out[:, c * 128 : (c + 1) * 128] = small[c * count : (c + 1) * count]


def early_end(ids, keep_0, keep_1, keep_2, came, small, down, align, up, out, total):
    def block(keep, base, at, count):
        return keep[at : at + count, :].astype(F32) + came[base + at : base + at + count, :].astype(F32)

    for c in range(3):
        down[c * 128 : (c + 1) * 128, :] = jnp.transpose(block(keep_0, 0, c * 192, 192))
    for c in range(5):
        up[:, c * 128 : (c + 1) * 128] = block(keep_1, 576, c * 96, 96)
    up[:, 640:768] = block(keep_2, 1056, 0, 96)
    for c in range(2):
        align[:, c * 128 : (c + 1) * 128] = block(keep_2, 1056, 96 + c * 96, 96)
    out[:, 0:128] = block(keep_2, 1056, 288, 96)
    out[:, 128:192] = block(keep_2, 1056, 384, 96)[:, 0:64]
    count = small.shape[0]
    both = both_small(small[...], came[1536 : 1536 + 2 * count, :])
    small_columns(both, total)


def joined_end(ids, keep, came, small, out, total):
    for part in range(2):
        rows = slice(part * 48, part * 48 + 48)
        for c in range(4):
            out[rows, c * 128 : (c + 1) * 128] = added(keep, came, part * 240 + c * 48, 48)
        out[rows, 512:576] = added(keep, came, part * 240 + 192, 48)[:, 0:64]
    count = small.shape[0]
    both = both_small(small[...], came[480 : 480 + 2 * count, :])
    small_columns(both, total)


def flip(value, axis, bit, peers, groups):
    pairs = []
    for b in range(peers):
        for g in range(groups):
            other = (b ^ bit, g) if axis == "batch" else (b, g ^ bit)
            pairs.append((b * groups + g, other[0] * groups + other[1]))
    return lax.ppermute(value, AXES, pairs)


def tie(value, *others):
    return lax.optimization_barrier((value,) + others)[0]


def tiled_blocks(matrix, row_parts, column_parts):
    r, c = matrix.shape
    shaped = matrix.reshape(row_parts, r // row_parts, column_parts, c // column_parts)
    return jnp.transpose(shaped, (0, 2, 1, 3)).reshape(
        row_parts * column_parts, r // row_parts, c // column_parts
    )


def scattered(left, right, peers, groups):
    matrix = lax.dot_general(left, right, (((0,), (0,)), ((), ())), preferred_element_type=F32)
    return lax.psum_scatter(
        tiled_blocks(matrix, peers, groups), AXES, scatter_dimension=0, tiled=True
    )[0]


class Traffic:
    def __init__(self, loads, flushes):
        self.loads, self.flushes, self.left = loads, flushes, {}

    def need(self, *which):
        for k in which:
            copy = self.loads.pop(k, None)
            if copy is not None:
                copy.wait()

    def ready(self, *which):
        for k in which:
            if k in self.flushes:
                self.left[k] = self.flushes.pop(k)
                self.left[k].start()

    def finish(self):
        self.need(*list(self.loads))
        self.ready(*list(self.flushes))
        for copy in self.left.values():
            copy.wait()


def call(kernel, name, grant, out_shape, scratch, ids, *args, far=(), kept=(), load=(), flush=(), lazy=False, cost=0.001):
    n_in, n_out, n_scratch = len(args), len(out_shape), len(scratch)
    in_hbm, out_hbm = set(far) | set(load), {-1 - k for k in far} | set(flush)
    outs = [pltpu.HBM(o.shape, o.dtype) if k in kept or k in out_hbm else o for k, o in enumerate(out_shape)]
    own = [pltpu.VMEM(args[k].shape, args[k].dtype) for k in load] + [pltpu.VMEM(out_shape[k].shape, out_shape[k].dtype) for k in flush]
    if own:
        own.append(pltpu.SemaphoreType.DMA((len(own),)))

    def body(ids, *refs):
        ins, made, rest = list(refs[:n_in]), list(refs[n_in : n_in + n_out]), refs[n_in + n_out :]
        buffers = rest[n_scratch:]
        loads, flushes = {}, {}
        for i, k in enumerate(load):
            loads[k] = pltpu.make_async_copy(ins[k], buffers[i], buffers[-1].at[i])
            loads[k].start()
            ins[k] = buffers[i]
        for i, k in enumerate(flush, len(load)):
            flushes[k] = pltpu.make_async_copy(buffers[i], made[k], buffers[-1].at[i])
            made[k] = buffers[i]
        traffic = Traffic(loads, flushes)
        if lazy:
            kernel(traffic, ids, *ins, *made, *rest[:n_scratch])
        else:
            traffic.need(*load)
            kernel(ids, *ins, *made, *rest[:n_scratch])
        traffic.finish()

    return pl.pallas_call(
        body,
        name=name,
        out_shape=outs,
        in_specs=[SMEM] + [HBM if k in in_hbm else VMEM for k in range(n_in)],
        out_specs=[HBM if k in out_hbm else VMEM for k in range(n_out)],
        scratch_shapes=list(scratch) + own,
        compiler_params=pltpu.CompilerParams(vmem_limit_bytes=grant * 1_000_000),
        cost_estimate=pl.CostEstimate(flops=int(cost * 10**9), bytes_accessed=1, transcendentals=0),
    )(ids, *(pltpu.with_memory_space_constraint(a, pltpu.HBM) if k in in_hbm else a for k, a in enumerate(args)))


def exchange(blocks, peers, groups):
    if len(blocks) == 1:
        shaped = blocks[0].reshape(peers, blocks[0].shape[0] // peers, blocks[0].shape[1])
        moved = lax.all_to_all(shaped, "batch", split_axis=0, concat_axis=0, tiled=True)
        return [moved.reshape(blocks[0].shape)]
    came = {k: flip(blocks[k], "batch", k, peers, groups) for k in range(1, peers)}
    return [blocks[0]] + [came[k] for k in range(1, peers)]


def per_device(
    tokens, dest, seg_ids, cot_out, cot_align,
    ln1_gain, ln1_bias, w_qkv, q_bias, v_bias, w_out, out_bias,
    ln2_gain, ln2_bias, w_up, up_bias, w_down, down_bias,
    ln3_gain, ln3_bias, w_align, align_bias,
):
    rows, width = tokens.shape
    align = cot_align.shape[1]
    wide = w_up.shape[1]
    slots = seg_ids.shape[1]
    peers, groups = lax.axis_size("batch"), lax.axis_size("grp")
    capacity = slots // peers
    fast = peers == 8 and groups == 4 and (width, wide, align) == (768, 3072, 1024)
    blocks = 8 if fast else 1
    dest_row = dest.reshape(1, rows)
    seg_col = seg_ids.reshape(slots, 1)
    line = lambda v: v.reshape(1, v.shape[0])
    shape = jax.ShapeDtypeStruct
    vmem = pltpu.VMEM
    dma = pltpu.SemaphoreType.DMA
    count = slots // CLIPMAX
    low = lambda c: shape((rows, c), BF16)
    flat = lambda n: shape((n, 128), BF16)
    move = lambda value, axis, bit: flip(value, axis, bit, peers, groups)
    b, g = lax.axis_index("batch"), lax.axis_index("grp")
    place_b = b ^ jnp.arange(8)
    place_b = (place_b >> 2) + (((place_b >> 1) & 1) << 1) + ((place_b & 1) << 2)
    place_g = g ^ jnp.arange(4)
    place_g = (place_g >> 1) + ((place_g & 1) << 1)
    ids = jnp.concatenate([jnp.stack([b, g]), place_b, place_g]).astype(jnp.int32)

    packed = call(
        functools.partial(pack_kernel, peers, capacity), "pack_tokens", 56,
        [shape((slots // blocks, width), BF16)] * blocks, [],
        ids, dest_row, tokens,
    )
    packed = exchange(packed, peers, groups)

    in_slots = shape((slots, width), BF16)
    ctx, qkv, natural, a1, lse = call(
        functools.partial(attention_kernel, blocks), "attention", 56,
        [in_slots, shape((slots, 3 * width), BF16), in_slots, in_slots, shape((width // 128, count, 2 * CLIPMAX), F32)],
        [vmem((count, 3 * CLIPMAX, 2 * CLIPMAX), F32), vmem((128, slots), BF16), vmem((width, 3 * width), BF16),
         vmem((slots, 3 * width), BF16), vmem((slots, width), BF16), dma((blocks,)), dma, dma((2,))],
        ids, *packed, seg_ids, seg_col, line(ln1_gain), line(ln1_bias), w_qkv, line(q_bias), line(v_bias),
        far=tuple(range(blocks)) + (blocks + 4, -2, -3), kept=(3, 4),
    )
    (ctx,) = exchange([ctx], peers, groups)

    full = shape((rows, width), F32)
    joined, extra = JOINED_ROWS, 12 * 16
    chain = lambda n: [flat(n * EARLY_PARTS[0] + extra)] + [flat(n * r) for r in EARLY_PARTS[1:]]
    held = lambda n: [flat(n * r) for r in EARLY_PARTS]
    small_early = shape((96, 128), F32)
    turned = shape((width, rows), BF16)
    y, al, g_packed, g_mid, hidden, gub, a2, a3, ctx_rows, gyb, gmb, small_0, *sent = call(
        functools.partial(rows_kernel, peers, capacity, fast), "rows", 46,
        [low(width), low(align), in_slots, full, low(wide), low(wide), low(width), low(width), low(width), low(width), low(width),
         shape((16, width), F32)] + ([flat(SENT_1 + extra), flat(SENT_2), turned, turned, turned, turned, small_early] if fast else []),
        [vmem((rows, width), F32), vmem((rows, width), F32), vmem((rows, width), F32), vmem((rows, 128), F32), vmem((rows, wide), F32),
         vmem((rows, 512), F32), vmem((rows, 512), F32), vmem((rows, 512), BF16), vmem((rows, 512), BF16),
         vmem((2, 8, width), F32), vmem(w_out.shape, BF16), vmem(w_up.shape, BF16), vmem(w_down.shape, BF16),
         vmem(w_align.shape, BF16), dma((4,))] + ([vmem((width, rows), BF16)] if fast else []),
        ids, ctx, tokens, dest, dest_row, cot_out, cot_align,
        w_out, line(out_bias), line(ln2_gain), line(ln2_bias), w_up, line(up_bias), w_down, line(down_bias),
        line(ln3_gain), line(ln3_bias), w_align, line(align_bias),
        far=(6, 10, 12, 16), flush=(0, 1, 2, 3, 4, 5, 10) + ((12, 13, 14, 15, 16, 17, 18) if fast else ()), kept=(6, 7, 8, 9, 11), lazy=True,
    )
    (g_arrived,) = exchange([g_packed], peers, groups)

    if fast:
        send_1, send_2, turned_d, turned_3, turned_2, turned_1, small_e = sent
        came_2 = move(send_2, "grp", 1)
        came_1 = move(send_1, "grp", 1)
        routes = (
            (("grp", 2), ("batch", 2), ("batch", 1)),
            (("batch", 1), ("grp", 2), ("batch", 2)),
            (("batch", 2), ("batch", 1), ("grp", 2)),
        )
        go = lambda sends, k: [move(send, *route[k]) for send, route in zip(sends, routes)]
        k1, s1, k2, s2 = call(
            second_keep, "second_keep", 24, [held(8)[1], held(8)[1], held(8)[2], held(8)[2]], [],
            ids, turned_3, turned_2, turned_1, cot_align, gub, gmb, came_2,
            load=(0, 1, 2, 3, 4, 5), flush=(0, 2),
        )
        k0, s0, small_e = call(
            first_keep, "first_keep", 20, [held(8)[0], chain(8)[0], small_early], [],
            ids, turned_d, hidden, tie(came_1, s1), small_e,
            load=(0, 1), flush=(0,),
        )
        keeps, sends = [k0, k1, k2], [s0, s1, s2]
        cames = go(sends, 0)
        g_arrived = tie(g_arrived, s0)

    more = 12 * 8
    outs = [in_slots, shape((slots, 3 * width), BF16), shape((8, width), F32)]
    turned = shape((width, slots), BF16)
    made = call(
        functools.partial(attention_back_kernel, fast), "attention_back", 28,
        outs + ([flat(32 * joined + more), turned] if fast else []),
        [vmem((count, 3 * CLIPMAX, 2 * CLIPMAX), F32), vmem((128, slots), BF16), vmem((slots, 128), F32), vmem((slots, 128), F32),
         vmem((slots, width), F32), vmem((2, 8, width), F32), vmem((width, 3 * width), BF16), dma]
        + ([vmem((width, slots), BF16)] if fast else []),
        ids, g_arrived, natural, qkv, lse, a1, seg_ids, seg_col, line(ln1_gain), w_qkv,
        far=(8,), load=(1, 6, 2, 3, 4), flush=(0, 4) if fast else (0,), lazy=True,
    )
    g_rows, g_joined, small_2 = made[:3]
    (g_back,) = exchange([g_rows], peers, groups)

    if fast:
        send, turned_c = made[3:]
        came = move(send, "grp", 1)
        small_shape = shape((48, 128), F32)

        def early_step(name, n, keeps, cames, small_e, before, cost, **more_of):
            made = call(
                step_parts, name, 14, held(n) + chain(n) + [small_early], [],
                ids, *keeps, tie(cames[0], before), *cames[1:], small_e, cost=cost, **more_of,
            )
            return made[0:3], made[3:6], made[6]

        keeps, sends, small_e = early_step("early_step_1", 4, keeps, cames, small_e, send, 15, load=(0, 1, 2, 6), flush=(0, 1, 2))
        cames = go(sends, 1)
        kx3, sx3, ky3, sy3, small_j = call(
            joined_keep, "joined_keep", 12, [flat(8 * joined), flat(8 * joined + more), flat(8 * joined), flat(8 * joined), small_shape], [],
            ids, turned_c, g_joined, tie(came, sends[0]), small_2,
        )
        cx3, cy3 = move(sx3, "grp", 2), move(sy3, "batch", 1)
        keeps, sends, small_e = early_step("early_step_2", 2, keeps, cames, small_e, sx3, 0.001, load=(0, 1, 2))
        cames = go(sends, 2)
        kx3, sx3, ky3, sy3, small_j = call(
            step_apart, "joined_apart", 10, [flat(4 * joined), flat(4 * joined + more), flat(4 * joined), flat(4 * joined), small_shape], [],
            ids, kx3, tie(cx3, sends[0]), ky3, cy3, small_j,
        )
        cx3, cy3 = move(sx3, "batch", 1), move(sy3, "grp", 2)
        *keeps, send, small_e = call(
            step_parts_last, "early_step_3", 10, held(1) + [flat(1536 + extra), small_early], [],
            ids, *keeps, tie(cames[0], sx3), *cames[1:], small_e,
        )
        last = move(send, "batch", 4)
        k3, s3, small_j = call(
            step_meet, "joined_meet", 10, [flat(4 * joined), flat(4 * joined + more), small_shape], [],
            ids, kx3, tie(cx3, send), ky3, cy3, small_j,
        )
        c3 = move(s3, "batch", 2)
        k3, s3, small_j = call(
            step_joint, "joined_joint", 10, [flat(2 * joined), flat(2 * joined + more), small_shape], [],
            ids, k3, c3, small_j,
        )
        c3 = move(s3, "batch", 4)
        sum_down, sum_align, sum_up, sum_out, small_e = call(
            early_end, "early_end", 10,
            [shape((384, 192), F32), shape((96, 256), F32), shape((96, 768), F32), shape((96, 192), F32), shape((16, width), F32)], [],
            ids, *keeps, tie(last, s3), small_e,
        )
        g_back = tie(g_back, s3)
        sum_qkv, small_j = call(
            joined_end, "joined_end", 10, [shape((96, 576), F32), shape((8, width), F32)], [],
            ids, k3, tie(c3, sum_out), small_j,
        )
        small_0, small_2 = small_e, small_j
    else:
        sum_up, sum_align, sum_out, sum_down, sum_qkv = (
            scattered(a2, gub, peers, groups),
            scattered(a3, cot_align, peers, groups),
            scattered(ctx_rows, gmb, peers, groups),
            scattered(hidden, gyb, peers, groups),
            scattered(a1, g_joined, peers, groups),
        )
        small_0, small_2 = lax.psum((small_0, small_2), AXES)

    (grad_tokens,) = call(
        functools.partial(last_kernel, peers, capacity), "grad_tokens", 8, [low(width)], [],
        ids, g_back, dest, g_mid,
    )
    sum_align_bias = small_0[3:5].reshape(2 * width)[:align]
    sum_up_bias = small_0[11:15].reshape(4 * width)[:wide]
    return (
        y, al, grad_tokens,
        small_2[0], small_2[1], sum_qkv, small_2[2], small_2[3],
        sum_out, small_0[10], small_0[8], small_0[9],
        sum_up, sum_up_bias, sum_down, small_0[2],
        small_0[0], small_0[1], sum_align, sum_align_bias,
    )


def solution(mesh):
    row, one = P(AXES, None), P()
    matrix = P("batch", "grp")
    return jax.shard_map(
        per_device,
        mesh=mesh,
        in_specs=(row,) * 5 + (one,) * 17,
        out_specs=(
            row, row, row, one, one, matrix, one, one, matrix, one,
            one, one, matrix, one, matrix, one, one, one, matrix, one,
        ),
        check_vma=False,
    )
```

time: 334 us -> 236 us (0.71)
  waiting for transfers between devices: 113 us -> 72.7 us
  other arithmetic: 21.6 us -> 0.1 us
  Pallas kernels: 121 us -> 99.8 us
  local copies, waits for them, and re-layouts: 30.9 us -> 12.6 us
  starting transfers between devices: 44.9 us -> 48.4 us
    all_to_all x4 -> x3, waiting for transfers between devices: 44.3 us -> 19.3 us  [exchange(): lax.all_to_all(shaped, 'batch', split_axis=0, concat_axis=0, tiled=True)]
    pallas_call x8 -> x16, Pallas kernels: 121 us -> 99.8 us  [call(): pl.pallas_call(body, name=name, out_shape=outs, in_specs=[SMEM] + [HBM if...]
    add x28 -> x2, other arithmetic: 19.5 us -> 0.02 us  [the longest x1 0.01 us: per_device(): place_b = (place_b >> 2) + ((place_b >> 1 & 1) << 1) + ((place_b & 1) << 2)]
    ppermute x25 -> x26, waiting for transfers between devices: 69 us -> 53.4 us  [flip(): return lax.ppermute(value, AXES, pairs)]
    slice x11 -> x4, local copies, waits for them, and re-layouts: 14.1 us -> 1.28 us  [the longest x1 0.67 us: per_device(): small_0[1]]
    ppermute x25 -> x26, starting transfers between devices: 26.3 us -> 34.3 us  [flip(): return lax.ppermute(value, AXES, pairs)]
    all_to_all x4 -> x3, starting transfers between devices: 18.6 us -> 14 us  [exchange(): lax.all_to_all(shaped, 'batch', split_axis=0, concat_axis=0, tiled=True)]
    reshape x12, local copies, waits for them, and re-layouts: 7.02 us -> 2.81 us  [per_device(): line = lambda v: v.reshape(1, v.shape[0])]
  transfers between devices with their start and end apart: 29 -> 29, of which waited for: 12 -> 10; matrix products, arithmetic and copies ran while one was open for 14% -> 2% of each run, Pallas kernels for 15% -> 22%
where the time goes in v2:
time: 236 us; the launch traced here: 235 us
  Pallas kernels  99.8 us (42%)
  waiting for transfers between devices  72.7 us (31%)
  starting transfers between devices  48.4 us (21%)
  local copies, waits for them, and re-layouts  12.6 us (5%)
    pallas_call x16, Pallas kernels, call(): pl.pallas_call(body, name=name, out_shape=outs, in_specs=[SMEM] + [HBM if...  99.8 us
    ppermute x26, waiting for transfers between devices, flip(): return lax.ppermute(value, AXES, pairs)  53.4 us
    ppermute x26, starting transfers between devices, flip(): return lax.ppermute(value, AXES, pairs)  34.3 us
    all_to_all x3, waiting for transfers between devices, exchange(): lax.all_to_all(shaped, 'batch', split_axis=0, concat_axis=0, tiled=True)  19.3 us
    all_to_all x3, starting transfers between devices, exchange(): lax.all_to_all(shaped, 'batch', split_axis=0, concat_axis=0, tiled=True)  14 us
    unnamed x62, local copies, waits for them, and re-layouts  7.12 us
  transfers between devices with their start and end apart: 29, of which 10 were waited for; matrix products, arithmetic and copies ran while one was open for 2% of the time, Pallas kernels for 22%

profile of v2, /device:TPU:0, one launch (start us, length us, event | category | flops | bytes accessed | tf_op | source)
XLA Modules:
  0.0 234.8 jit_solution(2809176495849747973)
XLA Ops:
  0.8 0.7 copy-done.10
  1.4 2.2 pack_tokens.1
  3.7 0.6 copy-done.6
  4.3 3.0 %collective-permute-start = (bf16[64,768]{1,0:T(8,128)(2,1)S(1)}, bf16[64,768]{1,0:T(8,128)(2,1)S(1)}, u32[]{:S(2)}, u32[]{:S(2)}) collective-permute-start(bf16[64,768]{1,0:T(8,128)(2,1)S(1)} %get-tuple-element.113), channel_id=1, source_target_pairs={{0,4},{1,5},{2,6},{3,7},{4,0},{5,1},{6,2},{7,3},{8,12},{9,13},{10,... | collective-permute-start | bytes 294920 | tf_op jit(solution)/shard_map/ppermute | solution.py:710
  7.3 1.6 collective-permute-start.1
  8.9 3.0 %collective-permute-start.3 = (bf16[64,768]{1,0:T(8,128)(2,1)S(1)}, bf16[64,768]{1,0:T(8,128)(2,1)S(1)}, u32[]{:S(2)}, u32[]{:S(2)}) collective-permute-start(bf16[64,768]{1,0:T(8,128)(2,1)S(1)} %get-tuple-element.116), channel_id=1, source_target_pairs={{0,16},{1,17},{2,18},{3,19},{4,20},{5,21},{6,22},{7,23},{8,24},{9,... | collective-permute-start | bytes 294920 | tf_op jit(solution)/shard_map/ppermute | solution.py:710
  11.9 1.3 collective-permute-start.4
  13.1 3.6 %collective-permute-start.5 = (bf16[64,768]{1,0:T(8,128)(2,1)}, bf16[64,768]{1,0:T(8,128)(2,1)S(1)}, u32[]{:S(2)}, u32[]{:S(2)}) collective-permute-start(bf16[64,768]{1,0:T(8,128)(2,1)} %get-tuple-element.118), channel_id=1, source_target_pairs={{0,24},{1,25},{2,26},{3,27},{4,28},{5,29},{6,30},{7,31},{8,16},{9,... | collective-permute-start | bytes 294920 | tf_op jit(solution)/shard_map/ppermute | solution.py:710
  16.8 0.7 reshape.109.refs_10_.refs_7_
  17.5 0.7 reshape.110.refs_11_
  18.2 0.7 reshape.111.refs_13_
  18.9 0.7 reshape.112.refs_14_
  19.6 0.8 copy.45.refs_9_.refs_6_
  20.4 6.6 %collective-permute-done.4.refs_5_ = bf16[64,768]{1,0:T(8,128)(2,1)S(1)} collective-permute-done((bf16[64,768]{1,0:T(8,128)(2,1)}, bf16[64,768]{1,0:T(8,128)(2,1)S(1)}, u32[]{:S(2)}, u32[]{:S(2)}) %collective-permute-start.4) | collective-permute-done | bytes 98336 | tf_op jit(solution)/shard_map/ppermute | solution.py:710
  27.1 0.6 copy-done.19
  27.8 0.7 copy-done.8
  28.5 15.6 %attention.1 = (bf16[512,768]{1,0:T(8,128)(2,1)}, bf16[512,2304]{1,0:T(8,128)(2,1)}, bf16[512,768]{1,0:T(8,128)(2,1)}, bf16[512,768]{1,0:T(8,128)(2,1)}, f32[6,4,256]{2,1,0:T(4,128)}) custom-call(s32[14]{0:T(128)S(1)} %pad_add_fusion.ids, bf16[64,768]{1,0:T(8,128)(2,1)} %copy-done.6, bf16[64,768]{1,0:T(8,128)(2,1)} %copy-done.15, ...), custom_call_target="tpu_custom_call" | custom-call | flops 1000000 | bytes 1 | tf_op jit(solution)/shard_map/attention/pallas_call | solution.py:782
  44.1 6.4 %all-to-all-start = ((bf16[8,64,768]{2,1,0:T(8,128)(2,1)}), bf16[8,64,768]{2,1,0:T(8,128)(2,1)S(1)}, u32[]{:S(2)}, u32[]{:S(2)}) async-start(bf16[8,64,768]{2,1,0:T(8,128)(2,1)} %bitcast.18), calls=%async_computation | async-start | bytes 1572864 | tf_op jit(solution)/shard_map/all_to_all | solution.py:797
  50.9 19.3 %all-to-all-done = bf16[8,64,768]{2,1,0:T(8,128)(2,1)S(1)} async-done(((bf16[8,64,768]{2,1,0:T(8,128)(2,1)}), bf16[8,64,768]{2,1,0:T(8,128)(2,1)S(1)}, u32[]{:S(2)}, u32[]{:S(2)}) %all-to-all-start) | async-done | bytes 786464 | tf_op jit(solution)/shard_map/all_to_all | solution.py:797
  70.1 28.0 %rows.1 = (bf16[256,768]{1,0:T(8,128)(2,1)}, bf16[256,1024]{1,0:T(8,128)(2,1)}, bf16[512,768]{1,0:T(8,128)(2,1)}, f32[256,768]{1,0:T(8,128)}, bf16[256,3072]{1,0...) custom-call(s32[14]{0:T(128)S(1)} %pad_add_fusion.ids, ...), custom_call_target="tpu_custom_call" | custom-call | flops 1000000 | bytes 1 | tf_op jit(solution)/shard_map/rows/pallas_call | solution.py:782
  98.7 3.8 %all-to-all-start.1 = ((bf16[8,64,768]{2,1,0:T(8,128)(2,1)}), bf16[8,64,768]{2,1,0:T(8,128)(2,1)S(1)}, u32[]{:S(2)}, u32[]{:S(2)}) async-start(bf16[8,64,768]{2,1,0:T(8,128)(2,1)} %bitcast.17), calls=%async_computation.1 | async-start | bytes 1572864 | tf_op jit(solution)/shard_map/all_to_all | solution.py:797
  102.5 6.3 %collective-permute-done.8.refs_6_ = bf16[15360,128]{1,0:T(8,128)(2,1)} collective-permute-done((bf16[15360,128]{1,0:T(8,128)(2,1)}, bf16[15360,128]{1,0:T(8,128)(2,1)}, u32[]{:S(2)}, u32[]{:S(2)}) %collective-permute-start.8) | collective-permute-done | bytes 3932192 | tf_op jit(solution)/shard_map/ppermute | solution.py:710
  108.8 7.7 %second_keep.1 = (bf16[3840,128]{1,0:T(8,128)(2,1)}, bf16[3840,128]{1,0:T(8,128)(2,1)}, bf16[3840,128]{1,0:T(8,128)(2,1)}, bf16[3840,128]{1,0:T(8,128)(2,1)}) custom-call(s32[14]{0:T(128)S(1)} %pad_add_fusion.ids, bf16[768,256]{1,0:T(8,128)(2,1)} %get-tuple-element.127.refs_0_, bf16[768,256]{1,0:T(8,128)(2,1)} %get-tuple-element.128.refs_1_, ...), custom_call_target="tpu_custom_call" | custom-call | flops 1000000 | bytes 1 | tf_op jit(solution)/shard_map/second_keep/pallas_call | solution.py:782
  116.5 5.2 %first_keep.1 = (bf16[4608,128]{1,0:T(8,128)(2,1)}, bf16[4800,128]{1,0:T(8,128)(2,1)}, f32[96,128]{1,0:T(8,128)S(1)}) custom-call(s32[14]{0:T(128)S(1)} %pad_add_fusion.ids, bf16[768,256]{1,0:T(8,128)(2,1)} %get-tuple-element.124.refs_0_, bf16[256,3072]{1,0:T(8,128)(2,1)} %get-tuple-element.125.refs_1_, ...), custom_call_target="tpu_custom_call" | custom-call | flops 1000000 | bytes 1 | tf_op jit(solution)/shard_map/first_keep/pallas_call | solution.py:782
  121.7 0.6 copy-done.14
  122.3 1.5 collective-permute-start.10
  124.1 1.1 collective-permute-start.11
  125.2 21.4 %attention_back.1 = (bf16[512,768]{1,0:T(8,128)(2,1)}, bf16[512,2304]{1,0:T(8,128)(2,1)S(1)}, f32[8,768]{1,0:T(8,128)S(1)}, bf16[7776,128]{1,0:T(8,128)(2,1)}, bf16[768,512]{1,0:T(8,128)(2,1)}) custom-call(s32[14]{0:T(128)S(1)} %pad_add_fusion.ids, bf16[512,768]{1,0:T(8,128)(2,1)S(1)} %bitcast.10, bf16[512,768]{1,0:T(8,128)(2,1)} %get-tuple-element.138.refs_1_, ...), custom_call_target="tpu_custom_call" | custom-call | flops 1000000 | bytes 1 | tf_op jit(solution)/shard_map/attention_back/pallas_call | solution.py:782
  146.6 5.0 %collective-permute-done.10.refs_3_ = bf16[4800,128]{1,0:T(8,128)(2,1)} collective-permute-done((bf16[4800,128]{1,0:T(8,128)(2,1)}, bf16[4800,128]{1,0:T(8,128)(2,1)}, u32[]{:S(2)}, u32[]{:S(2)}) %collective-permute-start.10) | collective-permute-done | bytes 1228832 | tf_op jit(solution)/shard_map/ppermute | solution.py:710
  151.7 5.9 %early_step_1.1 = (bf16[2304,128]{1,0:T(8,128)(2,1)}, bf16[1920,128]{1,0:T(8,128)(2,1)}, bf16[1920,128]{1,0:T(8,128)(2,1)}, bf16[2496,128]{1,0:T(8,128)(2,1)}, b...) custom-call(s32[14]{0:T(128)S(1)} %pad_add_fusion.ids, ...), custom_call_target="tpu_custom_call" | custom-call | flops 15000000512 | bytes 1 | tf_op jit(solution)/shard_map/early_step_1/pallas_call | solution.py:782
  157.7 0.8 copy-done.12
  158.5 0.8 copy-done.13
  159.6 3.8 %all-to-all-start.2 = ((bf16[8,64,768]{2,1,0:T(8,128)(2,1)}), bf16[8,64,768]{2,1,0:T(8,128)(2,1)S(1)}, u32[]{:S(2)}, u32[]{:S(2)}) async-start(bf16[8,64,768]{2,1,0:T(8,128)(2,1)} %bitcast.16), calls=%async_computation.2 | async-start | bytes 1572864 | tf_op jit(solution)/shard_map/all_to_all | solution.py:797
  163.4 1.6 collective-permute-start.15
  165.0 2.0 collective-permute-start.16
  166.9 1.1 copy-done.4
  168.1 3.3 %joined_keep.1 = (bf16[1920,128]{1,0:T(8,128)(2,1)S(1)}, bf16[2016,128]{1,0:T(8,128)(2,1)S(1)}, bf16[1920,128]{1,0:T(8,128)(2,1)S(1)}, bf16[1920,128]{1,0:T(8,128)(2,1)S(1)}, f32[48,128]{1,0:T(8,128)S(1)}) custom-call(s32[14]{0:T(128)S(1)} %pad_add_fusion.ids, bf16[768,512]{1,0:T(8,128)(2,1)S(1)} %copy-done.4, ...), custom_call_target="tpu_custom_call" | custom-call | flops 1000000 | bytes 1 | tf_op jit(solution)/shard_map/joined_keep/pallas_call | solution.py:782
  171.3 0.6 collective-permute-start.13
  172.0 13.4 %collective-permute-done.14.refs_3_ = bf16[2496,128]{1,0:T(8,128)(2,1)} collective-permute-done((bf16[2496,128]{1,0:T(8,128)(2,1)}, bf16[2496,128]{1,0:T(8,128)(2,1)}, u32[]{:S(2)}, u32[]{:S(2)}) %collective-permute-start.14) | collective-permute-done | bytes 639008 | tf_op jit(solution)/shard_map/ppermute | solution.py:710
  185.3 2.9 %early_step_2.1 = (bf16[1152,128]{1,0:T(8,128)(2,1)S(1)}, bf16[960,128]{1,0:T(8,128)(2,1)S(1)}, bf16[960,128]{1,0:T(8,128)(2,1)S(1)}, bf16[1344,128]{1,0:T(8,128...) custom-call(s32[14]{0:T(128)S(1)} %pad_add_fusion.ids, ...), custom_call_target="tpu_custom_call" | custom-call | flops 1000000 | bytes 1 | tf_op jit(solution)/shard_map/early_step_2/pallas_call | solution.py:782
  188.3 0.6 collective-permute-start.19
  188.9 1.1 collective-permute-start.20
  190.0 1.8 collective-permute-start.21
  191.8 4.6 %collective-permute-done.17.refs_3_ = bf16[1920,128]{1,0:T(8,128)(2,1)S(1)} collective-permute-done((bf16[1920,128]{1,0:T(8,128)(2,1)S(1)}, bf16[1920,128]{1,0:T(8,128)(2,1)S(1)}, u32[]{:S(2)}, u32[]{:S(2)}) %collective-permute-start.17) | collective-permute-done | bytes 491552 | tf_op jit(solution)/shard_map/ppermute | solution.py:710
  196.3 0.8 joined_apart.1
  197.1 1.2 collective-permute-start.18
  198.3 1.1 collective-permute-start.22
  199.4 4.3 %collective-permute-done.19.refs_3_ = bf16[1344,128]{1,0:T(8,128)(2,1)S(1)} collective-permute-done((bf16[1344,128]{1,0:T(8,128)(2,1)S(1)}, bf16[1344,128]{1,0:T(8,128)(2,1)S(1)}, u32[]{:S(2)}, u32[]{:S(2)}) %collective-permute-start.19) | collective-permute-done | bytes 344096 | tf_op jit(solution)/shard_map/ppermute | solution.py:710
  203.7 0.7 early_step_3.1
  204.5 2.7 %collective-permute-start.25 = (bf16[1728,128]{1,0:T(8,128)(2,1)S(1)}, bf16[1728,128]{1,0:T(8,128)(2,1)S(1)}, u32[]{:S(2)}, u32[]{:S(2)}) collective-permute-start(bf16[1728,128]{1,0:T(8,128)(2,1)S(1)} %get-tuple-element.178), channel_id=1, source_target_pairs={{0,16},{1,17},{2,18},{3,19},{4,20},{5,21},{6,22},{7,23},{8,24},{9,... | collective-permute-start | bytes 1327112 | tf_op jit(solution)/shard_map/ppermute | solution.py:710
  207.2 1.0 collective-permute-done.18.refs_1_
  208.1 0.7 joined_meet.1
  208.8 1.8 collective-permute-start.23
  210.6 8.7 %collective-permute-done.23.refs_1_ = bf16[1056,128]{1,0:T(8,128)(2,1)S(1)} collective-permute-done((bf16[1056,128]{1,0:T(8,128)(2,1)S(1)}, bf16[1056,128]{1,0:T(8,128)(2,1)S(1)}, u32[]{:S(2)}, u32[]{:S(2)}) %collective-permute-start.23) | collective-permute-done | bytes 270368 | tf_op jit(solution)/shard_map/ppermute | solution.py:710
  219.3 0.6 joined_joint.1
  219.9 3.8 %collective-permute-start.24 = (bf16[576,128]{1,0:T(8,128)(2,1)S(1)}, bf16[576,128]{1,0:T(8,128)(2,1)S(1)}, u32[]{:S(2)}, u32[]{:S(2)}) collective-permute-start(bf16[576,128]{1,0:T(8,128)(2,1)S(1)} %get-tuple-element.186), channel_id=1, source_target_pairs={{0,16},{1,17},{2,18},{3,19},{4,20},{5,21},{6,22},{7,23},{8,24},{9,... | collective-permute-start | bytes 442376 | tf_op jit(solution)/shard_map/ppermute | solution.py:710
  223.7 3.5 %collective-permute-done.25.refs_3_ = bf16[1728,128]{1,0:T(8,128)(2,1)S(1)} collective-permute-done((bf16[1728,128]{1,0:T(8,128)(2,1)S(1)}, bf16[1728,128]{1,0:T(8,128)(2,1)S(1)}, u32[]{:S(2)}, u32[]{:S(2)}) %collective-permute-start.25) | collective-permute-done | bytes 442400 | tf_op jit(solution)/shard_map/ppermute | solution.py:710
  227.2 1.4 early_end.1
  228.7 0.6 slice.52
  229.3 0.6 reshape.127
  229.9 0.9 copy.49
  230.8 2.1 grad_tokens.1
  232.8 1.3 joined_end.1
  234.1 0.7 slice_reduce_fusion
  (94 shorter events, 1.8 us)
Async XLA Ops:
  0.8 0.7 copy-start.10
  3.7 0.6 copy-start.6
  4.3 8.8 %collective-permute-start = (bf16[64,768]{1,0:T(8,128)(2,1)S(1)}, bf16[64,768]{1,0:T(8,128)(2,1)S(1)}, u32[]{:S(2)}, u32[]{:S(2)}) collective-permute-start(bf16[64,768]{1,0:T(8,128)(2,1)S(1)} %get-tuple-element.113), channel_id=1, source_target_pairs={{0,4},{1,5},{2,6},{3,7},{4,0},{5,1},{6,2},{7,3},{8,12},{9,13},{10,... | collective-permute-start | bytes 294920 | tf_op jit(solution)/shard_map/ppermute | solution.py:710
  7.3 9.5 %collective-permute-start.1 = (bf16[64,768]{1,0:T(8,128)(2,1)S(1)}, bf16[64,768]{1,0:T(8,128)(2,1)S(1)}, u32[]{:S(2)}, u32[]{:S(2)}) collective-permute-start(bf16[64,768]{1,0:T(8,128)(2,1)S(1)} %get-tuple-element.114), channel_id=1, source_target_pairs={{0,8},{1,9},{2,10},{3,11},{4,12},{5,13},{6,14},{7,15},{8,0},{9,1},... | collective-permute-start | bytes 294920 | tf_op jit(solution)/shard_map/ppermute | solution.py:710
  8.9 11.5 %collective-permute-start.2 = (bf16[64,768]{1,0:T(8,128)(2,1)S(1)}, bf16[64,768]{1,0:T(8,128)(2,1)S(1)}, u32[]{:S(2)}, u32[]{:S(2)}) collective-permute-start(bf16[64,768]{1,0:T(8,128)(2,1)S(1)} %get-tuple-element.115), channel_id=1, source_target_pairs={{0,12},{1,13},{2,14},{3,15},{4,8},{5,9},{6,10},{7,11},{8,4},{9,5},... | collective-permute-start | bytes 294920 | tf_op jit(solution)/shard_map/ppermute | solution.py:710
  8.9 11.5 %collective-permute-start.3 = (bf16[64,768]{1,0:T(8,128)(2,1)S(1)}, bf16[64,768]{1,0:T(8,128)(2,1)S(1)}, u32[]{:S(2)}, u32[]{:S(2)}) collective-permute-start(bf16[64,768]{1,0:T(8,128)(2,1)S(1)} %get-tuple-element.116), channel_id=1, source_target_pairs={{0,16},{1,17},{2,18},{3,19},{4,20},{5,21},{6,22},{7,23},{8,24},{9,... | collective-permute-start | bytes 294920 | tf_op jit(solution)/shard_map/ppermute | solution.py:710
  11.9 15.2 %collective-permute-start.4 = (bf16[64,768]{1,0:T(8,128)(2,1)}, bf16[64,768]{1,0:T(8,128)(2,1)S(1)}, u32[]{:S(2)}, u32[]{:S(2)}) collective-permute-start(bf16[64,768]{1,0:T(8,128)(2,1)} %get-tuple-element.117), channel_id=1, source_target_pairs={{0,20},{1,21},{2,22},{3,23},{4,16},{5,17},{6,18},{7,19},{8,28},{9,... | collective-permute-start | bytes 294920 | tf_op jit(solution)/shard_map/ppermute | solution.py:710
  13.1 13.9 %copy-start.15 = (bf16[64,768]{1,0:T(8,128)(2,1)}, bf16[64,768]{1,0:T(8,128)(2,1)S(1)}, u32[]{:S(2)}) copy-start(bf16[64,768]{1,0:T(8,128)(2,1)S(1)} %collective-permute-done.refs_1_) | copy-start | bytes 294916
  13.1 13.9 %collective-permute-start.5 = (bf16[64,768]{1,0:T(8,128)(2,1)}, bf16[64,768]{1,0:T(8,128)(2,1)S(1)}, u32[]{:S(2)}, u32[]{:S(2)}) collective-permute-start(bf16[64,768]{1,0:T(8,128)(2,1)} %get-tuple-element.118), channel_id=1, source_target_pairs={{0,24},{1,25},{2,26},{3,27},{4,28},{5,29},{6,30},{7,31},{8,16},{9,... | collective-permute-start | bytes 294920 | tf_op jit(solution)/shard_map/ppermute | solution.py:710
  16.8 10.3 %copy-start.16 = (bf16[64,768]{1,0:T(8,128)(2,1)}, bf16[64,768]{1,0:T(8,128)(2,1)S(1)}, u32[]{:S(2)}) copy-start(bf16[64,768]{1,0:T(8,128)(2,1)S(1)} %collective-permute-done.1.refs_2_) | copy-start | bytes 294916
  16.8 10.3 %collective-permute-start.6 = (bf16[64,768]{1,0:T(8,128)(2,1)}, bf16[64,768]{1,0:T(8,128)(2,1)S(1)}, u32[]{:S(2)}, u32[]{:S(2)}) collective-permute-start(bf16[64,768]{1,0:T(8,128)(2,1)} %get-tuple-element.119), channel_id=1, source_target_pairs={{0,28},{1,29},{2,30},{3,31},{4,24},{5,25},{6,26},{7,27},{8,20},{9,... | collective-permute-start | bytes 294920 | tf_op jit(solution)/shard_map/ppermute | solution.py:710
  20.4 23.7 %copy-start = (s32[512,1]{1,0:T(8,128)}, s32[512,1]{1,0:T(8,128)S(1)}, u32[]{:S(2)}) copy-start(s32[512,1]{1,0:T(8,128)S(1)} %copy.45.refs_9_.refs_6_) | copy-start | bytes 6148
  20.4 6.7 %copy-start.17 = (bf16[64,768]{1,0:T(8,128)(2,1)}, bf16[64,768]{1,0:T(8,128)(2,1)S(1)}, u32[]{:S(2)}) copy-start(bf16[64,768]{1,0:T(8,128)(2,1)S(1)} %collective-permute-done.2.refs_3_) | copy-start | bytes 294916
  20.4 6.7 %copy-start.18 = (bf16[64,768]{1,0:T(8,128)(2,1)}, bf16[64,768]{1,0:T(8,128)(2,1)S(1)}, u32[]{:S(2)}) copy-start(bf16[64,768]{1,0:T(8,128)(2,1)S(1)} %collective-permute-done.3.refs_4_) | copy-start | bytes 294916
  27.0 0.6 copy-start.19
  27.1 0.7 copy-start.20
  27.1 0.7 copy-start.21
  27.8 0.7 copy-start.8
  28.4 22.1 %copy-start.11 = (s32[256,1]{0,1:T(1,128)S(1)}, s32[256,1]{0,1:T(1,128)}, u32[]{:S(2)}) copy-start(s32[256,1]{0,1:T(1,128)} %param.23) | copy-start | bytes 3076
  28.4 22.2 %copy-start.24 = (bf16[768]{0:T(1024)(128)(2,1)S(1)}, bf16[768]{0:T(1024)(128)(2,1)}, u32[]{:S(2)}) copy-start(bf16[768]{0:T(1024)(128)(2,1)} %param.33) | copy-start | bytes 4612
  28.4 22.3 %copy-start.25 = (bf16[768]{0:T(1024)(128)(2,1)S(1)}, bf16[768]{0:T(1024)(128)(2,1)}, u32[]{:S(2)}) copy-start(bf16[768]{0:T(1024)(128)(2,1)} %param.34) | copy-start | bytes 4612
  28.4 22.3 %copy-start.26 = (bf16[768]{0:T(1024)(128)(2,1)S(1)}, bf16[768]{0:T(1024)(128)(2,1)}, u32[]{:S(2)}) copy-start(bf16[768]{0:T(1024)(128)(2,1)} %param.35) | copy-start | bytes 4612
  28.4 22.3 %copy-start.27 = (bf16[768]{0:T(1024)(128)(2,1)S(1)}, bf16[768]{0:T(1024)(128)(2,1)}, u32[]{:S(2)}) copy-start(bf16[768]{0:T(1024)(128)(2,1)} %param.39) | copy-start | bytes 4612
  28.5 22.3 %copy-start.28 = (bf16[768]{0:T(1024)(128)(2,1)S(1)}, bf16[768]{0:T(1024)(128)(2,1)}, u32[]{:S(2)}) copy-start(bf16[768]{0:T(1024)(128)(2,1)} %param.40) | copy-start | bytes 4612
  28.5 22.3 %copy-start.29 = (bf16[768]{0:T(1024)(128)(2,1)S(1)}, bf16[768]{0:T(1024)(128)(2,1)}, u32[]{:S(2)}) copy-start(bf16[768]{0:T(1024)(128)(2,1)} %param.41) | copy-start | bytes 4612
  28.5 22.3 %copy-start.23 = (bf16[1024]{0:T(1024)(128)(2,1)S(1)}, bf16[1024]{0:T(1024)(128)(2,1)}, u32[]{:S(2)}) copy-start(bf16[1024]{0:T(1024)(128)(2,1)} %param.43) | copy-start | bytes 6148
  28.5 22.4 %copy-start.22 = (bf16[3072]{0:T(1024)(128)(2,1)S(1)}, bf16[3072]{0:T(1024)(128)(2,1)}, u32[]{:S(2)}) copy-start(bf16[3072]{0:T(1024)(128)(2,1)} %param.37) | copy-start | bytes 18436
  28.5 41.6 %copy-start.1 = (bf16[256,1024]{1,0:T(8,128)(2,1)S(1)}, bf16[256,1024]{1,0:T(8,128)(2,1)}, u32[]{:S(2)}) copy-start(bf16[256,1024]{1,0:T(8,128)(2,1)} %refs_3_.1) | copy-start | bytes 1572868
  28.5 41.6 %copy-start.2 = (bf16[256,768]{1,0:T(8,128)(2,1)S(1)}, bf16[256,768]{1,0:T(8,128)(2,1)}, u32[]{:S(2)}) copy-start(bf16[256,768]{1,0:T(8,128)(2,1)} %refs_1_.4) | copy-start | bytes 1179652
  28.5 41.6 %copy-start.5 = (bf16[256,768]{1,0:T(8,128)(2,1)S(1)}, bf16[256,768]{1,0:T(8,128)(2,1)}, u32[]{:S(2)}) copy-start(bf16[256,768]{1,0:T(8,128)(2,1)} %refs_4_.1) | copy-start | bytes 1179652
  44.1 26.0 %all-to-all-start = ((bf16[8,64,768]{2,1,0:T(8,128)(2,1)}), bf16[8,64,768]{2,1,0:T(8,128)(2,1)S(1)}, u32[]{:S(2)}, u32[]{:S(2)}) async-start(bf16[8,64,768]{2,1,0:T(8,128)(2,1)} %bitcast.18), calls=%async_computation | async-start | bytes 1572864 | tf_op jit(solution)/shard_map/all_to_all | solution.py:797
  98.1 10.6 %collective-permute-start.8 = (bf16[15360,128]{1,0:T(8,128)(2,1)}, bf16[15360,128]{1,0:T(8,128)(2,1)}, u32[]{:S(2)}, u32[]{:S(2)}) collective-permute-start(bf16[15360,128]{1,0:T(8,128)(2,1)} %get-tuple-element.132), channel_id=1, source_target_pairs={{0,1},{1,0},{2,3},{3,2},{4,5},{5,4},{6,7},{7,6},{8,9},{9,8},{10,11... | collective-permute-start | bytes 11796488 | tf_op jit(solution)/shard_map/ppermute | solution.py:710
  98.2 18.3 %collective-permute-start.7 = (bf16[9408,128]{1,0:T(8,128)(2,1)}, bf16[9408,128]{1,0:T(8,128)(2,1)S(1)}, u32[]{:S(2)}, u32[]{:S(2)}) collective-permute-start(bf16[9408,128]{1,0:T(8,128)(2,1)} %get-tuple-element.126), channel_id=1, source_target_pairs={{0,1},{1,0},{2,3},{3,2},{4,5},{5,4},{6,7},{7,6},{8,9},{9,8},{10,11... | collective-permute-start | bytes 7225352 | tf_op jit(solution)/shard_map/ppermute | solution.py:710
  98.7 26.4 %all-to-all-start.1 = ((bf16[8,64,768]{2,1,0:T(8,128)(2,1)}), bf16[8,64,768]{2,1,0:T(8,128)(2,1)S(1)}, u32[]{:S(2)}, u32[]{:S(2)}) async-start(bf16[8,64,768]{2,1,0:T(8,128)(2,1)} %bitcast.17), calls=%async_computation.1 | async-start | bytes 1572864 | tf_op jit(solution)/shard_map/all_to_all | solution.py:797
  108.8 7.7 %copy-start.7 = (f32[96,128]{1,0:T(8,128)S(1)}, f32[96,128]{1,0:T(8,128)}, u32[]{:S(2)}) copy-start(f32[96,128]{1,0:T(8,128)} %get-tuple-element.135.refs_3_) | copy-start | bytes 147460
  116.5 8.7 %copy-start.9 = (s32[1,512]{1,0:T(1,128)S(1)}, s32[1,512]{1,0:T(1,128)}, u32[]{:S(2)}) copy-start(s32[1,512]{1,0:T(1,128)} %refs_5_.3) | copy-start | bytes 6148
  121.7 0.6 copy-start.14
  122.3 29.4 %collective-permute-start.10 = (bf16[4800,128]{1,0:T(8,128)(2,1)}, bf16[4800,128]{1,0:T(8,128)(2,1)}, u32[]{:S(2)}, u32[]{:S(2)}) collective-permute-start(bf16[4800,128]{1,0:T(8,128)(2,1)} %get-tuple-element.136), channel_id=1, source_target_pairs={{0,2},{1,3},{2,0},{3,1},{4,6},{5,7},{6,4},{7,5},{8,10},{9,11},{10,... | collective-permute-start | bytes 3686408 | tf_op jit(solution)/shard_map/ppermute | solution.py:710
  123.8 27.9 %collective-permute-start.12 = (bf16[3840,128]{1,0:T(8,128)(2,1)}, bf16[3840,128]{1,0:T(8,128)(2,1)}, u32[]{:S(2)}, u32[]{:S(2)}) collective-permute-start(bf16[3840,128]{1,0:T(8,128)(2,1)} %get-tuple-element.150), channel_id=1, source_target_pairs={{0,8},{1,9},{2,10},{3,11},{4,12},{5,13},{6,14},{7,15},{8,0},{9,1},... | collective-permute-start | bytes 2949128 | tf_op jit(solution)/shard_map/ppermute | solution.py:710
  124.1 27.6 %collective-permute-start.11 = (bf16[3840,128]{1,0:T(8,128)(2,1)}, bf16[3840,128]{1,0:T(8,128)(2,1)}, u32[]{:S(2)}, u32[]{:S(2)}) collective-permute-start(bf16[3840,128]{1,0:T(8,128)(2,1)} %get-tuple-element.133), channel_id=1, source_target_pairs={{0,4},{1,5},{2,6},{3,7},{4,0},{5,1},{6,2},{7,3},{8,12},{9,13},{10,... | collective-permute-start | bytes 2949128 | tf_op jit(solution)/shard_map/ppermute | solution.py:710
  146.6 20.4 %collective-permute-start.9 = (bf16[7776,128]{1,0:T(8,128)(2,1)}, bf16[7776,128]{1,0:T(8,128)(2,1)}, u32[]{:S(2)}, u32[]{:S(2)}) collective-permute-start(bf16[7776,128]{1,0:T(8,128)(2,1)} %get-tuple-element.145), channel_id=1, source_target_pairs={{0,1},{1,0},{2,3},{3,2},{4,5},{5,4},{6,7},{7,6},{8,9},{9,8},{10,11... | collective-permute-start | bytes 5971976 | tf_op jit(solution)/shard_map/ppermute | solution.py:710
  157.6 0.8 copy-start.12
  158.5 0.8 copy-start.13
  159.3 26.1 %collective-permute-start.14 = (bf16[2496,128]{1,0:T(8,128)(2,1)}, bf16[2496,128]{1,0:T(8,128)(2,1)}, u32[]{:S(2)}, u32[]{:S(2)}) collective-permute-start(bf16[2496,128]{1,0:T(8,128)(2,1)} %get-tuple-element.152), channel_id=1, source_target_pairs={{0,8},{1,9},{2,10},{3,11},{4,12},{5,13},{6,14},{7,15},{8,0},{9,1},... | collective-permute-start | bytes 1916936 | tf_op jit(solution)/shard_map/ppermute | solution.py:710
  159.6 69.1 %all-to-all-start.2 = ((bf16[8,64,768]{2,1,0:T(8,128)(2,1)}), bf16[8,64,768]{2,1,0:T(8,128)(2,1)S(1)}, u32[]{:S(2)}, u32[]{:S(2)}) async-start(bf16[8,64,768]{2,1,0:T(8,128)(2,1)} %bitcast.16), calls=%async_computation.2 | async-start | bytes 1572864 | tf_op jit(solution)/shard_map/all_to_all | solution.py:797
  163.4 22.0 %collective-permute-start.15 = (bf16[1920,128]{1,0:T(8,128)(2,1)}, bf16[1920,128]{1,0:T(8,128)(2,1)S(1)}, u32[]{:S(2)}, u32[]{:S(2)}) collective-permute-start(bf16[1920,128]{1,0:T(8,128)(2,1)} %copy-done.13), channel_id=1, source_target_pairs={{0,2},{1,3},{2,0},{3,1},{4,6},{5,7},{6,4},{7,5},{8,10},{9,11},{10,... | collective-permute-start | bytes 1474568 | tf_op jit(solution)/shard_map/ppermute | solution.py:710
  165.0 20.4 %collective-permute-start.16 = (bf16[1920,128]{1,0:T(8,128)(2,1)}, bf16[1920,128]{1,0:T(8,128)(2,1)S(1)}, u32[]{:S(2)}, u32[]{:S(2)}) collective-permute-start(bf16[1920,128]{1,0:T(8,128)(2,1)} %copy-done.12), channel_id=1, source_target_pairs={{0,4},{1,5},{2,6},{3,7},{4,0},{5,1},{6,2},{7,3},{8,12},{9,13},{10,... | collective-permute-start | bytes 1474568 | tf_op jit(solution)/shard_map/ppermute | solution.py:710
  166.9 1.1 copy-start.4
  171.3 20.4 %collective-permute-start.13 = (bf16[2016,128]{1,0:T(8,128)(2,1)S(1)}, bf16[2016,128]{1,0:T(8,128)(2,1)S(1)}, u32[]{:S(2)}, u32[]{:S(2)}) collective-permute-start(bf16[2016,128]{1,0:T(8,128)(2,1)S(1)} %get-tuple-element.156), channel_id=1, source_target_pairs={{0,2},{1,3},{2,0},{3,1},{4,6},{5,7},{6,4},{7,5},{8,10},{9,11},{10,... | collective-permute-start | bytes 1548296 | tf_op jit(solution)/shard_map/ppermute | solution.py:710
  171.9 24.4 %collective-permute-start.17 = (bf16[1920,128]{1,0:T(8,128)(2,1)S(1)}, bf16[1920,128]{1,0:T(8,128)(2,1)S(1)}, u32[]{:S(2)}, u32[]{:S(2)}) collective-permute-start(bf16[1920,128]{1,0:T(8,128)(2,1)S(1)} %get-tuple-element.167), channel_id=1, source_target_pairs={{0,4},{1,5},{2,6},{3,7},{4,0},{5,1},{6,2},{7,3},{8,12},{9,13},{10,... | collective-permute-start | bytes 1474568 | tf_op jit(solution)/shard_map/ppermute | solution.py:710
  188.3 15.4 %collective-permute-start.19 = (bf16[1344,128]{1,0:T(8,128)(2,1)S(1)}, bf16[1344,128]{1,0:T(8,128)(2,1)S(1)}, u32[]{:S(2)}, u32[]{:S(2)}) collective-permute-start(bf16[1344,128]{1,0:T(8,128)(2,1)S(1)} %get-tuple-element.164), channel_id=1, source_target_pairs={{0,4},{1,5},{2,6},{3,7},{4,0},{5,1},{6,2},{7,3},{8,12},{9,13},{10,... | collective-permute-start | bytes 1032200 | tf_op jit(solution)/shard_map/ppermute | solution.py:710
  188.9 14.8 %collective-permute-start.20 = (bf16[960,128]{1,0:T(8,128)(2,1)S(1)}, bf16[960,128]{1,0:T(8,128)(2,1)S(1)}, u32[]{:S(2)}, u32[]{:S(2)}) collective-permute-start(bf16[960,128]{1,0:T(8,128)(2,1)S(1)} %get-tuple-element.175), channel_id=1, source_target_pairs={{0,8},{1,9},{2,10},{3,11},{4,12},{5,13},{6,14},{7,15},{8,0},{9,1},... | collective-permute-start | bytes 737288 | tf_op jit(solution)/shard_map/ppermute | solution.py:710
  190.0 13.7 %collective-permute-start.21 = (bf16[960,128]{1,0:T(8,128)(2,1)S(1)}, bf16[960,128]{1,0:T(8,128)(2,1)S(1)}, u32[]{:S(2)}, u32[]{:S(2)}) collective-permute-start(bf16[960,128]{1,0:T(8,128)(2,1)S(1)} %get-tuple-element.176), channel_id=1, source_target_pairs={{0,2},{1,3},{2,0},{3,1},{4,6},{5,7},{6,4},{7,5},{8,10},{9,11},{10,... | collective-permute-start | bytes 737288 | tf_op jit(solution)/shard_map/ppermute | solution.py:710
  197.1 11.0 %collective-permute-start.18 = (bf16[1056,128]{1,0:T(8,128)(2,1)S(1)}, bf16[1056,128]{1,0:T(8,128)(2,1)S(1)}, u32[]{:S(2)}, u32[]{:S(2)}) collective-permute-start(bf16[1056,128]{1,0:T(8,128)(2,1)S(1)} %get-tuple-element.170), channel_id=1, source_target_pairs={{0,4},{1,5},{2,6},{3,7},{4,0},{5,1},{6,2},{7,3},{8,12},{9,13},{10,... | collective-permute-start | bytes 811016 | tf_op jit(solution)/shard_map/ppermute | solution.py:710
  198.3 9.8 %collective-permute-start.22 = (bf16[960,128]{1,0:T(8,128)(2,1)S(1)}, bf16[960,128]{1,0:T(8,128)(2,1)S(1)}, u32[]{:S(2)}, u32[]{:S(2)}) collective-permute-start(bf16[960,128]{1,0:T(8,128)(2,1)S(1)} %get-tuple-element.181), channel_id=1, source_target_pairs={{0,2},{1,3},{2,0},{3,1},{4,6},{5,7},{6,4},{7,5},{8,10},{9,11},{10,... | collective-permute-start | bytes 737288 | tf_op jit(solution)/shard_map/ppermute | solution.py:710
  203.7 27.0 %copy-start.3 = (f32[256,768]{1,0:T(8,128)S(1)}, f32[256,768]{1,0:T(8,128)}, u32[]{:S(2)}) copy-start(f32[256,768]{1,0:T(8,128)} %get-tuple-element.188.refs_2_) | copy-start | bytes 2359300
  204.5 22.7 %collective-permute-start.25 = (bf16[1728,128]{1,0:T(8,128)(2,1)S(1)}, bf16[1728,128]{1,0:T(8,128)(2,1)S(1)}, u32[]{:S(2)}, u32[]{:S(2)}) collective-permute-start(bf16[1728,128]{1,0:T(8,128)(2,1)S(1)} %get-tuple-element.178), channel_id=1, source_target_pairs={{0,16},{1,17},{2,18},{3,19},{4,20},{5,21},{6,22},{7,23},{8,24},{9,... | collective-permute-start | bytes 1327112 | tf_op jit(solution)/shard_map/ppermute | solution.py:710
  208.8 10.5 %collective-permute-start.23 = (bf16[1056,128]{1,0:T(8,128)(2,1)S(1)}, bf16[1056,128]{1,0:T(8,128)(2,1)S(1)}, u32[]{:S(2)}, u32[]{:S(2)}) collective-permute-start(bf16[1056,128]{1,0:T(8,128)(2,1)S(1)} %get-tuple-element.184), channel_id=1, source_target_pairs={{0,8},{1,9},{2,10},{3,11},{4,12},{5,13},{6,14},{7,15},{8,0},{9,1},... | collective-permute-start | bytes 811016 | tf_op jit(solution)/shard_map/ppermute | solution.py:710
  219.9 12.9 %collective-permute-start.24 = (bf16[576,128]{1,0:T(8,128)(2,1)S(1)}, bf16[576,128]{1,0:T(8,128)(2,1)S(1)}, u32[]{:S(2)}, u32[]{:S(2)}) collective-permute-start(bf16[576,128]{1,0:T(8,128)(2,1)S(1)} %get-tuple-element.186), channel_id=1, source_target_pairs={{0,16},{1,17},{2,18},{3,19},{4,20},{5,21},{6,22},{7,23},{8,24},{9,... | collective-permute-start | bytes 442376 | tf_op jit(solution)/shard_map/ppermute | solution.py:710

commit v3 on v2

--- a/solution.py
+++ b/solution.py
@@ -89,11 +89,14 @@
     return ids[0] if blocks > 1 else 0
 
 
+ORDER = (0, 1, 2, 3, 4, 5, 6, 7)
+
+
 def block_rows(ids, k, refs):
     size = refs[0].shape[0]
     if len(refs) == 1:
         return pl.ds(0, size)
-    return pl.ds(pl.multiple_of((ids[0] ^ k) * size, size), size)
+    return pl.ds(pl.multiple_of((ids[0] ^ ORDER[k]) * size, size), size)
 
 
 def pack_kernel(peers, capacity, ids, dest_row, tokens, *outs):
@@ -101,7 +104,7 @@
     held = jnp.sum(place.astype(F32), axis=1, keepdims=True)
     rows = jnp.where(held > 0.5, dot(place.astype(BF16), tokens[...]), DEAD).astype(BF16)
     size = outs[0].shape[0]
-    for k, out in enumerate(outs):
+    for out, k in zip(outs, ORDER):
         out[...] = rows[k * size : (k + 1) * size]
 
 
@@ -274,9 +277,9 @@
     small[0:1, :] = jnp.sum(sums[0], axis=0, keepdims=True)
     small[1:2, :] = jnp.sum(sums[1], axis=0, keepdims=True)
     if shared:
-        set_blocks(refs[8], turned, ids, 2, 8, 2)
-        joined_products(sender(send, joined_place, JOINED_BASE, (JOINED_ROWS,) * 2), 1, ids, turned, g_joined)
-        write_small(small, send, 32 * JOINED_ROWS)
+        set_blocks(refs[8], turned, 0, ids, 2, 8, JOINED_SPLIT)
+        joined_products(sender(send, joined_place, JOINED_BASE, JOINED_PARTS), 1, ids, turned, g_joined)
+        write_small(small, send, 16 * sum(JOINED_PARTS))
 
 
 def folded(rows):
@@ -305,7 +308,7 @@
      gain3, shift3, align_hbm, align_bias), refs = refs[:18], refs[18:]
     (y_out, al_out, g_packed, g_mid, hidden, gub, a2, a3, ctx, gyb, gmb, small), refs = refs[:12], refs[12:]
     if shared:
-        (send_1, send_2, turned_d, turned_3, turned_2, turned_1, small_e), refs = refs[:7], refs[7:]
+        (send, own), refs = refs[:2], refs[2:]
     (mid, acc, hat2, rstd2, slope, u_a, u_b, h_a, h_b, sums, w_out, w_up, w_down, w_align, sems), refs = refs[:15], refs[15:]
     rows, width = tokens.shape
     wide = hidden.shape[1]
@@ -429,20 +432,29 @@
     for c in range(wide // width):
         small[11 + c : 12 + c, :] = g_up[:, c * width : (c + 1) * width]
     if shared:
-        (natural,) = refs
-        turn(gyb, natural, turned_d, ids, 10, 4)
-        traffic.ready(14)
-        put = sender(send_1, early_place, (0,), EARLY_PARTS)
-        first_products(put, 1, ids, turned_d, hidden)
-        small_e[...] = rows_of_small(small[...])
-        write_small(small, send_1, SENT_1)
-        traffic.ready(12, 18)
-        turn(a2, natural, turned_2, ids, 2, 8)
-        turn(ctx, natural, turned_1, ids, 2, 8)
-        turn(a3, natural, turned_3, ids, 2, 8)
-        traffic.ready(15, 16, 17)
-        put = sender(send_2, early_place, (None, 0, SENT_BASE), EARLY_PARTS)
-        second_products(put, 1, ids, turned_3, turned_2, turned_1, cot_align, gub, gmb)
+        natural, turned_d = refs
+        turn(gyb, natural, turned_d, 0, ids, 10, 4)
+        own[OWN_D : OWN_D + 384, :] = turned_d[0:384, :]
+        send[AT_D : AT_D + 384, :] = turned_d[384:768, :]
+        for core, out, align_at, out_at in ((0, own, OWN_ALIGN, OWN_OUT), (1, send, AT_ALIGN, AT_OUT)):
+            for x in range(2):
+                at = slice(align_at + x * 256, align_at + x * 256 + 256)
+                out[at, :] = cot_align[:, own_columns(ids, core, x, 256)]
+                at = slice(out_at + x * 256, out_at + x * 256 + 256)
+                out[at, :] = spare_columns(gmb, ids[1] ^ (core + 2 * x), 192, 256)
+        turn(a3, natural, send, AT_3, ids, 2, 8)
+        turn(ctx, natural, send, AT_1, ids, 2, 8)
+        turn(a2, natural, send, AT_2, ids, 2, 8)
+        for core, out, up_at in ((0, own, OWN_UP), (1, send, AT_UP)):
+            for x in range(2):
+                for c in range(3):
+                    at = pl.ds(pl.multiple_of((ids[1] ^ (core + 2 * x)) * 768 + c * 256, 128), 256)
+                    to = up_at + (x * 3 + c) * 256
+                    out[to : to + 256, :] = gub[:, at]
+        for c in range(3):
+            high, rest = split_small(small[:, c * 256 : (c + 1) * 256])
+            send[AT_SMALL + c * 16 : AT_SMALL + c * 16 + 16, :] = high
+            send[AT_SMALL + 48 + c * 16 : AT_SMALL + 64 + c * 16, :] = rest
 
 
 def last_kernel(peers, capacity, ids, arrived, dest_col, g_mid, out):
@@ -450,24 +462,31 @@
     out[...] = (g_mid[...] + dot(fetch, arrived[...])).astype(BF16)
 
 
-EARLY_PARTS, JOINED_ROWS = (576, 480, 480), 240
-SENT_1, SENT_2, SENT_BASE, JOINED_BASE = 16 * 576, 16 * 960, 16 * 480, (0, 16 * 240)
-
-
-def set_blocks(natural, out, ids, first, count, parts):
-    size = natural.shape[0] // count // parts
+EARLY_PARTS, JOINED_PARTS, JOINED_SPLIT = (576, 576, 384), (240, 240), (48, 48)
+JOINED_BASE = (0, 16 * 240)
+AT_2, AT_3, AT_1, AT_D, AT_UP, AT_ALIGN, AT_OUT, AT_SMALL, SENT = 0, 768, 1536, 2304, 2688, 4224, 4736, 5248, 5344
+OWN_D, OWN_UP, OWN_ALIGN, OWN_OUT, OWN = 0, 384, 1920, 2432, 2944
+
+
+def set_blocks(natural, out, base, ids, first, count, sizes):
+    at = 0
     for j in range(count):
-        for part in range(parts):
-            to = part * count * size + ids[first + j] * size
-            at = (j * parts + part) * size
-            out[pl.ds(pl.multiple_of(to, size), size), :] = natural[at : at + size, :]
-
-
-def turn(source, natural, out, ids, first, count):
+        start = base
+        for size in sizes:
+            to = start + ids[first + j] * size
+            out[pl.ds(pl.multiple_of(to, 16), size), :] = natural[at : at + size, :]
+            at, start = at + size, start + count * size
+
+
+def turn_into(source, natural):
     for c in range(source.shape[1] // 128):
         at = slice(c * 128, (c + 1) * 128)
         natural[at, :] = jnp.transpose(source[:, at].astype(F32)).astype(BF16)
-    set_blocks(natural, out, ids, first, count, 1)
+
+
+def turn(source, natural, out, base, ids, first, count):
+    turn_into(source, natural)
+    set_blocks(natural, out, base, ids, first, count, (source.shape[1] // count,))
 
 
 def spare_columns(ref, index, step, load):
@@ -486,7 +505,7 @@
 
 def early_place(part, x, i):
     y, low, high = i >> 2, (i >> 1) & 1, i & 1
-    return (x * 8 + low * 4 + y * 2 + high, y * 8 + x * 4 + low * 2 + high, low * 8 + y * 4 + x * 2 + high)[part]
+    return (x * 8 + low * 4 + y * 2 + high, y * 8 + x * 4 + high * 2 + low, low * 8 + y * 4 + x * 2 + high)[part]
 
 
 def sender(send, place, bases, sizes):
@@ -536,63 +555,113 @@
     return pl.ds(pl.multiple_of((ids[1] ^ (core + 2 * x)) * step, 128), step)
 
 
-def first_products(put, core, ids, turned_d, hidden):
-    for i in range(8):
-        at = pl.ds(pl.multiple_of((ids[0] ^ batch_relative(i)) * 384, 128), 384)
-        made = dot(turned_d[core * 384 : core * 384 + 384, :], hidden[:, at])
-        for x in range(2):
-            for c in range(3):
-                put(0, x, i, c * 192, made[x * 192 : x * 192 + 192, c * 128 : c * 128 + 128])
-
-
-def second_products(put, core, ids, turned_3, turned_2, turned_1, da, gub, gmb):
-    for x in range(2):
-        for c in range(3):
-            at = pl.ds(pl.multiple_of((ids[1] ^ (core + 2 * x)) * 768 + c * 256, 128), 256)
-            made = dot(turned_2[...], gub[:, at])
-            for i in range(8):
-                for half in range(2):
-                    rows = made[i * 96 : i * 96 + 96, half * 128 : half * 128 + 128]
-                    slab = 2 * c + half
-                    put(1 + slab // 5, x, i, slab % 5 * 96, rows)
-        align = dot(turned_3[...], da[:, own_columns(ids, core, x, 256)])
-        out = dot(turned_1[...], spare_columns(gmb, ids[1] ^ (core + 2 * x), 192, 256))
-        for i in range(8):
-            for half in range(2):
-                part = slice(half * 128, half * 128 + 128)
-                put(2, x, i, 96 + half * 96, align[i * 96 : i * 96 + 96, part])
-                put(2, x, i, 288 + half * 96, out[i * 96 : i * 96 + 96, part])
-
-
 def joined_products(put, core, ids, turned, g_joined):
     for x in range(2):
         own = spare_columns(g_joined, ids[1] ^ (core + 2 * x), 576, 640)
         for c, slabs in ((0, 2), (2, 2), (4, 1)):
             made = dot(turned[...], own[:, c * 128 : (c + slabs) * 128])
-            for part in range(2):
+            for part, size in enumerate(JOINED_SPLIT):
                 for i in range(8):
-                    at = part * 384 + i * 48
+                    at = part * 8 * JOINED_SPLIT[0] + i * size
                     for k in range(slabs):
-                        put(part, x, i, (c + k) * 48, made[at : at + 48, k * 128 : k * 128 + 128])
-
-
-def first_keep(ids, turned_d, hidden, came, small, keep, send, total):
-    put = keeper(came, early_place, (0,), EARLY_PARTS, ((keep, send),))
-    first_products(put, 0, ids, turned_d, hidden)
-    pass_small(small, came, SENT_1, total, send, 8 * EARLY_PARTS[0])
-
-
-def second_keep(ids, turned_3, turned_2, turned_1, da, gub, gmb, came, keep_1, send_1, keep_2, send_2):
-    outs = (None, (keep_1, send_1), (keep_2, send_2))
-    put = keeper(came, early_place, (None, 0, SENT_BASE), EARLY_PARTS, outs)
-    second_products(put, 0, ids, turned_3, turned_2, turned_1, da, gub, gmb)
+                        put(part, x, i, (c + k) * size, made[at : at + size, k * 128 : k * 128 + 128])
+
+
+def writer(outs):
+    def put(part, x, i, at, value):
+        where, count = early_place(part, x, i), value.shape[0]
+        start = (where & 7) * EARLY_PARTS[part] + at
+        outs[part][where >> 3][start : start + count, :] = value.astype(BF16)
+
+    return put
+
+
+def fetch_rows(pieces, sems):
+    copies = []
+    for k, (source, at, buffer) in enumerate(pieces):
+        source = source if at is None else source.at[pl.ds(at, buffer.shape[0]), :]
+        copies.append(pltpu.make_async_copy(source, buffer, sems.at[k]))
+        copies[-1].start()
+    return copies
+
+
+def first_grads(
+    traffic, ids, hidden_hbm, came_hidden_hbm, sent, own, came, keep_1, send_1, keep_2, send_2,
+    turned_o, turned_c, ends_o, ends_c, down_o, down_c, hidden, came_hidden, sems,
+):
+    copies = fetch_rows(
+        ((sent, AT_3, turned_o), (came, AT_3, turned_c), (own, OWN_ALIGN, ends_o), (came, AT_ALIGN, ends_c),
+         (own, OWN_D, down_o), (came, AT_D, down_c), (hidden_hbm, None, hidden), (came_hidden_hbm, None, came_hidden)),
+        sems,
+    )
+    put = writer((None, (keep_1, send_1), (keep_2, send_2)))
+    for copy in copies[:4]:
+        copy.wait()
+    for x in range(2):
+        for k, shift in ((0, 0), (1, 192)):
+            turned = slice(k * 768, k * 768 + 768)
+            at = slice(k * 512 + x * 256, k * 512 + x * 256 + 256)
+            made = dot(turned_o[turned, :], ends_o[at, :])
+            made += dot(turned_c[turned, :], ends_c[at, :])
+            for i in range(8):
+                for half in range(2):
+                    put(2, x, i, shift + half * 96, made[i * 96 : i * 96 + 96, half * 128 : half * 128 + 128])
+    traffic.ready(2, 3)
+    for copy in copies[4:]:
+        copy.wait()
+    for i in (4, 5, 6, 7, 0, 1, 2, 3):
+        at = pl.ds(pl.multiple_of((ids[0] ^ batch_relative(i)) * 384, 128), 384)
+        made = dot(down_o[...], hidden[:, at])
+        made += dot(down_c[...], came_hidden[:, at])
+        for x in range(2):
+            for c in range(3):
+                put(1, x, i, c * 192, made[x * 192 : x * 192 + 192, c * 128 : c * 128 + 128])
+        if i == 7:
+            traffic.ready(1)
+
+
+def second_grads(
+    traffic, ids, sent, own, came, keep, send, total,
+    turned_o, turned_c, up_o, up_c, small_o, small_c, sems,
+):
+    copies = fetch_rows(
+        ((sent, AT_2, turned_o), (came, AT_2, turned_c), (own, OWN_UP, up_o), (came, AT_UP, up_c),
+         (sent, AT_SMALL, small_o), (came, AT_SMALL, small_c)),
+        sems,
+    )
+    put = writer(((keep, send),))
+    for copy in copies:
+        copy.wait()
+    to = 8 * EARLY_PARTS[0]
+    for c in range(6):
+        lanes = slice(c % 2 * 128, c % 2 * 128 + 128)
+        both = None
+        for ref in (small_o, small_c):
+            at = c // 2 * 16
+            value = ref[at : at + 16, lanes].astype(F32) + ref[at + 48 : at + 64, lanes].astype(F32)
+            both = value if both is None else both + value
+        total[c * 16 : c * 16 + 16, :] = both
+        high, rest = split_small(both)
+        send[to + c * 16 : to + c * 16 + 16, :] = high
+        send[to + 96 + c * 16 : to + 112 + c * 16, :] = rest
+    for x in (1, 0):
+        for c in range(3):
+            at = slice((x * 3 + c) * 256, (x * 3 + c) * 256 + 256)
+            made = dot(turned_o[...], up_o[at, :])
+            made += dot(turned_c[...], up_c[at, :])
+            for i in range(8):
+                for half in range(2):
+                    rows = made[i * 96 : i * 96 + 96, half * 128 : half * 128 + 128]
+                    put(0, x, i, (2 * c + half) * 96, rows)
+        if x == 1:
+            traffic.ready(1)
 
 
 def joined_keep(ids, turned, g_joined, came, small, keep_x, send_x, keep_y, send_y, total):
     outs = ((keep_x, send_x), (keep_y, send_y))
-    put = keeper(came, joined_place, JOINED_BASE, (JOINED_ROWS,) * 2, outs)
+    put = keeper(came, joined_place, JOINED_BASE, JOINED_PARTS, outs)
     joined_products(put, 0, ids, turned, g_joined)
-    pass_small_of(rows_of_small(small[...]), came, 32 * JOINED_ROWS, total, send_x, 8 * JOINED_ROWS)
+    pass_small_of(rows_of_small(small[...]), came, 16 * sum(JOINED_PARTS), total, send_x, 8 * JOINED_PARTS[0])
 
 
 def pass_small(small, came, from_row, total, send, to_row):
@@ -609,61 +678,66 @@
         send[to_row + count : to_row + 2 * count, :] = rest
 
 
+def joined_half(keep, came, at, count):
+    rows = slice(at, at + count)
+    return keep[rows, :] + came[rows, :]
+
+
 def added(keep, came, at, count):
     rows = slice(at, at + count)
     return keep[rows, :].astype(F32) + came[rows, :].astype(F32)
 
 
-def step_parts(ids, *refs):
+def step_parts(traffic, ids, *refs):
     keeps, cames, small = refs[0:3], refs[3:6], refs[6]
     outs, sends, total = refs[7:10], refs[10:13], refs[13]
-    for keep, came, out, send in zip(keeps, cames, outs, sends):
+    for k, (keep, came, out, send) in enumerate(zip(keeps, cames, outs, sends)):
         half = keep.shape[0] // 2
-        out[...] = added(keep, came, 0, half).astype(BF16)
-        send[0:half, :] = added(keep, came, half, half).astype(BF16)
-    half = keeps[0].shape[0] // 2
-    pass_small(small, cames[0], 2 * half, total, sends[0], half)
+        traffic.need(k, 3 + k)
+        send[0:half, :] = joined_half(keep, came, half, half)
+        if k == 0:
+            traffic.need(6)
+            pass_small(small, came, 2 * half, total, send, half)
+        traffic.ready(3 + k)
+        out[...] = joined_half(keep, came, 0, half)
+        traffic.ready(k)
 
 
 def step_parts_last(ids, *refs):
     keeps, cames, small = refs[0:3], refs[3:6], refs[6]
-    outs, send, total = refs[7:10], refs[10], refs[11]
+    outs, sends, total = refs[7:10], refs[10:12], refs[12]
+    for k, to, at in ((0, 0, 0), (1, 1, 0), (2, 0, EARLY_PARTS[0])):
+        half = keeps[k].shape[0] // 2
+        outs[k][...] = joined_half(keeps[k], cames[k], 0, half)
+        sends[to][at : at + half, :] = joined_half(keeps[k], cames[k], half, half)
+    pass_small(small, cames[0], keeps[0].shape[0], total, sends[0], EARLY_PARTS[0] + EARLY_PARTS[2])
+
+
+def step_apart(ids, keep_x, came_x, keep_y, came_y, small, out_x, send_x, out_y, send_y, total):
+    for keep, came, out, send in ((keep_x, came_x, out_x, send_x), (keep_y, came_y, out_y, send_y)):
+        half = keep.shape[0] // 2
+        out[...] = joined_half(keep, came, 0, half)
+        send[0:half, :] = joined_half(keep, came, half, half)
+    pass_small(small, came_x, keep_x.shape[0], total, send_x, keep_x.shape[0] // 2)
+
+
+def step_meet(ids, keep_x, came_x, keep_y, came_y, small, out, send, total):
     at = 0
-    for keep, came, out in zip(keeps, cames, outs):
+    for keep, came in ((keep_x, came_x), (keep_y, came_y)):
         half = keep.shape[0] // 2
-        out[...] = added(keep, came, 0, half).astype(BF16)
-        send[at : at + half, :] = added(keep, came, half, half).astype(BF16)
+        out[at : at + half, :] = joined_half(keep, came, 0, half)
+        send[at : at + half, :] = joined_half(keep, came, half, half)
         at += half
-    pass_small(small, cames[0], keeps[0].shape[0], total, send, at)
-
-
-def step_apart(ids, keep_x, came_x, keep_y, came_y, *refs):
-    small, out_x, send_x, out_y, send_y, total = refs
-    half = keep_x.shape[0] // 2
-    for keep, came, out, send in ((keep_x, came_x, out_x, send_x), (keep_y, came_y, out_y, send_y)):
-        out[...] = added(keep, came, 0, half).astype(BF16)
-        send[0:half, :] = added(keep, came, half, half).astype(BF16)
-    pass_small(small, came_x, 2 * half, total, send_x, half)
-
-
-def step_meet(ids, keep_x, came_x, keep_y, came_y, *refs):
-    small, out, send, total = refs
-    half = keep_x.shape[0] // 2
-    for part, (keep, came) in enumerate(((keep_x, came_x), (keep_y, came_y))):
-        at = slice(part * half, (part + 1) * half)
-        out[at, :] = added(keep, came, 0, half).astype(BF16)
-        send[at, :] = added(keep, came, half, half).astype(BF16)
-    pass_small(small, came_x, 2 * half, total, send, 2 * half)
-
-
-def step_joint(ids, keep, came, *refs):
-    small, out, send, total = refs
-    half = keep.shape[0] // 4
-    for part in range(2):
-        at = slice(part * half, (part + 1) * half)
-        out[at, :] = added(keep, came, part * 2 * half, half).astype(BF16)
-        send[at, :] = added(keep, came, part * 2 * half + half, half).astype(BF16)
-    pass_small(small, came, 4 * half, total, send, 2 * half)
+    pass_small(small, came_x, keep_x.shape[0], total, send, at)
+
+
+def step_joint(ids, keep, came, small, out, send, total):
+    at = 0
+    for half in JOINED_PARTS:
+        out[at : at + half, :] = joined_half(keep, came, 2 * at, half)
+        send[at : at + half, :] = joined_half(keep, came, 2 * at + half, half)
+        at += half
+    pass_small(small, came, 2 * at, total, send, at)
 
 
 def small_columns(small, out):
@@ -672,32 +746,33 @@
         out[:, c * 128 : (c + 1) * 128] = small[c * count : (c + 1) * count]
 
 
-def early_end(ids, keep_0, keep_1, keep_2, came, small, down, align, up, out, total):
-    def block(keep, base, at, count):
-        return keep[at : at + count, :].astype(F32) + came[base + at : base + at + count, :].astype(F32)
+def early_end(ids, keep_0, keep_1, keep_2, came, came_1, small, down, align, up, out, total):
+    def block(at, count):
+        return keep_2[at : at + count, :].astype(F32) + came[576 + at : 576 + at + count, :].astype(F32)
 
     for c in range(3):
-        down[c * 128 : (c + 1) * 128, :] = jnp.transpose(block(keep_0, 0, c * 192, 192))
-    for c in range(5):
-        up[:, c * 128 : (c + 1) * 128] = block(keep_1, 576, c * 96, 96)
-    up[:, 640:768] = block(keep_2, 1056, 0, 96)
+        down[c * 128 : (c + 1) * 128, :] = jnp.transpose(added(keep_1, came_1, c * 192, 192))
+    for c in range(6):
+        up[:, c * 128 : (c + 1) * 128] = added(keep_0, came, c * 96, 96)
     for c in range(2):
-        align[:, c * 128 : (c + 1) * 128] = block(keep_2, 1056, 96 + c * 96, 96)
-    out[:, 0:128] = block(keep_2, 1056, 288, 96)
-    out[:, 128:192] = block(keep_2, 1056, 384, 96)[:, 0:64]
+        align[:, c * 128 : (c + 1) * 128] = block(c * 96, 96)
+    out[:, 0:128] = block(192, 96)
+    out[:, 128:192] = block(288, 96)[:, 0:64]
     count = small.shape[0]
-    both = both_small(small[...], came[1536 : 1536 + 2 * count, :])
+    both = both_small(small[...], came[960 : 960 + 2 * count, :])
     small_columns(both, total)
 
 
 def joined_end(ids, keep, came, small, out, total):
-    for part in range(2):
-        rows = slice(part * 48, part * 48 + 48)
+    start, at = 0, 0
+    for part, size in enumerate(JOINED_SPLIT):
+        rows = slice(start, start + size)
         for c in range(4):
-            out[rows, c * 128 : (c + 1) * 128] = added(keep, came, part * 240 + c * 48, 48)
-        out[rows, 512:576] = added(keep, came, part * 240 + 192, 48)[:, 0:64]
+            out[rows, c * 128 : (c + 1) * 128] = added(keep, came, at + c * size, size)
+        out[rows, 512:576] = added(keep, came, at + 4 * size, size)[:, 0:64]
+        start, at = start + size, at + 5 * size
     count = small.shape[0]
-    both = both_small(small[...], came[480 : 480 + 2 * count, :])
+    both = both_small(small[...], came[at : at + 2 * count, :])
     small_columns(both, total)
 
 
@@ -796,8 +871,7 @@
         shaped = blocks[0].reshape(peers, blocks[0].shape[0] // peers, blocks[0].shape[1])
         moved = lax.all_to_all(shaped, "batch", split_axis=0, concat_axis=0, tiled=True)
         return [moved.reshape(blocks[0].shape)]
-    came = {k: flip(blocks[k], "batch", k, peers, groups) for k in range(1, peers)}
-    return [blocks[0]] + [came[k] for k in range(1, peers)]
+    return [blocks[0]] + [flip(block, "batch", k, peers, groups) for k, block in zip(ORDER[1:], blocks[1:])]
 
 
 def per_device(
@@ -850,7 +924,10 @@
     (ctx,) = exchange([ctx], peers, groups)
 
     full = shape((rows, width), F32)
-    joined, extra = JOINED_ROWS, 12 * 16
+    extra = 12 * 16
+    parts = lambda n: [flat(n * JOINED_PARTS[0]), flat(n * JOINED_PARTS[0] + more), flat(n * JOINED_PARTS[1]), flat(n * JOINED_PARTS[1])]
+    both = sum(JOINED_PARTS)
+    more = 12 * 8
     chain = lambda n: [flat(n * EARLY_PARTS[0] + extra)] + [flat(n * r) for r in EARLY_PARTS[1:]]
     held = lambda n: [flat(n * r) for r in EARLY_PARTS]
     small_early = shape((96, 128), F32)
@@ -858,53 +935,56 @@
     y, al, g_packed, g_mid, hidden, gub, a2, a3, ctx_rows, gyb, gmb, small_0, *sent = call(
         functools.partial(rows_kernel, peers, capacity, fast), "rows", 46,
         [low(width), low(align), in_slots, full, low(wide), low(wide), low(width), low(width), low(width), low(width), low(width),
-         shape((16, width), F32)] + ([flat(SENT_1 + extra), flat(SENT_2), turned, turned, turned, turned, small_early] if fast else []),
+         shape((16, width), F32)] + ([shape((SENT, 256), BF16), shape((OWN, 256), BF16)] if fast else []),
         [vmem((rows, width), F32), vmem((rows, width), F32), vmem((rows, width), F32), vmem((rows, 128), F32), vmem((rows, wide), F32),
          vmem((rows, 512), F32), vmem((rows, 512), F32), vmem((rows, 512), BF16), vmem((rows, 512), BF16),
          vmem((2, 8, width), F32), vmem(w_out.shape, BF16), vmem(w_up.shape, BF16), vmem(w_down.shape, BF16),
-         vmem(w_align.shape, BF16), dma((4,))] + ([vmem((width, rows), BF16)] if fast else []),
+         vmem(w_align.shape, BF16), dma((4,))] + ([vmem((width, rows), BF16)] * 2 if fast else []),
         ids, ctx, tokens, dest, dest_row, cot_out, cot_align,
         w_out, line(out_bias), line(ln2_gain), line(ln2_bias), w_up, line(up_bias), w_down, line(down_bias),
         line(ln3_gain), line(ln3_bias), w_align, line(align_bias),
-        far=(6, 10, 12, 16), flush=(0, 1, 2, 3, 4, 5, 10) + ((12, 13, 14, 15, 16, 17, 18) if fast else ()), kept=(6, 7, 8, 9, 11), lazy=True,
+        far=(6, 10, 12, 16), flush=(0, 1, 2, 3, 4) + ((12, 13) if fast else ()), kept=(5, 6, 7, 8, 9, 10, 11), lazy=True,
     )
     (g_arrived,) = exchange([g_packed], peers, groups)
 
     if fast:
-        send_1, send_2, turned_d, turned_3, turned_2, turned_1, small_e = sent
-        came_2 = move(send_2, "grp", 1)
-        came_1 = move(send_1, "grp", 1)
+        sent, own = sent
+        came = move(sent, "grp", 1)
+        came_hidden = move(hidden, "grp", 1)
         routes = (
             (("grp", 2), ("batch", 2), ("batch", 1)),
-            (("batch", 1), ("grp", 2), ("batch", 2)),
+            (("batch", 1), ("grp", 2), ("batch", 4)),
             (("batch", 2), ("batch", 1), ("grp", 2)),
         )
         go = lambda sends, k: [move(send, *route[k]) for send, route in zip(sends, routes)]
+        square = lambda n: vmem((n, rows), BF16)
+        k0, s0, small_e = call(
+            second_grads, "second_grads", 16, [held(8)[0], chain(8)[0], small_early],
+            [square(768), square(768), square(1536), square(1536), square(96), square(96), dma((6,))],
+            ids, sent, own, came,
+            far=(0, 1, 2), flush=(0, 1), kept=(2,), lazy=True,
+        )
         k1, s1, k2, s2 = call(
-            second_keep, "second_keep", 24, [held(8)[1], held(8)[1], held(8)[2], held(8)[2]], [],
-            ids, turned_3, turned_2, turned_1, cot_align, gub, gmb, came_2,
-            load=(0, 1, 2, 3, 4, 5), flush=(0, 2),
-        )
-        k0, s0, small_e = call(
-            first_keep, "first_keep", 20, [held(8)[0], chain(8)[0], small_early], [],
-            ids, turned_d, hidden, tie(came_1, s1), small_e,
-            load=(0, 1), flush=(0,),
+            first_grads, "first_grads", 20, [held(8)[1], held(8)[1], held(8)[2], held(8)[2]],
+            [square(1536), square(1536), square(1024), square(1024), square(384), square(384),
+             vmem((rows, wide), BF16), vmem((rows, wide), BF16), dma((8,))],
+            ids, hidden, came_hidden, sent, own, tie(came, s0),
+            far=(0, 1, 2, 3, 4), flush=(0, 1, 2, 3), lazy=True,
         )
         keeps, sends = [k0, k1, k2], [s0, s1, s2]
         cames = go(sends, 0)
-        g_arrived = tie(g_arrived, s0)
-
-    more = 12 * 8
+        g_arrived = tie(g_arrived, s1)
+
     outs = [in_slots, shape((slots, 3 * width), BF16), shape((8, width), F32)]
     turned = shape((width, slots), BF16)
     made = call(
         functools.partial(attention_back_kernel, fast), "attention_back", 28,
-        outs + ([flat(32 * joined + more), turned] if fast else []),
+        outs + ([flat(16 * both + more), turned] if fast else []),
         [vmem((count, 3 * CLIPMAX, 2 * CLIPMAX), F32), vmem((128, slots), BF16), vmem((slots, 128), F32), vmem((slots, 128), F32),
          vmem((slots, width), F32), vmem((2, 8, width), F32), vmem((width, 3 * width), BF16), dma]
         + ([vmem((width, slots), BF16)] if fast else []),
         ids, g_arrived, natural, qkv, lse, a1, seg_ids, seg_col, line(ln1_gain), w_qkv,
-        far=(8,), load=(1, 6, 2, 3, 4), flush=(0, 4) if fast else (0,), lazy=True,
+        far=(8,), load=(1, 6, 2, 3, 4), flush=(0, 1, 4) if fast else (0,), lazy=True,
     )
     g_rows, g_joined, small_2 = made[:3]
     (g_back,) = exchange([g_rows], peers, groups)
@@ -917,45 +997,46 @@
         def early_step(name, n, keeps, cames, small_e, before, cost, **more_of):
             made = call(
                 step_parts, name, 14, held(n) + chain(n) + [small_early], [],
-                ids, *keeps, tie(cames[0], before), *cames[1:], small_e, cost=cost, **more_of,
+                ids, *keeps, tie(cames[0], before), *cames[1:], small_e, cost=cost, lazy=True, **more_of,
             )
             return made[0:3], made[3:6], made[6]
 
-        keeps, sends, small_e = early_step("early_step_1", 4, keeps, cames, small_e, send, 15, load=(0, 1, 2, 6), flush=(0, 1, 2))
+        keeps, sends, small_e = early_step("early_step_1", 4, keeps, cames, small_e, send, 15, load=(0, 3, 6, 1, 4, 2, 5), flush=(0, 1, 2, 3, 4, 5))
         cames = go(sends, 1)
         kx3, sx3, ky3, sy3, small_j = call(
-            joined_keep, "joined_keep", 12, [flat(8 * joined), flat(8 * joined + more), flat(8 * joined), flat(8 * joined), small_shape], [],
-            ids, turned_c, g_joined, tie(came, sends[0]), small_2,
+            joined_keep, "joined_keep", 12, parts(8) + [small_shape], [],
+            ids, turned_c, g_joined, tie(came, sends[0]), small_2, load=(0, 1),
         )
         cx3, cy3 = move(sx3, "grp", 2), move(sy3, "batch", 1)
-        keeps, sends, small_e = early_step("early_step_2", 2, keeps, cames, small_e, sx3, 0.001, load=(0, 1, 2))
+        keeps, sends, small_e = early_step("early_step_2", 2, keeps, cames, small_e, sx3, 3.0, load=(0, 1, 2))
         cames = go(sends, 2)
         kx3, sx3, ky3, sy3, small_j = call(
-            step_apart, "joined_apart", 10, [flat(4 * joined), flat(4 * joined + more), flat(4 * joined), flat(4 * joined), small_shape], [],
+            step_apart, "joined_apart", 10, parts(4) + [small_shape], [],
             ids, kx3, tie(cx3, sends[0]), ky3, cy3, small_j,
         )
         cx3, cy3 = move(sx3, "batch", 1), move(sy3, "grp", 2)
-        *keeps, send, small_e = call(
-            step_parts_last, "early_step_3", 10, held(1) + [flat(1536 + extra), small_early], [],
-            ids, *keeps, tie(cames[0], sx3), *cames[1:], small_e,
+        *keeps, send, send_1, small_e = call(
+            step_parts_last, "early_step_3", 10, held(1) + [flat(960 + extra), held(1)[1], small_early], [],
+            ids, *keeps, tie(cames[0], sx3), *cames[1:], small_e, cost=1.0,
         )
         last = move(send, "batch", 4)
+        last_1 = move(send_1, "batch", 2)
+        g_back = tie(g_back, send)
         k3, s3, small_j = call(
-            step_meet, "joined_meet", 10, [flat(4 * joined), flat(4 * joined + more), small_shape], [],
+            step_meet, "joined_meet", 10, [flat(2 * both), flat(2 * both + more), small_shape], [],
             ids, kx3, tie(cx3, send), ky3, cy3, small_j,
         )
         c3 = move(s3, "batch", 2)
         k3, s3, small_j = call(
-            step_joint, "joined_joint", 10, [flat(2 * joined), flat(2 * joined + more), small_shape], [],
+            step_joint, "joined_joint", 10, [flat(both), flat(both + more), small_shape], [],
             ids, k3, c3, small_j,
         )
         c3 = move(s3, "batch", 4)
         sum_down, sum_align, sum_up, sum_out, small_e = call(
             early_end, "early_end", 10,
             [shape((384, 192), F32), shape((96, 256), F32), shape((96, 768), F32), shape((96, 192), F32), shape((16, width), F32)], [],
-            ids, *keeps, tie(last, s3), small_e,
-        )
-        g_back = tie(g_back, s3)
+            ids, *keeps, tie(last, s3), last_1, small_e,
+        )
         sum_qkv, small_j = call(
             joined_end, "joined_end", 10, [shape((96, 576), F32), shape((8, width), F32)], [],
             ids, k3, tie(c3, sum_out), small_j,

time: 236 us -> 220 us (0.932)
  starting transfers between devices: 48.4 us -> 42.2 us
  waiting for transfers between devices: 72.7 us -> 68.4 us
  Pallas kernels: 99.8 us -> 96.8 us
    ppermute x26 -> x27, starting transfers between devices: 34.3 us -> 28.1 us  [flip(): return lax.ppermute(value, AXES, pairs)]
    ppermute x26 -> x27, waiting for transfers between devices: 53.4 us -> 48.2 us  [flip(): return lax.ppermute(value, AXES, pairs)]
    pallas_call x16, Pallas kernels: 99.8 us -> 96.8 us  [call(): pl.pallas_call(body, name=name, out_shape=outs, in_specs=[SMEM] + [HBM if...]
    unnamed x62 -> x54, local copies, waits for them, and re-layouts: 7.12 us -> 4.89 us
  transfers between devices with their start and end apart: 29 -> 30, of which waited for: 10 -> 13; matrix products, arithmetic and copies ran while one was open for 2% -> 3% of each run, Pallas kernels for 22% -> 24%
where the time goes in v3:
time: 220 us; the launch traced here: 219 us
  Pallas kernels  96.8 us (44%)
  waiting for transfers between devices  68.4 us (31%)
  starting transfers between devices  42.2 us (19%)
  local copies, waits for them, and re-layouts  10.4 us (5%)
    pallas_call x16, Pallas kernels, call(): pl.pallas_call(body, name=name, out_shape=outs, in_specs=[SMEM] + [HBM if...  96.8 us
    ppermute x27, waiting for transfers between devices, flip(): return lax.ppermute(value, AXES, pairs)  48.2 us
    ppermute x27, starting transfers between devices, flip(): return lax.ppermute(value, AXES, pairs)  28.1 us
    all_to_all x3, waiting for transfers between devices, exchange(): lax.all_to_all(shaped, 'batch', split_axis=0, concat_axis=0, tiled=True)  20.3 us
    all_to_all x3, starting transfers between devices, exchange(): lax.all_to_all(shaped, 'batch', split_axis=0, concat_axis=0, tiled=True)  14.1 us
    unnamed x54, local copies, waits for them, and re-layouts  4.89 us
  transfers between devices with their start and end apart: 30, of which 13 were waited for; matrix products, arithmetic and copies ran while one was open for 3% of the time, Pallas kernels for 24%

profile of v3, /device:TPU:0, one launch (start us, length us, event | category | flops | bytes accessed | tf_op | source)
XLA Modules:
  0.0 219.2 jit_solution(7310832654909134087)
XLA Ops:
  0.8 0.7 copy-done.8
  1.4 2.2 %pack_tokens.1 = (bf16[64,768]{1,0:T(8,128)(2,1)S(1)}, bf16[64,768]{1,0:T(8,128)(2,1)S(1)}, bf16[64,768]{1,0:T(8,128)(2,1)S(1)}, bf16[64,768]{1,0:T(8,128)(2,1)S...) custom-call(s32[14]{0:T(128)S(1)} %pad_add_fusion.ids, ...), custom_call_target="tpu_custom_call" | custom-call | flops 1000000 | bytes 1 | tf_op jit(solution)/shard_map/pack_tokens/pallas_call | solution.py:857
  3.7 0.6 copy-done.5
  4.3 3.0 %collective-permute-start = (bf16[64,768]{1,0:T(8,128)(2,1)S(1)}, bf16[64,768]{1,0:T(8,128)(2,1)S(1)}, u32[]{:S(2)}, u32[]{:S(2)}) collective-permute-start(bf16[64,768]{1,0:T(8,128)(2,1)S(1)} %get-tuple-element.107), channel_id=1, source_target_pairs={{0,4},{1,5},{2,6},{3,7},{4,0},{5,1},{6,2},{7,3},{8,12},{9,13},{10,... | collective-permute-start | bytes 294920 | tf_op jit(solution)/shard_map/ppermute | solution.py:785
  7.3 1.6 collective-permute-start.1
  8.9 3.0 %collective-permute-start.3 = (bf16[64,768]{1,0:T(8,128)(2,1)S(1)}, bf16[64,768]{1,0:T(8,128)(2,1)S(1)}, u32[]{:S(2)}, u32[]{:S(2)}) collective-permute-start(bf16[64,768]{1,0:T(8,128)(2,1)S(1)} %get-tuple-element.110), channel_id=1, source_target_pairs={{0,16},{1,17},{2,18},{3,19},{4,20},{5,21},{6,22},{7,23},{8,24},{9,... | collective-permute-start | bytes 294920 | tf_op jit(solution)/shard_map/ppermute | solution.py:785
  11.9 1.3 collective-permute-start.4
  13.1 3.6 %collective-permute-start.5 = (bf16[64,768]{1,0:T(8,128)(2,1)}, bf16[64,768]{1,0:T(8,128)(2,1)S(1)}, u32[]{:S(2)}, u32[]{:S(2)}) collective-permute-start(bf16[64,768]{1,0:T(8,128)(2,1)} %get-tuple-element.112), channel_id=1, source_target_pairs={{0,24},{1,25},{2,26},{3,27},{4,28},{5,29},{6,30},{7,31},{8,16},{9,... | collective-permute-start | bytes 294920 | tf_op jit(solution)/shard_map/ppermute | solution.py:785
  16.8 0.7 reshape.109.refs_10_.refs_7_
  17.5 0.7 reshape.110.refs_11_
  18.2 0.7 reshape.111.refs_13_
  18.9 0.7 reshape.112.refs_14_
  19.6 0.8 copy.45.refs_9_.refs_6_
  20.4 6.6 %collective-permute-done.4.refs_5_ = bf16[64,768]{1,0:T(8,128)(2,1)S(1)} collective-permute-done((bf16[64,768]{1,0:T(8,128)(2,1)}, bf16[64,768]{1,0:T(8,128)(2,1)S(1)}, u32[]{:S(2)}, u32[]{:S(2)}) %collective-permute-start.4) | collective-permute-done | bytes 98336 | tf_op jit(solution)/shard_map/ppermute | solution.py:785
  27.1 0.6 copy-done.15
  27.8 0.7 copy-done.6
  28.4 15.6 %attention.1 = (bf16[512,768]{1,0:T(8,128)(2,1)}, bf16[512,2304]{1,0:T(8,128)(2,1)}, bf16[512,768]{1,0:T(8,128)(2,1)}, bf16[512,768]{1,0:T(8,128)(2,1)}, f32[6,4,256]{2,1,0:T(4,128)}) custom-call(s32[14]{0:T(128)S(1)} %pad_add_fusion.ids, bf16[64,768]{1,0:T(8,128)(2,1)} %copy-done.5, bf16[64,768]{1,0:T(8,128)(2,1)} %copy-done.11, ...), custom_call_target="tpu_custom_call" | custom-call | flops 1000000 | bytes 1 | tf_op jit(solution)/shard_map/attention/pallas_call | solution.py:857
  44.1 6.5 %all-to-all-start = ((bf16[8,64,768]{2,1,0:T(8,128)(2,1)}), bf16[8,64,768]{2,1,0:T(8,128)(2,1)S(1)}, u32[]{:S(2)}, u32[]{:S(2)}) async-start(bf16[8,64,768]{2,1,0:T(8,128)(2,1)} %bitcast.18), calls=%async_computation | async-start | bytes 1572864 | tf_op jit(solution)/shard_map/all_to_all | solution.py:872
  51.0 19.3 %all-to-all-done = bf16[8,64,768]{2,1,0:T(8,128)(2,1)S(1)} async-done(((bf16[8,64,768]{2,1,0:T(8,128)(2,1)}), bf16[8,64,768]{2,1,0:T(8,128)(2,1)S(1)}, u32[]{:S(2)}, u32[]{:S(2)}) %all-to-all-start) | async-done | bytes 786464 | tf_op jit(solution)/shard_map/all_to_all | solution.py:872
  70.3 25.8 %rows.1 = (bf16[256,768]{1,0:T(8,128)(2,1)}, bf16[256,1024]{1,0:T(8,128)(2,1)}, bf16[512,768]{1,0:T(8,128)(2,1)}, f32[256,768]{1,0:T(8,128)}, bf16[256,3072]{1,0...) custom-call(s32[14]{0:T(128)S(1)} %pad_add_fusion.ids, ...), custom_call_target="tpu_custom_call" | custom-call | flops 1000000 | bytes 1 | tf_op jit(solution)/shard_map/rows/pallas_call | solution.py:857
  96.2 0.5 collective-permute-start.7
  96.7 3.8 %all-to-all-start.1 = ((bf16[8,64,768]{2,1,0:T(8,128)(2,1)}), bf16[8,64,768]{2,1,0:T(8,128)(2,1)S(1)}, u32[]{:S(2)}, u32[]{:S(2)}) async-start(bf16[8,64,768]{2,1,0:T(8,128)(2,1)} %bitcast.17), calls=%async_computation.1 | async-start | bytes 1572864 | tf_op jit(solution)/shard_map/all_to_all | solution.py:872
  100.5 3.4 %collective-permute-done.8.refs_2_.refs_4_ = bf16[5344,256]{1,0:T(8,128)(2,1)} collective-permute-done((bf16[5344,256]{1,0:T(8,128)(2,1)}, bf16[5344,256]{1,0:T(8,128)(2,1)}, u32[]{:S(2)}, u32[]{:S(2)}) %collective-permute-start.8) | collective-permute-done | bytes 2736160 | tf_op jit(solution)/shard_map/ppermute | solution.py:785
  103.9 5.6 %second_grads.1 = (bf16[4608,128]{1,0:T(8,128)(2,1)}, bf16[4800,128]{1,0:T(8,128)(2,1)}, f32[96,128]{1,0:T(8,128)}) custom-call(s32[14]{0:T(128)S(1)} %pad_add_fusion.ids, bf16[5344,256]{1,0:T(8,128)(2,1)} %get-tuple-element.119.refs_0_.refs_2_, bf16[2944,256]{1,0:T(8,128)(2,1)} %get-tuple-element.120.refs_1_.refs_3_, ...), custom_call_target="tpu_custom_call" | custom-call | flops 1000000 | bytes 1 | tf_op jit(solution)/shard_map/second_grads/pallas_call | solution.py:857
  109.5 1.6 collective-permute-start.9
  111.0 1.1 copy-done.10
  112.2 6.3 %first_grads.1 = (bf16[4608,128]{1,0:T(8,128)(2,1)}, bf16[4608,128]{1,0:T(8,128)(2,1)}, bf16[3072,128]{1,0:T(8,128)(2,1)}, bf16[3072,128]{1,0:T(8,128)(2,1)}) custom-call(s32[14]{0:T(128)S(1)} %pad_add_fusion.ids, bf16[256,3072]{1,0:T(8,128)(2,1)} %get-tuple-element.118.refs_0_, bf16[256,3072]{1,0:T(8,128)(2,1)} %copy-done.10, ...), custom_call_target="tpu_custom_call" | custom-call | flops 1000000 | bytes 1 | tf_op jit(solution)/shard_map/first_grads/pallas_call | solution.py:857
  118.5 1.4 collective-permute-start.10
  119.9 1.0 all-to-all-done.1
  120.9 21.6 %attention_back.1 = (bf16[512,768]{1,0:T(8,128)(2,1)}, bf16[512,2304]{1,0:T(8,128)(2,1)}, f32[8,768]{1,0:T(8,128)S(1)}, bf16[7776,128]{1,0:T(8,128)(2,1)}, bf16[768,512]{1,0:T(8,128)(2,1)}) custom-call(s32[14]{0:T(128)S(1)} %pad_add_fusion.ids, bf16[512,768]{1,0:T(8,128)(2,1)S(1)} %bitcast.10, bf16[512,768]{1,0:T(8,128)(2,1)} %get-tuple-element.125.refs_1_, ...), custom_call_target="tpu_custom_call" | custom-call | flops 1000000 | bytes 1 | tf_op jit(solution)/shard_map/attention_back/pallas_call | solution.py:857
  142.6 4.0 %collective-permute-done.10.refs_4_ = bf16[4608,128]{1,0:T(8,128)(2,1)} collective-permute-done((bf16[4608,128]{1,0:T(8,128)(2,1)}, bf16[4608,128]{1,0:T(8,128)(2,1)}, u32[]{:S(2)}, u32[]{:S(2)}) %collective-permute-start.10) | collective-permute-done | bytes 1179680 | tf_op jit(solution)/shard_map/ppermute | solution.py:785
  146.6 4.6 %early_step_1.1 = (bf16[2304,128]{1,0:T(8,128)(2,1)}, bf16[2304,128]{1,0:T(8,128)(2,1)}, bf16[1536,128]{1,0:T(8,128)(2,1)}, bf16[2496,128]{1,0:T(8,128)(2,1)}, b...) custom-call(s32[14]{0:T(128)S(1)} %pad_add_fusion.ids, ...), custom_call_target="tpu_custom_call" | custom-call | flops 15000000512 | bytes 1 | tf_op jit(solution)/shard_map/early_step_1/pallas_call | solution.py:857
  151.2 0.3 collective-permute-start.12
  151.6 0.8 collective-permute-start.14
  152.4 0.8 collective-permute-start.15
  153.2 3.8 %all-to-all-start.2 = ((bf16[8,64,768]{2,1,0:T(8,128)(2,1)}), bf16[8,64,768]{2,1,0:T(8,128)(2,1)S(1)}, u32[]{:S(2)}, u32[]{:S(2)}) async-start(bf16[8,64,768]{2,1,0:T(8,128)(2,1)} %bitcast.16), calls=%async_computation.2 | async-start | bytes 1572864 | tf_op jit(solution)/shard_map/all_to_all | solution.py:872
  157.1 4.2 %joined_keep.1 = (bf16[1920,128]{1,0:T(8,128)(2,1)S(1)}, bf16[2016,128]{1,0:T(8,128)(2,1)S(1)}, bf16[1920,128]{1,0:T(8,128)(2,1)S(1)}, bf16[1920,128]{1,0:T(8,128)(2,1)S(1)}, f32[48,128]{1,0:T(8,128)S(1)}) custom-call(s32[14]{0:T(128)S(1)} %pad_add_fusion.ids, bf16[768,512]{1,0:T(8,128)(2,1)} %get-tuple-element.141.refs_0_, ...), custom_call_target="tpu_custom_call" | custom-call | flops 1000000 | bytes 1 | tf_op jit(solution)/shard_map/joined_keep/pallas_call | solution.py:857
  161.2 1.6 collective-permute-start.17
  162.8 1.6 collective-permute-start.18
  164.4 13.0 %collective-permute-done.12.refs_3_ = bf16[2496,128]{1,0:T(8,128)(2,1)} collective-permute-done((bf16[2496,128]{1,0:T(8,128)(2,1)}, bf16[2496,128]{1,0:T(8,128)(2,1)}, u32[]{:S(2)}, u32[]{:S(2)}) %collective-permute-start.12) | collective-permute-done | bytes 639008 | tf_op jit(solution)/shard_map/ppermute | solution.py:785
  177.4 2.8 %early_step_2.1 = (bf16[1152,128]{1,0:T(8,128)(2,1)S(1)}, bf16[1152,128]{1,0:T(8,128)(2,1)S(1)}, bf16[768,128]{1,0:T(8,128)(2,1)S(1)}, bf16[1344,128]{1,0:T(8,12...) custom-call(s32[14]{0:T(128)S(1)} %pad_add_fusion.ids, ...), custom_call_target="tpu_custom_call" | custom-call | flops 3000000000 | bytes 1 | tf_op jit(solution)/shard_map/early_step_2/pallas_call | solution.py:857
  180.2 0.3 collective-permute-start.16
  180.5 0.5 collective-permute-start.20
  181.0 2.6 %collective-permute-done.18.refs_3_ = bf16[1920,128]{1,0:T(8,128)(2,1)S(1)} collective-permute-done((bf16[1920,128]{1,0:T(8,128)(2,1)S(1)}, bf16[1920,128]{1,0:T(8,128)(2,1)S(1)}, u32[]{:S(2)}, u32[]{:S(2)}) %collective-permute-start.18) | collective-permute-done | bytes 491552 | tf_op jit(solution)/shard_map/ppermute | solution.py:785
  183.6 0.8 joined_apart.1
  184.5 2.3 %collective-permute-start.22 = (bf16[960,128]{1,0:T(8,128)(2,1)S(1)}, bf16[960,128]{1,0:T(8,128)(2,1)S(1)}, u32[]{:S(2)}, u32[]{:S(2)}) collective-permute-start(bf16[960,128]{1,0:T(8,128)(2,1)S(1)} %get-tuple-element.170), channel_id=1, source_target_pairs={{0,2},{1,3},{2,0},{3,1},{4,6},{5,7},{6,4},{7,5},{8,10},{9,11},{10,... | collective-permute-start | bytes 737288 | tf_op jit(solution)/shard_map/ppermute | solution.py:785
  186.8 4.5 %collective-permute-done.16.refs_3_ = bf16[1344,128]{1,0:T(8,128)(2,1)S(1)} collective-permute-done((bf16[1344,128]{1,0:T(8,128)(2,1)S(1)}, bf16[1344,128]{1,0:T(8,128)(2,1)S(1)}, u32[]{:S(2)}, u32[]{:S(2)}) %collective-permute-start.16) | collective-permute-done | bytes 344096 | tf_op jit(solution)/shard_map/ppermute | solution.py:785
  191.5 1.4 early_step_3.1
  192.8 1.6 collective-permute-done.21.refs_1_
  194.5 0.7 joined_meet.1
  195.2 1.2 collective-permute-start.23
  196.4 0.5 collective-permute-start.25
  196.8 1.3 collective-permute-start.26
  198.1 10.5 %collective-permute-done.23.refs_1_ = bf16[1056,128]{1,0:T(8,128)(2,1)S(1)} collective-permute-done((bf16[1056,128]{1,0:T(8,128)(2,1)S(1)}, bf16[1056,128]{1,0:T(8,128)(2,1)S(1)}, u32[]{:S(2)}, u32[]{:S(2)}) %collective-permute-start.23) | collective-permute-done | bytes 270368 | tf_op jit(solution)/shard_map/ppermute | solution.py:785
  208.6 0.6 joined_joint.1
  209.2 0.7 collective-permute-start.24
  209.9 2.1 grad_tokens.1
  211.9 1.6 collective-permute-done.25.refs_3_
  213.5 1.4 early_end.1
  215.0 0.6 slice.52
  215.6 0.6 reshape.127
  216.2 0.9 copy.49
  217.2 1.3 joined_end.1
  218.5 0.7 slice_reduce_fusion
  (88 shorter events, 1.1 us)
Async XLA Ops:
  0.8 0.7 copy-start.8
  3.7 0.6 copy-start.5
  4.3 8.8 %collective-permute-start = (bf16[64,768]{1,0:T(8,128)(2,1)S(1)}, bf16[64,768]{1,0:T(8,128)(2,1)S(1)}, u32[]{:S(2)}, u32[]{:S(2)}) collective-permute-start(bf16[64,768]{1,0:T(8,128)(2,1)S(1)} %get-tuple-element.107), channel_id=1, source_target_pairs={{0,4},{1,5},{2,6},{3,7},{4,0},{5,1},{6,2},{7,3},{8,12},{9,13},{10,... | collective-permute-start | bytes 294920 | tf_op jit(solution)/shard_map/ppermute | solution.py:785
  7.3 9.5 %collective-permute-start.1 = (bf16[64,768]{1,0:T(8,128)(2,1)S(1)}, bf16[64,768]{1,0:T(8,128)(2,1)S(1)}, u32[]{:S(2)}, u32[]{:S(2)}) collective-permute-start(bf16[64,768]{1,0:T(8,128)(2,1)S(1)} %get-tuple-element.108), channel_id=1, source_target_pairs={{0,8},{1,9},{2,10},{3,11},{4,12},{5,13},{6,14},{7,15},{8,0},{9,1},... | collective-permute-start | bytes 294920 | tf_op jit(solution)/shard_map/ppermute | solution.py:785
  8.9 11.5 %collective-permute-start.2 = (bf16[64,768]{1,0:T(8,128)(2,1)S(1)}, bf16[64,768]{1,0:T(8,128)(2,1)S(1)}, u32[]{:S(2)}, u32[]{:S(2)}) collective-permute-start(bf16[64,768]{1,0:T(8,128)(2,1)S(1)} %get-tuple-element.109), channel_id=1, source_target_pairs={{0,12},{1,13},{2,14},{3,15},{4,8},{5,9},{6,10},{7,11},{8,4},{9,5},... | collective-permute-start | bytes 294920 | tf_op jit(solution)/shard_map/ppermute | solution.py:785
  8.9 11.5 %collective-permute-start.3 = (bf16[64,768]{1,0:T(8,128)(2,1)S(1)}, bf16[64,768]{1,0:T(8,128)(2,1)S(1)}, u32[]{:S(2)}, u32[]{:S(2)}) collective-permute-start(bf16[64,768]{1,0:T(8,128)(2,1)S(1)} %get-tuple-element.110), channel_id=1, source_target_pairs={{0,16},{1,17},{2,18},{3,19},{4,20},{5,21},{6,22},{7,23},{8,24},{9,... | collective-permute-start | bytes 294920 | tf_op jit(solution)/shard_map/ppermute | solution.py:785
  11.9 15.2 %collective-permute-start.4 = (bf16[64,768]{1,0:T(8,128)(2,1)}, bf16[64,768]{1,0:T(8,128)(2,1)S(1)}, u32[]{:S(2)}, u32[]{:S(2)}) collective-permute-start(bf16[64,768]{1,0:T(8,128)(2,1)} %get-tuple-element.111), channel_id=1, source_target_pairs={{0,20},{1,21},{2,22},{3,23},{4,16},{5,17},{6,18},{7,19},{8,28},{9,... | collective-permute-start | bytes 294920 | tf_op jit(solution)/shard_map/ppermute | solution.py:785
  13.1 13.9 %copy-start.11 = (bf16[64,768]{1,0:T(8,128)(2,1)}, bf16[64,768]{1,0:T(8,128)(2,1)S(1)}, u32[]{:S(2)}) copy-start(bf16[64,768]{1,0:T(8,128)(2,1)S(1)} %collective-permute-done.refs_1_) | copy-start | bytes 294916
  13.1 13.9 %collective-permute-start.5 = (bf16[64,768]{1,0:T(8,128)(2,1)}, bf16[64,768]{1,0:T(8,128)(2,1)S(1)}, u32[]{:S(2)}, u32[]{:S(2)}) collective-permute-start(bf16[64,768]{1,0:T(8,128)(2,1)} %get-tuple-element.112), channel_id=1, source_target_pairs={{0,24},{1,25},{2,26},{3,27},{4,28},{5,29},{6,30},{7,31},{8,16},{9,... | collective-permute-start | bytes 294920 | tf_op jit(solution)/shard_map/ppermute | solution.py:785
  16.8 10.3 %copy-start.12 = (bf16[64,768]{1,0:T(8,128)(2,1)}, bf16[64,768]{1,0:T(8,128)(2,1)S(1)}, u32[]{:S(2)}) copy-start(bf16[64,768]{1,0:T(8,128)(2,1)S(1)} %collective-permute-done.1.refs_2_) | copy-start | bytes 294916
  16.8 10.3 %collective-permute-start.6 = (bf16[64,768]{1,0:T(8,128)(2,1)}, bf16[64,768]{1,0:T(8,128)(2,1)S(1)}, u32[]{:S(2)}, u32[]{:S(2)}) collective-permute-start(bf16[64,768]{1,0:T(8,128)(2,1)} %get-tuple-element.113), channel_id=1, source_target_pairs={{0,28},{1,29},{2,30},{3,31},{4,24},{5,25},{6,26},{7,27},{8,20},{9,... | collective-permute-start | bytes 294920 | tf_op jit(solution)/shard_map/ppermute | solution.py:785
  20.4 23.6 %copy-start = (s32[512,1]{1,0:T(8,128)}, s32[512,1]{1,0:T(8,128)S(1)}, u32[]{:S(2)}) copy-start(s32[512,1]{1,0:T(8,128)S(1)} %copy.45.refs_9_.refs_6_) | copy-start | bytes 6148
  20.4 6.7 %copy-start.13 = (bf16[64,768]{1,0:T(8,128)(2,1)}, bf16[64,768]{1,0:T(8,128)(2,1)S(1)}, u32[]{:S(2)}) copy-start(bf16[64,768]{1,0:T(8,128)(2,1)S(1)} %collective-permute-done.2.refs_3_) | copy-start | bytes 294916
  20.4 6.7 %copy-start.14 = (bf16[64,768]{1,0:T(8,128)(2,1)}, bf16[64,768]{1,0:T(8,128)(2,1)S(1)}, u32[]{:S(2)}) copy-start(bf16[64,768]{1,0:T(8,128)(2,1)S(1)} %collective-permute-done.3.refs_4_) | copy-start | bytes 294916
  27.0 0.6 copy-start.15
  27.1 0.7 copy-start.16
  27.1 0.7 copy-start.17
  27.8 0.7 copy-start.6
  44.0 6.7 %copy-start.9 = (s32[256,1]{0,1:T(1,128)S(1)}, s32[256,1]{0,1:T(1,128)}, u32[]{:S(2)}) copy-start(s32[256,1]{0,1:T(1,128)} %param.23) | copy-start | bytes 3076
  44.0 6.8 %copy-start.20 = (bf16[768]{0:T(1024)(128)(2,1)S(1)}, bf16[768]{0:T(1024)(128)(2,1)}, u32[]{:S(2)}) copy-start(bf16[768]{0:T(1024)(128)(2,1)} %param.33) | copy-start | bytes 4612
  44.0 6.8 %copy-start.21 = (bf16[768]{0:T(1024)(128)(2,1)S(1)}, bf16[768]{0:T(1024)(128)(2,1)}, u32[]{:S(2)}) copy-start(bf16[768]{0:T(1024)(128)(2,1)} %param.34) | copy-start | bytes 4612
  44.0 6.9 %copy-start.22 = (bf16[768]{0:T(1024)(128)(2,1)S(1)}, bf16[768]{0:T(1024)(128)(2,1)}, u32[]{:S(2)}) copy-start(bf16[768]{0:T(1024)(128)(2,1)} %param.35) | copy-start | bytes 4612
  44.0 6.9 %copy-start.23 = (bf16[768]{0:T(1024)(128)(2,1)S(1)}, bf16[768]{0:T(1024)(128)(2,1)}, u32[]{:S(2)}) copy-start(bf16[768]{0:T(1024)(128)(2,1)} %param.39) | copy-start | bytes 4612
  44.1 6.9 %copy-start.24 = (bf16[768]{0:T(1024)(128)(2,1)S(1)}, bf16[768]{0:T(1024)(128)(2,1)}, u32[]{:S(2)}) copy-start(bf16[768]{0:T(1024)(128)(2,1)} %param.40) | copy-start | bytes 4612
  44.1 6.9 %copy-start.25 = (bf16[768]{0:T(1024)(128)(2,1)S(1)}, bf16[768]{0:T(1024)(128)(2,1)}, u32[]{:S(2)}) copy-start(bf16[768]{0:T(1024)(128)(2,1)} %param.41) | copy-start | bytes 4612
  44.1 6.9 %copy-start.19 = (bf16[1024]{0:T(1024)(128)(2,1)S(1)}, bf16[1024]{0:T(1024)(128)(2,1)}, u32[]{:S(2)}) copy-start(bf16[1024]{0:T(1024)(128)(2,1)} %param.43) | copy-start | bytes 6148
  44.1 6.9 %copy-start.18 = (bf16[3072]{0:T(1024)(128)(2,1)S(1)}, bf16[3072]{0:T(1024)(128)(2,1)}, u32[]{:S(2)}) copy-start(bf16[3072]{0:T(1024)(128)(2,1)} %param.37) | copy-start | bytes 18436
  44.1 26.2 %copy-start.1 = (bf16[256,768]{1,0:T(8,128)(2,1)S(1)}, bf16[256,768]{1,0:T(8,128)(2,1)}, u32[]{:S(2)}) copy-start(bf16[256,768]{1,0:T(8,128)(2,1)} %refs_1_.4) | copy-start | bytes 1179652
  44.1 26.2 %copy-start.3 = (bf16[256,1024]{1,0:T(8,128)(2,1)S(1)}, bf16[256,1024]{1,0:T(8,128)(2,1)}, u32[]{:S(2)}) copy-start(bf16[256,1024]{1,0:T(8,128)(2,1)} %refs_5_.2) | copy-start | bytes 1572868
  44.1 26.2 %copy-start.4 = (bf16[256,768]{1,0:T(8,128)(2,1)S(1)}, bf16[256,768]{1,0:T(8,128)(2,1)}, u32[]{:S(2)}) copy-start(bf16[256,768]{1,0:T(8,128)(2,1)} %refs_4_.1) | copy-start | bytes 1179652
  44.1 26.1 %all-to-all-start = ((bf16[8,64,768]{2,1,0:T(8,128)(2,1)}), bf16[8,64,768]{2,1,0:T(8,128)(2,1)S(1)}, u32[]{:S(2)}, u32[]{:S(2)}) async-start(bf16[8,64,768]{2,1,0:T(8,128)(2,1)} %bitcast.18), calls=%async_computation | async-start | bytes 1572864 | tf_op jit(solution)/shard_map/all_to_all | solution.py:872
  96.1 7.7 %collective-permute-start.8 = (bf16[5344,256]{1,0:T(8,128)(2,1)}, bf16[5344,256]{1,0:T(8,128)(2,1)}, u32[]{:S(2)}, u32[]{:S(2)}) collective-permute-start(bf16[5344,256]{1,0:T(8,128)(2,1)} %get-tuple-element.119.refs_0_.refs_2_), channel_id=1, source_target_pairs={{0,1},{1,0},{2,3},{3,2},{4,5},{5,4},{6,7},{7,6},{8,9},{9,8},{10,11... | collective-permute-start | bytes 8208392 | tf_op jit(solution)/shard_map/ppermute | solution.py:785
  96.2 14.8 %collective-permute-start.7 = (bf16[256,3072]{1,0:T(8,128)(2,1)}, bf16[256,3072]{1,0:T(8,128)(2,1)S(1)}, u32[]{:S(2)}, u32[]{:S(2)}) collective-permute-start(bf16[256,3072]{1,0:T(8,128)(2,1)} %get-tuple-element.118.refs_0_), channel_id=1, source_target_pairs={{0,1},{1,0},{2,3},{3,2},{4,5},{5,4},{6,7},{7,6},{8,9},{9,8},{10,11... | collective-permute-start | bytes 4718600 | tf_op jit(solution)/shard_map/ppermute | solution.py:785
  96.7 24.1 %all-to-all-start.1 = ((bf16[8,64,768]{2,1,0:T(8,128)(2,1)}), bf16[8,64,768]{2,1,0:T(8,128)(2,1)S(1)}, u32[]{:S(2)}, u32[]{:S(2)}) async-start(bf16[8,64,768]{2,1,0:T(8,128)(2,1)} %bitcast.17), calls=%async_computation.1 | async-start | bytes 1572864 | tf_op jit(solution)/shard_map/all_to_all | solution.py:872
  109.5 11.4 %copy-start.7 = (s32[1,512]{1,0:T(1,128)S(1)}, s32[1,512]{1,0:T(1,128)}, u32[]{:S(2)}) copy-start(s32[1,512]{1,0:T(1,128)} %refs_5_.3) | copy-start | bytes 6148
  109.5 33.1 %collective-permute-start.9 = (bf16[4800,128]{1,0:T(8,128)(2,1)}, bf16[4800,128]{1,0:T(8,128)(2,1)}, u32[]{:S(2)}, u32[]{:S(2)}) collective-permute-start(bf16[4800,128]{1,0:T(8,128)(2,1)} %get-tuple-element.121), channel_id=1, source_target_pairs={{0,2},{1,3},{2,0},{3,1},{4,6},{5,7},{6,4},{7,5},{8,10},{9,11},{10,... | collective-permute-start | bytes 3686408 | tf_op jit(solution)/shard_map/ppermute | solution.py:785
  111.0 1.1 copy-start.10
  118.5 28.1 %collective-permute-start.10 = (bf16[4608,128]{1,0:T(8,128)(2,1)}, bf16[4608,128]{1,0:T(8,128)(2,1)}, u32[]{:S(2)}, u32[]{:S(2)}) collective-permute-start(bf16[4608,128]{1,0:T(8,128)(2,1)} %get-tuple-element.123), channel_id=1, source_target_pairs={{0,4},{1,5},{2,6},{3,7},{4,0},{5,1},{6,2},{7,3},{8,12},{9,13},{10,... | collective-permute-start | bytes 3538952 | tf_op jit(solution)/shard_map/ppermute | solution.py:785
  119.9 22.7 %collective-permute-start.11 = (bf16[3072,128]{1,0:T(8,128)(2,1)}, bf16[3072,128]{1,0:T(8,128)(2,1)}, u32[]{:S(2)}, u32[]{:S(2)}) collective-permute-start(bf16[3072,128]{1,0:T(8,128)(2,1)} %get-tuple-element.135), channel_id=1, source_target_pairs={{0,8},{1,9},{2,10},{3,11},{4,12},{5,13},{6,14},{7,15},{8,0},{9,1},... | collective-permute-start | bytes 2359304 | tf_op jit(solution)/shard_map/ppermute | solution.py:785
  142.5 14.6 %collective-permute-start.13 = (bf16[7776,128]{1,0:T(8,128)(2,1)}, bf16[7776,128]{1,0:T(8,128)(2,1)S(1)}, u32[]{:S(2)}, u32[]{:S(2)}) collective-permute-start(bf16[7776,128]{1,0:T(8,128)(2,1)} %get-tuple-element.133), channel_id=1, source_target_pairs={{0,1},{1,0},{2,3},{3,2},{4,5},{5,4},{6,7},{7,6},{8,9},{9,8},{10,11... | collective-permute-start | bytes 5971976 | tf_op jit(solution)/shard_map/ppermute | solution.py:785
  151.2 26.2 %collective-permute-start.12 = (bf16[2496,128]{1,0:T(8,128)(2,1)}, bf16[2496,128]{1,0:T(8,128)(2,1)}, u32[]{:S(2)}, u32[]{:S(2)}) collective-permute-start(bf16[2496,128]{1,0:T(8,128)(2,1)} %get-tuple-element.140), channel_id=1, source_target_pairs={{0,8},{1,9},{2,10},{3,11},{4,12},{5,13},{6,14},{7,15},{8,0},{9,1},... | collective-permute-start | bytes 1916936 | tf_op jit(solution)/shard_map/ppermute | solution.py:785
  151.6 25.9 %collective-permute-start.14 = (bf16[2304,128]{1,0:T(8,128)(2,1)}, bf16[2304,128]{1,0:T(8,128)(2,1)}, u32[]{:S(2)}, u32[]{:S(2)}) collective-permute-start(bf16[2304,128]{1,0:T(8,128)(2,1)} %get-tuple-element.147), channel_id=1, source_target_pairs={{0,2},{1,3},{2,0},{3,1},{4,6},{5,7},{6,4},{7,5},{8,10},{9,11},{10,... | collective-permute-start | bytes 1769480 | tf_op jit(solution)/shard_map/ppermute | solution.py:785
  152.4 25.0 %collective-permute-start.15 = (bf16[1536,128]{1,0:T(8,128)(2,1)}, bf16[1536,128]{1,0:T(8,128)(2,1)S(1)}, u32[]{:S(2)}, u32[]{:S(2)}) collective-permute-start(bf16[1536,128]{1,0:T(8,128)(2,1)} %get-tuple-element.148), channel_id=1, source_target_pairs={{0,4},{1,5},{2,6},{3,7},{4,0},{5,1},{6,2},{7,3},{8,12},{9,13},{10,... | collective-permute-start | bytes 1179656 | tf_op jit(solution)/shard_map/ppermute | solution.py:785
  153.2 56.6 %all-to-all-start.2 = ((bf16[8,64,768]{2,1,0:T(8,128)(2,1)}), bf16[8,64,768]{2,1,0:T(8,128)(2,1)S(1)}, u32[]{:S(2)}, u32[]{:S(2)}) async-start(bf16[8,64,768]{2,1,0:T(8,128)(2,1)} %bitcast.16), calls=%async_computation.2 | async-start | bytes 1572864 | tf_op jit(solution)/shard_map/all_to_all | solution.py:872
  161.2 19.8 %collective-permute-start.17 = (bf16[2016,128]{1,0:T(8,128)(2,1)S(1)}, bf16[2016,128]{1,0:T(8,128)(2,1)S(1)}, u32[]{:S(2)}, u32[]{:S(2)}) collective-permute-start(bf16[2016,128]{1,0:T(8,128)(2,1)S(1)} %get-tuple-element.145), channel_id=1, source_target_pairs={{0,2},{1,3},{2,0},{3,1},{4,6},{5,7},{6,4},{7,5},{8,10},{9,11},{10,... | collective-permute-start | bytes 1548296 | tf_op jit(solution)/shard_map/ppermute | solution.py:785
  162.8 20.8 %collective-permute-start.18 = (bf16[1920,128]{1,0:T(8,128)(2,1)S(1)}, bf16[1920,128]{1,0:T(8,128)(2,1)S(1)}, u32[]{:S(2)}, u32[]{:S(2)}) collective-permute-start(bf16[1920,128]{1,0:T(8,128)(2,1)S(1)} %get-tuple-element.157), channel_id=1, source_target_pairs={{0,4},{1,5},{2,6},{3,7},{4,0},{5,1},{6,2},{7,3},{8,12},{9,13},{10,... | collective-permute-start | bytes 1474568 | tf_op jit(solution)/shard_map/ppermute | solution.py:785
  180.2 11.1 %collective-permute-start.16 = (bf16[1344,128]{1,0:T(8,128)(2,1)S(1)}, bf16[1344,128]{1,0:T(8,128)(2,1)S(1)}, u32[]{:S(2)}, u32[]{:S(2)}) collective-permute-start(bf16[1344,128]{1,0:T(8,128)(2,1)S(1)} %get-tuple-element.153), channel_id=1, source_target_pairs={{0,4},{1,5},{2,6},{3,7},{4,0},{5,1},{6,2},{7,3},{8,12},{9,13},{10,... | collective-permute-start | bytes 1032200 | tf_op jit(solution)/shard_map/ppermute | solution.py:785
  180.5 11.0 %collective-permute-start.19 = (bf16[1152,128]{1,0:T(8,128)(2,1)S(1)}, bf16[1152,128]{1,0:T(8,128)(2,1)S(1)}, u32[]{:S(2)}, u32[]{:S(2)}) collective-permute-start(bf16[1152,128]{1,0:T(8,128)(2,1)S(1)} %get-tuple-element.161), channel_id=1, source_target_pairs={{0,16},{1,17},{2,18},{3,19},{4,20},{5,21},{6,22},{7,23},{8,24},{9,... | collective-permute-start | bytes 884744 | tf_op jit(solution)/shard_map/ppermute | solution.py:785
  180.5 10.8 %collective-permute-start.20 = (bf16[768,128]{1,0:T(8,128)(2,1)S(1)}, bf16[768,128]{1,0:T(8,128)(2,1)S(1)}, u32[]{:S(2)}, u32[]{:S(2)}) collective-permute-start(bf16[768,128]{1,0:T(8,128)(2,1)S(1)} %get-tuple-element.162), channel_id=1, source_target_pairs={{0,2},{1,3},{2,0},{3,1},{4,6},{5,7},{6,4},{7,5},{8,10},{9,11},{10,... | collective-permute-start | bytes 589832 | tf_op jit(solution)/shard_map/ppermute | solution.py:785
  184.4 10.1 %collective-permute-start.21 = (bf16[1056,128]{1,0:T(8,128)(2,1)S(1)}, bf16[1056,128]{1,0:T(8,128)(2,1)S(1)}, u32[]{:S(2)}, u32[]{:S(2)}) collective-permute-start(bf16[1056,128]{1,0:T(8,128)(2,1)S(1)} %get-tuple-element.159), channel_id=1, source_target_pairs={{0,4},{1,5},{2,6},{3,7},{4,0},{5,1},{6,2},{7,3},{8,12},{9,13},{10,... | collective-permute-start | bytes 811016 | tf_op jit(solution)/shard_map/ppermute | solution.py:785
  184.5 10.0 %collective-permute-start.22 = (bf16[960,128]{1,0:T(8,128)(2,1)S(1)}, bf16[960,128]{1,0:T(8,128)(2,1)S(1)}, u32[]{:S(2)}, u32[]{:S(2)}) collective-permute-start(bf16[960,128]{1,0:T(8,128)(2,1)S(1)} %get-tuple-element.170), channel_id=1, source_target_pairs={{0,2},{1,3},{2,0},{3,1},{4,6},{5,7},{6,4},{7,5},{8,10},{9,11},{10,... | collective-permute-start | bytes 737288 | tf_op jit(solution)/shard_map/ppermute | solution.py:785
  192.8 17.0 %copy-start.2 = (f32[256,768]{1,0:T(8,128)S(1)}, f32[256,768]{1,0:T(8,128)}, u32[]{:S(2)}) copy-start(f32[256,768]{1,0:T(8,128)} %get-tuple-element.166.refs_2_) | copy-start | bytes 2359300
  195.2 13.4 %collective-permute-start.23 = (bf16[1056,128]{1,0:T(8,128)(2,1)S(1)}, bf16[1056,128]{1,0:T(8,128)(2,1)S(1)}, u32[]{:S(2)}, u32[]{:S(2)}) collective-permute-start(bf16[1056,128]{1,0:T(8,128)(2,1)S(1)} %get-tuple-element.173), channel_id=1, source_target_pairs={{0,8},{1,9},{2,10},{3,11},{4,12},{5,13},{6,14},{7,15},{8,0},{9,1},... | collective-permute-start | bytes 811016 | tf_op jit(solution)/shard_map/ppermute | solution.py:785
  196.4 17.2 %collective-permute-start.25 = (bf16[1152,128]{1,0:T(8,128)(2,1)S(1)}, bf16[1152,128]{1,0:T(8,128)(2,1)S(1)}, u32[]{:S(2)}, u32[]{:S(2)}) collective-permute-start(bf16[1152,128]{1,0:T(8,128)(2,1)S(1)} %get-tuple-element.164), channel_id=1, source_target_pairs={{0,16},{1,17},{2,18},{3,19},{4,20},{5,21},{6,22},{7,23},{8,24},{9,... | collective-permute-start | bytes 884744 | tf_op jit(solution)/shard_map/ppermute | solution.py:785
  196.8 16.7 %collective-permute-start.26 = (bf16[576,128]{1,0:T(8,128)(2,1)}, bf16[576,128]{1,0:T(8,128)(2,1)S(1)}, u32[]{:S(2)}, u32[]{:S(2)}) collective-permute-start(bf16[576,128]{1,0:T(8,128)(2,1)} %get-tuple-element.181), channel_id=1, source_target_pairs={{0,8},{1,9},{2,10},{3,11},{4,12},{5,13},{6,14},{7,15},{8,0},{9,1},... | collective-permute-start | bytes 442376 | tf_op jit(solution)/shard_map/ppermute | solution.py:785
  209.2 8.0 %collective-permute-start.24 = (bf16[576,128]{1,0:T(8,128)(2,1)S(1)}, bf16[576,128]{1,0:T(8,128)(2,1)S(1)}, u32[]{:S(2)}, u32[]{:S(2)}) collective-permute-start(bf16[576,128]{1,0:T(8,128)(2,1)S(1)} %get-tuple-element.176), channel_id=1, source_target_pairs={{0,16},{1,17},{2,18},{3,19},{4,20},{5,21},{6,22},{7,23},{8,24},{9,... | collective-permute-start | bytes 442376 | tf_op jit(solution)/shard_map/ppermute | solution.py:785

commit v4 on v3

--- a/solution.py
+++ b/solution.py
@@ -66,18 +66,20 @@
     return (dest_col ^ me) * capacity + offset
 
 
-def slot_row(dest_row, me, peers, capacity):
+def placing_row(dest_row, me, peers, capacity):
     rows = dest_row.shape[1]
     onehot = (dest_row == iota((peers, rows), 0)).astype(F32)
     before = (iota((rows, rows), 0) < iota((rows, rows), 1)).astype(BF16)
     earlier = dot(onehot.astype(BF16), before)
     offset = jnp.sum(earlier * onehot, axis=0, keepdims=True).astype(jnp.int32)
-    return (dest_row ^ me) * capacity + offset
-
-
-def placing(dest_row, me, peers, capacity):
-    shape = (peers * capacity, dest_row.shape[1])
-    return iota(shape, 0) == slot_row(dest_row, me, peers, capacity)
+    return iota((peers * capacity, rows), 0) == (dest_row ^ me) * capacity + offset
+
+
+def placing(dest_col, me, peers, capacity):
+    rows = dest_col.shape[0]
+    slot = slot_column(dest_col, me, peers, capacity).astype(F32)
+    slot = jnp.transpose(jnp.broadcast_to(slot, (rows, 128)))[0:1, :].astype(jnp.int32)
+    return iota((peers * capacity, rows), 0) == slot
 
 
 def fetching(dest_col, me, peers, capacity):
@@ -100,7 +102,7 @@
 
 
 def pack_kernel(peers, capacity, ids, dest_row, tokens, *outs):
-    place = placing(dest_row[...], own_index(ids, len(outs)), peers, capacity)
+    place = placing_row(dest_row[...], own_index(ids, len(outs)), peers, capacity)
     held = jnp.sum(place.astype(F32), axis=1, keepdims=True)
     rows = jnp.where(held > 0.5, dot(place.astype(BF16), tokens[...]), DEAD).astype(BF16)
     size = outs[0].shape[0]
@@ -140,11 +142,12 @@
     return jnp.transpose(jnp.where(upper, turned[:, :half], turned[:, half:]))
 
 
-def attention_kernel(blocks, ids, *refs):
+def attention_kernel(blocks, traffic, ids, *refs):
     arrived, refs = refs[:blocks], refs[blocks:]
-    (seg_row, seg_col, gain, shift, w_hbm, q_bias, v_bias,
-     ctx, qkv_out, natural_out, a1, lse,
-     bias, turned_v, w_qkv, qkv, packed, in_sems, w_sem, out_sems) = refs
+    (seg_row, seg_col, gain, shift, w_hbm, q_bias, v_bias), refs = refs[:7], refs[7:]
+    outs, refs = refs[:blocks], refs[blocks:]
+    (qkv_out, natural_out, a1, lse,
+     bias, turned_v, w_qkv, qkv, packed, ctx, in_sems, w_sem, out_sems) = refs
     slots, width = packed.shape
     block = CLIPMAX
     fetches = []
@@ -158,6 +161,7 @@
         fetch.wait()
     keep = pltpu.make_async_copy(packed, natural_out, out_sems.at[0])
     keep.start()
+    traffic.need(blocks, blocks + 1)
     write_bias(packed, seg_row, seg_col, bias)
     gain_f, shift_f = gain[...].astype(F32), shift[...].astype(F32)
 
@@ -168,6 +172,7 @@
         a1[r, :] = (hat * gain_f + shift_f).astype(BF16)
 
     row_loop(slots, 32, norm_rows)
+    traffic.ready(blocks + 2)
     weights.wait()
 
     piece = 256
@@ -203,8 +208,14 @@
         return carry
 
     lax.fori_loop(0, width // 128, pair, 0)
+    sends = []
+    for k, ref in enumerate(outs):
+        sends.append(pltpu.make_async_copy(ctx.at[block_rows(ids, k, outs), :], ref, in_sems.at[k]))
+        sends[-1].start()
     keep.wait()
     keep_qkv.wait()
+    for copy in sends:
+        copy.wait()
 
 
 def attention_back_kernel(shared, traffic, ids, *refs):
@@ -303,13 +314,14 @@
     return below, below + u * (bell * 0.3989422804014327)
 
 
-def rows_kernel(peers, capacity, shared, traffic, ids, *refs):
-    (whole, tokens, dest_col, dest_row, cot_out, cot_align, out_hbm, out_bias, gain2, shift2, up_hbm, up_bias, down_hbm, down_bias,
-     gain3, shift3, align_hbm, align_bias), refs = refs[:18], refs[18:]
+def rows_kernel(peers, capacity, blocks, shared, traffic, ids, *refs):
+    arrived, refs = refs[:blocks], refs[blocks:]
+    (tokens, dest_col, cot_out, cot_align, out_hbm, out_bias, gain2, shift2, up_hbm, up_bias, down_hbm, down_bias,
+     gain3, shift3, align_hbm, align_bias), refs = refs[:16], refs[16:]
     (y_out, al_out, g_packed, g_mid, hidden, gub, a2, a3, ctx, gyb, gmb, small), refs = refs[:12], refs[12:]
     if shared:
         (send, own), refs = refs[:2], refs[2:]
-    (mid, acc, hat2, rstd2, slope, u_a, u_b, h_a, h_b, sums, w_out, w_up, w_down, w_align, sems), refs = refs[:15], refs[15:]
+    (mid, acc, hat2, rstd2, slope, u_a, u_b, h_a, h_b, sums, w_out, w_up, w_down, w_align, sems, whole, in_sems), refs = refs[:17], refs[17:]
     rows, width = tokens.shape
     wide = hidden.shape[1]
     piece = u_a.shape[1]
@@ -319,11 +331,20 @@
             ((out_hbm, w_out), (up_hbm, w_up), (down_hbm, w_down), (align_hbm, w_align))
         )
     ]
-    for load in loads:
+    size = arrived[0].shape[0]
+    copies = []
+    for k, ref in enumerate(arrived):
+        copies.append(pltpu.make_async_copy(ref, whole.at[pl.ds(ORDER[k] * size, size), :], in_sems.at[k]))
+        copies[-1].start()
+    loads[0].start()
+    traffic.need(blocks + 1)
+    fetch = fetching(dest_col[...], own_index(ids, blocks), peers, capacity)
+    for copy in copies:
+        copy.wait()
+    for load in loads[1:]:
         load.start()
-
-    fetch = fetching(dest_col[...], 0, peers, capacity)
     ctx[...] = dot(fetch, whole[...]).astype(BF16)
+    traffic.need(blocks)
     loads[0].wait()
     acc[...] = dot(ctx[...], w_out[...])
 
@@ -378,6 +399,7 @@
 
     row_loop(rows, 32, to_a3)
     loads[3].wait()
+    traffic.need(blocks + 2, blocks + 3)
     al_out[...] = (dot(a3[...], w_align[...]) + align_bias[...].astype(F32)).astype(BF16)
     traffic.ready(0, 1)
     mid[...] = dot_nt(cot_align[...], w_align[...])
@@ -422,7 +444,7 @@
     row_loop(rows, 32, back2)
     traffic.ready(3, 10)
     g_ctx = dot_nt(gmb[...], w_out[...]).astype(BF16)
-    place = placing(dest_row[...], 0, peers, capacity).astype(BF16)
+    place = placing(dest_col[...], 0, peers, capacity).astype(BF16)
     g_packed[...] = dot(place, g_ctx).astype(BF16)
     traffic.ready(2)
     small[8:9, :] = jnp.sum(sums[0], axis=0, keepdims=True)
@@ -434,6 +456,9 @@
     if shared:
         natural, turned_d = refs
         turn(gyb, natural, turned_d, 0, ids, 10, 4)
+        turn(a3, natural, send, AT_3, ids, 2, 8)
+        turn(ctx, natural, send, AT_1, ids, 2, 8)
+        turn(a2, natural, send, AT_2, ids, 2, 8)
         own[OWN_D : OWN_D + 384, :] = turned_d[0:384, :]
         send[AT_D : AT_D + 384, :] = turned_d[384:768, :]
         for core, out, align_at, out_at in ((0, own, OWN_ALIGN, OWN_OUT), (1, send, AT_ALIGN, AT_OUT)):
@@ -442,9 +467,6 @@
                 out[at, :] = cot_align[:, own_columns(ids, core, x, 256)]
                 at = slice(out_at + x * 256, out_at + x * 256 + 256)
                 out[at, :] = spare_columns(gmb, ids[1] ^ (core + 2 * x), 192, 256)
-        turn(a3, natural, send, AT_3, ids, 2, 8)
-        turn(ctx, natural, send, AT_1, ids, 2, 8)
-        turn(a2, natural, send, AT_2, ids, 2, 8)
         for core, out, up_at in ((0, own, OWN_UP), (1, send, AT_UP)):
             for x in range(2):
                 for c in range(3):
@@ -462,7 +484,7 @@
     out[...] = (g_mid[...] + dot(fetch, arrived[...])).astype(BF16)
 
 
-EARLY_PARTS, JOINED_PARTS, JOINED_SPLIT = (576, 576, 384), (240, 240), (48, 48)
+EARLY_PARTS, JOINED_PARTS, JOINED_SPLIT = (576, 480, 480), (240, 240), (48, 48)
 JOINED_BASE = (0, 16 * 240)
 AT_2, AT_3, AT_1, AT_D, AT_UP, AT_ALIGN, AT_OUT, AT_SMALL, SENT = 0, 768, 1536, 2304, 2688, 4224, 4736, 5248, 5344
 OWN_D, OWN_UP, OWN_ALIGN, OWN_OUT, OWN = 0, 384, 1920, 2432, 2944
@@ -598,15 +620,15 @@
     for copy in copies[:4]:
         copy.wait()
     for x in range(2):
-        for k, shift in ((0, 0), (1, 192)):
+        for k in range(2):
             turned = slice(k * 768, k * 768 + 768)
             at = slice(k * 512 + x * 256, k * 512 + x * 256 + 256)
             made = dot(turned_o[turned, :], ends_o[at, :])
             made += dot(turned_c[turned, :], ends_c[at, :])
             for i in range(8):
                 for half in range(2):
-                    put(2, x, i, shift + half * 96, made[i * 96 : i * 96 + 96, half * 128 : half * 128 + 128])
-    traffic.ready(2, 3)
+                    part, at = ((1, 384), (2, 192), (2, 288), (2, 384))[2 * k + half]
+                    put(part, x, i, at, made[i * 96 : i * 96 + 96, half * 128 : half * 128 + 128])
     for copy in copies[4:]:
         copy.wait()
     for i in (4, 5, 6, 7, 0, 1, 2, 3):
@@ -614,8 +636,8 @@
         made = dot(down_o[...], hidden[:, at])
         made += dot(down_c[...], came_hidden[:, at])
         for x in range(2):
-            for c in range(3):
-                put(1, x, i, c * 192, made[x * 192 : x * 192 + 192, c * 128 : c * 128 + 128])
+            for c, (part, to) in enumerate(((1, 0), (1, 192), (2, 0))):
+                put(part, x, i, to, made[x * 192 : x * 192 + 192, c * 128 : c * 128 + 128])
         if i == 7:
             traffic.ready(1)
 
@@ -688,29 +710,21 @@
     return keep[rows, :].astype(F32) + came[rows, :].astype(F32)
 
 
-def step_parts(traffic, ids, *refs):
-    keeps, cames, small = refs[0:3], refs[3:6], refs[6]
-    outs, sends, total = refs[7:10], refs[10:13], refs[13]
-    for k, (keep, came, out, send) in enumerate(zip(keeps, cames, outs, sends)):
-        half = keep.shape[0] // 2
-        traffic.need(k, 3 + k)
-        send[0:half, :] = joined_half(keep, came, half, half)
-        if k == 0:
-            traffic.need(6)
-            pass_small(small, came, 2 * half, total, send, half)
-        traffic.ready(3 + k)
-        out[...] = joined_half(keep, came, 0, half)
+def step_parts(count, small_with, traffic, ids, *refs):
+    keeps, cames, refs = refs[:count], refs[count : 2 * count], refs[2 * count :]
+    if small_with is not None:
+        small, total, refs = refs[0], refs[-1], refs[1:-1]
+    outs, sends = refs[:count], refs[count:]
+    for k in range(count):
+        half = keeps[k].shape[0] // 2
+        traffic.need(k, count + k)
+        sends[k][0:half, :] = joined_half(keeps[k], cames[k], half, half)
+        if k == small_with:
+            traffic.need(2 * count)
+            pass_small(small, cames[k], 2 * half, total, sends[k], half)
+        traffic.ready(count + k)
+        outs[k][...] = joined_half(keeps[k], cames[k], 0, half)
         traffic.ready(k)
-
-
-def step_parts_last(ids, *refs):
-    keeps, cames, small = refs[0:3], refs[3:6], refs[6]
-    outs, sends, total = refs[7:10], refs[10:12], refs[12]
-    for k, to, at in ((0, 0, 0), (1, 1, 0), (2, 0, EARLY_PARTS[0])):
-        half = keeps[k].shape[0] // 2
-        outs[k][...] = joined_half(keeps[k], cames[k], 0, half)
-        sends[to][at : at + half, :] = joined_half(keeps[k], cames[k], half, half)
-    pass_small(small, cames[0], keeps[0].shape[0], total, sends[0], EARLY_PARTS[0] + EARLY_PARTS[2])
 
 
 def step_apart(ids, keep_x, came_x, keep_y, came_y, small, out_x, send_x, out_y, send_y, total):
@@ -746,20 +760,21 @@
         out[:, c * 128 : (c + 1) * 128] = small[c * count : (c + 1) * count]
 
 
-def early_end(ids, keep_0, keep_1, keep_2, came, came_1, small, down, align, up, out, total):
-    def block(at, count):
-        return keep_2[at : at + count, :].astype(F32) + came[576 + at : 576 + at + count, :].astype(F32)
-
-    for c in range(3):
-        down[c * 128 : (c + 1) * 128, :] = jnp.transpose(added(keep_1, came_1, c * 192, 192))
+def early_end_a(ids, keep_1, keep_2, came_1, came_2, down, align, out):
+    down[0:128, :] = jnp.transpose(added(keep_1, came_1, 0, 192))
+    down[128:256, :] = jnp.transpose(added(keep_1, came_1, 192, 192))
+    down[256:384, :] = jnp.transpose(added(keep_2, came_2, 0, 192))
+    align[:, 0:128] = added(keep_1, came_1, 384, 96)
+    align[:, 128:256] = added(keep_2, came_2, 192, 96)
+    out[:, 0:128] = added(keep_2, came_2, 288, 96)
+    out[:, 128:192] = added(keep_2, came_2, 384, 96)[:, 0:64]
+
+
+def early_end_b(ids, keep, came, small, up, total):
     for c in range(6):
-        up[:, c * 128 : (c + 1) * 128] = added(keep_0, came, c * 96, 96)
-    for c in range(2):
-        align[:, c * 128 : (c + 1) * 128] = block(c * 96, 96)
-    out[:, 0:128] = block(192, 96)
-    out[:, 128:192] = block(288, 96)[:, 0:64]
+        up[:, c * 128 : (c + 1) * 128] = added(keep, came, c * 96, 96)
     count = small.shape[0]
-    both = both_small(small[...], came[960 : 960 + 2 * count, :])
+    both = both_small(small[...], came[576 : 576 + 2 * count, :])
     small_columns(both, total)
 
 
@@ -888,7 +903,6 @@
     capacity = slots // peers
     fast = peers == 8 and groups == 4 and (width, wide, align) == (768, 3072, 1024)
     blocks = 8 if fast else 1
-    dest_row = dest.reshape(1, rows)
     seg_col = seg_ids.reshape(slots, 1)
     line = lambda v: v.reshape(1, v.shape[0])
     shape = jax.ShapeDtypeStruct
@@ -908,20 +922,22 @@
     packed = call(
         functools.partial(pack_kernel, peers, capacity), "pack_tokens", 56,
         [shape((slots // blocks, width), BF16)] * blocks, [],
-        ids, dest_row, tokens,
+        ids, dest.reshape(1, rows), tokens, kept=tuple(range(blocks)), load=(1,),
     )
     packed = exchange(packed, peers, groups)
 
     in_slots = shape((slots, width), BF16)
-    ctx, qkv, natural, a1, lse = call(
+    apart = [shape((slots // blocks, width), BF16)] * blocks
+    made = call(
         functools.partial(attention_kernel, blocks), "attention", 56,
-        [in_slots, shape((slots, 3 * width), BF16), in_slots, in_slots, shape((width // 128, count, 2 * CLIPMAX), F32)],
+        apart + [shape((slots, 3 * width), BF16), in_slots, in_slots, shape((width // 128, count, 2 * CLIPMAX), F32)],
         [vmem((count, 3 * CLIPMAX, 2 * CLIPMAX), F32), vmem((128, slots), BF16), vmem((width, 3 * width), BF16),
-         vmem((slots, 3 * width), BF16), vmem((slots, width), BF16), dma((blocks,)), dma, dma((2,))],
+         vmem((slots, 3 * width), BF16), vmem((slots, width), BF16), vmem((slots, width), BF16), dma((blocks,)), dma, dma((2,))],
         ids, *packed, seg_ids, seg_col, line(ln1_gain), line(ln1_bias), w_qkv, line(q_bias), line(v_bias),
-        far=tuple(range(blocks)) + (blocks + 4, -2, -3), kept=(3, 4),
+        far=tuple(range(blocks)) + (blocks + 4,) + tuple(-1 - k for k in range(blocks + 2)),
+        load=(blocks, blocks + 1), flush=(blocks + 2,), kept=(blocks + 3,), lazy=True,
     )
-    (ctx,) = exchange([ctx], peers, groups)
+    ctx, (qkv, natural, a1, lse) = exchange(made[:blocks], peers, groups), made[blocks:]
 
     full = shape((rows, width), F32)
     extra = 12 * 16
@@ -933,17 +949,17 @@
     small_early = shape((96, 128), F32)
     turned = shape((width, rows), BF16)
     y, al, g_packed, g_mid, hidden, gub, a2, a3, ctx_rows, gyb, gmb, small_0, *sent = call(
-        functools.partial(rows_kernel, peers, capacity, fast), "rows", 46,
+        functools.partial(rows_kernel, peers, capacity, blocks, fast), "rows", 46,
         [low(width), low(align), in_slots, full, low(wide), low(wide), low(width), low(width), low(width), low(width), low(width),
          shape((16, width), F32)] + ([shape((SENT, 256), BF16), shape((OWN, 256), BF16)] if fast else []),
         [vmem((rows, width), F32), vmem((rows, width), F32), vmem((rows, width), F32), vmem((rows, 128), F32), vmem((rows, wide), F32),
          vmem((rows, 512), F32), vmem((rows, 512), F32), vmem((rows, 512), BF16), vmem((rows, 512), BF16),
          vmem((2, 8, width), F32), vmem(w_out.shape, BF16), vmem(w_up.shape, BF16), vmem(w_down.shape, BF16),
-         vmem(w_align.shape, BF16), dma((4,))] + ([vmem((width, rows), BF16)] * 2 if fast else []),
-        ids, ctx, tokens, dest, dest_row, cot_out, cot_align,
+         vmem(w_align.shape, BF16), dma((4,)), vmem((slots, width), BF16), dma((blocks,))] + ([vmem((width, rows), BF16)] * 2 if fast else []),
+        ids, *ctx, tokens, dest, cot_out, cot_align,
         w_out, line(out_bias), line(ln2_gain), line(ln2_bias), w_up, line(up_bias), w_down, line(down_bias),
         line(ln3_gain), line(ln3_bias), w_align, line(align_bias),
-        far=(6, 10, 12, 16), flush=(0, 1, 2, 3, 4) + ((12, 13) if fast else ()), kept=(5, 6, 7, 8, 9, 10, 11), lazy=True,
+        far=tuple(range(blocks)) + tuple(blocks + k for k in (4, 8, 10, 14)), load=(), flush=(0, 1, 2, 3, 4) + ((12, 13) if fast else ()), kept=(5, 6, 7, 8, 9, 10, 11), lazy=True,
     )
     (g_arrived,) = exchange([g_packed], peers, groups)
 
@@ -952,11 +968,11 @@
         came = move(sent, "grp", 1)
         came_hidden = move(hidden, "grp", 1)
         routes = (
-            (("grp", 2), ("batch", 2), ("batch", 1)),
-            (("batch", 1), ("grp", 2), ("batch", 4)),
-            (("batch", 2), ("batch", 1), ("grp", 2)),
+            (("grp", 2), ("batch", 2), ("batch", 1), ("batch", 4)),
+            (("batch", 1), ("grp", 2), ("batch", 4), ("batch", 2)),
+            (("batch", 2), ("batch", 1), ("grp", 2), ("batch", 4)),
         )
-        go = lambda sends, k: [move(send, *route[k]) for send, route in zip(sends, routes)]
+        go = lambda sends, k, which=(0, 1, 2): [move(send, *routes[p][k]) for send, p in zip(sends, which)]
         square = lambda n: vmem((n, rows), BF16)
         k0, s0, small_e = call(
             second_grads, "second_grads", 16, [held(8)[0], chain(8)[0], small_early],
@@ -994,52 +1010,60 @@
         came = move(send, "grp", 1)
         small_shape = shape((48, 128), F32)
 
-        def early_step(name, n, keeps, cames, small_e, before, cost, **more_of):
+        def early_step(name, which, n, keeps, cames, small_e, before, cost, **more_of):
+            count = len(which)
+            first = which[0] == 0
             made = call(
-                step_parts, name, 14, held(n) + chain(n) + [small_early], [],
-                ids, *keeps, tie(cames[0], before), *cames[1:], small_e, cost=cost, lazy=True, **more_of,
+                functools.partial(step_parts, count, 0 if first else None), name, 14,
+                [held(n)[p] for p in which] + [chain(n)[p] for p in which] + ([small_early] if first else []), [],
+                ids, *keeps, tie(cames[0], before), *cames[1:], *((small_e,) if first else ()), cost=cost, lazy=True, **more_of,
             )
-            return made[0:3], made[3:6], made[6]
-
-        keeps, sends, small_e = early_step("early_step_1", 4, keeps, cames, small_e, send, 15, load=(0, 3, 6, 1, 4, 2, 5), flush=(0, 1, 2, 3, 4, 5))
+            return list(made[:count]), list(made[count : 2 * count]), (made[-1] if first else small_e)
+
+        both_, one_ = (1, 2), (0,)
+        C1, CK, C2A, C2B, CA, C3A, C3B, CEA = 15,.001,3,.001,.001,4,.001,3
+        keeps, sends, small_e = early_step("early_step_1", (0, 1, 2), 4, keeps, cames, small_e, send, C1, load=(0, 3, 6, 1, 4, 2, 5), flush=(0, 1, 2, 3, 4, 5))
         cames = go(sends, 1)
         kx3, sx3, ky3, sy3, small_j = call(
             joined_keep, "joined_keep", 12, parts(8) + [small_shape], [],
-            ids, turned_c, g_joined, tie(came, sends[0]), small_2, load=(0, 1),
+            ids, turned_c, g_joined, tie(came, sends[0]), small_2, load=(0, 1), cost=CK,
         )
         cx3, cy3 = move(sx3, "grp", 2), move(sy3, "batch", 1)
-        keeps, sends, small_e = early_step("early_step_2", 2, keeps, cames, small_e, sx3, 3.0, load=(0, 1, 2))
-        cames = go(sends, 2)
+        keeps_a, sends_a, _ = early_step("early_step_2a", both_, 2, keeps[1:], cames[1:], None, sx3, C2A, load=(0, 1))
+        cames_a = go(sends_a, 2, both_)
+        keeps_b, sends_b, small_e = early_step("early_step_2b", one_, 2, keeps[:1], cames[:1], small_e, sends_a[0], C2B, load=(0,))
+        cames_b = go(sends_b, 2, one_)
         kx3, sx3, ky3, sy3, small_j = call(
             step_apart, "joined_apart", 10, parts(4) + [small_shape], [],
-            ids, kx3, tie(cx3, sends[0]), ky3, cy3, small_j,
+            ids, kx3, tie(cx3, sends_b[0]), ky3, cy3, small_j, cost=CA,
         )
         cx3, cy3 = move(sx3, "batch", 1), move(sy3, "grp", 2)
-        *keeps, send, send_1, small_e = call(
-            step_parts_last, "early_step_3", 10, held(1) + [flat(960 + extra), held(1)[1], small_early], [],
-            ids, *keeps, tie(cames[0], sx3), *cames[1:], small_e, cost=1.0,
-        )
-        last = move(send, "batch", 4)
-        last_1 = move(send_1, "batch", 2)
-        g_back = tie(g_back, send)
+        keeps_a, sends_a, _ = early_step("early_step_3a", both_, 1, keeps_a, cames_a, None, sx3, C3A)
+        cames_a = go(sends_a, 3, both_)
+        keeps_b, sends_b, small_e = early_step("early_step_3b", one_, 1, keeps_b, cames_b, small_e, sends_a[0], C3B)
+        cames_b = go(sends_b, 3, one_)
+        g_back = tie(g_back, sends_b[0])
         k3, s3, small_j = call(
             step_meet, "joined_meet", 10, [flat(2 * both), flat(2 * both + more), small_shape], [],
-            ids, kx3, tie(cx3, send), ky3, cy3, small_j,
+            ids, kx3, tie(cx3, sends_b[0]), ky3, cy3, small_j,
         )
         c3 = move(s3, "batch", 2)
+        sum_down, sum_align, sum_out = call(
+            early_end_a, "early_end_a", 10, [shape((384, 192), F32), shape((96, 256), F32), shape((96, 192), F32)], [],
+            ids, *keeps_a, tie(cames_a[0], s3), cames_a[1], cost=CEA,
+        )
+        sum_up, small_e = call(
+            early_end_b, "early_end_b", 10, [shape((96, 768), F32), shape((16, width), F32)], [],
+            ids, *keeps_b, tie(cames_b[0], sum_out), small_e, cost=CEA,
+        )
         k3, s3, small_j = call(
             step_joint, "joined_joint", 10, [flat(both), flat(both + more), small_shape], [],
-            ids, k3, c3, small_j,
+            ids, k3, tie(c3, sum_up), small_j,
         )
         c3 = move(s3, "batch", 4)
-        sum_down, sum_align, sum_up, sum_out, small_e = call(
-            early_end, "early_end", 10,
-            [shape((384, 192), F32), shape((96, 256), F32), shape((96, 768), F32), shape((96, 192), F32), shape((16, width), F32)], [],
-            ids, *keeps, tie(last, s3), last_1, small_e,
-        )
         sum_qkv, small_j = call(
             joined_end, "joined_end", 10, [shape((96, 576), F32), shape((8, width), F32)], [],
-            ids, k3, tie(c3, sum_out), small_j,
+            ids, k3, c3, small_j,
         )
         small_0, small_2 = small_e, small_j
     else:
@@ -1054,7 +1078,7 @@
 
     (grad_tokens,) = call(
         functools.partial(last_kernel, peers, capacity), "grad_tokens", 8, [low(width)], [],
-        ids, g_back, dest, g_mid,
+        ids, g_back, dest, g_mid, load=(1, 2),
     )
     sum_align_bias = small_0[3:5].reshape(2 * width)[:align]
     sum_up_bias = small_0[11:15].reshape(4 * width)[:wide]

time: 220 us -> 216 us (0.982)
  waiting for transfers between devices: 68.4 us -> 41.9 us
  starting transfers between devices: 42.2 us -> 58.1 us
  Pallas kernels: 96.8 us -> 103 us
    ppermute x27 -> x35, starting transfers between devices: 28.1 us -> 48.5 us  [flip(): return lax.ppermute(value, AXES, pairs)]
    all_to_all x3 -> x2, waiting for transfers between devices: 20.3 us -> 0.01 us  [exchange(): lax.all_to_all(shaped, 'batch', split_axis=0, concat_axis=0, tiled=True)]
    ppermute x27 -> x35, waiting for transfers between devices: 48.2 us -> 41.9 us  [flip(): return lax.ppermute(value, AXES, pairs)]
    pallas_call x16 -> x19, Pallas kernels: 96.8 us -> 103 us  [call(): pl.pallas_call(body, name=name, out_shape=outs, in_specs=[SMEM] + [HBM if...]
    all_to_all x3 -> x2, starting transfers between devices: 14.1 us -> 9.61 us  [exchange(): lax.all_to_all(shaped, 'batch', split_axis=0, concat_axis=0, tiled=True)]
    unnamed x54 -> x62, local copies, waits for them, and re-layouts: 4.89 us -> 4.25 us
  transfers between devices with their start and end apart: 30 -> 37, of which waited for: 13 -> 15; matrix products, arithmetic and copies ran while one was open for 3% -> 3% of each run, Pallas kernels for 24% -> 26%
where the time goes in v4:
time: 216 us
  Pallas kernels  103 us (48%)
  starting transfers between devices  58.1 us (27%)
  waiting for transfers between devices  41.9 us (19%)
  local copies, waits for them, and re-layouts  11.1 us (5%)
    pallas_call x19, Pallas kernels, call(): pl.pallas_call(body, name=name, out_shape=outs, in_specs=[SMEM] + [HBM if...  103 us
    ppermute x35, starting transfers between devices, flip(): return lax.ppermute(value, AXES, pairs)  48.5 us
    ppermute x35, waiting for transfers between devices, flip(): return lax.ppermute(value, AXES, pairs)  41.9 us
    all_to_all x2, starting transfers between devices, exchange(): lax.all_to_all(shaped, 'batch', split_axis=0, concat_axis=0, tiled=True)  9.61 us
  transfers between devices with their start and end apart: 37, of which 15 were waited for; matrix products, arithmetic and copies ran while one was open for 3% of the time, Pallas kernels for 26%

profile of v4, /device:TPU:0, one launch (start us, length us, event | category | flops | bytes accessed | tf_op | source)
XLA Modules:
  0.0 215.6 jit_solution(15615133781775107457)
XLA Ops:
  0.8 0.7 copy-done.5
  1.4 2.8 %pack_tokens.1 = (bf16[64,768]{1,0:T(8,128)(2,1)}, bf16[64,768]{1,0:T(8,128)(2,1)}, bf16[64,768]{1,0:T(8,128)(2,1)}, bf16[64,768]{1,0:T(8,128)(2,1)}, bf16[64,76...) custom-call(s32[14]{0:T(128)S(1)} %pad_add_fusion.ids, ...), custom_call_target="tpu_custom_call" | custom-call | flops 1000000 | bytes 1 | tf_op jit(solution)/shard_map/pack_tokens/pallas_call | solution.py:872
  4.3 3.0 %collective-permute-start = (bf16[64,768]{1,0:T(8,128)(2,1)}, bf16[64,768]{1,0:T(8,128)(2,1)S(1)}, u32[]{:S(2)}, u32[]{:S(2)}) collective-permute-start(bf16[64,768]{1,0:T(8,128)(2,1)} %get-tuple-element.118), channel_id=1, source_target_pairs={{0,4},{1,5},{2,6},{3,7},{4,0},{5,1},{6,2},{7,3},{8,12},{9,13},{10,... | collective-permute-start | bytes 294920 | tf_op jit(solution)/shard_map/ppermute | solution.py:800
  7.3 1.6 collective-permute-start.1
  8.9 3.0 %collective-permute-start.3 = (bf16[64,768]{1,0:T(8,128)(2,1)}, bf16[64,768]{1,0:T(8,128)(2,1)S(1)}, u32[]{:S(2)}, u32[]{:S(2)}) collective-permute-start(bf16[64,768]{1,0:T(8,128)(2,1)} %get-tuple-element.121), channel_id=1, source_target_pairs={{0,16},{1,17},{2,18},{3,19},{4,20},{5,21},{6,22},{7,23},{8,24},{9,... | collective-permute-start | bytes 294920 | tf_op jit(solution)/shard_map/ppermute | solution.py:800
  11.9 1.3 collective-permute-start.4
  13.2 3.6 %collective-permute-start.5 = (bf16[64,768]{1,0:T(8,128)(2,1)}, bf16[64,768]{1,0:T(8,128)(2,1)S(1)}, u32[]{:S(2)}, u32[]{:S(2)}) collective-permute-start(bf16[64,768]{1,0:T(8,128)(2,1)} %get-tuple-element.123), channel_id=1, source_target_pairs={{0,24},{1,25},{2,26},{3,27},{4,28},{5,29},{6,30},{7,31},{8,16},{9,... | collective-permute-start | bytes 294920 | tf_op jit(solution)/shard_map/ppermute | solution.py:800
  16.8 0.7 reshape.103.refs_10_.refs_7_
  17.5 0.7 reshape.104.refs_11_
  18.2 0.7 reshape.105.refs_13_
  18.9 0.7 reshape.106.refs_14_
  19.6 1.5 copy.45.refs_9_.refs_6_
  21.1 6.1 %collective-permute-done.4.refs_5_ = bf16[64,768]{1,0:T(8,128)(2,1)S(1)} collective-permute-done((bf16[64,768]{1,0:T(8,128)(2,1)}, bf16[64,768]{1,0:T(8,128)(2,1)S(1)}, u32[]{:S(2)}, u32[]{:S(2)}) %collective-permute-start.4) | collective-permute-done | bytes 98336 | tf_op jit(solution)/shard_map/ppermute | solution.py:800
  28.1 16.1 %attention.1 = (bf16[64,768]{1,0:T(8,128)(2,1)}, bf16[64,768]{1,0:T(8,128)(2,1)}, bf16[64,768]{1,0:T(8,128)(2,1)}, bf16[64,768]{1,0:T(8,128)(2,1)}, bf16[64,768]...) custom-call(s32[14]{0:T(128)S(1)} %pad_add_fusion.ids, ...), custom_call_target="tpu_custom_call" | custom-call | flops 1000000 | bytes 1 | tf_op jit(solution)/shard_map/attention/pallas_call | solution.py:872
  44.2 1.0 collective-permute-start.7
  45.2 3.5 %collective-permute-start.8 = (bf16[64,768]{1,0:T(8,128)(2,1)}, bf16[64,768]{1,0:T(8,128)(2,1)S(1)}, u32[]{:S(2)}, u32[]{:S(2)}) collective-permute-start(bf16[64,768]{1,0:T(8,128)(2,1)} %get-tuple-element.127), channel_id=1, source_target_pairs={{0,8},{1,9},{2,10},{3,11},{4,12},{5,13},{6,14},{7,15},{8,0},{9,1},... | collective-permute-start | bytes 294920 | tf_op jit(solution)/shard_map/ppermute | solution.py:800
  48.7 0.9 collective-permute-start.9
  49.6 3.2 %collective-permute-start.10 = (bf16[64,768]{1,0:T(8,128)(2,1)}, bf16[64,768]{1,0:T(8,128)(2,1)S(1)}, u32[]{:S(2)}, u32[]{:S(2)}) collective-permute-start(bf16[64,768]{1,0:T(8,128)(2,1)} %get-tuple-element.129), channel_id=1, source_target_pairs={{0,16},{1,17},{2,18},{3,19},{4,20},{5,21},{6,22},{7,23},{8,24},{9,... | collective-permute-start | bytes 294920 | tf_op jit(solution)/shard_map/ppermute | solution.py:800
  52.9 2.4 %collective-permute-start.12 = (bf16[64,768]{1,0:T(8,128)(2,1)}, bf16[64,768]{1,0:T(8,128)(2,1)S(1)}, u32[]{:S(2)}, u32[]{:S(2)}) collective-permute-start(bf16[64,768]{1,0:T(8,128)(2,1)} %get-tuple-element.131), channel_id=1, source_target_pairs={{0,24},{1,25},{2,26},{3,27},{4,28},{5,29},{6,30},{7,31},{8,16},{9,... | collective-permute-start | bytes 294920 | tf_op jit(solution)/shard_map/ppermute | solution.py:800
  55.2 2.4 %collective-permute-start.13 = (bf16[64,768]{1,0:T(8,128)(2,1)}, bf16[64,768]{1,0:T(8,128)(2,1)S(1)}, u32[]{:S(2)}, u32[]{:S(2)}) collective-permute-start(bf16[64,768]{1,0:T(8,128)(2,1)} %get-tuple-element.132), channel_id=1, source_target_pairs={{0,28},{1,29},{2,30},{3,31},{4,24},{5,25},{6,26},{7,27},{8,20},{9,... | collective-permute-start | bytes 294920 | tf_op jit(solution)/shard_map/ppermute | solution.py:800
  58.0 6.5 %collective-permute-done.10.refs_4_ = bf16[64,768]{1,0:T(8,128)(2,1)S(1)} collective-permute-done((bf16[64,768]{1,0:T(8,128)(2,1)}, bf16[64,768]{1,0:T(8,128)(2,1)S(1)}, u32[]{:S(2)}, u32[]{:S(2)}) %collective-permute-start.10) | collective-permute-done | bytes 98336 | tf_op jit(solution)/shard_map/ppermute | solution.py:800
  64.5 2.5 %collective-permute-done.11.refs_5_ = bf16[64,768]{1,0:T(8,128)(2,1)S(1)} collective-permute-done((bf16[64,768]{1,0:T(8,128)(2,1)}, bf16[64,768]{1,0:T(8,128)(2,1)S(1)}, u32[]{:S(2)}, u32[]{:S(2)}) %collective-permute-start.11) | collective-permute-done | bytes 98336 | tf_op jit(solution)/shard_map/ppermute | solution.py:800
  67.6 26.6 %rows.1 = (bf16[256,768]{1,0:T(8,128)(2,1)}, bf16[256,1024]{1,0:T(8,128)(2,1)}, bf16[512,768]{1,0:T(8,128)(2,1)}, f32[256,768]{1,0:T(8,128)}, bf16[256,3072]{1,0...) custom-call(s32[14]{0:T(128)S(1)} %pad_add_fusion.ids, ...), custom_call_target="tpu_custom_call" | custom-call | flops 1000000 | bytes 1 | tf_op jit(solution)/shard_map/rows/pallas_call | solution.py:872
  94.8 5.8 %all-to-all-start = ((bf16[8,64,768]{2,1,0:T(8,128)(2,1)}), bf16[8,64,768]{2,1,0:T(8,128)(2,1)S(1)}, u32[]{:S(2)}, u32[]{:S(2)}) async-start(bf16[8,64,768]{2,1,0:T(8,128)(2,1)} %bitcast.13), calls=%async_computation | async-start | bytes 1572864 | tf_op jit(solution)/shard_map/all_to_all | solution.py:887
  100.6 1.4 collective-permute-done.15.refs_2_.refs_4_
  102.0 5.6 %second_grads.1 = (bf16[4608,128]{1,0:T(8,128)(2,1)}, bf16[4800,128]{1,0:T(8,128)(2,1)}, f32[96,128]{1,0:T(8,128)}) custom-call(s32[14]{0:T(128)S(1)} %pad_add_fusion.ids, bf16[5344,256]{1,0:T(8,128)(2,1)} %get-tuple-element.137.refs_0_.refs_2_, bf16[2944,256]{1,0:T(8,128)(2,1)} %get-tuple-element.138.refs_1_.refs_3_, ...), custom_call_target="tpu_custom_call" | custom-call | flops 1000000 | bytes 1 | tf_op jit(solution)/shard_map/second_grads/pallas_call | solution.py:872
  107.6 1.5 collective-permute-start.16
  109.1 1.2 copy-done.7
  110.3 6.8 %first_grads.1 = (bf16[3840,128]{1,0:T(8,128)(2,1)}, bf16[3840,128]{1,0:T(8,128)(2,1)}, bf16[3840,128]{1,0:T(8,128)(2,1)}, bf16[3840,128]{1,0:T(8,128)(2,1)}) custom-call(s32[14]{0:T(128)S(1)} %pad_add_fusion.ids, bf16[256,3072]{1,0:T(8,128)(2,1)} %get-tuple-element.136.refs_0_, bf16[256,3072]{1,0:T(8,128)(2,1)} %copy-done.7, ...), custom_call_target="tpu_custom_call" | custom-call | flops 1000000 | bytes 1 | tf_op jit(solution)/shard_map/first_grads/pallas_call | solution.py:872
  117.1 3.8 %collective-permute-start.18 = (bf16[3840,128]{1,0:T(8,128)(2,1)}, bf16[3840,128]{1,0:T(8,128)(2,1)}, u32[]{:S(2)}, u32[]{:S(2)}) collective-permute-start(bf16[3840,128]{1,0:T(8,128)(2,1)} %get-tuple-element.153), channel_id=1, source_target_pairs={{0,8},{1,9},{2,10},{3,11},{4,12},{5,13},{6,14},{7,15},{8,0},{9,1},... | collective-permute-start | bytes 2949128 | tf_op jit(solution)/shard_map/ppermute | solution.py:800
  120.9 1.0 collective-permute-start.17
  121.9 21.5 %attention_back.1 = (bf16[512,768]{1,0:T(8,128)(2,1)}, bf16[512,2304]{1,0:T(8,128)(2,1)}, f32[8,768]{1,0:T(8,128)S(1)}, bf16[7776,128]{1,0:T(8,128)(2,1)}, bf16[768,512]{1,0:T(8,128)(2,1)}) custom-call(s32[14]{0:T(128)S(1)} %pad_add_fusion.ids, bf16[512,768]{1,0:T(8,128)(2,1)S(1)} %bitcast.8, bf16[512,768]{1,0:T(8,128)(2,1)} %get-tuple-element.143.refs_1_, ...), custom_call_target="tpu_custom_call" | custom-call | flops 1000000 | bytes 1 | tf_op jit(solution)/shard_map/attention_back/pallas_call | solution.py:872
  143.5 0.9 collective-permute-done.17.refs_4_
  144.5 4.8 %early_step_1.1 = (bf16[2304,128]{1,0:T(8,128)(2,1)}, bf16[1920,128]{1,0:T(8,128)(2,1)}, bf16[1920,128]{1,0:T(8,128)(2,1)}, bf16[2496,128]{1,0:T(8,128)(2,1)}, b...) custom-call(s32[14]{0:T(128)S(1)} %pad_add_fusion.ids, ...), custom_call_target="tpu_custom_call" | custom-call | flops 15000000512 | bytes 1 | tf_op jit(solution)/shard_map/early_step_1/pallas_call | solution.py:872
  149.8 1.0 collective-permute-start.22
  151.1 3.8 %all-to-all-start.1 = ((bf16[8,64,768]{2,1,0:T(8,128)(2,1)}), bf16[8,64,768]{2,1,0:T(8,128)(2,1)S(1)}, u32[]{:S(2)}, u32[]{:S(2)}) async-start(bf16[8,64,768]{2,1,0:T(8,128)(2,1)} %bitcast.12), calls=%async_computation.1 | async-start | bytes 1572864 | tf_op jit(solution)/shard_map/all_to_all | solution.py:887
  155.0 4.2 %joined_keep.1 = (bf16[1920,128]{1,0:T(8,128)(2,1)S(1)}, bf16[2016,128]{1,0:T(8,128)(2,1)S(1)}, bf16[1920,128]{1,0:T(8,128)(2,1)S(1)}, bf16[1920,128]{1,0:T(8,128)(2,1)S(1)}, f32[48,128]{1,0:T(8,128)S(1)}) custom-call(s32[14]{0:T(128)S(1)} %pad_add_fusion.ids, bf16[768,512]{1,0:T(8,128)(2,1)} %get-tuple-element.160.refs_0_, ...), custom_call_target="tpu_custom_call" | custom-call | flops 1000000 | bytes 1 | tf_op jit(solution)/shard_map/joined_keep/pallas_call | solution.py:872
  159.1 1.6 collective-permute-start.25
  160.7 2.7 %collective-permute-done.20.refs_2_ = bf16[1920,128]{1,0:T(8,128)(2,1)} collective-permute-done((bf16[1920,128]{1,0:T(8,128)(2,1)}, bf16[1920,128]{1,0:T(8,128)(2,1)}, u32[]{:S(2)}, u32[]{:S(2)}) %collective-permute-start.20) | collective-permute-done | bytes 491552 | tf_op jit(solution)/shard_map/ppermute | solution.py:800
  163.4 0.7 collective-permute-start.26
  164.1 2.3 %collective-permute-done.22.refs_3_ = bf16[1920,128]{1,0:T(8,128)(2,1)} collective-permute-done((bf16[1920,128]{1,0:T(8,128)(2,1)}, bf16[1920,128]{1,0:T(8,128)(2,1)}, u32[]{:S(2)}, u32[]{:S(2)}) %collective-permute-start.22) | collective-permute-done | bytes 491552 | tf_op jit(solution)/shard_map/ppermute | solution.py:800
  166.4 2.5 %early_step_2a.1 = (bf16[960,128]{1,0:T(8,128)(2,1)S(1)}, bf16[960,128]{1,0:T(8,128)(2,1)S(1)}, bf16[960,128]{1,0:T(8,128)(2,1)S(1)}, bf16[960,128]{1,0:T(8,128)(2,1)S(1)}) custom-call(s32[14]{0:T(128)S(1)} %pad_add_fusion.ids, bf16[1920,128]{1,0:T(8,128)(2,1)} %get-tuple-element.157.refs_0_, bf16[1920,128]{1,0:T(8,128)(2,1)} %get-tuple-element.158.refs_1_, ...), custom_call_target="tpu_custom_call" | custom-call | flops 3000000000 | bytes 1 | tf_op jit(solution)/shard_map/early_step_2a/pallas_call | solution.py:872
  168.9 1.5 collective-permute-start.24
  170.4 1.9 collective-permute-start.27
  172.3 6.9 %collective-permute-done.19.refs_1_ = bf16[2496,128]{1,0:T(8,128)(2,1)S(1)} collective-permute-done((bf16[2496,128]{1,0:T(8,128)(2,1)}, bf16[2496,128]{1,0:T(8,128)(2,1)S(1)}, u32[]{:S(2)}, u32[]{:S(2)}) %collective-permute-start.19) | collective-permute-done | bytes 639008 | tf_op jit(solution)/shard_map/ppermute | solution.py:800
  179.2 1.8 early_step_2b.1
  181.0 1.9 collective-permute-start.23
  182.9 0.8 joined_apart.1
  183.6 1.3 collective-permute-start.28
  184.9 2.4 %collective-permute-done.24.refs_2_ = bf16[960,128]{1,0:T(8,128)(2,1)S(1)} collective-permute-done((bf16[960,128]{1,0:T(8,128)(2,1)S(1)}, bf16[960,128]{1,0:T(8,128)(2,1)S(1)}, u32[]{:S(2)}, u32[]{:S(2)}) %collective-permute-start.24) | collective-permute-done | bytes 245792 | tf_op jit(solution)/shard_map/ppermute | solution.py:800
  187.3 1.1 collective-permute-start.29
  189.2 2.1 collective-permute-start.33
  191.3 0.7 collective-permute-done.23.refs_1_
  192.9 2.0 collective-permute-done.28.refs_1_
  194.9 0.7 joined_meet.1
  195.6 0.9 collective-permute-start.30
  196.5 5.3 %collective-permute-done.33.refs_3_ = bf16[480,128]{1,0:T(8,128)(2,1)S(1)} collective-permute-done((bf16[480,128]{1,0:T(8,128)(2,1)S(1)}, bf16[480,128]{1,0:T(8,128)(2,1)S(1)}, u32[]{:S(2)}, u32[]{:S(2)}) %collective-permute-start.33) | collective-permute-done | bytes 122912 | tf_op jit(solution)/shard_map/ppermute | solution.py:800
  201.8 1.3 early_end_a.1
  203.1 1.2 collective-permute-done.31.refs_1_
  204.4 1.3 early_end_b.1
  206.8 3.3 %grad_tokens.1 = bf16[256,768]{1,0:T(8,128)(2,1)} custom-call(s32[14]{0:T(128)S(1)} %pad_add_fusion.ids, bf16[512,768]{1,0:T(8,128)(2,1)S(1)} %bitcast.9, s32[256,1]{1,0:T(8,128)} %copy-done.1, f32[256,768]{1,0:T(8,128)} %get-tuple-element.187.refs_2_), custom_call_target="tpu_custom_call" | custom-call | flops 1000000 | bytes 1 | tf_op jit(solution)/shard_map/grad_tokens/pallas_call | solution.py:872
  210.2 0.9 copy.49
  212.9 0.8 collective-permute-done.34.refs_1_
  213.7 1.3 joined_end.1
  (114 shorter events, 8.6 us)
Async XLA Ops:
  0.8 0.7 copy-start.5
  4.3 8.9 %collective-permute-start = (bf16[64,768]{1,0:T(8,128)(2,1)}, bf16[64,768]{1,0:T(8,128)(2,1)S(1)}, u32[]{:S(2)}, u32[]{:S(2)}) collective-permute-start(bf16[64,768]{1,0:T(8,128)(2,1)} %get-tuple-element.118), channel_id=1, source_target_pairs={{0,4},{1,5},{2,6},{3,7},{4,0},{5,1},{6,2},{7,3},{8,12},{9,13},{10,... | collective-permute-start | bytes 294920 | tf_op jit(solution)/shard_map/ppermute | solution.py:800
  7.3 9.5 %collective-permute-start.1 = (bf16[64,768]{1,0:T(8,128)(2,1)}, bf16[64,768]{1,0:T(8,128)(2,1)S(1)}, u32[]{:S(2)}, u32[]{:S(2)}) collective-permute-start(bf16[64,768]{1,0:T(8,128)(2,1)} %get-tuple-element.119), channel_id=1, source_target_pairs={{0,8},{1,9},{2,10},{3,11},{4,12},{5,13},{6,14},{7,15},{8,0},{9,1},... | collective-permute-start | bytes 294920 | tf_op jit(solution)/shard_map/ppermute | solution.py:800
  8.9 12.2 %collective-permute-start.2 = (bf16[64,768]{1,0:T(8,128)(2,1)}, bf16[64,768]{1,0:T(8,128)(2,1)S(1)}, u32[]{:S(2)}, u32[]{:S(2)}) collective-permute-start(bf16[64,768]{1,0:T(8,128)(2,1)} %get-tuple-element.120), channel_id=1, source_target_pairs={{0,12},{1,13},{2,14},{3,15},{4,8},{5,9},{6,10},{7,11},{8,4},{9,5},... | collective-permute-start | bytes 294920 | tf_op jit(solution)/shard_map/ppermute | solution.py:800
  8.9 12.2 %collective-permute-start.3 = (bf16[64,768]{1,0:T(8,128)(2,1)}, bf16[64,768]{1,0:T(8,128)(2,1)S(1)}, u32[]{:S(2)}, u32[]{:S(2)}) collective-permute-start(bf16[64,768]{1,0:T(8,128)(2,1)} %get-tuple-element.121), channel_id=1, source_target_pairs={{0,16},{1,17},{2,18},{3,19},{4,20},{5,21},{6,22},{7,23},{8,24},{9,... | collective-permute-start | bytes 294920 | tf_op jit(solution)/shard_map/ppermute | solution.py:800
  11.9 15.4 %collective-permute-start.4 = (bf16[64,768]{1,0:T(8,128)(2,1)}, bf16[64,768]{1,0:T(8,128)(2,1)S(1)}, u32[]{:S(2)}, u32[]{:S(2)}) collective-permute-start(bf16[64,768]{1,0:T(8,128)(2,1)} %get-tuple-element.122), channel_id=1, source_target_pairs={{0,20},{1,21},{2,22},{3,23},{4,16},{5,17},{6,18},{7,19},{8,28},{9,... | collective-permute-start | bytes 294920 | tf_op jit(solution)/shard_map/ppermute | solution.py:800
  13.2 14.1 %copy-start.15 = (bf16[64,768]{1,0:T(8,128)(2,1)}, bf16[64,768]{1,0:T(8,128)(2,1)S(1)}, u32[]{:S(2)}) copy-start(bf16[64,768]{1,0:T(8,128)(2,1)S(1)} %collective-permute-done.refs_1_) | copy-start | bytes 294916
  13.2 14.1 %collective-permute-start.5 = (bf16[64,768]{1,0:T(8,128)(2,1)}, bf16[64,768]{1,0:T(8,128)(2,1)S(1)}, u32[]{:S(2)}, u32[]{:S(2)}) collective-permute-start(bf16[64,768]{1,0:T(8,128)(2,1)} %get-tuple-element.123), channel_id=1, source_target_pairs={{0,24},{1,25},{2,26},{3,27},{4,28},{5,29},{6,30},{7,31},{8,16},{9,... | collective-permute-start | bytes 294920 | tf_op jit(solution)/shard_map/ppermute | solution.py:800
  16.8 10.5 %copy-start.16 = (bf16[64,768]{1,0:T(8,128)(2,1)}, bf16[64,768]{1,0:T(8,128)(2,1)S(1)}, u32[]{:S(2)}) copy-start(bf16[64,768]{1,0:T(8,128)(2,1)S(1)} %collective-permute-done.1.refs_2_) | copy-start | bytes 294916
  16.8 10.5 %collective-permute-start.6 = (bf16[64,768]{1,0:T(8,128)(2,1)}, bf16[64,768]{1,0:T(8,128)(2,1)S(1)}, u32[]{:S(2)}, u32[]{:S(2)}) collective-permute-start(bf16[64,768]{1,0:T(8,128)(2,1)} %get-tuple-element.124), channel_id=1, source_target_pairs={{0,28},{1,29},{2,30},{3,31},{4,24},{5,25},{6,26},{7,27},{8,20},{9,... | collective-permute-start | bytes 294920 | tf_op jit(solution)/shard_map/ppermute | solution.py:800
  21.1 6.2 %copy-start.17 = (bf16[64,768]{1,0:T(8,128)(2,1)}, bf16[64,768]{1,0:T(8,128)(2,1)S(1)}, u32[]{:S(2)}) copy-start(bf16[64,768]{1,0:T(8,128)(2,1)S(1)} %collective-permute-done.2.refs_3_) | copy-start | bytes 294916
  21.1 6.2 %copy-start.18 = (bf16[64,768]{1,0:T(8,128)(2,1)}, bf16[64,768]{1,0:T(8,128)(2,1)S(1)}, u32[]{:S(2)}) copy-start(bf16[64,768]{1,0:T(8,128)(2,1)S(1)} %collective-permute-done.3.refs_4_) | copy-start | bytes 294916
  27.3 0.7 copy-start.21
  28.0 29.6 %copy-start.6 = (s32[256,1]{0,1:T(1,128)S(1)}, s32[256,1]{0,1:T(1,128)}, u32[]{:S(2)}) copy-start(s32[256,1]{0,1:T(1,128)} %param.23) | copy-start | bytes 3076
  28.0 29.7 %copy-start.24 = (bf16[768]{0:T(1024)(128)(2,1)S(1)}, bf16[768]{0:T(1024)(128)(2,1)}, u32[]{:S(2)}) copy-start(bf16[768]{0:T(1024)(128)(2,1)} %param.33) | copy-start | bytes 4612
  28.0 29.8 %copy-start.25 = (bf16[768]{0:T(1024)(128)(2,1)S(1)}, bf16[768]{0:T(1024)(128)(2,1)}, u32[]{:S(2)}) copy-start(bf16[768]{0:T(1024)(128)(2,1)} %param.34) | copy-start | bytes 4612
  28.0 29.8 %copy-start.26 = (bf16[768]{0:T(1024)(128)(2,1)S(1)}, bf16[768]{0:T(1024)(128)(2,1)}, u32[]{:S(2)}) copy-start(bf16[768]{0:T(1024)(128)(2,1)} %param.35) | copy-start | bytes 4612
  28.0 29.8 %copy-start.27 = (bf16[768]{0:T(1024)(128)(2,1)S(1)}, bf16[768]{0:T(1024)(128)(2,1)}, u32[]{:S(2)}) copy-start(bf16[768]{0:T(1024)(128)(2,1)} %param.39) | copy-start | bytes 4612
  28.0 29.8 %copy-start.28 = (bf16[768]{0:T(1024)(128)(2,1)S(1)}, bf16[768]{0:T(1024)(128)(2,1)}, u32[]{:S(2)}) copy-start(bf16[768]{0:T(1024)(128)(2,1)} %param.40) | copy-start | bytes 4612
  28.0 29.8 %copy-start.29 = (bf16[768]{0:T(1024)(128)(2,1)S(1)}, bf16[768]{0:T(1024)(128)(2,1)}, u32[]{:S(2)}) copy-start(bf16[768]{0:T(1024)(128)(2,1)} %param.41) | copy-start | bytes 4612
  28.0 29.8 %copy-start.23 = (bf16[1024]{0:T(1024)(128)(2,1)S(1)}, bf16[1024]{0:T(1024)(128)(2,1)}, u32[]{:S(2)}) copy-start(bf16[1024]{0:T(1024)(128)(2,1)} %param.43) | copy-start | bytes 6148
  28.1 29.9 %copy-start.22 = (bf16[3072]{0:T(1024)(128)(2,1)S(1)}, bf16[3072]{0:T(1024)(128)(2,1)}, u32[]{:S(2)}) copy-start(bf16[3072]{0:T(1024)(128)(2,1)} %param.37) | copy-start | bytes 18436
  28.1 39.6 %copy-start = (bf16[256,768]{1,0:T(8,128)(2,1)S(1)}, bf16[256,768]{1,0:T(8,128)(2,1)}, u32[]{:S(2)}) copy-start(bf16[256,768]{1,0:T(8,128)(2,1)} %refs_8_.4) | copy-start | bytes 1179652
  28.1 39.6 %copy-start.2 = (bf16[256,1024]{1,0:T(8,128)(2,1)S(1)}, bf16[256,1024]{1,0:T(8,128)(2,1)}, u32[]{:S(2)}) copy-start(bf16[256,1024]{1,0:T(8,128)(2,1)} %refs_11_.1) | copy-start | bytes 1572868
  28.1 39.6 %copy-start.3 = (bf16[256,768]{1,0:T(8,128)(2,1)S(1)}, bf16[256,768]{1,0:T(8,128)(2,1)}, u32[]{:S(2)}) copy-start(bf16[256,768]{1,0:T(8,128)(2,1)} %refs_10_.1) | copy-start | bytes 1179652
  44.2 8.7 %collective-permute-start.7 = (bf16[64,768]{1,0:T(8,128)(2,1)}, bf16[64,768]{1,0:T(8,128)(2,1)S(1)}, u32[]{:S(2)}, u32[]{:S(2)}) collective-permute-start(bf16[64,768]{1,0:T(8,128)(2,1)} %get-tuple-element.126), channel_id=1, source_target_pairs={{0,4},{1,5},{2,6},{3,7},{4,0},{5,1},{6,2},{7,3},{8,12},{9,13},{10,... | collective-permute-start | bytes 294920 | tf_op jit(solution)/shard_map/ppermute | solution.py:800
  45.2 10.0 %collective-permute-start.8 = (bf16[64,768]{1,0:T(8,128)(2,1)}, bf16[64,768]{1,0:T(8,128)(2,1)S(1)}, u32[]{:S(2)}, u32[]{:S(2)}) collective-permute-start(bf16[64,768]{1,0:T(8,128)(2,1)} %get-tuple-element.127), channel_id=1, source_target_pairs={{0,8},{1,9},{2,10},{3,11},{4,12},{5,13},{6,14},{7,15},{8,0},{9,1},... | collective-permute-start | bytes 294920 | tf_op jit(solution)/shard_map/ppermute | solution.py:800
  48.7 9.2 %collective-permute-start.9 = (bf16[64,768]{1,0:T(8,128)(2,1)}, bf16[64,768]{1,0:T(8,128)(2,1)S(1)}, u32[]{:S(2)}, u32[]{:S(2)}) collective-permute-start(bf16[64,768]{1,0:T(8,128)(2,1)} %get-tuple-element.128), channel_id=1, source_target_pairs={{0,12},{1,13},{2,14},{3,15},{4,8},{5,9},{6,10},{7,11},{8,4},{9,5},... | collective-permute-start | bytes 294920 | tf_op jit(solution)/shard_map/ppermute | solution.py:800
  49.6 14.8 %collective-permute-start.10 = (bf16[64,768]{1,0:T(8,128)(2,1)}, bf16[64,768]{1,0:T(8,128)(2,1)S(1)}, u32[]{:S(2)}, u32[]{:S(2)}) collective-permute-start(bf16[64,768]{1,0:T(8,128)(2,1)} %get-tuple-element.129), channel_id=1, source_target_pairs={{0,16},{1,17},{2,18},{3,19},{4,20},{5,21},{6,22},{7,23},{8,24},{9,... | collective-permute-start | bytes 294920 | tf_op jit(solution)/shard_map/ppermute | solution.py:800
  52.9 14.1 %collective-permute-start.11 = (bf16[64,768]{1,0:T(8,128)(2,1)}, bf16[64,768]{1,0:T(8,128)(2,1)S(1)}, u32[]{:S(2)}, u32[]{:S(2)}) collective-permute-start(bf16[64,768]{1,0:T(8,128)(2,1)} %get-tuple-element.130), channel_id=1, source_target_pairs={{0,20},{1,21},{2,22},{3,23},{4,16},{5,17},{6,18},{7,19},{8,28},{9,... | collective-permute-start | bytes 294920 | tf_op jit(solution)/shard_map/ppermute | solution.py:800
  52.9 14.1 %copy-start.8 = (bf16[64,768]{1,0:T(8,128)(2,1)}, bf16[64,768]{1,0:T(8,128)(2,1)S(1)}, u32[]{:S(2)}) copy-start(bf16[64,768]{1,0:T(8,128)(2,1)S(1)} %collective-permute-done.7.refs_1_) | copy-start | bytes 294916
  52.9 14.1 %collective-permute-start.12 = (bf16[64,768]{1,0:T(8,128)(2,1)}, bf16[64,768]{1,0:T(8,128)(2,1)S(1)}, u32[]{:S(2)}, u32[]{:S(2)}) collective-permute-start(bf16[64,768]{1,0:T(8,128)(2,1)} %get-tuple-element.131), channel_id=1, source_target_pairs={{0,24},{1,25},{2,26},{3,27},{4,28},{5,29},{6,30},{7,31},{8,16},{9,... | collective-permute-start | bytes 294920 | tf_op jit(solution)/shard_map/ppermute | solution.py:800
  55.2 11.7 %copy-start.9 = (bf16[64,768]{1,0:T(8,128)(2,1)}, bf16[64,768]{1,0:T(8,128)(2,1)S(1)}, u32[]{:S(2)}) copy-start(bf16[64,768]{1,0:T(8,128)(2,1)S(1)} %collective-permute-done.8.refs_2_) | copy-start | bytes 294916
  55.2 11.7 %collective-permute-start.13 = (bf16[64,768]{1,0:T(8,128)(2,1)}, bf16[64,768]{1,0:T(8,128)(2,1)S(1)}, u32[]{:S(2)}, u32[]{:S(2)}) collective-permute-start(bf16[64,768]{1,0:T(8,128)(2,1)} %get-tuple-element.132), channel_id=1, source_target_pairs={{0,28},{1,29},{2,30},{3,31},{4,24},{5,25},{6,26},{7,27},{8,20},{9,... | collective-permute-start | bytes 294920 | tf_op jit(solution)/shard_map/ppermute | solution.py:800
  57.7 36.5 %copy-start.1 = (s32[256,1]{1,0:T(8,128)}, s32[256,1]{1,0:T(8,128)S(1)}, u32[]{:S(2)}) copy-start(s32[256,1]{1,0:T(8,128)S(1)} %copy.46.refs_9_.refs_1_) | copy-start | bytes 3076
  57.9 9.0 %copy-start.10 = (bf16[64,768]{1,0:T(8,128)(2,1)}, bf16[64,768]{1,0:T(8,128)(2,1)S(1)}, u32[]{:S(2)}) copy-start(bf16[64,768]{1,0:T(8,128)(2,1)S(1)} %collective-permute-done.9.refs_3_) | copy-start | bytes 294916
  64.5 2.5 %copy-start.11 = (bf16[64,768]{1,0:T(8,128)(2,1)}, bf16[64,768]{1,0:T(8,128)(2,1)S(1)}, u32[]{:S(2)}) copy-start(bf16[64,768]{1,0:T(8,128)(2,1)S(1)} %collective-permute-done.10.refs_4_) | copy-start | bytes 294916
  66.9 0.7 copy-start.13
  66.9 0.7 copy-start.14
  94.3 7.7 %collective-permute-start.15 = (bf16[5344,256]{1,0:T(8,128)(2,1)}, bf16[5344,256]{1,0:T(8,128)(2,1)}, u32[]{:S(2)}, u32[]{:S(2)}) collective-permute-start(bf16[5344,256]{1,0:T(8,128)(2,1)} %get-tuple-element.137.refs_0_.refs_2_), channel_id=1, source_target_pairs={{0,1},{1,0},{2,3},{3,2},{4,5},{5,4},{6,7},{7,6},{8,9},{9,8},{10,11... | collective-permute-start | bytes 8208392 | tf_op jit(solution)/shard_map/ppermute | solution.py:800
  94.3 14.8 %collective-permute-start.14 = (bf16[256,3072]{1,0:T(8,128)(2,1)}, bf16[256,3072]{1,0:T(8,128)(2,1)S(1)}, u32[]{:S(2)}, u32[]{:S(2)}) collective-permute-start(bf16[256,3072]{1,0:T(8,128)(2,1)} %get-tuple-element.136.refs_0_), channel_id=1, source_target_pairs={{0,1},{1,0},{2,3},{3,2},{4,5},{5,4},{6,7},{7,6},{8,9},{9,8},{10,11... | collective-permute-start | bytes 4718600 | tf_op jit(solution)/shard_map/ppermute | solution.py:800
  94.8 27.0 %all-to-all-start = ((bf16[8,64,768]{2,1,0:T(8,128)(2,1)}), bf16[8,64,768]{2,1,0:T(8,128)(2,1)S(1)}, u32[]{:S(2)}, u32[]{:S(2)}) async-start(bf16[8,64,768]{2,1,0:T(8,128)(2,1)} %bitcast.13), calls=%async_computation | async-start | bytes 1572864 | tf_op jit(solution)/shard_map/all_to_all | solution.py:887
  107.6 14.3 %copy-start.4 = (s32[1,512]{1,0:T(1,128)S(1)}, s32[1,512]{1,0:T(1,128)}, u32[]{:S(2)}) copy-start(s32[1,512]{1,0:T(1,128)} %refs_5_.1) | copy-start | bytes 6148
  107.6 35.9 %collective-permute-start.16 = (bf16[4800,128]{1,0:T(8,128)(2,1)}, bf16[4800,128]{1,0:T(8,128)(2,1)}, u32[]{:S(2)}, u32[]{:S(2)}) collective-permute-start(bf16[4800,128]{1,0:T(8,128)(2,1)} %get-tuple-element.139), channel_id=1, source_target_pairs={{0,2},{1,3},{2,0},{3,1},{4,6},{5,7},{6,4},{7,5},{8,10},{9,11},{10,... | collective-permute-start | bytes 3686408 | tf_op jit(solution)/shard_map/ppermute | solution.py:800
  109.1 1.2 copy-start.7
  117.1 26.4 %collective-permute-start.18 = (bf16[3840,128]{1,0:T(8,128)(2,1)}, bf16[3840,128]{1,0:T(8,128)(2,1)}, u32[]{:S(2)}, u32[]{:S(2)}) collective-permute-start(bf16[3840,128]{1,0:T(8,128)(2,1)} %get-tuple-element.153), channel_id=1, source_target_pairs={{0,8},{1,9},{2,10},{3,11},{4,12},{5,13},{6,14},{7,15},{8,0},{9,1},... | collective-permute-start | bytes 2949128 | tf_op jit(solution)/shard_map/ppermute | solution.py:800
  120.9 23.6 %collective-permute-start.17 = (bf16[3840,128]{1,0:T(8,128)(2,1)}, bf16[3840,128]{1,0:T(8,128)(2,1)}, u32[]{:S(2)}, u32[]{:S(2)}) collective-permute-start(bf16[3840,128]{1,0:T(8,128)(2,1)} %get-tuple-element.141), channel_id=1, source_target_pairs={{0,4},{1,5},{2,6},{3,7},{4,0},{5,1},{6,2},{7,3},{8,12},{9,13},{10,... | collective-permute-start | bytes 2949128 | tf_op jit(solution)/shard_map/ppermute | solution.py:800
  143.4 11.6 %collective-permute-start.21 = (bf16[7776,128]{1,0:T(8,128)(2,1)}, bf16[7776,128]{1,0:T(8,128)(2,1)S(1)}, u32[]{:S(2)}, u32[]{:S(2)}) collective-permute-start(bf16[7776,128]{1,0:T(8,128)(2,1)} %get-tuple-element.151), channel_id=1, source_target_pairs={{0,1},{1,0},{2,3},{3,2},{4,5},{5,4},{6,7},{7,6},{8,9},{9,8},{10,11... | collective-permute-start | bytes 5971976 | tf_op jit(solution)/shard_map/ppermute | solution.py:800
  149.2 14.2 %collective-permute-start.20 = (bf16[1920,128]{1,0:T(8,128)(2,1)}, bf16[1920,128]{1,0:T(8,128)(2,1)}, u32[]{:S(2)}, u32[]{:S(2)}) collective-permute-start(bf16[1920,128]{1,0:T(8,128)(2,1)} %get-tuple-element.159), channel_id=1, source_target_pairs={{0,2},{1,3},{2,0},{3,1},{4,6},{5,7},{6,4},{7,5},{8,10},{9,11},{10,... | collective-permute-start | bytes 1474568 | tf_op jit(solution)/shard_map/ppermute | solution.py:800
  149.8 16.6 %collective-permute-start.22 = (bf16[1920,128]{1,0:T(8,128)(2,1)}, bf16[1920,128]{1,0:T(8,128)(2,1)}, u32[]{:S(2)}, u32[]{:S(2)}) collective-permute-start(bf16[1920,128]{1,0:T(8,128)(2,1)} %get-tuple-element.166), channel_id=1, source_target_pairs={{0,4},{1,5},{2,6},{3,7},{4,0},{5,1},{6,2},{7,3},{8,12},{9,13},{10,... | collective-permute-start | bytes 1474568 | tf_op jit(solution)/shard_map/ppermute | solution.py:800
  150.8 28.4 %collective-permute-start.19 = (bf16[2496,128]{1,0:T(8,128)(2,1)}, bf16[2496,128]{1,0:T(8,128)(2,1)S(1)}, u32[]{:S(2)}, u32[]{:S(2)}) collective-permute-start(bf16[2496,128]{1,0:T(8,128)(2,1)} %get-tuple-element.156), channel_id=1, source_target_pairs={{0,8},{1,9},{2,10},{3,11},{4,12},{5,13},{6,14},{7,15},{8,0},{9,1},... | collective-permute-start | bytes 1916936 | tf_op jit(solution)/shard_map/ppermute | solution.py:800
  151.1 55.7 %all-to-all-start.1 = ((bf16[8,64,768]{2,1,0:T(8,128)(2,1)}), bf16[8,64,768]{2,1,0:T(8,128)(2,1)S(1)}, u32[]{:S(2)}, u32[]{:S(2)}) async-start(bf16[8,64,768]{2,1,0:T(8,128)(2,1)} %bitcast.12), calls=%async_computation.1 | async-start | bytes 1572864 | tf_op jit(solution)/shard_map/all_to_all | solution.py:887
  159.1 23.7 %collective-permute-start.25 = (bf16[2016,128]{1,0:T(8,128)(2,1)S(1)}, bf16[2016,128]{1,0:T(8,128)(2,1)S(1)}, u32[]{:S(2)}, u32[]{:S(2)}) collective-permute-start(bf16[2016,128]{1,0:T(8,128)(2,1)S(1)} %get-tuple-element.164), channel_id=1, source_target_pairs={{0,2},{1,3},{2,0},{3,1},{4,6},{5,7},{6,4},{7,5},{8,10},{9,11},{10,... | collective-permute-start | bytes 1548296 | tf_op jit(solution)/shard_map/ppermute | solution.py:800
  163.4 19.5 %collective-permute-start.26 = (bf16[1920,128]{1,0:T(8,128)(2,1)S(1)}, bf16[1920,128]{1,0:T(8,128)(2,1)S(1)}, u32[]{:S(2)}, u32[]{:S(2)}) collective-permute-start(bf16[1920,128]{1,0:T(8,128)(2,1)S(1)} %get-tuple-element.177), channel_id=1, source_target_pairs={{0,4},{1,5},{2,6},{3,7},{4,0},{5,1},{6,2},{7,3},{8,12},{9,13},{10,... | collective-permute-start | bytes 1474568 | tf_op jit(solution)/shard_map/ppermute | solution.py:800
  168.9 18.4 %collective-permute-start.24 = (bf16[960,128]{1,0:T(8,128)(2,1)S(1)}, bf16[960,128]{1,0:T(8,128)(2,1)S(1)}, u32[]{:S(2)}, u32[]{:S(2)}) collective-permute-start(bf16[960,128]{1,0:T(8,128)(2,1)S(1)} %get-tuple-element.167), channel_id=1, source_target_pairs={{0,16},{1,17},{2,18},{3,19},{4,20},{5,21},{6,22},{7,23},{8,24},{9,... | collective-permute-start | bytes 737288 | tf_op jit(solution)/shard_map/ppermute | solution.py:800
  170.4 18.1 %collective-permute-start.27 = (bf16[960,128]{1,0:T(8,128)(2,1)S(1)}, bf16[960,128]{1,0:T(8,128)(2,1)S(1)}, u32[]{:S(2)}, u32[]{:S(2)}) collective-permute-start(bf16[960,128]{1,0:T(8,128)(2,1)S(1)} %get-tuple-element.181), channel_id=1, source_target_pairs={{0,2},{1,3},{2,0},{3,1},{4,6},{5,7},{6,4},{7,5},{8,10},{9,11},{10,... | collective-permute-start | bytes 737288 | tf_op jit(solution)/shard_map/ppermute | solution.py:800
  181.0 11.0 %collective-permute-start.23 = (bf16[1344,128]{1,0:T(8,128)(2,1)S(1)}, bf16[1344,128]{1,0:T(8,128)(2,1)S(1)}, u32[]{:S(2)}, u32[]{:S(2)}) collective-permute-start(bf16[1344,128]{1,0:T(8,128)(2,1)S(1)} %get-tuple-element.171), channel_id=1, source_target_pairs={{0,4},{1,5},{2,6},{3,7},{4,0},{5,1},{6,2},{7,3},{8,12},{9,13},{10,... | collective-permute-start | bytes 1032200 | tf_op jit(solution)/shard_map/ppermute | solution.py:800
  183.6 11.3 %collective-permute-start.28 = (bf16[1056,128]{1,0:T(8,128)(2,1)S(1)}, bf16[1056,128]{1,0:T(8,128)(2,1)S(1)}, u32[]{:S(2)}, u32[]{:S(2)}) collective-permute-start(bf16[1056,128]{1,0:T(8,128)(2,1)S(1)} %get-tuple-element.179), channel_id=1, source_target_pairs={{0,4},{1,5},{2,6},{3,7},{4,0},{5,1},{6,2},{7,3},{8,12},{9,13},{10,... | collective-permute-start | bytes 811016 | tf_op jit(solution)/shard_map/ppermute | solution.py:800
  187.3 7.6 %collective-permute-start.29 = (bf16[960,128]{1,0:T(8,128)(2,1)S(1)}, bf16[960,128]{1,0:T(8,128)(2,1)S(1)}, u32[]{:S(2)}, u32[]{:S(2)}) collective-permute-start(bf16[960,128]{1,0:T(8,128)(2,1)S(1)} %get-tuple-element.191), channel_id=1, source_target_pairs={{0,2},{1,3},{2,0},{3,1},{4,6},{5,7},{6,4},{7,5},{8,10},{9,11},{10,... | collective-permute-start | bytes 737288 | tf_op jit(solution)/shard_map/ppermute | solution.py:800
  189.1 7.4 %collective-permute-start.32 = (bf16[480,128]{1,0:T(8,128)(2,1)S(1)}, bf16[480,128]{1,0:T(8,128)(2,1)S(1)}, u32[]{:S(2)}, u32[]{:S(2)}) collective-permute-start(bf16[480,128]{1,0:T(8,128)(2,1)S(1)} %get-tuple-element.182), channel_id=1, source_target_pairs={{0,8},{1,9},{2,10},{3,11},{4,12},{5,13},{6,14},{7,15},{8,0},{9,1},... | collective-permute-start | bytes 368648 | tf_op jit(solution)/shard_map/ppermute | solution.py:800
  189.2 12.6 %collective-permute-start.33 = (bf16[480,128]{1,0:T(8,128)(2,1)S(1)}, bf16[480,128]{1,0:T(8,128)(2,1)S(1)}, u32[]{:S(2)}, u32[]{:S(2)}) collective-permute-start(bf16[480,128]{1,0:T(8,128)(2,1)S(1)} %get-tuple-element.199), channel_id=1, source_target_pairs={{0,16},{1,17},{2,18},{3,19},{4,20},{5,21},{6,22},{7,23},{8,24},{9,... | collective-permute-start | bytes 368648 | tf_op jit(solution)/shard_map/ppermute | solution.py:800
  192.6 11.7 %collective-permute-start.31 = (bf16[768,128]{1,0:T(8,128)(2,1)S(1)}, bf16[768,128]{1,0:T(8,128)(2,1)S(1)}, u32[]{:S(2)}, u32[]{:S(2)}) collective-permute-start(bf16[768,128]{1,0:T(8,128)(2,1)S(1)} %get-tuple-element.185), channel_id=1, source_target_pairs={{0,16},{1,17},{2,18},{3,19},{4,20},{5,21},{6,22},{7,23},{8,24},{9,... | collective-permute-start | bytes 589832 | tf_op jit(solution)/shard_map/ppermute | solution.py:800
  195.6 10.2 %collective-permute-start.30 = (bf16[1056,128]{1,0:T(8,128)(2,1)S(1)}, bf16[1056,128]{1,0:T(8,128)(2,1)S(1)}, u32[]{:S(2)}, u32[]{:S(2)}) collective-permute-start(bf16[1056,128]{1,0:T(8,128)(2,1)S(1)} %get-tuple-element.194), channel_id=1, source_target_pairs={{0,8},{1,9},{2,10},{3,11},{4,12},{5,13},{6,14},{7,15},{8,0},{9,1},... | collective-permute-start | bytes 811016 | tf_op jit(solution)/shard_map/ppermute | solution.py:800
  206.3 7.3 %collective-permute-start.34 = (bf16[576,128]{1,0:T(8,128)(2,1)S(1)}, bf16[576,128]{1,0:T(8,128)(2,1)S(1)}, u32[]{:S(2)}, u32[]{:S(2)}) collective-permute-start(bf16[576,128]{1,0:T(8,128)(2,1)S(1)} %get-tuple-element.207), channel_id=1, source_target_pairs={{0,16},{1,17},{2,18},{3,19},{4,20},{5,21},{6,22},{7,23},{8,24},{9,... | collective-permute-start | bytes 442376 | tf_op jit(solution)/shard_map/ppermute | solution.py:800
  (3 other events, 1.9 us)

commit v5 on v4

--- a/solution.py
+++ b/solution.py
@@ -269,9 +269,11 @@
     weights.wait()
     acc[...] = dot_nt(g_joined[...], w_qkv[...])
     ones = jnp.ones((8, slots), BF16)
-    small[2:3, :] = dot(ones, g_joined[:, 0:width])[0:1]
-    small[3:4, :] = dot(ones, g_joined[:, 2 * width :])[0:1]
-    small[4:8, :] = jnp.zeros_like(small[4:8, :])
+    half = width // 2
+    for k, part in ((2, 0), (3, 2)):
+        made = dot(ones, g_joined[:, part * width : (part + 1) * width])[0:1]
+        small[k : k + 1, :] = made[:, :half]
+        small[4 + k : 5 + k, :] = made[:, half:]
     sums[...] = jnp.zeros_like(sums)
     gain_f = gain[...].astype(F32)
 
@@ -285,8 +287,10 @@
         g_rows[r, :] = norm_back(g_out, gain_f, hat, rstd).astype(BF16)
 
     row_loop(slots, 32, back_rows)
-    small[0:1, :] = jnp.sum(sums[0], axis=0, keepdims=True)
-    small[1:2, :] = jnp.sum(sums[1], axis=0, keepdims=True)
+    for k in range(2):
+        made = jnp.sum(sums[k], axis=0, keepdims=True)
+        small[k : k + 1, :] = made[:, :half]
+        small[4 + k : 5 + k, :] = made[:, half:]
     if shared:
         set_blocks(refs[8], turned, 0, ids, 2, 8, JOINED_SPLIT)
         joined_products(sender(send, joined_place, JOINED_BASE, JOINED_PARTS), 1, ids, turned, g_joined)
@@ -555,11 +559,11 @@
 
 
 def write_small(small, out, base):
-    count = small.shape[0]
-    for c in range(6):
+    count, slabs = small.shape[0], small.shape[1] // 128
+    for c in range(slabs):
         high, rest = split_small(small[:, c * 128 : (c + 1) * 128])
         out[base + c * count : base + (c + 1) * count, :] = high
-        out[base + (6 + c) * count : base + (7 + c) * count, :] = rest
+        out[base + (slabs + c) * count : base + (slabs + 1 + c) * count, :] = rest
 
 
 def both_small(small, came):
@@ -570,7 +574,7 @@
 
 
 def rows_of_small(small):
-    return jnp.concatenate([small[:, c * 128 : (c + 1) * 128] for c in range(6)], axis=0)
+    return jnp.concatenate([small[:, c * 128 : (c + 1) * 128] for c in range(small.shape[1] // 128)], axis=0)
 
 
 def own_columns(ids, core, x, step):
@@ -756,7 +760,7 @@
 
 def small_columns(small, out):
     count = out.shape[0]
-    for c in range(6):
+    for c in range(out.shape[1] // 128):
         out[:, c * 128 : (c + 1) * 128] = small[c * count : (c + 1) * count]
 
 
@@ -943,7 +947,7 @@
     extra = 12 * 16
     parts = lambda n: [flat(n * JOINED_PARTS[0]), flat(n * JOINED_PARTS[0] + more), flat(n * JOINED_PARTS[1]), flat(n * JOINED_PARTS[1])]
     both = sum(JOINED_PARTS)
-    more = 12 * 8
+    more = 6 * 8
     chain = lambda n: [flat(n * EARLY_PARTS[0] + extra)] + [flat(n * r) for r in EARLY_PARTS[1:]]
     held = lambda n: [flat(n * r) for r in EARLY_PARTS]
     small_early = shape((96, 128), F32)
@@ -991,7 +995,7 @@
         cames = go(sends, 0)
         g_arrived = tie(g_arrived, s1)
 
-    outs = [in_slots, shape((slots, 3 * width), BF16), shape((8, width), F32)]
+    outs = [in_slots, shape((slots, 3 * width), BF16), shape((8, width // 2), F32)]
     turned = shape((width, slots), BF16)
     made = call(
         functools.partial(attention_back_kernel, fast), "attention_back", 28,
@@ -1008,7 +1012,7 @@
     if fast:
         send, turned_c = made[3:]
         came = move(send, "grp", 1)
-        small_shape = shape((48, 128), F32)
+        small_shape = shape((24, 128), F32)
 
         def early_step(name, which, n, keeps, cames, small_e, before, cost, **more_of):
             count = len(which)
@@ -1062,7 +1066,7 @@
         )
         c3 = move(s3, "batch", 4)
         sum_qkv, small_j = call(
-            joined_end, "joined_end", 10, [shape((96, 576), F32), shape((8, width), F32)], [],
+            joined_end, "joined_end", 10, [shape((96, 576), F32), shape((8, width // 2), F32)], [],
             ids, k3, c3, small_j,
         )
         small_0, small_2 = small_e, small_j
@@ -1082,9 +1086,10 @@
     )
     sum_align_bias = small_0[3:5].reshape(2 * width)[:align]
     sum_up_bias = small_0[11:15].reshape(4 * width)[:wide]
+    late = [jnp.concatenate([small_2[k], small_2[4 + k]]) for k in range(4)]
     return (
         y, al, grad_tokens,
-        small_2[0], small_2[1], sum_qkv, small_2[2], small_2[3],
+        late[0], late[1], sum_qkv, late[2], late[3],
         sum_out, small_0[10], small_0[8], small_0[9],
         sum_up, sum_up_bias, sum_down, small_0[2],
         small_0[0], small_0[1], sum_align, sum_align_bias,

time: 216 us -> 216 us (level)
  transfers between devices with their start and end apart: 37 -> 37, of which waited for: 15 -> 14; matrix products, arithmetic and copies ran while one was open for 3% -> 3% of each run, Pallas kernels for 26% -> 26%
where the time goes in v5:
time: 216 us; the launch traced here: 215 us
  Pallas kernels  103 us (48%)
  starting transfers between devices  58.1 us (27%)
  waiting for transfers between devices  41.1 us (19%)
  local copies, waits for them, and re-layouts  10.5 us (5%)
    pallas_call x19, Pallas kernels, call(): pl.pallas_call(body, name=name, out_shape=outs, in_specs=[SMEM] + [HBM if...  103 us
    ppermute x35, starting transfers between devices, flip(): return lax.ppermute(value, AXES, pairs)  48.5 us
    ppermute x35, waiting for transfers between devices, flip(): return lax.ppermute(value, AXES, pairs)  41.1 us
    all_to_all x2, starting transfers between devices, exchange(): lax.all_to_all(shaped, 'batch', split_axis=0, concat_axis=0, tiled=True)  9.63 us
  transfers between devices with their start and end apart: 37, of which 14 were waited for; matrix products, arithmetic and copies ran while one was open for 3% of the time, Pallas kernels for 26%

profile of v5, /device:TPU:0, one launch (start us, length us, event | category | flops | bytes accessed | tf_op | source)
XLA Modules:
  0.0 215.4 jit_solution(12969126888839519165)
XLA Ops:
  0.8 0.7 copy-done.5
  1.4 2.8 %pack_tokens.1 = (bf16[64,768]{1,0:T(8,128)(2,1)}, bf16[64,768]{1,0:T(8,128)(2,1)}, bf16[64,768]{1,0:T(8,128)(2,1)}, bf16[64,768]{1,0:T(8,128)(2,1)}, bf16[64,76...) custom-call(s32[14]{0:T(128)S(1)} %pad_add_fusion.ids, ...), custom_call_target="tpu_custom_call" | custom-call | flops 1000000 | bytes 1 | tf_op jit(solution)/shard_map/pack_tokens/pallas_call | solution.py:876
  4.3 3.0 %collective-permute-start = (bf16[64,768]{1,0:T(8,128)(2,1)}, bf16[64,768]{1,0:T(8,128)(2,1)S(1)}, u32[]{:S(2)}, u32[]{:S(2)}) collective-permute-start(bf16[64,768]{1,0:T(8,128)(2,1)} %get-tuple-element.118), channel_id=1, source_target_pairs={{0,4},{1,5},{2,6},{3,7},{4,0},{5,1},{6,2},{7,3},{8,12},{9,13},{10,... | collective-permute-start | bytes 294920 | tf_op jit(solution)/shard_map/ppermute | solution.py:804
  7.3 1.6 collective-permute-start.1
  8.9 3.0 %collective-permute-start.3 = (bf16[64,768]{1,0:T(8,128)(2,1)}, bf16[64,768]{1,0:T(8,128)(2,1)S(1)}, u32[]{:S(2)}, u32[]{:S(2)}) collective-permute-start(bf16[64,768]{1,0:T(8,128)(2,1)} %get-tuple-element.121), channel_id=1, source_target_pairs={{0,16},{1,17},{2,18},{3,19},{4,20},{5,21},{6,22},{7,23},{8,24},{9,... | collective-permute-start | bytes 294920 | tf_op jit(solution)/shard_map/ppermute | solution.py:804
  11.9 1.3 collective-permute-start.4
  13.2 3.6 %collective-permute-start.5 = (bf16[64,768]{1,0:T(8,128)(2,1)}, bf16[64,768]{1,0:T(8,128)(2,1)S(1)}, u32[]{:S(2)}, u32[]{:S(2)}) collective-permute-start(bf16[64,768]{1,0:T(8,128)(2,1)} %get-tuple-element.123), channel_id=1, source_target_pairs={{0,24},{1,25},{2,26},{3,27},{4,28},{5,29},{6,30},{7,31},{8,16},{9,... | collective-permute-start | bytes 294920 | tf_op jit(solution)/shard_map/ppermute | solution.py:804
  16.8 0.7 reshape.103.refs_10_.refs_7_
  17.5 0.7 reshape.104.refs_11_
  18.2 0.7 reshape.105.refs_13_
  18.9 0.7 reshape.106.refs_14_
  19.6 1.5 copy.45.refs_9_.refs_6_
  21.1 6.1 %collective-permute-done.4.refs_5_ = bf16[64,768]{1,0:T(8,128)(2,1)S(1)} collective-permute-done((bf16[64,768]{1,0:T(8,128)(2,1)}, bf16[64,768]{1,0:T(8,128)(2,1)S(1)}, u32[]{:S(2)}, u32[]{:S(2)}) %collective-permute-start.4) | collective-permute-done | bytes 98336 | tf_op jit(solution)/shard_map/ppermute | solution.py:804
  28.1 16.1 %attention.1 = (bf16[64,768]{1,0:T(8,128)(2,1)}, bf16[64,768]{1,0:T(8,128)(2,1)}, bf16[64,768]{1,0:T(8,128)(2,1)}, bf16[64,768]{1,0:T(8,128)(2,1)}, bf16[64,768]...) custom-call(s32[14]{0:T(128)S(1)} %pad_add_fusion.ids, ...), custom_call_target="tpu_custom_call" | custom-call | flops 1000000 | bytes 1 | tf_op jit(solution)/shard_map/attention/pallas_call | solution.py:876
  44.2 1.0 collective-permute-start.7
  45.2 3.5 %collective-permute-start.8 = (bf16[64,768]{1,0:T(8,128)(2,1)}, bf16[64,768]{1,0:T(8,128)(2,1)S(1)}, u32[]{:S(2)}, u32[]{:S(2)}) collective-permute-start(bf16[64,768]{1,0:T(8,128)(2,1)} %get-tuple-element.127), channel_id=1, source_target_pairs={{0,8},{1,9},{2,10},{3,11},{4,12},{5,13},{6,14},{7,15},{8,0},{9,1},... | collective-permute-start | bytes 294920 | tf_op jit(solution)/shard_map/ppermute | solution.py:804
  48.8 0.9 collective-permute-start.9
  49.7 3.2 %collective-permute-start.10 = (bf16[64,768]{1,0:T(8,128)(2,1)}, bf16[64,768]{1,0:T(8,128)(2,1)S(1)}, u32[]{:S(2)}, u32[]{:S(2)}) collective-permute-start(bf16[64,768]{1,0:T(8,128)(2,1)} %get-tuple-element.129), channel_id=1, source_target_pairs={{0,16},{1,17},{2,18},{3,19},{4,20},{5,21},{6,22},{7,23},{8,24},{9,... | collective-permute-start | bytes 294920 | tf_op jit(solution)/shard_map/ppermute | solution.py:804
  52.9 2.4 %collective-permute-start.12 = (bf16[64,768]{1,0:T(8,128)(2,1)}, bf16[64,768]{1,0:T(8,128)(2,1)S(1)}, u32[]{:S(2)}, u32[]{:S(2)}) collective-permute-start(bf16[64,768]{1,0:T(8,128)(2,1)} %get-tuple-element.131), channel_id=1, source_target_pairs={{0,24},{1,25},{2,26},{3,27},{4,28},{5,29},{6,30},{7,31},{8,16},{9,... | collective-permute-start | bytes 294920 | tf_op jit(solution)/shard_map/ppermute | solution.py:804
  55.3 2.4 %collective-permute-start.13 = (bf16[64,768]{1,0:T(8,128)(2,1)}, bf16[64,768]{1,0:T(8,128)(2,1)S(1)}, u32[]{:S(2)}, u32[]{:S(2)}) collective-permute-start(bf16[64,768]{1,0:T(8,128)(2,1)} %get-tuple-element.132), channel_id=1, source_target_pairs={{0,28},{1,29},{2,30},{3,31},{4,24},{5,25},{6,26},{7,27},{8,20},{9,... | collective-permute-start | bytes 294920 | tf_op jit(solution)/shard_map/ppermute | solution.py:804
  58.0 6.5 %collective-permute-done.10.refs_4_ = bf16[64,768]{1,0:T(8,128)(2,1)S(1)} collective-permute-done((bf16[64,768]{1,0:T(8,128)(2,1)}, bf16[64,768]{1,0:T(8,128)(2,1)S(1)}, u32[]{:S(2)}, u32[]{:S(2)}) %collective-permute-start.10) | collective-permute-done | bytes 98336 | tf_op jit(solution)/shard_map/ppermute | solution.py:804
  64.5 2.5 %collective-permute-done.11.refs_5_ = bf16[64,768]{1,0:T(8,128)(2,1)S(1)} collective-permute-done((bf16[64,768]{1,0:T(8,128)(2,1)}, bf16[64,768]{1,0:T(8,128)(2,1)S(1)}, u32[]{:S(2)}, u32[]{:S(2)}) %collective-permute-start.11) | collective-permute-done | bytes 98336 | tf_op jit(solution)/shard_map/ppermute | solution.py:804
  67.7 26.6 %rows.1 = (bf16[256,768]{1,0:T(8,128)(2,1)}, bf16[256,1024]{1,0:T(8,128)(2,1)}, bf16[512,768]{1,0:T(8,128)(2,1)}, f32[256,768]{1,0:T(8,128)}, bf16[256,3072]{1,0...) custom-call(s32[14]{0:T(128)S(1)} %pad_add_fusion.ids, ...), custom_call_target="tpu_custom_call" | custom-call | flops 1000000 | bytes 1 | tf_op jit(solution)/shard_map/rows/pallas_call | solution.py:876
  94.9 5.8 %all-to-all-start = ((bf16[8,64,768]{2,1,0:T(8,128)(2,1)}), bf16[8,64,768]{2,1,0:T(8,128)(2,1)S(1)}, u32[]{:S(2)}, u32[]{:S(2)}) async-start(bf16[8,64,768]{2,1,0:T(8,128)(2,1)} %bitcast.13), calls=%async_computation | async-start | bytes 1572864 | tf_op jit(solution)/shard_map/all_to_all | solution.py:891
  100.7 1.4 collective-permute-done.15.refs_2_.refs_4_
  102.0 5.6 %second_grads.1 = (bf16[4608,128]{1,0:T(8,128)(2,1)}, bf16[4800,128]{1,0:T(8,128)(2,1)}, f32[96,128]{1,0:T(8,128)}) custom-call(s32[14]{0:T(128)S(1)} %pad_add_fusion.ids, bf16[5344,256]{1,0:T(8,128)(2,1)} %get-tuple-element.137.refs_0_.refs_2_, bf16[2944,256]{1,0:T(8,128)(2,1)} %get-tuple-element.138.refs_1_.refs_3_, ...), custom_call_target="tpu_custom_call" | custom-call | flops 1000000 | bytes 1 | tf_op jit(solution)/shard_map/second_grads/pallas_call | solution.py:876
  107.6 1.5 collective-permute-start.16
  109.1 1.2 copy-done.7
  110.3 6.8 %first_grads.1 = (bf16[3840,128]{1,0:T(8,128)(2,1)}, bf16[3840,128]{1,0:T(8,128)(2,1)}, bf16[3840,128]{1,0:T(8,128)(2,1)}, bf16[3840,128]{1,0:T(8,128)(2,1)}) custom-call(s32[14]{0:T(128)S(1)} %pad_add_fusion.ids, bf16[256,3072]{1,0:T(8,128)(2,1)} %get-tuple-element.136.refs_0_, bf16[256,3072]{1,0:T(8,128)(2,1)} %copy-done.7, ...), custom_call_target="tpu_custom_call" | custom-call | flops 1000000 | bytes 1 | tf_op jit(solution)/shard_map/first_grads/pallas_call | solution.py:876
  117.1 3.8 %collective-permute-start.18 = (bf16[3840,128]{1,0:T(8,128)(2,1)}, bf16[3840,128]{1,0:T(8,128)(2,1)}, u32[]{:S(2)}, u32[]{:S(2)}) collective-permute-start(bf16[3840,128]{1,0:T(8,128)(2,1)} %get-tuple-element.153), channel_id=1, source_target_pairs={{0,8},{1,9},{2,10},{3,11},{4,12},{5,13},{6,14},{7,15},{8,0},{9,1},... | collective-permute-start | bytes 2949128 | tf_op jit(solution)/shard_map/ppermute | solution.py:804
  120.9 1.0 collective-permute-start.17
  121.9 21.5 %attention_back.1 = (bf16[512,768]{1,0:T(8,128)(2,1)}, bf16[512,2304]{1,0:T(8,128)(2,1)}, f32[8,384]{1,0:T(8,128)S(1)}, bf16[7728,128]{1,0:T(8,128)(2,1)}, bf16[768,512]{1,0:T(8,128)(2,1)}) custom-call(s32[14]{0:T(128)S(1)} %pad_add_fusion.ids, bf16[512,768]{1,0:T(8,128)(2,1)S(1)} %bitcast.8, bf16[512,768]{1,0:T(8,128)(2,1)} %get-tuple-element.143.refs_1_, ...), custom_call_target="tpu_custom_call" | custom-call | flops 1000000 | bytes 1 | tf_op jit(solution)/shard_map/attention_back/pallas_call | solution.py:876
  143.5 1.0 collective-permute-done.17.refs_4_
  144.5 4.8 %early_step_1.1 = (bf16[2304,128]{1,0:T(8,128)(2,1)}, bf16[1920,128]{1,0:T(8,128)(2,1)}, bf16[1920,128]{1,0:T(8,128)(2,1)}, bf16[2496,128]{1,0:T(8,128)(2,1)}, b...) custom-call(s32[14]{0:T(128)S(1)} %pad_add_fusion.ids, ...), custom_call_target="tpu_custom_call" | custom-call | flops 15000000512 | bytes 1 | tf_op jit(solution)/shard_map/early_step_1/pallas_call | solution.py:876
  149.9 1.0 collective-permute-start.22
  151.2 3.8 %all-to-all-start.1 = ((bf16[8,64,768]{2,1,0:T(8,128)(2,1)}), bf16[8,64,768]{2,1,0:T(8,128)(2,1)S(1)}, u32[]{:S(2)}, u32[]{:S(2)}) async-start(bf16[8,64,768]{2,1,0:T(8,128)(2,1)} %bitcast.12), calls=%async_computation.1 | async-start | bytes 1572864 | tf_op jit(solution)/shard_map/all_to_all | solution.py:891
  155.0 4.1 %joined_keep.1 = (bf16[1920,128]{1,0:T(8,128)(2,1)S(1)}, bf16[1968,128]{1,0:T(8,128)(2,1)S(1)}, bf16[1920,128]{1,0:T(8,128)(2,1)S(1)}, bf16[1920,128]{1,0:T(8,128)(2,1)S(1)}, f32[24,128]{1,0:T(8,128)S(1)}) custom-call(s32[14]{0:T(128)S(1)} %pad_add_fusion.ids, bf16[768,512]{1,0:T(8,128)(2,1)} %get-tuple-element.160.refs_0_, ...), custom_call_target="tpu_custom_call" | custom-call | flops 1000000 | bytes 1 | tf_op jit(solution)/shard_map/joined_keep/pallas_call | solution.py:876
  159.1 1.6 collective-permute-start.25
  160.7 2.7 %collective-permute-done.20.refs_2_ = bf16[1920,128]{1,0:T(8,128)(2,1)} collective-permute-done((bf16[1920,128]{1,0:T(8,128)(2,1)}, bf16[1920,128]{1,0:T(8,128)(2,1)}, u32[]{:S(2)}, u32[]{:S(2)}) %collective-permute-start.20) | collective-permute-done | bytes 491552 | tf_op jit(solution)/shard_map/ppermute | solution.py:804
  163.4 0.7 collective-permute-start.26
  164.1 2.3 %collective-permute-done.22.refs_3_ = bf16[1920,128]{1,0:T(8,128)(2,1)} collective-permute-done((bf16[1920,128]{1,0:T(8,128)(2,1)}, bf16[1920,128]{1,0:T(8,128)(2,1)}, u32[]{:S(2)}, u32[]{:S(2)}) %collective-permute-start.22) | collective-permute-done | bytes 491552 | tf_op jit(solution)/shard_map/ppermute | solution.py:804
  166.5 2.5 %early_step_2a.1 = (bf16[960,128]{1,0:T(8,128)(2,1)S(1)}, bf16[960,128]{1,0:T(8,128)(2,1)S(1)}, bf16[960,128]{1,0:T(8,128)(2,1)S(1)}, bf16[960,128]{1,0:T(8,128)(2,1)S(1)}) custom-call(s32[14]{0:T(128)S(1)} %pad_add_fusion.ids, bf16[1920,128]{1,0:T(8,128)(2,1)} %get-tuple-element.157.refs_0_, bf16[1920,128]{1,0:T(8,128)(2,1)} %get-tuple-element.158.refs_1_, ...), custom_call_target="tpu_custom_call" | custom-call | flops 3000000000 | bytes 1 | tf_op jit(solution)/shard_map/early_step_2a/pallas_call | solution.py:876
  169.0 1.6 collective-permute-start.24
  170.5 1.8 collective-permute-start.27
  172.3 7.0 %collective-permute-done.19.refs_1_ = bf16[2496,128]{1,0:T(8,128)(2,1)S(1)} collective-permute-done((bf16[2496,128]{1,0:T(8,128)(2,1)}, bf16[2496,128]{1,0:T(8,128)(2,1)S(1)}, u32[]{:S(2)}, u32[]{:S(2)}) %collective-permute-start.19) | collective-permute-done | bytes 639008 | tf_op jit(solution)/shard_map/ppermute | solution.py:804
  179.3 1.8 early_step_2b.1
  181.1 1.8 collective-permute-start.23
  182.9 0.8 joined_apart.1
  183.7 1.2 collective-permute-start.28
  184.9 2.3 %collective-permute-done.24.refs_2_ = bf16[960,128]{1,0:T(8,128)(2,1)S(1)} collective-permute-done((bf16[960,128]{1,0:T(8,128)(2,1)S(1)}, bf16[960,128]{1,0:T(8,128)(2,1)S(1)}, u32[]{:S(2)}, u32[]{:S(2)}) %collective-permute-start.24) | collective-permute-done | bytes 245792 | tf_op jit(solution)/shard_map/ppermute | solution.py:804
  187.3 1.0 collective-permute-start.29
  188.3 0.7 early_step_3a.1
  189.1 2.2 %collective-permute-start.33 = (bf16[480,128]{1,0:T(8,128)(2,1)S(1)}, bf16[480,128]{1,0:T(8,128)(2,1)S(1)}, u32[]{:S(2)}, u32[]{:S(2)}) collective-permute-start(bf16[480,128]{1,0:T(8,128)(2,1)S(1)} %get-tuple-element.199), channel_id=1, source_target_pairs={{0,16},{1,17},{2,18},{3,19},{4,20},{5,21},{6,22},{7,23},{8,24},{9,... | collective-permute-start | bytes 368648 | tf_op jit(solution)/shard_map/ppermute | solution.py:804
  192.8 1.8 collective-permute-done.28.refs_1_
  194.6 0.7 joined_meet.1
  195.3 1.1 collective-permute-start.30
  196.3 5.0 %collective-permute-done.33.refs_3_ = bf16[480,128]{1,0:T(8,128)(2,1)S(1)} collective-permute-done((bf16[480,128]{1,0:T(8,128)(2,1)S(1)}, bf16[480,128]{1,0:T(8,128)(2,1)S(1)}, u32[]{:S(2)}, u32[]{:S(2)}) %collective-permute-start.33) | collective-permute-done | bytes 122912 | tf_op jit(solution)/shard_map/ppermute | solution.py:804
  201.3 1.3 early_end_a.1
  202.6 1.5 collective-permute-done.31.refs_1_
  204.2 1.3 early_end_b.1
  206.3 3.3 %grad_tokens.1 = bf16[256,768]{1,0:T(8,128)(2,1)} custom-call(s32[14]{0:T(128)S(1)} %pad_add_fusion.ids, bf16[512,768]{1,0:T(8,128)(2,1)S(1)} %bitcast.9, s32[256,1]{1,0:T(8,128)} %copy-done.1, f32[256,768]{1,0:T(8,128)} %get-tuple-element.187.refs_2_), custom_call_target="tpu_custom_call" | custom-call | flops 1000000 | bytes 1 | tf_op jit(solution)/shard_map/grad_tokens/pallas_call | solution.py:876
  209.7 0.9 copy.49
  211.8 0.6 slice_reduce_fusion
  212.9 1.3 joined_end.1
  (116 shorter events, 8.8 us)
Async XLA Ops:
  0.8 0.7 copy-start.5
  4.3 8.9 %collective-permute-start = (bf16[64,768]{1,0:T(8,128)(2,1)}, bf16[64,768]{1,0:T(8,128)(2,1)S(1)}, u32[]{:S(2)}, u32[]{:S(2)}) collective-permute-start(bf16[64,768]{1,0:T(8,128)(2,1)} %get-tuple-element.118), channel_id=1, source_target_pairs={{0,4},{1,5},{2,6},{3,7},{4,0},{5,1},{6,2},{7,3},{8,12},{9,13},{10,... | collective-permute-start | bytes 294920 | tf_op jit(solution)/shard_map/ppermute | solution.py:804
  7.3 9.5 %collective-permute-start.1 = (bf16[64,768]{1,0:T(8,128)(2,1)}, bf16[64,768]{1,0:T(8,128)(2,1)S(1)}, u32[]{:S(2)}, u32[]{:S(2)}) collective-permute-start(bf16[64,768]{1,0:T(8,128)(2,1)} %get-tuple-element.119), channel_id=1, source_target_pairs={{0,8},{1,9},{2,10},{3,11},{4,12},{5,13},{6,14},{7,15},{8,0},{9,1},... | collective-permute-start | bytes 294920 | tf_op jit(solution)/shard_map/ppermute | solution.py:804
  8.9 12.2 %collective-permute-start.2 = (bf16[64,768]{1,0:T(8,128)(2,1)}, bf16[64,768]{1,0:T(8,128)(2,1)S(1)}, u32[]{:S(2)}, u32[]{:S(2)}) collective-permute-start(bf16[64,768]{1,0:T(8,128)(2,1)} %get-tuple-element.120), channel_id=1, source_target_pairs={{0,12},{1,13},{2,14},{3,15},{4,8},{5,9},{6,10},{7,11},{8,4},{9,5},... | collective-permute-start | bytes 294920 | tf_op jit(solution)/shard_map/ppermute | solution.py:804
  8.9 12.2 %collective-permute-start.3 = (bf16[64,768]{1,0:T(8,128)(2,1)}, bf16[64,768]{1,0:T(8,128)(2,1)S(1)}, u32[]{:S(2)}, u32[]{:S(2)}) collective-permute-start(bf16[64,768]{1,0:T(8,128)(2,1)} %get-tuple-element.121), channel_id=1, source_target_pairs={{0,16},{1,17},{2,18},{3,19},{4,20},{5,21},{6,22},{7,23},{8,24},{9,... | collective-permute-start | bytes 294920 | tf_op jit(solution)/shard_map/ppermute | solution.py:804
  11.9 15.4 %collective-permute-start.4 = (bf16[64,768]{1,0:T(8,128)(2,1)}, bf16[64,768]{1,0:T(8,128)(2,1)S(1)}, u32[]{:S(2)}, u32[]{:S(2)}) collective-permute-start(bf16[64,768]{1,0:T(8,128)(2,1)} %get-tuple-element.122), channel_id=1, source_target_pairs={{0,20},{1,21},{2,22},{3,23},{4,16},{5,17},{6,18},{7,19},{8,28},{9,... | collective-permute-start | bytes 294920 | tf_op jit(solution)/shard_map/ppermute | solution.py:804
  13.2 14.1 %copy-start.15 = (bf16[64,768]{1,0:T(8,128)(2,1)}, bf16[64,768]{1,0:T(8,128)(2,1)S(1)}, u32[]{:S(2)}) copy-start(bf16[64,768]{1,0:T(8,128)(2,1)S(1)} %collective-permute-done.refs_1_) | copy-start | bytes 294916
  13.2 14.1 %collective-permute-start.5 = (bf16[64,768]{1,0:T(8,128)(2,1)}, bf16[64,768]{1,0:T(8,128)(2,1)S(1)}, u32[]{:S(2)}, u32[]{:S(2)}) collective-permute-start(bf16[64,768]{1,0:T(8,128)(2,1)} %get-tuple-element.123), channel_id=1, source_target_pairs={{0,24},{1,25},{2,26},{3,27},{4,28},{5,29},{6,30},{7,31},{8,16},{9,... | collective-permute-start | bytes 294920 | tf_op jit(solution)/shard_map/ppermute | solution.py:804
  16.8 10.5 %copy-start.16 = (bf16[64,768]{1,0:T(8,128)(2,1)}, bf16[64,768]{1,0:T(8,128)(2,1)S(1)}, u32[]{:S(2)}) copy-start(bf16[64,768]{1,0:T(8,128)(2,1)S(1)} %collective-permute-done.1.refs_2_) | copy-start | bytes 294916
  16.8 10.5 %collective-permute-start.6 = (bf16[64,768]{1,0:T(8,128)(2,1)}, bf16[64,768]{1,0:T(8,128)(2,1)S(1)}, u32[]{:S(2)}, u32[]{:S(2)}) collective-permute-start(bf16[64,768]{1,0:T(8,128)(2,1)} %get-tuple-element.124), channel_id=1, source_target_pairs={{0,28},{1,29},{2,30},{3,31},{4,24},{5,25},{6,26},{7,27},{8,20},{9,... | collective-permute-start | bytes 294920 | tf_op jit(solution)/shard_map/ppermute | solution.py:804
  21.1 6.2 %copy-start.17 = (bf16[64,768]{1,0:T(8,128)(2,1)}, bf16[64,768]{1,0:T(8,128)(2,1)S(1)}, u32[]{:S(2)}) copy-start(bf16[64,768]{1,0:T(8,128)(2,1)S(1)} %collective-permute-done.2.refs_3_) | copy-start | bytes 294916
  21.1 6.2 %copy-start.18 = (bf16[64,768]{1,0:T(8,128)(2,1)}, bf16[64,768]{1,0:T(8,128)(2,1)S(1)}, u32[]{:S(2)}) copy-start(bf16[64,768]{1,0:T(8,128)(2,1)S(1)} %collective-permute-done.3.refs_4_) | copy-start | bytes 294916
  27.3 0.7 copy-start.20
  27.3 0.7 copy-start.21
  28.0 29.6 %copy-start.6 = (s32[256,1]{0,1:T(1,128)S(1)}, s32[256,1]{0,1:T(1,128)}, u32[]{:S(2)}) copy-start(s32[256,1]{0,1:T(1,128)} %param.23) | copy-start | bytes 3076
  28.0 29.8 %copy-start.24 = (bf16[768]{0:T(1024)(128)(2,1)S(1)}, bf16[768]{0:T(1024)(128)(2,1)}, u32[]{:S(2)}) copy-start(bf16[768]{0:T(1024)(128)(2,1)} %param.33) | copy-start | bytes 4612
  28.0 29.8 %copy-start.25 = (bf16[768]{0:T(1024)(128)(2,1)S(1)}, bf16[768]{0:T(1024)(128)(2,1)}, u32[]{:S(2)}) copy-start(bf16[768]{0:T(1024)(128)(2,1)} %param.34) | copy-start | bytes 4612
  28.0 29.8 %copy-start.26 = (bf16[768]{0:T(1024)(128)(2,1)S(1)}, bf16[768]{0:T(1024)(128)(2,1)}, u32[]{:S(2)}) copy-start(bf16[768]{0:T(1024)(128)(2,1)} %param.35) | copy-start | bytes 4612
  28.0 29.8 %copy-start.27 = (bf16[768]{0:T(1024)(128)(2,1)S(1)}, bf16[768]{0:T(1024)(128)(2,1)}, u32[]{:S(2)}) copy-start(bf16[768]{0:T(1024)(128)(2,1)} %param.39) | copy-start | bytes 4612
  28.0 29.9 %copy-start.28 = (bf16[768]{0:T(1024)(128)(2,1)S(1)}, bf16[768]{0:T(1024)(128)(2,1)}, u32[]{:S(2)}) copy-start(bf16[768]{0:T(1024)(128)(2,1)} %param.40) | copy-start | bytes 4612
  28.0 29.9 %copy-start.29 = (bf16[768]{0:T(1024)(128)(2,1)S(1)}, bf16[768]{0:T(1024)(128)(2,1)}, u32[]{:S(2)}) copy-start(bf16[768]{0:T(1024)(128)(2,1)} %param.41) | copy-start | bytes 4612
  28.0 29.9 %copy-start.23 = (bf16[1024]{0:T(1024)(128)(2,1)S(1)}, bf16[1024]{0:T(1024)(128)(2,1)}, u32[]{:S(2)}) copy-start(bf16[1024]{0:T(1024)(128)(2,1)} %param.43) | copy-start | bytes 6148
  28.1 29.9 %copy-start.22 = (bf16[3072]{0:T(1024)(128)(2,1)S(1)}, bf16[3072]{0:T(1024)(128)(2,1)}, u32[]{:S(2)}) copy-start(bf16[3072]{0:T(1024)(128)(2,1)} %param.37) | copy-start | bytes 18436
  28.1 39.6 %copy-start = (bf16[256,768]{1,0:T(8,128)(2,1)S(1)}, bf16[256,768]{1,0:T(8,128)(2,1)}, u32[]{:S(2)}) copy-start(bf16[256,768]{1,0:T(8,128)(2,1)} %refs_8_.4) | copy-start | bytes 1179652
  28.1 39.6 %copy-start.2 = (bf16[256,1024]{1,0:T(8,128)(2,1)S(1)}, bf16[256,1024]{1,0:T(8,128)(2,1)}, u32[]{:S(2)}) copy-start(bf16[256,1024]{1,0:T(8,128)(2,1)} %refs_11_.1) | copy-start | bytes 1572868
  28.1 39.6 %copy-start.3 = (bf16[256,768]{1,0:T(8,128)(2,1)S(1)}, bf16[256,768]{1,0:T(8,128)(2,1)}, u32[]{:S(2)}) copy-start(bf16[256,768]{1,0:T(8,128)(2,1)} %refs_10_.1) | copy-start | bytes 1179652
  44.2 8.7 %collective-permute-start.7 = (bf16[64,768]{1,0:T(8,128)(2,1)}, bf16[64,768]{1,0:T(8,128)(2,1)S(1)}, u32[]{:S(2)}, u32[]{:S(2)}) collective-permute-start(bf16[64,768]{1,0:T(8,128)(2,1)} %get-tuple-element.126), channel_id=1, source_target_pairs={{0,4},{1,5},{2,6},{3,7},{4,0},{5,1},{6,2},{7,3},{8,12},{9,13},{10,... | collective-permute-start | bytes 294920 | tf_op jit(solution)/shard_map/ppermute | solution.py:804
  45.2 10.0 %collective-permute-start.8 = (bf16[64,768]{1,0:T(8,128)(2,1)}, bf16[64,768]{1,0:T(8,128)(2,1)S(1)}, u32[]{:S(2)}, u32[]{:S(2)}) collective-permute-start(bf16[64,768]{1,0:T(8,128)(2,1)} %get-tuple-element.127), channel_id=1, source_target_pairs={{0,8},{1,9},{2,10},{3,11},{4,12},{5,13},{6,14},{7,15},{8,0},{9,1},... | collective-permute-start | bytes 294920 | tf_op jit(solution)/shard_map/ppermute | solution.py:804
  48.8 9.2 %collective-permute-start.9 = (bf16[64,768]{1,0:T(8,128)(2,1)}, bf16[64,768]{1,0:T(8,128)(2,1)S(1)}, u32[]{:S(2)}, u32[]{:S(2)}) collective-permute-start(bf16[64,768]{1,0:T(8,128)(2,1)} %get-tuple-element.128), channel_id=1, source_target_pairs={{0,12},{1,13},{2,14},{3,15},{4,8},{5,9},{6,10},{7,11},{8,4},{9,5},... | collective-permute-start | bytes 294920 | tf_op jit(solution)/shard_map/ppermute | solution.py:804
  49.7 14.8 %collective-permute-start.10 = (bf16[64,768]{1,0:T(8,128)(2,1)}, bf16[64,768]{1,0:T(8,128)(2,1)S(1)}, u32[]{:S(2)}, u32[]{:S(2)}) collective-permute-start(bf16[64,768]{1,0:T(8,128)(2,1)} %get-tuple-element.129), channel_id=1, source_target_pairs={{0,16},{1,17},{2,18},{3,19},{4,20},{5,21},{6,22},{7,23},{8,24},{9,... | collective-permute-start | bytes 294920 | tf_op jit(solution)/shard_map/ppermute | solution.py:804
  52.9 14.1 %collective-permute-start.11 = (bf16[64,768]{1,0:T(8,128)(2,1)}, bf16[64,768]{1,0:T(8,128)(2,1)S(1)}, u32[]{:S(2)}, u32[]{:S(2)}) collective-permute-start(bf16[64,768]{1,0:T(8,128)(2,1)} %get-tuple-element.130), channel_id=1, source_target_pairs={{0,20},{1,21},{2,22},{3,23},{4,16},{5,17},{6,18},{7,19},{8,28},{9,... | collective-permute-start | bytes 294920 | tf_op jit(solution)/shard_map/ppermute | solution.py:804
  52.9 14.1 %copy-start.8 = (bf16[64,768]{1,0:T(8,128)(2,1)}, bf16[64,768]{1,0:T(8,128)(2,1)S(1)}, u32[]{:S(2)}) copy-start(bf16[64,768]{1,0:T(8,128)(2,1)S(1)} %collective-permute-done.7.refs_1_) | copy-start | bytes 294916
  52.9 14.1 %collective-permute-start.12 = (bf16[64,768]{1,0:T(8,128)(2,1)}, bf16[64,768]{1,0:T(8,128)(2,1)S(1)}, u32[]{:S(2)}, u32[]{:S(2)}) collective-permute-start(bf16[64,768]{1,0:T(8,128)(2,1)} %get-tuple-element.131), channel_id=1, source_target_pairs={{0,24},{1,25},{2,26},{3,27},{4,28},{5,29},{6,30},{7,31},{8,16},{9,... | collective-permute-start | bytes 294920 | tf_op jit(solution)/shard_map/ppermute | solution.py:804
  55.3 11.7 %copy-start.9 = (bf16[64,768]{1,0:T(8,128)(2,1)}, bf16[64,768]{1,0:T(8,128)(2,1)S(1)}, u32[]{:S(2)}) copy-start(bf16[64,768]{1,0:T(8,128)(2,1)S(1)} %collective-permute-done.8.refs_2_) | copy-start | bytes 294916
  55.3 11.7 %collective-permute-start.13 = (bf16[64,768]{1,0:T(8,128)(2,1)}, bf16[64,768]{1,0:T(8,128)(2,1)S(1)}, u32[]{:S(2)}, u32[]{:S(2)}) collective-permute-start(bf16[64,768]{1,0:T(8,128)(2,1)} %get-tuple-element.132), channel_id=1, source_target_pairs={{0,28},{1,29},{2,30},{3,31},{4,24},{5,25},{6,26},{7,27},{8,20},{9,... | collective-permute-start | bytes 294920 | tf_op jit(solution)/shard_map/ppermute | solution.py:804
  57.8 36.5 %copy-start.1 = (s32[256,1]{1,0:T(8,128)}, s32[256,1]{1,0:T(8,128)S(1)}, u32[]{:S(2)}) copy-start(s32[256,1]{1,0:T(8,128)S(1)} %copy.46.refs_9_.refs_1_) | copy-start | bytes 3076
  58.0 9.0 %copy-start.10 = (bf16[64,768]{1,0:T(8,128)(2,1)}, bf16[64,768]{1,0:T(8,128)(2,1)S(1)}, u32[]{:S(2)}) copy-start(bf16[64,768]{1,0:T(8,128)(2,1)S(1)} %collective-permute-done.9.refs_3_) | copy-start | bytes 294916
  64.5 2.5 %copy-start.11 = (bf16[64,768]{1,0:T(8,128)(2,1)}, bf16[64,768]{1,0:T(8,128)(2,1)S(1)}, u32[]{:S(2)}) copy-start(bf16[64,768]{1,0:T(8,128)(2,1)S(1)} %collective-permute-done.10.refs_4_) | copy-start | bytes 294916
  67.0 0.7 copy-start.14
  94.3 7.7 %collective-permute-start.15 = (bf16[5344,256]{1,0:T(8,128)(2,1)}, bf16[5344,256]{1,0:T(8,128)(2,1)}, u32[]{:S(2)}, u32[]{:S(2)}) collective-permute-start(bf16[5344,256]{1,0:T(8,128)(2,1)} %get-tuple-element.137.refs_0_.refs_2_), channel_id=1, source_target_pairs={{0,1},{1,0},{2,3},{3,2},{4,5},{5,4},{6,7},{7,6},{8,9},{9,8},{10,11... | collective-permute-start | bytes 8208392 | tf_op jit(solution)/shard_map/ppermute | solution.py:804
  94.4 14.8 %collective-permute-start.14 = (bf16[256,3072]{1,0:T(8,128)(2,1)}, bf16[256,3072]{1,0:T(8,128)(2,1)S(1)}, u32[]{:S(2)}, u32[]{:S(2)}) collective-permute-start(bf16[256,3072]{1,0:T(8,128)(2,1)} %get-tuple-element.136.refs_0_), channel_id=1, source_target_pairs={{0,1},{1,0},{2,3},{3,2},{4,5},{5,4},{6,7},{7,6},{8,9},{9,8},{10,11... | collective-permute-start | bytes 4718600 | tf_op jit(solution)/shard_map/ppermute | solution.py:804
  94.9 27.0 %all-to-all-start = ((bf16[8,64,768]{2,1,0:T(8,128)(2,1)}), bf16[8,64,768]{2,1,0:T(8,128)(2,1)S(1)}, u32[]{:S(2)}, u32[]{:S(2)}) async-start(bf16[8,64,768]{2,1,0:T(8,128)(2,1)} %bitcast.13), calls=%async_computation | async-start | bytes 1572864 | tf_op jit(solution)/shard_map/all_to_all | solution.py:891
  107.6 14.3 %copy-start.4 = (s32[1,512]{1,0:T(1,128)S(1)}, s32[1,512]{1,0:T(1,128)}, u32[]{:S(2)}) copy-start(s32[1,512]{1,0:T(1,128)} %refs_5_.1) | copy-start | bytes 6148
  107.6 35.9 %collective-permute-start.16 = (bf16[4800,128]{1,0:T(8,128)(2,1)}, bf16[4800,128]{1,0:T(8,128)(2,1)}, u32[]{:S(2)}, u32[]{:S(2)}) collective-permute-start(bf16[4800,128]{1,0:T(8,128)(2,1)} %get-tuple-element.139), channel_id=1, source_target_pairs={{0,2},{1,3},{2,0},{3,1},{4,6},{5,7},{6,4},{7,5},{8,10},{9,11},{10,... | collective-permute-start | bytes 3686408 | tf_op jit(solution)/shard_map/ppermute | solution.py:804
  109.1 1.2 copy-start.7
  117.1 26.3 %collective-permute-start.18 = (bf16[3840,128]{1,0:T(8,128)(2,1)}, bf16[3840,128]{1,0:T(8,128)(2,1)}, u32[]{:S(2)}, u32[]{:S(2)}) collective-permute-start(bf16[3840,128]{1,0:T(8,128)(2,1)} %get-tuple-element.153), channel_id=1, source_target_pairs={{0,8},{1,9},{2,10},{3,11},{4,12},{5,13},{6,14},{7,15},{8,0},{9,1},... | collective-permute-start | bytes 2949128 | tf_op jit(solution)/shard_map/ppermute | solution.py:804
  120.9 23.5 %collective-permute-start.17 = (bf16[3840,128]{1,0:T(8,128)(2,1)}, bf16[3840,128]{1,0:T(8,128)(2,1)}, u32[]{:S(2)}, u32[]{:S(2)}) collective-permute-start(bf16[3840,128]{1,0:T(8,128)(2,1)} %get-tuple-element.141), channel_id=1, source_target_pairs={{0,4},{1,5},{2,6},{3,7},{4,0},{5,1},{6,2},{7,3},{8,12},{9,13},{10,... | collective-permute-start | bytes 2949128 | tf_op jit(solution)/shard_map/ppermute | solution.py:804
  143.4 11.6 %collective-permute-start.21 = (bf16[7728,128]{1,0:T(8,128)(2,1)}, bf16[7728,128]{1,0:T(8,128)(2,1)S(1)}, u32[]{:S(2)}, u32[]{:S(2)}) collective-permute-start(bf16[7728,128]{1,0:T(8,128)(2,1)} %get-tuple-element.151), channel_id=1, source_target_pairs={{0,1},{1,0},{2,3},{3,2},{4,5},{5,4},{6,7},{7,6},{8,9},{9,8},{10,11... | collective-permute-start | bytes 5935112 | tf_op jit(solution)/shard_map/ppermute | solution.py:804
  149.3 14.2 %collective-permute-start.20 = (bf16[1920,128]{1,0:T(8,128)(2,1)}, bf16[1920,128]{1,0:T(8,128)(2,1)}, u32[]{:S(2)}, u32[]{:S(2)}) collective-permute-start(bf16[1920,128]{1,0:T(8,128)(2,1)} %get-tuple-element.159), channel_id=1, source_target_pairs={{0,2},{1,3},{2,0},{3,1},{4,6},{5,7},{6,4},{7,5},{8,10},{9,11},{10,... | collective-permute-start | bytes 1474568 | tf_op jit(solution)/shard_map/ppermute | solution.py:804
  149.9 16.6 %collective-permute-start.22 = (bf16[1920,128]{1,0:T(8,128)(2,1)}, bf16[1920,128]{1,0:T(8,128)(2,1)}, u32[]{:S(2)}, u32[]{:S(2)}) collective-permute-start(bf16[1920,128]{1,0:T(8,128)(2,1)} %get-tuple-element.166), channel_id=1, source_target_pairs={{0,4},{1,5},{2,6},{3,7},{4,0},{5,1},{6,2},{7,3},{8,12},{9,13},{10,... | collective-permute-start | bytes 1474568 | tf_op jit(solution)/shard_map/ppermute | solution.py:804
  150.8 28.5 %collective-permute-start.19 = (bf16[2496,128]{1,0:T(8,128)(2,1)}, bf16[2496,128]{1,0:T(8,128)(2,1)S(1)}, u32[]{:S(2)}, u32[]{:S(2)}) collective-permute-start(bf16[2496,128]{1,0:T(8,128)(2,1)} %get-tuple-element.156), channel_id=1, source_target_pairs={{0,8},{1,9},{2,10},{3,11},{4,12},{5,13},{6,14},{7,15},{8,0},{9,1},... | collective-permute-start | bytes 1916936 | tf_op jit(solution)/shard_map/ppermute | solution.py:804
  151.2 55.2 %all-to-all-start.1 = ((bf16[8,64,768]{2,1,0:T(8,128)(2,1)}), bf16[8,64,768]{2,1,0:T(8,128)(2,1)S(1)}, u32[]{:S(2)}, u32[]{:S(2)}) async-start(bf16[8,64,768]{2,1,0:T(8,128)(2,1)} %bitcast.12), calls=%async_computation.1 | async-start | bytes 1572864 | tf_op jit(solution)/shard_map/all_to_all | solution.py:891
  159.1 23.8 %collective-permute-start.25 = (bf16[1968,128]{1,0:T(8,128)(2,1)S(1)}, bf16[1968,128]{1,0:T(8,128)(2,1)S(1)}, u32[]{:S(2)}, u32[]{:S(2)}) collective-permute-start(bf16[1968,128]{1,0:T(8,128)(2,1)S(1)} %get-tuple-element.164), channel_id=1, source_target_pairs={{0,2},{1,3},{2,0},{3,1},{4,6},{5,7},{6,4},{7,5},{8,10},{9,11},{10,... | collective-permute-start | bytes 1511432 | tf_op jit(solution)/shard_map/ppermute | solution.py:804
  163.4 19.5 %collective-permute-start.26 = (bf16[1920,128]{1,0:T(8,128)(2,1)S(1)}, bf16[1920,128]{1,0:T(8,128)(2,1)S(1)}, u32[]{:S(2)}, u32[]{:S(2)}) collective-permute-start(bf16[1920,128]{1,0:T(8,128)(2,1)S(1)} %get-tuple-element.177), channel_id=1, source_target_pairs={{0,4},{1,5},{2,6},{3,7},{4,0},{5,1},{6,2},{7,3},{8,12},{9,13},{10,... | collective-permute-start | bytes 1474568 | tf_op jit(solution)/shard_map/ppermute | solution.py:804
  169.0 18.3 %collective-permute-start.24 = (bf16[960,128]{1,0:T(8,128)(2,1)S(1)}, bf16[960,128]{1,0:T(8,128)(2,1)S(1)}, u32[]{:S(2)}, u32[]{:S(2)}) collective-permute-start(bf16[960,128]{1,0:T(8,128)(2,1)S(1)} %get-tuple-element.167), channel_id=1, source_target_pairs={{0,16},{1,17},{2,18},{3,19},{4,20},{5,21},{6,22},{7,23},{8,24},{9,... | collective-permute-start | bytes 737288 | tf_op jit(solution)/shard_map/ppermute | solution.py:804
  170.5 17.8 %collective-permute-start.27 = (bf16[960,128]{1,0:T(8,128)(2,1)S(1)}, bf16[960,128]{1,0:T(8,128)(2,1)S(1)}, u32[]{:S(2)}, u32[]{:S(2)}) collective-permute-start(bf16[960,128]{1,0:T(8,128)(2,1)S(1)} %get-tuple-element.181), channel_id=1, source_target_pairs={{0,2},{1,3},{2,0},{3,1},{4,6},{5,7},{6,4},{7,5},{8,10},{9,11},{10,... | collective-permute-start | bytes 737288 | tf_op jit(solution)/shard_map/ppermute | solution.py:804
  181.1 10.7 %collective-permute-start.23 = (bf16[1344,128]{1,0:T(8,128)(2,1)S(1)}, bf16[1344,128]{1,0:T(8,128)(2,1)S(1)}, u32[]{:S(2)}, u32[]{:S(2)}) collective-permute-start(bf16[1344,128]{1,0:T(8,128)(2,1)S(1)} %get-tuple-element.171), channel_id=1, source_target_pairs={{0,4},{1,5},{2,6},{3,7},{4,0},{5,1},{6,2},{7,3},{8,12},{9,13},{10,... | collective-permute-start | bytes 1032200 | tf_op jit(solution)/shard_map/ppermute | solution.py:804
  183.7 10.9 %collective-permute-start.28 = (bf16[1008,128]{1,0:T(8,128)(2,1)S(1)}, bf16[1008,128]{1,0:T(8,128)(2,1)S(1)}, u32[]{:S(2)}, u32[]{:S(2)}) collective-permute-start(bf16[1008,128]{1,0:T(8,128)(2,1)S(1)} %get-tuple-element.179), channel_id=1, source_target_pairs={{0,4},{1,5},{2,6},{3,7},{4,0},{5,1},{6,2},{7,3},{8,12},{9,13},{10,... | collective-permute-start | bytes 774152 | tf_op jit(solution)/shard_map/ppermute | solution.py:804
  187.3 7.3 %collective-permute-start.29 = (bf16[960,128]{1,0:T(8,128)(2,1)S(1)}, bf16[960,128]{1,0:T(8,128)(2,1)S(1)}, u32[]{:S(2)}, u32[]{:S(2)}) collective-permute-start(bf16[960,128]{1,0:T(8,128)(2,1)S(1)} %get-tuple-element.191), channel_id=1, source_target_pairs={{0,2},{1,3},{2,0},{3,1},{4,6},{5,7},{6,4},{7,5},{8,10},{9,11},{10,... | collective-permute-start | bytes 737288 | tf_op jit(solution)/shard_map/ppermute | solution.py:804
  189.0 7.3 %collective-permute-start.32 = (bf16[480,128]{1,0:T(8,128)(2,1)S(1)}, bf16[480,128]{1,0:T(8,128)(2,1)S(1)}, u32[]{:S(2)}, u32[]{:S(2)}) collective-permute-start(bf16[480,128]{1,0:T(8,128)(2,1)S(1)} %get-tuple-element.182), channel_id=1, source_target_pairs={{0,8},{1,9},{2,10},{3,11},{4,12},{5,13},{6,14},{7,15},{8,0},{9,1},... | collective-permute-start | bytes 368648 | tf_op jit(solution)/shard_map/ppermute | solution.py:804
  189.1 12.2 %collective-permute-start.33 = (bf16[480,128]{1,0:T(8,128)(2,1)S(1)}, bf16[480,128]{1,0:T(8,128)(2,1)S(1)}, u32[]{:S(2)}, u32[]{:S(2)}) collective-permute-start(bf16[480,128]{1,0:T(8,128)(2,1)S(1)} %get-tuple-element.199), channel_id=1, source_target_pairs={{0,16},{1,17},{2,18},{3,19},{4,20},{5,21},{6,22},{7,23},{8,24},{9,... | collective-permute-start | bytes 368648 | tf_op jit(solution)/shard_map/ppermute | solution.py:804
  192.5 11.7 %collective-permute-start.31 = (bf16[768,128]{1,0:T(8,128)(2,1)S(1)}, bf16[768,128]{1,0:T(8,128)(2,1)S(1)}, u32[]{:S(2)}, u32[]{:S(2)}) collective-permute-start(bf16[768,128]{1,0:T(8,128)(2,1)S(1)} %get-tuple-element.185), channel_id=1, source_target_pairs={{0,16},{1,17},{2,18},{3,19},{4,20},{5,21},{6,22},{7,23},{8,24},{9,... | collective-permute-start | bytes 589832 | tf_op jit(solution)/shard_map/ppermute | solution.py:804
  195.3 10.2 %collective-permute-start.30 = (bf16[1008,128]{1,0:T(8,128)(2,1)S(1)}, bf16[1008,128]{1,0:T(8,128)(2,1)S(1)}, u32[]{:S(2)}, u32[]{:S(2)}) collective-permute-start(bf16[1008,128]{1,0:T(8,128)(2,1)S(1)} %get-tuple-element.194), channel_id=1, source_target_pairs={{0,8},{1,9},{2,10},{3,11},{4,12},{5,13},{6,14},{7,15},{8,0},{9,1},... | collective-permute-start | bytes 774152 | tf_op jit(solution)/shard_map/ppermute | solution.py:804
  206.0 6.8 %collective-permute-start.34 = (bf16[528,128]{1,0:T(8,128)(2,1)S(1)}, bf16[528,128]{1,0:T(8,128)(2,1)S(1)}, u32[]{:S(2)}, u32[]{:S(2)}) collective-permute-start(bf16[528,128]{1,0:T(8,128)(2,1)S(1)} %get-tuple-element.207), channel_id=1, source_target_pairs={{0,16},{1,17},{2,18},{3,19},{4,20},{5,21},{6,22},{7,23},{8,24},{9,... | collective-permute-start | bytes 405512 | tf_op jit(solution)/shard_map/ppermute | solution.py:804
  (3 other events, 1.9 us)
